TPU v7x, 32 devices: a whole 2x2x4 slice. The times are simulated.
32 devices in a mesh: parts: 2 (over y), seq: 8 (over z, x), dp: 2 (over core).
Axes of the slice: x: 2, y: 2, z: 4, core: 2. Of those that a mesh axis runs over, the one named last changes fastest.
Arguments:
- queries: bfloat16 [4, 3072, 1024], P(('parts', 'dp'), 'seq'), parts along dimension 0, may hold values from -6 to 6
- keys: bfloat16 [4, 3072, 1024], P(('parts', 'dp'), 'seq'), parts along dimension 0, may hold values from -6 to 6
- values: bfloat16 [4, 3072, 1024], P(('parts', 'dp'), 'seq'), parts along dimension 0, may hold values from -61 to 61, as said below
- out_weight: bfloat16 [1024, 2048], replicated, may hold values from -0.1875 to 0.1875
- out_grad: bfloat16 [4, 3072, 2048], P(('parts', 'dp'), 'seq'), parts along dimension 0, may hold values from -6 to 6
Outputs:
- output: bfloat16 [4, 3072, 2048], P(('parts', 'dp'), 'seq'), parts along dimension 0
- query_grad: bfloat16 [4, 3072, 1024], P(('parts', 'dp'), 'seq'), parts along dimension 0
- key_grad: bfloat16 [4, 3072, 1024], P(('parts', 'dp'), 'seq'), parts along dimension 0
- value_grad: bfloat16 [4, 3072, 1024], P(('parts', 'dp'), 'seq'), parts along dimension 0
- weight_grad: float32 [2048, 2048], P(('parts', 'seq'), 'dp'), parts along dimension 0
There are 2 independent parts, one for each index of `parts`. A program takes and returns all parts, laid end to end along the dimension named above; an argument that names none is the same for every part. Nothing has to cross between parts.
Inputs may be any that keep to these rules, and one draw needn't show every extreme that they name: `values`: entries are real-valued.
All inputs are finite; a program needn't handle non-finite values.
Results may differ from a plain program's by a relative error of at most 0.0055.
Values sent between devices are 32-bit elements; how exact they have to be, the bound alone decides.
No kernel may reach another device: no remote copies, remote signals or barrier semaphores. Data moves between devices by JAX's collectives and lax.ppermute only.
A program may use at most 128 MiB of HBM per device.

v0:
```python
import math

import jax
import jax.numpy as jnp
from jax import lax
from jax.sharding import PartitionSpec as P

H = 8
HD = 128


EPSILON = 1e-06
PRECISE = lax.Precision.HIGHEST
THREE_PASS = lax.Precision.HIGH


def prefix(x, axis, combine, identity, reverse):
    count, place = (lax.axis_size(axis), lax.axis_index(axis))
    everything = lax.all_gather(x, axis)
    start = jnp.broadcast_to(jnp.asarray(identity, x.dtype), x.shape)

    def turn(k, before):
        at = count - 1 - k if reverse else k
        reached = at > place if reverse else at < place
        new = combine(before, everything[at])
        return jnp.where(reached, new, before)

    return lax.fori_loop(0, count, turn, start)


def add_states(earlier, later):
    return earlier + later


def per_device(queries, keys, values, out_weight, out_grad):
    length = queries.shape[1]
    features = queries.shape[2]
    query_low = queries[0].reshape(length, H, HD)
    key_low = keys[0].reshape(length, H, HD)
    value_low = values[0].reshape(length, H, HD)
    row_index = lax.broadcasted_iota(jnp.int32, (length, length), 0)
    col_index = lax.broadcasted_iota(jnp.int32, (length, length), 1)
    causal = jnp.where(row_index >= col_index, 1.0, 0.0).astype(jnp.float32)
    zero_state = jnp.zeros((H, HD, HD), jnp.float32)
    local_state = jnp.einsum("thd,the->hde", key_low, value_low, preferred_element_type=jnp.float32)
    prior_state = prefix(local_state, "seq", add_states, zero_state, False)
    scores = (
        jnp.einsum("thd,shd->hts", query_low, key_low, preferred_element_type=jnp.float32) * causal
    )
    attended = jnp.einsum(
        "hts,she->the", scores, value_low.astype(jnp.float32), precision=THREE_PASS
    )
    attended = attended + jnp.einsum(
        "thd,hde->the", query_low.astype(jnp.float32), prior_state, precision=PRECISE
    )
    inverse = lax.rsqrt(jnp.mean(attended * attended, axis=-1, keepdims=True) + EPSILON)
    normed = attended * inverse
    normed_b = normed.reshape(length, features).astype(jnp.bfloat16)
    output = jnp.dot(normed_b, out_weight, preferred_element_type=jnp.float32).astype(jnp.bfloat16)
    grad_rows = out_grad[0]
    d_normed = lax.dot_general(
        grad_rows, out_weight, (((1,), (1,)), ((), ())), preferred_element_type=jnp.float32
    )
    d_normed = d_normed.reshape(length, H, HD)
    d_att = inverse * (d_normed - normed * jnp.mean(d_normed * normed, axis=-1, keepdims=True))
    d_att_b = d_att.astype(jnp.bfloat16)
    local_grad = jnp.einsum("thd,the->hde", query_low, d_att_b, preferred_element_type=jnp.float32)
    later_grad = prefix(local_grad, "seq", add_states, zero_state, True)
    cross_terms = (
        jnp.einsum("the,she->hts", d_att_b, value_low, preferred_element_type=jnp.float32) * causal
    )
    query_part = jnp.einsum(
        "hts,shd->thd", cross_terms, key_low.astype(jnp.float32), precision=THREE_PASS
    )
    query_part = query_part + jnp.einsum(
        "the,hde->thd", d_att_b.astype(jnp.float32), prior_state, precision=PRECISE
    )
    key_part = jnp.einsum(
        "hts,thd->shd", cross_terms, query_low.astype(jnp.float32), precision=THREE_PASS
    )
    key_part = key_part + jnp.einsum(
        "she,hde->shd", value_low.astype(jnp.float32), later_grad, precision=PRECISE
    )
    value_part = jnp.einsum(
        "hts,the->she", scores, d_att_b.astype(jnp.float32), precision=THREE_PASS
    )
    value_part = value_part + jnp.einsum(
        "shd,hde->she", key_low.astype(jnp.float32), later_grad, precision=PRECISE
    )
    grad_scale = 1.0 / math.sqrt(length * lax.axis_size("seq") * lax.axis_size("dp"))
    row_block = lax.psum_scatter(
        lax.dot_general(
            normed_b, grad_rows, (((0,), (0,)), ((), ())), preferred_element_type=jnp.float32
        ),
        "seq",
        scatter_dimension=0,
        tiled=True,
    )
    summed = lax.psum_scatter(row_block, "dp", scatter_dimension=1, tiled=True)
    weight_grad = summed * grad_scale
    query_grad = query_part.reshape(1, length, features).astype(jnp.bfloat16)
    key_grad = key_part.reshape(1, length, features).astype(jnp.bfloat16)
    value_grad = value_part.reshape(1, length, features).astype(jnp.bfloat16)
    return (output[None], query_grad, key_grad, value_grad, weight_grad)


def solution(mesh):
    return jax.shard_map(
        per_device,
        mesh=mesh,
        in_specs=(
            P(("parts", "dp"), "seq", None),
            P(("parts", "dp"), "seq", None),
            P(("parts", "dp"), "seq", None),
            P(),
            P(("parts", "dp"), "seq", None),
        ),
        out_specs=(
            P(("parts", "dp"), "seq", None),
            P(("parts", "dp"), "seq", None),
            P(("parts", "dp"), "seq", None),
            P(("parts", "dp"), "seq", None),
            P(("parts", "seq"), "dp"),
        ),
        check_vma=False,
    )
```

profile of v0, /device:TPU:12, one launch (start us, length us, event | category | flops | bytes accessed | tf_op | source)
XLA Modules:
  0.0 366.9 jit_solution(9992587233812412564)
XLA Ops:
  7.2 0.0 copy-start
  7.2 0.0 all-gather.5.cloned.1.call-start
  7.2 1.4 copy.55
  8.7 0.6 copy.33
  9.2 0.3 copy-done.8
  9.5 1.6 copy.56
  11.1 1.2 fusion.34
  12.3 0.0 all-gather.5.cloned.1.call-update
  12.3 0.0 reduce-scatter.3.cloned.1.call-start
  12.4 0.0 copy-start.9
  12.4 1.4 copy.54
  13.9 0.8 copy-done.2
  14.7 2.9 fusion.26
  17.6 68.8 %all-gather.5.cloned.1.call-done = f32[64,128,128]{2,1,0:T(8,128)} async-done(((f32[8,128,128]{2,1,0:T(8,128)}), f32[64,128,128]{2,1,0:T(8,128)}) %all-gather.5.cloned.1.call-update) | async-done | bytes 4194320 | tf_op jit(solution)/shard_map/all_gather | solution.py:19
  86.3 10.0 %while.30 = (s32[]{:T(128)}, f32[8,128,128]{2,1,0:T(8,128)S(1)}, s32[]{:T(128)}, f32[8,8,128,128]{3,2,1,0:T(8,128)}, s32[]{:T(128)}, /*index=5*/s32[]{:T(128)}) while((s32[]{:T(128)}, f32[8,128,128]{2,1,0:T(8,128)S(1)}, s32[]{:T(128)}, f32[8,8,128,128]{3,2,1,0:T(8,128)}, s32[]{:T(128)}, /*index=5*/s32[]{:T(128)}) %tuple.92), condition=%wide.region_1.2_spmd.clone, body=%wide.region_0.1_spmd.clone.sunk | while | flops 393220 | bytes 1572957 | solution.py:28
  86.3 1.2 add_select_fusion.4
  87.6 1.2 add_select_fusion.4
  88.8 1.2 add_select_fusion.4
  90.1 1.2 add_select_fusion.4
  91.3 1.2 add_select_fusion.4
  92.6 1.2 add_select_fusion.4
  93.8 1.2 add_select_fusion.4
  95.1 1.2 add_select_fusion.4
  96.3 2.1 fusion.39
  98.5 4.3 %multiply_reduce_fusion.1 = (f32[384,8]{0,1:T(8,128)S(1)}, f32[384,8,128]{0,2,1:T(8,128)S(1)}) fusion(f32[8,128,384]{2,1,0:T(8,128)S(1)} %fusion.39, bf16[384,8,128]{2,1,0:T(8,128)(2,1)S(1)} %bitcast.69, f32[8,384,384]{2,1,0:T(8,128)} %fusion.26, f32[384,384]{1,0:T(8,128)S(1)} %fusion.28), kind=kOutput, calls=%fused_computation.28 | convolution fusion | flops 908325888 | bytes 9252864 | tf_op jit(solution)/shard_map/hts,she->the/dot_general | solution.py:50
  102.9 2.4 multiply_reduce_fusion
  105.3 1.3 multiply_convert_fusion
  106.6 1.0 copy-done.12
  107.5 5.6 %fusion.17 = f32[1024,2048]{1,0:T(8,128)} fusion(bf16[384,1024]{0,1:T(8,128)(2,1)S(1)} %bitcast.82, bf16[1,384,2048]{2,1,0:T(8,128)(2,1)S(1)} %copy-done), kind=kOutput, calls=%fused_computation.22 | convolution fusion | flops 1610612736 | bytes 10747904 | tf_op jit(solution)/shard_map/dot_general | solution.py:92
  113.1 0.0 reduce-scatter.3.cloned.1.call-update
  113.1 0.0 all-gather.7.cloned.1.call-start
  113.2 1.7 convolution_bitcast_fusion
  114.9 1.0 copy.43
  115.9 0.0 all-gather.7.cloned.1.call-update
  116.0 0.2 reduce-scatter.5.cloned.1.call-start
  116.2 0.0 copy-start.4
  116.2 2.0 fusion.41
  118.2 0.8 fusion.32
  119.1 0.2 copy-done.6
  119.3 0.3 copy-done.11
  119.5 2.6 fusion.14
  122.1 2.3 copy.47
  124.4 5.5 %fusion.4 = f32[8,128,384]{2,1,0:T(8,128)} fusion(bf16[384,8,128]{0,2,1:T(8,128)(2,1)} %get-tuple-element.256, f32[8,384,384]{2,1,0:T(8,128)} %fusion.26, f32[384,384]{1,0:T(8,128)} %copy-done.5), kind=kOutput, calls=%fused_computation.6 | convolution fusion | flops 907149312 | bytes 7667712 | tf_op jit(solution)/shard_map/hts,the->she/dot_general | solution.py:84
  129.9 3.0 fusion.8
  132.9 126.9 %reduce-scatter.3.cloned.1.call-done = f32[128,2048]{1,0:T(8,128)} async-done(((f32[1024,2048]{1,0:T(8,128)}), f32[128,2048]{1,0:T(8,128)}) %reduce-scatter.3.cloned.1.call-update) | async-done | bytes 1048592 | tf_op jit(solution)/shard_map/reduce_scatter | solution.py:91
  259.8 0.0 reduce-scatter.5.cloned.1.call-update
  259.9 76.0 %all-gather.7.cloned.1.call-done = f32[64,128,128]{2,1,0:T(8,128)} async-done(((f32[8,128,128]{2,1,0:T(8,128)}), f32[64,128,128]{2,1,0:T(8,128)}) %all-gather.7.cloned.1.call-update) | async-done | bytes 4194320 | tf_op jit(solution)/shard_map/all_gather | solution.py:19
  335.9 10.1 %while.31 = (s32[]{:T(128)}, f32[8,128,128]{2,1,0:T(8,128)S(1)}, s32[]{:T(128)}, f32[8,8,128,128]{3,2,1,0:T(8,128)}, s32[]{:T(128)}, /*index=5*/s32[]{:T(128)}, s32[]{:T(128)}, s32[]{:T(128)}) while((s32[]{:T(128)}, f32[8,128,128]{2,1,0:T(8,128)S(1)}, s32[]{:T(128)}, f32[8,8,128,128]{3,2,1,0:T(8,128)}, s32[]{:T(128)}, ...), condition=%wide.region_5.6_spmd.clone, body=%wide.region_4.5_spmd.clone.sunk | while | flops 393224 | bytes 1573019 | solution.py:28
  335.9 1.2 add_select_fusion.5
  337.2 1.2 add_select_fusion.5
  338.4 1.2 add_select_fusion.5
  339.7 1.2 add_select_fusion.5
  340.9 1.2 add_select_fusion.5
  342.2 1.2 add_select_fusion.5
  343.5 1.2 add_select_fusion.5
  344.7 1.2 add_select_fusion.5
  346.0 3.5 add_convert_fusion
  349.5 2.3 copy.49
  351.8 1.1 fusion.30
  352.9 0.0 copy-done.3
  353.0 0.2 copy-done.7
  353.1 4.1 %fusion.13 = bf16[384,8,128]{0,2,1:T(8,128)(2,1)S(1)} fusion(f32[8,128,384]{2,1,0:T(8,128)S(1)} %fusion.30, f32[8,384,384]{2,1,0:T(8,128)} %copy-done.1, f32[384,384]{1,0:T(8,128)S(1)} %copy-done.7, bf16[384,8,128]{2,1,0:T(8,128)(2,1)S(1)} %bitcast.75), kind=kOutput, calls=%fused_computation.17 | convolution fusion | flops 907935744 | bytes 8454144 | tf_op jit(solution)/shard_map/hts,thd->shd/dot_general | solution.py:78
  357.3 1.2 copy.48
  358.5 1.9 broadcast_multiply_fusion
  (28 shorter events, 0.1 us)
Async XLA Ops:
  7.2 95.7 %copy-start = (bf16[1,384,2048]{2,1,0:T(8,128)(2,1)S(1)}, bf16[1,384,2048]{2,1,0:T(8,128)(2,1)}, u32[]{:S(2)}) copy-start(bf16[1,384,2048]{2,1,0:T(8,128)(2,1)} %param.13) | copy-start | bytes 4718596
  7.2 79.2 %all-gather.5.cloned.1.call-start = ((), (), s32[]{:S(2)}) async-start(), calls=%async_computation.4 | async-start | bytes 4718592 | tf_op jit(solution)/shard_map/all_gather | solution.py:19
  8.6 0.9 copy-start.8
  9.5 2.8 copy-start.10
  12.3 247.5 %reduce-scatter.3.cloned.1.call-start = ((), (), s32[]{:S(2)}) async-start(), calls=%async_computation.2 | async-start | bytes 9437184 | tf_op jit(solution)/shard_map/reduce_scatter | solution.py:91
  12.4 2.3 copy-start.9
  13.8 0.9 copy-start.2
  13.9 84.6 %copy-start.5 = (f32[384,384]{1,0:T(8,128)}, f32[384,384]{1,0:T(8,128)S(1)}, u32[]{:S(2)}) copy-start(f32[384,384]{1,0:T(8,128)S(1)} %fusion.28) | copy-start | bytes 1769476
  98.5 4.4 %copy-start.14 = (bf16[1024,2048]{1,0:T(8,128)(2,1)S(1)}, bf16[1024,2048]{1,0:T(8,128)(2,1)}, u32[]{:S(2)}) copy-start(bf16[1024,2048]{1,0:T(8,128)(2,1)} %param.12) | copy-start | bytes 12582916
  106.6 1.0 copy-start.12
  113.1 222.8 %all-gather.7.cloned.1.call-start = ((), (), s32[]{:S(2)}) async-start(), calls=%async_computation.5 | async-start | bytes 4718592 | tf_op jit(solution)/shard_map/all_gather | solution.py:19
  116.0 242.5 %reduce-scatter.5.cloned.1.call-start = ((), (), s32[]{:S(2)}) async-start(), calls=%async_computation.3 | async-start | bytes 1572864 | tf_op jit(solution)/shard_map/reduce_scatter | solution.py:99
  116.2 2.0 copy-start.4
  118.2 1.1 copy-start.6
  118.2 1.3 copy-start.11
  119.5 2.6 copy-start.1
  124.4 5.5 %copy-start.13 = (bf16[384,8,128]{0,2,1:T(8,128)(2,1)S(1)}, bf16[384,8,128]{0,2,1:T(8,128)(2,1)}, u32[]{:S(2)}) copy-start(bf16[384,8,128]{0,2,1:T(8,128)(2,1)} %copy-done.12) | copy-start | bytes 2359300
  124.4 5.5 %copy-start.15 = (bf16[1024,2048]{1,0:T(8,128)(2,1)S(1)}, bf16[1024,2048]{1,0:T(8,128)(2,1)}, u32[]{:S(2)}) copy-start(bf16[1024,2048]{1,0:T(8,128)(2,1)} %param.12) | copy-start | bytes 12582916
  351.8 1.1 copy-start.3
  351.8 1.3 copy-start.7
Sparse Core Ops, SparseCore 0:
  12.5 73.8 all-gather.4
  113.3 146.5 reduce-scatter.2
  262.8 73.0 all-gather.6
  338.1 7.7 reduce-scatter.4
where the time goes:
time: 370 us; the launch traced here: 367 us
  waiting for transfers between devices  272 us (74%)
  matrix products  42.9 us (12%)
  other arithmetic  22.9 us (6%)
  local copies, waits for them, and re-layouts  14.5 us (4%)
  between operations  14 us (4%)
    all_gather x2, waiting for transfers between devices, prefix(): everything = lax.all_gather(x, axis)  145 us
    reduce_scatter x1, waiting for transfers between devices, per_device(): lax.psum_scatter(lax.dot_general(normed_b, grad_rows, (((0,), (0,)), ((),...  127 us
    select_n x16, other arithmetic, turn(): return jnp.where(reached, new, before)  19.7 us
    unnamed x38, local copies, waits for them, and re-layouts  12.9 us
  transfers between devices with their start and end apart: 4, of which 3 were waited for; matrix products, arithmetic and copies ran while one was open for 12% of the time, Pallas kernels for 0%

commit v1 on v0

v1 whole, which is shorter than its diff:
```python
import functools
import math

import jax
import jax.numpy as jnp
from jax import lax
from jax.experimental import pallas as pl
from jax.experimental.pallas import tpu as pltpu
from jax.sharding import PartitionSpec as P

H = 8
HD = 128
PAIRS = H // 2
EPSILON = 1e-06
F32 = jnp.float32
BF16 = jnp.bfloat16
VMEM = pltpu.VMEM
VMEM_LIMIT = 48 << 20

NN = (((1,), (0,)), ((), ()))
NT = (((1,), (1,)), ((), ()))
TN = (((0,), (0,)), ((), ()))


def dot(a, b, dims):
    return lax.dot_general(a, b, dims, preferred_element_type=F32)


def halves(a):
    high = a.astype(BF16)
    return high, (a - high.astype(F32)).astype(BF16)


def two_pass(a, b, dims):
    high, low = halves(a)
    return dot(high, b, dims) + dot(low, b, dims)


def two_pass_right(a, b, dims):
    high, low = halves(b)
    return dot(a, high, dims) + dot(a, low, dims)


def causal(length, lower):
    rows = lax.broadcasted_iota(jnp.int32, (length, length), 0)
    cols = lax.broadcasted_iota(jnp.int32, (length, length), 1)
    return rows >= cols if lower else rows <= cols


def lanes(head):
    if isinstance(head, int):
        return pl.ds(head * HD, HD)
    return pl.ds(pl.multiple_of(head * HD, HD), HD)


def call(body, out_shapes, operands, flops, name):
    specs = []
    for operand in operands:
        space = pltpu.SMEM if operand.dtype == jnp.int32 else VMEM
        specs.append(pl.BlockSpec(memory_space=space))
    total = sum(math.prod(o.shape) * o.dtype.itemsize for o in operands)
    total += sum(math.prod(o.shape) * o.dtype.itemsize for o in out_shapes)
    return pl.pallas_call(
        body,
        out_shape=tuple(out_shapes),
        in_specs=specs,
        out_specs=tuple(pl.BlockSpec(memory_space=VMEM) for _ in out_shapes),
        compiler_params=pltpu.CompilerParams(vmem_limit_bytes=VMEM_LIMIT),
        cost_estimate=pl.CostEstimate(flops=flops, bytes_accessed=total, transcendentals=0),
        name=name,
    )(*operands)


def shape(dims, dtype):
    return jax.ShapeDtypeStruct(dims, dtype)


def state_body(place, k_ref, v_ref, keep_ref, send_ref):
    low = place[0]
    for j in range(PAIRS):
        for out, head in ((keep_ref, 2 * j + low), (send_ref, 2 * j + 1 - low)):
            out[j] = dot(k_ref[:, lanes(head)], v_ref[:, lanes(head)], TN)


def local_body(q_ref, k_ref, v_ref, out_ref):
    mask = causal(q_ref.shape[0], True)
    for h in range(H):
        scores = dot(q_ref[:, lanes(h)], k_ref[:, lanes(h)], NT)
        scores = jnp.where(mask, scores, 0.0)
        out_ref[:, lanes(h)] = two_pass(scores, v_ref[:, lanes(h)], NN)


def norm_body(
    place, q_ref, att_ref, dn_ref, own_ref, other_ref, nb_ref, nb32_ref, da_ref, keep_ref, send_ref
):
    low = place[0]
    for j in range(PAIRS):
        for prior, out, head in (
            (own_ref, keep_ref, 2 * j + low),
            (other_ref, send_ref, 2 * j + 1 - low),
        ):
            at = lanes(head)
            q = q_ref[:, at]
            attended = att_ref[:, at] + two_pass_right(q, prior[j], NN)
            inverse = lax.rsqrt(jnp.mean(attended * attended, axis=-1, keepdims=True) + EPSILON)
            normed = attended * inverse
            rounded = normed.astype(BF16)
            nb_ref[:, at] = rounded
            nb32_ref[:, at] = rounded.astype(F32)
            d_normed = dn_ref[:, at]
            mean = jnp.mean(d_normed * normed, axis=-1, keepdims=True)
            d_att = (inverse * (d_normed - normed * mean)).astype(BF16)
            da_ref[:, at] = d_att
            out[j] = dot(q, d_att, TN)


def grads_body(
    place, q_ref, k_ref, v_ref, da_ref, own_ref, other_ref, qg_ref, kl_ref, vl_ref
):
    low = place[0]
    lower = causal(q_ref.shape[0], True)
    upper = causal(q_ref.shape[0], False)
    for j in range(PAIRS):
        for prior, head in ((own_ref, 2 * j + low), (other_ref, 2 * j + 1 - low)):
            at = lanes(head)
            q, k, v, d_att = q_ref[:, at], k_ref[:, at], v_ref[:, at], da_ref[:, at]
            cross = jnp.where(lower, dot(d_att, v, NT), 0.0)
            part = two_pass(cross, k, NN) + two_pass_right(d_att, prior[j], NT)
            qg_ref[:, at] = part.astype(BF16)
            cross = jnp.where(upper, dot(v, d_att, NT), 0.0)
            kl_ref[:, at] = two_pass(cross, q, NN)
            scores = jnp.where(upper, dot(k, q, NT), 0.0)
            vl_ref[:, at] = two_pass(scores, d_att, NN)


def final_body(place, k_ref, v_ref, kl_ref, vl_ref, own_ref, other_ref, kg_ref, vg_ref):
    low = place[0]
    for j in range(PAIRS):
        for later, head in ((own_ref, 2 * j + low), (other_ref, 2 * j + 1 - low)):
            at = lanes(head)
            high, rest = halves(later[j])
            v, k = v_ref[:, at], k_ref[:, at]
            kg_ref[:, at] = (kl_ref[:, at] + (dot(v, high, NT) + dot(v, rest, NT))).astype(BF16)
            vg_ref[:, at] = (vl_ref[:, at] + (dot(k, high, NN) + dot(k, rest, NN))).astype(BF16)


def weight_body(
    rows, place, nb_ref, g_ref, nbo_ref, go_ref, keep0, keep1, send0, send1
):
    low, core = place[0], place[1]
    width = go_ref.shape[1] // 2
    for i, j in enumerate(rows):
        for outs, head in (((keep0, keep1), 2 * j + low), ((send0, send1), 2 * j + 1 - low)):
            mine = nb_ref[:, lanes(head)]
            theirs = nbo_ref[:, lanes(head)].astype(BF16)
            for c in range(2):
                start = pl.multiple_of((core * 2 + c) * width, width)
                ours = g_ref[:, pl.ds(start, width)]
                other = go_ref[:, c * width : (c + 1) * width].astype(BF16)
                outs[c][i] = dot(mine, ours, TN) + dot(theirs, other, TN)


def exclusive(keep, send, count, low, reverse):
    swap = [(s, s ^ 1) for s in range(count)]
    received = lax.ppermute(send, "seq", swap)
    base = keep + received
    pairs = count // 2
    shift = -2 if reverse else 2

    def links(step):
        jump = shift * step
        return [(s, s + jump) for s in range(count) if 0 <= s + jump < count]

    outside = lax.ppermute(base, "seq", links(1))
    step = 1
    total = base + outside
    while 2 * step < pairs:
        step *= 2
        if 2 * step < pairs:
            got = lax.ppermute(total, "seq", links(step))
            outside, total = outside + got, total + got
        else:
            outside = outside + lax.ppermute(total, "seq", links(step))
    first = low == (1 if reverse else 0)
    mine = jnp.where(first, outside, outside + received)
    theirs = jnp.where(first, outside + keep, outside)
    return mine, lax.ppermute(theirs, "seq", swap)


def per_device(queries, keys, values, out_weight, out_grad):
    count = lax.axis_size("seq")
    cores = lax.axis_size("dp")
    spot = lax.axis_index("seq")
    core = lax.axis_index("dp")
    low, level = spot % 2, spot // 2
    q, k, v, g = queries[0], keys[0], values[0], out_grad[0]
    length, features = q.shape
    width = g.shape[1]
    place = jnp.stack([low, core]).astype(jnp.int32)
    state = shape((PAIRS, HD, HD), F32)
    rows32 = shape((length, features), F32)
    rows16 = shape((length, features), BF16)
    unit = 2 * H * length * HD

    keep, send = call(state_body, (state, state), (place, k, v), unit * HD, "state")
    own, other = exclusive(keep, send, count, low, False)

    fast = count == 8 and cores == 2
    half = width // 2
    swap = [(0, 1), (1, 0)]
    if fast:
        away = lax.dynamic_slice_in_dim(g, (1 - core) * half, half, axis=1).astype(F32)
        go = lax.ppermute(away, "dp", swap)
    (att,) = call(local_body, (rows32,), (q, k, v), 3 * unit * length, "local")
    d_normed = lax.dot_general(g, out_weight, NT, preferred_element_type=F32)

    nb, nb32, da, gkeep, gsend = call(
        norm_body,
        (rows16, rows32, rows16, state, state),
        (place, q, att, d_normed, own, other),
        3 * unit * HD,
        "norm",
    )
    own_later, other_later = exclusive(gkeep, gsend, count, low, True)
    scale = 1.0 / math.sqrt(length * count * cores)
    if fast:
        nbo = lax.ppermute(nb32, "dp", swap)
        block = shape((2, HD, half // 2), F32)
        chunks = {}
        for name, rows in (("far", (0, 3)), ("near", (1, 2))):
            out = call(
                functools.partial(weight_body, rows),
                (block,) * 4,
                (place, nb, g, nbo, go),
                2 * length * features * half,
                "weight_" + name,
            )
            for c in range(2):
                chunks[name, c] = out[c], out[2 + c]
        weight_grad = scatter(chunks, level) * scale
    else:
        product = lax.dot_general(nb, g, TN, preferred_element_type=F32)
        product = lax.psum_scatter(product, "dp", scatter_dimension=1, tiled=True)
        weight_grad = lax.psum_scatter(product, "seq", scatter_dimension=0, tiled=True) * scale

    output = jnp.dot(nb, out_weight, preferred_element_type=F32).astype(BF16)
    query_grad, key_local, value_local = call(
        grads_body,
        (rows16, rows32, rows32),
        (place, q, k, v, da, own, other),
        9 * unit * length,
        "grads",
    )
    key_grad, value_grad = call(
        final_body,
        (rows16, rows16),
        (place, k, v, key_local, value_local, own_later, other_later),
        4 * unit * HD,
        "final",
    )
    return output[None], query_grad[None], key_grad[None], value_grad[None], weight_grad


def scatter(chunks, level):
    swap = [(s, s ^ 1) for s in range(8)]

    def on(links):
        return [(2 * a + i, 2 * b + i) for a, b in links for i in range(2)]

    inward = on([(0, 1), (3, 2)])
    middle = on([(1, 2), (2, 1)])
    outward = on([(2, 3), (1, 0)])
    lower = level < 2
    parts = []
    for c in range(2):
        keep, send = chunks["far", c]
        base = keep + lax.ppermute(send, "seq", swap)
        up = jnp.where(lower, base[1], base[0])
        down = jnp.where(lower, base[0], base[1])
        got = lax.ppermute(up, "seq", inward)
        got = lax.ppermute(up + got, "seq", middle)
        got = lax.ppermute(down + got, "seq", outward)
        far = down + got

        keep, send = chunks["near", c]
        base = keep + lax.ppermute(send, "seq", swap)
        up = jnp.where(lower, base[1], base[0])
        down = jnp.where(lower, base[0], base[1])
        got = lax.ppermute(up, "seq", inward)
        direct = lax.ppermute(down, "seq", inward)
        got = lax.ppermute(up + got, "seq", middle)
        near = (down + direct) + got
        outer = (level == 0) | (level == 3)
        parts.append(jnp.where(outer, far, near))
    return jnp.concatenate(parts, axis=1)


def solution(mesh):
    rows = P(("parts", "dp"), "seq", None)
    return jax.shard_map(
        per_device,
        mesh=mesh,
        in_specs=(rows, rows, rows, P(), rows),
        out_specs=(rows, rows, rows, rows, P(("parts", "seq"), "dp")),
        check_vma=False,
    )
```

time: 370 us -> 169 us (0.46)
  waiting for transfers between devices: 272 us -> 69.1 us
  starting transfers between devices: 0.34 us -> 45.3 us
  matrix products: 42.9 us -> 10.6 us
  Pallas kernels: 0 us -> 28.7 us
  other arithmetic: 22.9 us -> 5.61 us
  between operations: 14 us -> 1.14 us
  local copies, waits for them, and re-layouts: 14.5 us -> 5.95 us
    all_gather x2 -> x0, waiting for transfers between devices: 145 us -> none  [prefix(): everything = lax.all_gather(x, axis)]
    reduce_scatter x2 -> x0, waiting for transfers between devices: 127 us -> none  [the longest x1 127 us: per_device(): lax.psum_scatter(lax.dot_general(normed_b, grad_rows, (((0,), (0,)), ((),...]
    ppermute x0 -> x26, waiting for transfers between devices: none -> 69.1 us  [the longest x4 29.5 us: scatter(): base = keep + lax.ppermute(send, 'seq', swap)]
    ppermute x0 -> x26, starting transfers between devices: none -> 45.3 us  [the longest x4 14.7 us: scatter(): got = lax.ppermute(up + got, 'seq', middle)]
    dot_general x15 -> x2, matrix products: 42.9 us -> 10.6 us  [the longest x1 5.43 us: per_device(): output = jnp.dot(nb, out_weight, preferred_element_type=F32).astype(BF16)]
    pallas_call x0 -> x7, Pallas kernels: none -> 28.7 us  [call(): pl.pallas_call(body, out_shape=tuple(out_shapes), in_specs=specs, out_spe...]
    select_n x17 -> x8, other arithmetic: 19.7 us -> 1.57 us  [the longest x2 1.1 us: exclusive(): theirs = jnp.where(first, outside + keep, outside)]
    unnamed x38, local copies, waits for them, and re-layouts: 12.9 us -> 5.95 us
  transfers between devices with their start and end apart: 4 -> 26, of which waited for: 3 -> 12; matrix products, arithmetic and copies ran while one was open for 12% -> 9% of each run, Pallas kernels for 0% -> 17%
where the time goes in v1:
time: 169 us; the launch traced here: 166 us
  waiting for transfers between devices  69.1 us (41%)
  starting transfers between devices  45.3 us (27%)
  Pallas kernels  28.7 us (17%)
  matrix products  10.6 us (6%)
  local copies, waits for them, and re-layouts  5.95 us (4%)
  other arithmetic  5.61 us (3%)
    ppermute x4, waiting for transfers between devices, scatter(): base = keep + lax.ppermute(send, 'seq', swap)  29.5 us
    pallas_call x7, Pallas kernels, call(): pl.pallas_call(body, out_shape=tuple(out_shapes), in_specs=specs, out_spe...  28.7 us
    ppermute x2, waiting for transfers between devices, exclusive(): received = lax.ppermute(send, 'seq', swap)  15 us
    ppermute x4, starting transfers between devices, scatter(): got = lax.ppermute(up + got, 'seq', middle)  14.7 us
    ppermute x2, waiting for transfers between devices, exclusive(): outside = lax.ppermute(base, 'seq', links(1))  8.03 us
    ppermute x2, waiting for transfers between devices, exclusive(): outside = outside + lax.ppermute(total, 'seq', links(step))  7.87 us
    ppermute x4, waiting for transfers between devices, scatter(): got = lax.ppermute(up + got, 'seq', middle)  7.16 us
    ppermute x2, starting transfers between devices, exclusive(): outside = outside + lax.ppermute(total, 'seq', links(step))  5.98 us
  transfers between devices with their start and end apart: 26, of which 12 were waited for; matrix products, arithmetic and copies ran while one was open for 9% of the time, Pallas kernels for 17%

profile of v1, /device:TPU:12, one launch (start us, length us, event | category | flops | bytes accessed | tf_op | source)
XLA Modules:
  0.0 166.4 jit_solution(7451009002126093544)
XLA Ops:
  0.6 0.1 pad_add_fusion.place
  0.7 1.1 copy-done.1
  1.9 1.1 copy-done.3
  3.0 1.1 state.1
  4.1 1.6 collective-permute-start
  5.7 6.6 %collective-permute-done = f32[4,128,128]{2,1,0:T(8,128)S(1)} collective-permute-done((f32[4,128,128]{2,1,0:T(8,128)S(1)}, f32[4,128,128]{2,1,0:T(8,128)S(1)}, u32[]{:S(2)}, u32[]{:S(2)}) %collective-permute-start) | collective-permute-done | bytes 262176 | tf_op jit(solution)/shard_map/ppermute | solution.py:165
  12.3 3.6 %collective-permute-start.1 = (f32[4,128,128]{2,1,0:T(8,128)S(1)}, f32[4,128,128]{2,1,0:T(8,128)S(1)}, u32[]{:S(2)}, u32[]{:S(2)}) collective-permute-start(f32[4,128,128]{2,1,0:T(8,128)S(1)} %add.87), channel_id=1, source_target_pairs={{0,4},{2,6},{4,8},{6,10},{8,12},{10,14},{1,5},{3,7},{5,9},{7,11},{... | collective-permute-start | bytes 786440 | tf_op jit(solution)/shard_map/ppermute | solution.py:174
  15.9 5.6 %collective-permute-done.1 = f32[4,128,128]{2,1,0:T(8,128)S(1)} collective-permute-done((f32[4,128,128]{2,1,0:T(8,128)S(1)}, f32[4,128,128]{2,1,0:T(8,128)S(1)}, u32[]{:S(2)}, u32[]{:S(2)}) %collective-permute-start.1) | collective-permute-done | bytes 262176 | tf_op jit(solution)/shard_map/ppermute | solution.py:174
  21.5 4.5 %collective-permute-start.2 = (f32[4,128,128]{2,1,0:T(8,128)S(1)}, f32[4,128,128]{2,1,0:T(8,128)S(1)}, u32[]{:S(2)}, u32[]{:S(2)}) collective-permute-start(f32[4,128,128]{2,1,0:T(8,128)S(1)} %add.88), channel_id=1, source_target_pairs={{0,8},{2,10},{4,12},{6,14},{1,9},{3,11},{5,13},{7,15},{16,24},{18,... | collective-permute-start | bytes 786440 | tf_op jit(solution)/shard_map/ppermute | solution.py:183
  26.0 1.3 bitcast_convert_fusion
  27.4 7.9 %collective-permute-done.2 = f32[4,128,128]{2,1,0:T(8,128)S(1)} collective-permute-done((f32[4,128,128]{2,1,0:T(8,128)S(1)}, f32[4,128,128]{2,1,0:T(8,128)S(1)}, u32[]{:S(2)}, u32[]{:S(2)}) %collective-permute-start.2) | collective-permute-done | bytes 262176 | tf_op jit(solution)/shard_map/ppermute | solution.py:183
  35.3 0.1 add_select_fusion.2
  35.4 1.6 collective-permute-start.3
  36.9 5.2 %fusion.3.dn_ref = f32[384,1024]{1,0:T(8,128)} fusion(bf16[1024,2048]{1,0:T(8,128)(2,1)} %param.8, bf16[1,384,2048]{2,1,0:T(8,128)(2,1)S(1)} %copy-done), kind=kOutput, calls=%fused_computation.23 | convolution fusion | flops 1610612736 | bytes 7340032 | tf_op jit(solution)/shard_map/dot_general | solution.py:215
  42.1 2.4 %local.1.att_ref = f32[384,1024]{1,0:T(8,128)S(1)} custom-call(bf16[384,1024]{1,0:T(8,128)(2,1)S(1)} %bitcast.55, bf16[384,1024]{1,0:T(8,128)(2,1)S(1)} %bitcast.48, bf16[384,1024]{1,0:T(8,128)(2,1)S(1)} %bitcast.52), custom_call_target="tpu_custom_call" | custom-call | flops 905969664 | bytes 3932160 | tf_op jit(solution)/shard_map/local/pallas_call | solution.py:63
  44.6 1.1 copy-done.5
  45.7 6.9 %norm.1 = (bf16[384,1024]{1,0:T(8,128)(2,1)S(1)}, f32[384,1024]{1,0:T(8,128)}, bf16[384,1024]{1,0:T(8,128)(2,1)S(1)}, f32[4,128,128]{2,1,0:T(8,128)S(1)}, f32[4,128,128]{2,1,0:T(8,128)}) custom-call(s32[2]{0:T(128)S(1)} %pad_add_fusion.place, bf16[384,1024]{1,0:T(8,128)(2,1)S(1)} %bitcast.56, f32[384,1024]{1,0:T(8,128)} %copy-done.5, ...), custom_call_target="tpu_custom_call" | custom-call | flops 301989888 | bytes 8126472 | tf_op jit(solution)/shard_map/norm/pallas_call | solution.py:63
  52.6 0.9 copy-done.8
  53.4 0.7 copy-done.11
  54.2 0.9 copy-done.17
  55.0 0.6 collective-permute-start.4
  55.6 8.4 %collective-permute-done.4 = f32[4,128,128]{2,1,0:T(8,128)} collective-permute-done((f32[4,128,128]{2,1,0:T(8,128)}, f32[4,128,128]{2,1,0:T(8,128)}, u32[]{:S(2)}, u32[]{:S(2)}) %collective-permute-start.4) | collective-permute-done | bytes 262176 | tf_op jit(solution)/shard_map/ppermute | solution.py:165
  64.1 1.1 add.92
  65.1 1.9 %collective-permute-start.5 = (f32[4,128,128]{2,1,0:T(8,128)S(1)}, f32[4,128,128]{2,1,0:T(8,128)S(1)}, u32[]{:S(2)}, u32[]{:S(2)}) collective-permute-start(f32[4,128,128]{2,1,0:T(8,128)S(1)} %add.92), channel_id=1, source_target_pairs={{4,0},{6,2},{8,4},{10,6},{12,8},{14,10},{5,1},{7,3},{9,5},{11,7},{... | collective-permute-start | bytes 786440 | tf_op jit(solution)/shard_map/ppermute | solution.py:174
  67.1 5.4 %fusion = bf16[1,384,2048]{2,1,0:T(8,128)(2,1)} fusion(bf16[384,1024]{1,0:T(8,128)(2,1)} %copy-done.8, bf16[1024,2048]{1,0:T(8,128)(2,1)} %param.8), kind=kOutput, calls=%fused_computation.1 | convolution fusion | flops 1611399168 | bytes 6553600 | tf_op jit(solution)/shard_map/dot_general | solution.py:246
  72.5 2.5 %collective-permute-done.5 = f32[4,128,128]{2,1,0:T(8,128)S(1)} collective-permute-done((f32[4,128,128]{2,1,0:T(8,128)S(1)}, f32[4,128,128]{2,1,0:T(8,128)S(1)}, u32[]{:S(2)}, u32[]{:S(2)}) %collective-permute-start.5) | collective-permute-done | bytes 262176 | tf_op jit(solution)/shard_map/ppermute | solution.py:174
  75.0 1.5 collective-permute-start.6
  76.5 3.2 %weight_far.1 = (f32[2,128,512]{2,1,0:T(8,128)S(1)}, f32[2,128,512]{2,1,0:T(8,128)S(1)}, f32[2,128,512]{2,1,0:T(8,128)S(1)}, f32[2,128,512]{2,1,0:T(8,128)S(1)}) custom-call(s32[2]{0:T(128)S(1)} %pad_add_fusion.place, bf16[384,1024]{1,0:T(8,128)(2,1)S(1)} %copy-done.9, bf16[384,2048]{1,0:T(8,128)(2,1)S(1)} %bitcast.45, ...), custom_call_target="tpu_custom_call" | custom-call | flops 805306368 | bytes 7602184 | tf_op jit(solution)/shard_map/weight_far/pallas_call | solution.py:63
  79.8 0.7 collective-permute-start.10
  80.4 3.2 %weight_near.1 = (f32[2,128,512]{2,1,0:T(8,128)S(1)}, f32[2,128,512]{2,1,0:T(8,128)S(1)}, f32[2,128,512]{2,1,0:T(8,128)S(1)}, f32[2,128,512]{2,1,0:T(8,128)S(1)}) custom-call(s32[2]{0:T(128)S(1)} %pad_add_fusion.place, bf16[384,1024]{1,0:T(8,128)(2,1)S(1)} %copy-done.9, bf16[384,2048]{1,0:T(8,128)(2,1)S(1)} %bitcast.46, ...), custom_call_target="tpu_custom_call" | custom-call | flops 805306368 | bytes 7602184 | tf_op jit(solution)/shard_map/weight_near/pallas_call | solution.py:63
  83.7 1.5 collective-permute-start.14
  85.2 9.1 %grads.1 = (bf16[384,1024]{1,0:T(8,128)(2,1)}, f32[384,1024]{1,0:T(8,128)S(1)}, f32[384,1024]{1,0:T(8,128)}) custom-call(s32[2]{0:T(128)S(1)} %pad_add_fusion.place, bf16[384,1024]{1,0:T(8,128)(2,1)S(1)} %bitcast.57, bf16[384,1024]{1,0:T(8,128)(2,1)S(1)} %bitcast.49, bf16[384,1024]{1,0:T(8,128)(2,1)S(1)} %bitcast.53, bf16[384,1024]{1,0:T(8,128)(2,1)S(1)} %copy-done.18, ...), custom_call_target="tpu_custom_call" | custom-call | flops 2717908992 | bytes 7602184 | tf_op jit(solution)/shard_map/grads/pallas_call | solution.py:63
  94.2 0.6 collective-permute-start.18
  94.9 1.0 add_select_fusion
  95.9 1.5 collective-permute-start.7
  97.4 0.6 collective-permute-start.22
  98.0 0.1 add.98
  98.1 1.3 collective-permute-start.11
  99.4 6.5 %collective-permute-done.14 = f32[2,128,512]{2,1,0:T(8,128)S(1)} collective-permute-done((f32[2,128,512]{2,1,0:T(8,128)S(1)}, f32[2,128,512]{2,1,0:T(8,128)S(1)}, u32[]{:S(2)}, u32[]{:S(2)}) %collective-permute-start.14) | collective-permute-done | bytes 524320 | tf_op jit(solution)/shard_map/ppermute | solution.py:286
  105.9 0.1 add.102
  106.1 1.3 collective-permute-start.16
  107.4 9.8 %collective-permute-done.18 = f32[2,128,512]{2,1,0:T(8,128)S(1)} collective-permute-done((f32[2,128,512]{2,1,0:T(8,128)S(1)}, f32[2,128,512]{2,1,0:T(8,128)S(1)}, u32[]{:S(2)}, u32[]{:S(2)}) %collective-permute-start.18) | collective-permute-done | bytes 524320 | tf_op jit(solution)/shard_map/ppermute | solution.py:277
  117.2 1.3 collective-permute-start.15
  118.5 0.1 add.106
  118.6 13.2 %collective-permute-done.22 = f32[2,128,512]{2,1,0:T(8,128)S(1)} collective-permute-done((f32[2,128,512]{2,1,0:T(8,128)S(1)}, f32[2,128,512]{2,1,0:T(8,128)S(1)}, u32[]{:S(2)}, u32[]{:S(2)}) %collective-permute-start.22) | collective-permute-done | bytes 524320 | tf_op jit(solution)/shard_map/ppermute | solution.py:286
  131.8 1.3 collective-permute-start.19
  133.1 0.1 add.110
  133.3 4.3 %collective-permute-start.12 = (f32[128,512]{1,0:T(8,128)S(1)}, f32[128,512]{1,0:T(8,128)S(1)}, u32[]{:S(2)}, u32[]{:S(2)}) collective-permute-start(f32[128,512]{1,0:T(8,128)S(1)} %fusion.8), channel_id=1, source_target_pairs={{4,8},{6,10},{8,4},{10,6},{5,9},{7,11},{9,5},{11,7},{20,24},{22,26... | collective-permute-start | bytes 786440 | tf_op jit(solution)/shard_map/ppermute | solution.py:281
  137.7 1.4 collective-permute-start.24
  139.1 1.0 collective-permute-done.19
  140.1 6.6 %collective-permute-start.17 = (f32[128,512]{1,0:T(8,128)S(1)}, f32[128,512]{1,0:T(8,128)S(1)}, u32[]{:S(2)}, u32[]{:S(2)}) collective-permute-start(f32[128,512]{1,0:T(8,128)S(1)} %add.104), channel_id=1, source_target_pairs={{4,8},{6,10},{8,4},{10,6},{5,9},{7,11},{9,5},{11,7},{20,24},{22,26... | collective-permute-start | bytes 786440 | tf_op jit(solution)/shard_map/ppermute | solution.py:291
  146.7 0.1 fusion.9
  146.8 1.9 %collective-permute-start.20 = (f32[128,512]{1,0:T(8,128)S(1)}, f32[128,512]{1,0:T(8,128)S(1)}, u32[]{:S(2)}, u32[]{:S(2)}) collective-permute-start(f32[128,512]{1,0:T(8,128)S(1)} %fusion.9), channel_id=1, source_target_pairs={{4,8},{6,10},{8,4},{10,6},{5,9},{7,11},{9,5},{11,7},{20,24},{22,26... | collective-permute-start | bytes 786440 | tf_op jit(solution)/shard_map/ppermute | solution.py:281
  148.8 1.3 collective-permute-start.13
  150.1 2.8 %final.1 = (bf16[384,1024]{1,0:T(8,128)(2,1)}, bf16[384,1024]{1,0:T(8,128)(2,1)}) custom-call(s32[2]{0:T(128)S(1)} %pad_add_fusion.place, bf16[384,1024]{1,0:T(8,128)(2,1)S(1)} %bitcast.50, bf16[384,1024]{1,0:T(8,128)(2,1)S(1)} %bitcast.54, f32[384,1024]{1,0:T(8,128)S(1)} %get-tuple-element.30.kl_ref, f32[384,1024]{1,0:T(8,128)S(1)} %copy-done.10, ...), custom_call_target="tpu_custom_call" | custom-call | flops 402653184 | bytes 6815752 | tf_op jit(solution)/shard_map/final/pallas_call | solution.py:63
  152.9 1.3 collective-permute-start.23
  154.2 2.9 %collective-permute-done.20 = f32[128,512]{1,0:T(8,128)S(1)} collective-permute-done((f32[128,512]{1,0:T(8,128)S(1)}, f32[128,512]{1,0:T(8,128)S(1)}, u32[]{:S(2)}, u32[]{:S(2)}) %collective-permute-start.20) | collective-permute-done | bytes 262176 | tf_op jit(solution)/shard_map/ppermute | solution.py:281
  157.1 1.9 %collective-permute-start.25 = (f32[128,512]{1,0:T(8,128)S(1)}, f32[128,512]{1,0:T(8,128)S(1)}, u32[]{:S(2)}, u32[]{:S(2)}) collective-permute-start(f32[128,512]{1,0:T(8,128)S(1)} %add.112), channel_id=1, source_target_pairs={{4,8},{6,10},{8,4},{10,6},{5,9},{7,11},{9,5},{11,7},{20,24},{22,26... | collective-permute-start | bytes 786440 | tf_op jit(solution)/shard_map/ppermute | solution.py:291
  159.1 1.3 collective-permute-start.21
  160.5 0.2 fusion.2
  160.6 0.5 collective-permute-done.23
  161.2 4.2 %collective-permute-done.25 = f32[128,512]{1,0:T(8,128)S(1)} collective-permute-done((f32[128,512]{1,0:T(8,128)S(1)}, f32[128,512]{1,0:T(8,128)S(1)}, u32[]{:S(2)}, u32[]{:S(2)}) %collective-permute-start.25) | collective-permute-done | bytes 262176 | tf_op jit(solution)/shard_map/ppermute | solution.py:291
  165.4 0.2 fusion.1
  165.6 0.8 maximum_multiply_fusion
  (60 shorter events, 0.6 us)
Async XLA Ops:
  0.7 1.1 copy-start.1
  1.9 1.1 copy-start.3
  3.0 23.0 %copy-start = (bf16[1,384,2048]{2,1,0:T(8,128)(2,1)S(1)}, bf16[1,384,2048]{2,1,0:T(8,128)(2,1)}, u32[]{:S(2)}) copy-start(bf16[1,384,2048]{2,1,0:T(8,128)(2,1)} %param.9) | copy-start | bytes 4718596
  4.1 8.1 %copy-start.13 = (f32[4,128,128]{2,1,0:T(8,128)}, f32[4,128,128]{2,1,0:T(8,128)S(1)}, u32[]{:S(2)}) copy-start(f32[4,128,128]{2,1,0:T(8,128)S(1)} %get-tuple-element.25) | copy-start | bytes 786436
  4.1 8.1 %collective-permute-start = (f32[4,128,128]{2,1,0:T(8,128)S(1)}, f32[4,128,128]{2,1,0:T(8,128)S(1)}, u32[]{:S(2)}, u32[]{:S(2)}) collective-permute-start(f32[4,128,128]{2,1,0:T(8,128)S(1)} %get-tuple-element.26), channel_id=1, source_target_pairs={{0,2},{2,0},{4,6},{6,4},{8,10},{10,8},{12,14},{14,12},{1,3},{3,1},... | collective-permute-start | bytes 786440 | tf_op jit(solution)/shard_map/ppermute | solution.py:165
  12.3 23.0 %copy-start.14 = (f32[4,128,128]{2,1,0:T(8,128)S(1)}, f32[4,128,128]{2,1,0:T(8,128)}, u32[]{:S(2)}) copy-start(f32[4,128,128]{2,1,0:T(8,128)} %copy-done.13) | copy-start | bytes 786436
  12.3 9.2 %collective-permute-start.1 = (f32[4,128,128]{2,1,0:T(8,128)S(1)}, f32[4,128,128]{2,1,0:T(8,128)S(1)}, u32[]{:S(2)}, u32[]{:S(2)}) collective-permute-start(f32[4,128,128]{2,1,0:T(8,128)S(1)} %add.87), channel_id=1, source_target_pairs={{0,4},{2,6},{4,8},{6,10},{8,12},{10,14},{1,5},{3,7},{5,9},{7,11},{... | collective-permute-start | bytes 786440 | tf_op jit(solution)/shard_map/ppermute | solution.py:174
  21.5 13.7 %collective-permute-start.2 = (f32[4,128,128]{2,1,0:T(8,128)S(1)}, f32[4,128,128]{2,1,0:T(8,128)S(1)}, u32[]{:S(2)}, u32[]{:S(2)}) collective-permute-start(f32[4,128,128]{2,1,0:T(8,128)S(1)} %add.88), channel_id=1, source_target_pairs={{0,8},{2,10},{4,12},{6,14},{1,9},{3,11},{5,13},{7,15},{16,24},{18,... | collective-permute-start | bytes 786440 | tf_op jit(solution)/shard_map/ppermute | solution.py:183
  27.4 49.1 %collective-permute-start.9 = (f32[384,1024]{1,0:T(8,128)}, f32[384,1024]{1,0:T(8,128)}, u32[]{:S(2)}, u32[]{:S(2)}) collective-permute-start(f32[384,1024]{1,0:T(8,128)} %bitcast_convert_fusion), channel_id=1, source_target_pairs={{0,1},{1,0},{2,3},{3,2},{4,5},{5,4},{6,7},{7,6},{8,9},{9,8},{10,11... | collective-permute-start | bytes 4718600 | tf_op jit(solution)/shard_map/ppermute | solution.py:213
  35.3 6.8 %copy-start.2 = (bf16[1,384,1024]{2,1,0:T(8,128)(2,1)S(1)}, bf16[1,384,1024]{2,1,0:T(8,128)(2,1)}, u32[]{:S(2)}) copy-start(bf16[1,384,1024]{2,1,0:T(8,128)(2,1)} %param.6) | copy-start | bytes 2359300
  35.3 6.8 %copy-start.4 = (bf16[1,384,1024]{2,1,0:T(8,128)(2,1)S(1)}, bf16[1,384,1024]{2,1,0:T(8,128)(2,1)}, u32[]{:S(2)}) copy-start(bf16[1,384,1024]{2,1,0:T(8,128)(2,1)} %param.7) | copy-start | bytes 2359300
  35.3 6.8 %copy-start.6 = (bf16[1,384,1024]{2,1,0:T(8,128)(2,1)S(1)}, bf16[1,384,1024]{2,1,0:T(8,128)(2,1)}, u32[]{:S(2)}) copy-start(bf16[1,384,1024]{2,1,0:T(8,128)(2,1)} %param.5) | copy-start | bytes 2359300
  35.4 10.3 %collective-permute-start.3 = (f32[4,128,128]{2,1,0:T(8,128)S(1)}, f32[4,128,128]{2,1,0:T(8,128)S(1)}, u32[]{:S(2)}, u32[]{:S(2)}) collective-permute-start(f32[4,128,128]{2,1,0:T(8,128)S(1)} %get-tuple-element.51), channel_id=1, source_target_pairs={{0,2},{2,0},{4,6},{6,4},{8,10},{10,8},{12,14},{14,12},{1,3},{3,1},... | collective-permute-start | bytes 786440 | tf_op jit(solution)/shard_map/ppermute | solution.py:187
  44.6 1.1 copy-start.5
  45.7 6.9 %copy-start.15 = (f32[4,128,128]{2,1,0:T(8,128)}, f32[4,128,128]{2,1,0:T(8,128)S(1)}, u32[]{:S(2)}) copy-start(f32[4,128,128]{2,1,0:T(8,128)S(1)} %collective-permute-done.3.other_ref) | copy-start | bytes 786436
  52.6 0.9 copy-start.8
  53.4 0.7 copy-start.11
  54.2 0.9 copy-start.17
  55.0 21.5 %collective-permute-start.8 = (f32[384,1024]{1,0:T(8,128)}, f32[384,1024]{1,0:T(8,128)}, u32[]{:S(2)}, u32[]{:S(2)}) collective-permute-start(f32[384,1024]{1,0:T(8,128)} %get-tuple-element.36), channel_id=1, source_target_pairs={{0,1},{1,0},{2,3},{3,2},{4,5},{5,4},{6,7},{7,6},{8,9},{9,8},{10,11... | collective-permute-start | bytes 4718600 | tf_op jit(solution)/shard_map/ppermute | solution.py:227
  55.0 9.0 %collective-permute-start.4 = (f32[4,128,128]{2,1,0:T(8,128)}, f32[4,128,128]{2,1,0:T(8,128)}, u32[]{:S(2)}, u32[]{:S(2)}) collective-permute-start(f32[4,128,128]{2,1,0:T(8,128)} %get-tuple-element.33), channel_id=1, source_target_pairs={{0,2},{2,0},{4,6},{6,4},{8,10},{10,8},{12,14},{14,12},{1,3},{3,1},... | collective-permute-start | bytes 786440 | tf_op jit(solution)/shard_map/ppermute | solution.py:165
  65.1 9.8 %collective-permute-start.5 = (f32[4,128,128]{2,1,0:T(8,128)S(1)}, f32[4,128,128]{2,1,0:T(8,128)S(1)}, u32[]{:S(2)}, u32[]{:S(2)}) collective-permute-start(f32[4,128,128]{2,1,0:T(8,128)S(1)} %add.92), channel_id=1, source_target_pairs={{4,0},{6,2},{8,4},{10,6},{12,8},{14,10},{5,1},{7,3},{9,5},{11,7},{... | collective-permute-start | bytes 786440 | tf_op jit(solution)/shard_map/ppermute | solution.py:174
  67.1 9.4 %copy-start.9 = (bf16[384,1024]{1,0:T(8,128)(2,1)S(1)}, bf16[384,1024]{1,0:T(8,128)(2,1)}, u32[]{:S(2)}) copy-start(bf16[384,1024]{1,0:T(8,128)(2,1)} %copy-done.8) | copy-start | bytes 2359300
  75.0 19.9 %collective-permute-start.6 = (f32[4,128,128]{2,1,0:T(8,128)S(1)}, f32[4,128,128]{2,1,0:T(8,128)S(1)}, u32[]{:S(2)}, u32[]{:S(2)}) collective-permute-start(f32[4,128,128]{2,1,0:T(8,128)S(1)} %add.93), channel_id=1, source_target_pairs={{8,0},{10,2},{12,4},{14,6},{9,1},{11,3},{13,5},{15,7},{24,16},{26,... | collective-permute-start | bytes 786440 | tf_op jit(solution)/shard_map/ppermute | solution.py:183
  79.7 5.4 %copy-start.7 = (bf16[1,384,1024]{2,1,0:T(8,128)(2,1)S(1)}, bf16[1,384,1024]{2,1,0:T(8,128)(2,1)}, u32[]{:S(2)}) copy-start(bf16[1,384,1024]{2,1,0:T(8,128)(2,1)} %param.5) | copy-start | bytes 2359300
  79.8 5.4 %copy-start.16 = (f32[4,128,128]{2,1,0:T(8,128)S(1)}, f32[4,128,128]{2,1,0:T(8,128)}, u32[]{:S(2)}) copy-start(f32[4,128,128]{2,1,0:T(8,128)} %copy-done.15) | copy-start | bytes 786436
  79.8 5.4 %copy-start.18 = (bf16[384,1024]{1,0:T(8,128)(2,1)S(1)}, bf16[384,1024]{1,0:T(8,128)(2,1)}, u32[]{:S(2)}) copy-start(bf16[384,1024]{1,0:T(8,128)(2,1)} %copy-done.17) | copy-start | bytes 2359300
  79.8 18.2 %collective-permute-start.10 = (f32[2,128,512]{2,1,0:T(8,128)S(1)}, f32[2,128,512]{2,1,0:T(8,128)S(1)}, u32[]{:S(2)}, u32[]{:S(2)}) collective-permute-start(f32[2,128,512]{2,1,0:T(8,128)S(1)} %get-tuple-element.38), channel_id=1, source_target_pairs={{0,2},{2,0},{4,6},{6,4},{8,10},{10,8},{12,14},{14,12},{1,3},{3,1},... | collective-permute-start | bytes 1572872 | tf_op jit(solution)/shard_map/ppermute | solution.py:277
  83.7 22.3 %collective-permute-start.14 = (f32[2,128,512]{2,1,0:T(8,128)S(1)}, f32[2,128,512]{2,1,0:T(8,128)S(1)}, u32[]{:S(2)}, u32[]{:S(2)}) collective-permute-start(f32[2,128,512]{2,1,0:T(8,128)S(1)} %get-tuple-element.40), channel_id=1, source_target_pairs={{0,2},{2,0},{4,6},{6,4},{8,10},{10,8},{12,14},{14,12},{1,3},{3,1},... | collective-permute-start | bytes 1572872 | tf_op jit(solution)/shard_map/ppermute | solution.py:286
  85.2 9.7 %copy-start.12 = (f32[4,128,128]{2,1,0:T(8,128)S(1)}, f32[4,128,128]{2,1,0:T(8,128)}, u32[]{:S(2)}) copy-start(f32[4,128,128]{2,1,0:T(8,128)} %copy-done.11) | copy-start | bytes 786436
  94.2 22.9 %collective-permute-start.18 = (f32[2,128,512]{2,1,0:T(8,128)S(1)}, f32[2,128,512]{2,1,0:T(8,128)S(1)}, u32[]{:S(2)}, u32[]{:S(2)}) collective-permute-start(f32[2,128,512]{2,1,0:T(8,128)S(1)} %get-tuple-element.42), channel_id=1, source_target_pairs={{0,2},{2,0},{4,6},{6,4},{8,10},{10,8},{12,14},{14,12},{1,3},{3,1},... | collective-permute-start | bytes 1572872 | tf_op jit(solution)/shard_map/ppermute | solution.py:277
  95.9 52.8 %collective-permute-start.7 = (f32[4,128,128]{2,1,0:T(8,128)S(1)}, f32[4,128,128]{2,1,0:T(8,128)S(1)}, u32[]{:S(2)}, u32[]{:S(2)}) collective-permute-start(f32[4,128,128]{2,1,0:T(8,128)S(1)} %get-tuple-element.49), channel_id=1, source_target_pairs={{0,2},{2,0},{4,6},{6,4},{8,10},{10,8},{12,14},{14,12},{1,3},{3,1},... | collective-permute-start | bytes 786440 | tf_op jit(solution)/shard_map/ppermute | solution.py:187
  97.4 34.4 %collective-permute-start.22 = (f32[2,128,512]{2,1,0:T(8,128)S(1)}, f32[2,128,512]{2,1,0:T(8,128)S(1)}, u32[]{:S(2)}, u32[]{:S(2)}) collective-permute-start(f32[2,128,512]{2,1,0:T(8,128)S(1)} %get-tuple-element.44), channel_id=1, source_target_pairs={{0,2},{2,0},{4,6},{6,4},{8,10},{10,8},{12,14},{14,12},{1,3},{3,1},... | collective-permute-start | bytes 1572872 | tf_op jit(solution)/shard_map/ppermute | solution.py:286
  98.1 35.1 %collective-permute-start.11 = (f32[128,512]{1,0:T(8,128)S(1)}, f32[128,512]{1,0:T(8,128)S(1)}, u32[]{:S(2)}, u32[]{:S(2)}) collective-permute-start(f32[128,512]{1,0:T(8,128)S(1)} %select_bitcast_fusion.5), channel_id=1, source_target_pairs={{0,4},{2,6},{12,8},{14,10},{1,5},{3,7},{13,9},{15,11},{16,20},{18,... | collective-permute-start | bytes 786440 | tf_op jit(solution)/shard_map/ppermute | solution.py:280
  106.1 31.6 %collective-permute-start.16 = (f32[128,512]{1,0:T(8,128)S(1)}, f32[128,512]{1,0:T(8,128)S(1)}, u32[]{:S(2)}, u32[]{:S(2)}) collective-permute-start(f32[128,512]{1,0:T(8,128)S(1)} %get-tuple-element.46), channel_id=1, source_target_pairs={{0,4},{2,6},{12,8},{14,10},{1,5},{3,7},{13,9},{15,11},{16,20},{18,... | collective-permute-start | bytes 786440 | tf_op jit(solution)/shard_map/ppermute | solution.py:289
  117.2 41.9 %collective-permute-start.15 = (f32[128,512]{1,0:T(8,128)S(1)}, f32[128,512]{1,0:T(8,128)S(1)}, u32[]{:S(2)}, u32[]{:S(2)}) collective-permute-start(f32[128,512]{1,0:T(8,128)S(1)} %get-tuple-element.45), channel_id=1, source_target_pairs={{0,4},{2,6},{12,8},{14,10},{1,5},{3,7},{13,9},{15,11},{16,20},{18,... | collective-permute-start | bytes 786440 | tf_op jit(solution)/shard_map/ppermute | solution.py:290
  131.8 8.3 %collective-permute-start.19 = (f32[128,512]{1,0:T(8,128)S(1)}, f32[128,512]{1,0:T(8,128)S(1)}, u32[]{:S(2)}, u32[]{:S(2)}) collective-permute-start(f32[128,512]{1,0:T(8,128)S(1)} %select_bitcast_fusion.2), channel_id=1, source_target_pairs={{0,4},{2,6},{12,8},{14,10},{1,5},{3,7},{13,9},{15,11},{16,20},{18,... | collective-permute-start | bytes 786440 | tf_op jit(solution)/shard_map/ppermute | solution.py:280
  133.3 13.5 %collective-permute-start.12 = (f32[128,512]{1,0:T(8,128)S(1)}, f32[128,512]{1,0:T(8,128)S(1)}, u32[]{:S(2)}, u32[]{:S(2)}) collective-permute-start(f32[128,512]{1,0:T(8,128)S(1)} %fusion.8), channel_id=1, source_target_pairs={{4,8},{6,10},{8,4},{10,6},{5,9},{7,11},{9,5},{11,7},{20,24},{22,26... | collective-permute-start | bytes 786440 | tf_op jit(solution)/shard_map/ppermute | solution.py:281
  137.7 12.4 %copy-start.10 = (f32[384,1024]{1,0:T(8,128)S(1)}, f32[384,1024]{1,0:T(8,128)}, u32[]{:S(2)}) copy-start(f32[384,1024]{1,0:T(8,128)} %get-tuple-element.31.vl_ref) | copy-start | bytes 4718596
  137.7 15.2 %collective-permute-start.24 = (f32[128,512]{1,0:T(8,128)S(1)}, f32[128,512]{1,0:T(8,128)S(1)}, u32[]{:S(2)}, u32[]{:S(2)}) collective-permute-start(f32[128,512]{1,0:T(8,128)S(1)} %get-tuple-element.48), channel_id=1, source_target_pairs={{0,4},{2,6},{12,8},{14,10},{1,5},{3,7},{13,9},{15,11},{16,20},{18,... | collective-permute-start | bytes 786440 | tf_op jit(solution)/shard_map/ppermute | solution.py:289
  140.1 20.3 %collective-permute-start.17 = (f32[128,512]{1,0:T(8,128)S(1)}, f32[128,512]{1,0:T(8,128)S(1)}, u32[]{:S(2)}, u32[]{:S(2)}) collective-permute-start(f32[128,512]{1,0:T(8,128)S(1)} %add.104), channel_id=1, source_target_pairs={{4,8},{6,10},{8,4},{10,6},{5,9},{7,11},{9,5},{11,7},{20,24},{22,26... | collective-permute-start | bytes 786440 | tf_op jit(solution)/shard_map/ppermute | solution.py:291
  146.8 10.4 %collective-permute-start.20 = (f32[128,512]{1,0:T(8,128)S(1)}, f32[128,512]{1,0:T(8,128)S(1)}, u32[]{:S(2)}, u32[]{:S(2)}) collective-permute-start(f32[128,512]{1,0:T(8,128)S(1)} %fusion.9), channel_id=1, source_target_pairs={{4,8},{6,10},{8,4},{10,6},{5,9},{7,11},{9,5},{11,7},{20,24},{22,26... | collective-permute-start | bytes 786440 | tf_op jit(solution)/shard_map/ppermute | solution.py:281
  148.8 11.7 %collective-permute-start.13 = (f32[128,512]{1,0:T(8,128)S(1)}, f32[128,512]{1,0:T(8,128)S(1)}, u32[]{:S(2)}, u32[]{:S(2)}) collective-permute-start(f32[128,512]{1,0:T(8,128)S(1)} %bitcast_add_fusion.3), channel_id=1, source_target_pairs={{8,12},{10,14},{4,0},{6,2},{9,13},{11,15},{5,1},{7,3},{24,28},{26,... | collective-permute-start | bytes 786440 | tf_op jit(solution)/shard_map/ppermute | solution.py:282
  152.9 8.3 %collective-permute-start.23 = (f32[128,512]{1,0:T(8,128)S(1)}, f32[128,512]{1,0:T(8,128)S(1)}, u32[]{:S(2)}, u32[]{:S(2)}) collective-permute-start(f32[128,512]{1,0:T(8,128)S(1)} %get-tuple-element.47), channel_id=1, source_target_pairs={{0,4},{2,6},{12,8},{14,10},{1,5},{3,7},{13,9},{15,11},{16,20},{18,... | collective-permute-start | bytes 786440 | tf_op jit(solution)/shard_map/ppermute | solution.py:290
  157.1 8.3 %collective-permute-start.25 = (f32[128,512]{1,0:T(8,128)S(1)}, f32[128,512]{1,0:T(8,128)S(1)}, u32[]{:S(2)}, u32[]{:S(2)}) collective-permute-start(f32[128,512]{1,0:T(8,128)S(1)} %add.112), channel_id=1, source_target_pairs={{4,8},{6,10},{8,4},{10,6},{5,9},{7,11},{9,5},{11,7},{20,24},{22,26... | collective-permute-start | bytes 786440 | tf_op jit(solution)/shard_map/ppermute | solution.py:291
  159.1 6.3 %collective-permute-start.21 = (f32[128,512]{1,0:T(8,128)S(1)}, f32[128,512]{1,0:T(8,128)S(1)}, u32[]{:S(2)}, u32[]{:S(2)}) collective-permute-start(f32[128,512]{1,0:T(8,128)S(1)} %bitcast_add_fusion.1), channel_id=1, source_target_pairs={{8,12},{10,14},{4,0},{6,2},{9,13},{11,15},{5,1},{7,3},{24,28},{26,... | collective-permute-start | bytes 786440 | tf_op jit(solution)/shard_map/ppermute | solution.py:282

commit v2 on v1

v2 whole, which is shorter than its diff:
```python
import functools
import math

import jax
import jax.numpy as jnp
from jax import lax
from jax.experimental import pallas as pl
from jax.experimental.pallas import tpu as pltpu
from jax.sharding import PartitionSpec as P

H = 8
HD = 128
PAIR = 2 * HD
GROUPS = ((0, 3), (1, 2))
EPSILON = 1e-06
F32 = jnp.float32
BF16 = jnp.bfloat16
VMEM = pltpu.VMEM
VMEM_LIMIT = 16 << 20
COST = 16

NN = (((1,), (0,)), ((), ()))
NT = (((1,), (1,)), ((), ()))
TN = (((0,), (0,)), ((), ()))


def dot(a, b, dims):
    return lax.dot_general(a, b, dims, preferred_element_type=F32)


def halves(a):
    high = a.astype(BF16)
    return high, (a - high.astype(F32)).astype(BF16)


def two_pass(a, b, dims):
    high, low = halves(a)
    return dot(high, b, dims) + dot(low, b, dims)


def two_pass_right(a, b, dims):
    high, low = halves(b)
    return dot(a, high, dims) + dot(a, low, dims)


def causal(length, lower):
    rows = lax.broadcasted_iota(jnp.int32, (length, length), 0)
    cols = lax.broadcasted_iota(jnp.int32, (length, length), 1)
    return rows >= cols if lower else rows <= cols


def at(position, size=HD):
    if isinstance(position, int):
        return pl.ds(position * size, size)
    return pl.ds(pl.multiple_of(position * size, size), size)


def shape(dims, dtype):
    return jax.ShapeDtypeStruct(dims, dtype)


def call(body, out_shapes, operands, flops, name):
    specs = []
    for operand in operands:
        space = pltpu.SMEM if operand.dtype == jnp.int32 else VMEM
        specs.append(pl.BlockSpec(memory_space=space))
    return pl.pallas_call(
        body,
        out_shape=tuple(out_shapes),
        in_specs=specs,
        out_specs=tuple(pl.BlockSpec(memory_space=VMEM) for _ in out_shapes),
        compiler_params=pltpu.CompilerParams(vmem_limit_bytes=VMEM_LIMIT),
        cost_estimate=pl.CostEstimate(flops=flops // COST, bytes_accessed=0, transcendentals=0),
        name=name,
    )(*operands)


def after(value, *others):
    return lax.optimization_barrier((value, *others))[0]


def state_body(place, k_ref, v_ref, *outs):
    low = place[0]
    for g, rows in enumerate(GROUPS):
        for i, j in enumerate(rows):
            for out, head in ((outs[2 * g], 2 * j + low), (outs[2 * g + 1], 2 * j + 1 - low)):
                out[i] = dot(k_ref[:, at(head)], v_ref[:, at(head)], TN)


def local_body(q_ref, k_ref, v_ref, out_ref):
    mask = causal(q_ref.shape[0], True)
    for h in range(H):
        scores = dot(q_ref[:, at(h)], k_ref[:, at(h)], NT)
        scores = jnp.where(mask, scores, 0.0)
        out_ref[:, at(h)] = two_pass(scores, v_ref[:, at(h)], NN)


def d_normed_body(g_ref, w_ref, out_ref):
    @pl.loop(0, H // 2)
    def _(j):
        out_ref[:, at(j, PAIR)] = dot(g_ref[...], w_ref[at(j, PAIR), :], NT)


def norm_body(
    rows, place, q_ref, att_ref, dn_ref, own_ref, other_ref, nb_ref, nb32_ref, da_ref, keep_ref, send_ref
):
    low = place[0]
    for i, j in enumerate(rows):
        for prior, out, part in ((own_ref, keep_ref, low), (other_ref, send_ref, 1 - low)):
            here, there = at(2 * j + part), at(2 * i + part)
            q = q_ref[:, here]
            attended = att_ref[:, here] + two_pass_right(q, prior[i], NN)
            inverse = lax.rsqrt(jnp.mean(attended * attended, axis=-1, keepdims=True) + EPSILON)
            normed = attended * inverse
            rounded = normed.astype(BF16)
            nb_ref[:, there] = rounded
            nb32_ref[:, there] = rounded.astype(F32)
            d_normed = dn_ref[:, here]
            mean = jnp.mean(d_normed * normed, axis=-1, keepdims=True)
            d_att = (inverse * (d_normed - normed * mean)).astype(BF16)
            da_ref[:, there] = d_att
            out[i] = dot(q, d_att, TN)


def grads_body(
    rows, place, q_ref, k_ref, v_ref, da_ref, own_ref, other_ref, qg_ref, kl_ref, vl_ref
):
    low = place[0]
    lower = causal(q_ref.shape[0], True)
    upper = causal(q_ref.shape[0], False)
    for i, j in enumerate(rows):
        for prior, part in ((own_ref, low), (other_ref, 1 - low)):
            here, there = at(2 * j + part), at(2 * i + part)
            q, k, v, d_att = q_ref[:, here], k_ref[:, here], v_ref[:, here], da_ref[:, there]
            cross = jnp.where(lower, dot(d_att, v, NT), 0.0)
            part_sum = two_pass(cross, k, NN) + two_pass_right(d_att, prior[i], NT)
            qg_ref[:, there] = part_sum.astype(BF16)
            cross = jnp.where(upper, dot(v, d_att, NT), 0.0)
            kl_ref[:, there] = two_pass(cross, q, NN)
            scores = jnp.where(upper, dot(k, q, NT), 0.0)
            vl_ref[:, there] = two_pass(scores, d_att, NN)


def final_body(place, k_ref, v_ref, *refs):
    low = place[0]
    kg_ref, vg_ref = refs[-2:]
    for g, rows in enumerate(GROUPS):
        kl_ref, vl_ref, own_ref, other_ref = refs[4 * g : 4 * g + 4]
        for i, j in enumerate(rows):
            for later, part in ((own_ref, low), (other_ref, 1 - low)):
                here, there = at(2 * j + part), at(2 * i + part)
                high, rest = halves(later[i])
                v, k = v_ref[:, here], k_ref[:, here]
                k_sum = kl_ref[:, there] + (dot(v, high, NT) + dot(v, rest, NT))
                kg_ref[:, here] = k_sum.astype(BF16)
                v_sum = vl_ref[:, there] + (dot(k, high, NN) + dot(k, rest, NN))
                vg_ref[:, here] = v_sum.astype(BF16)


def weight_body(place, nb_ref, g_ref, nbo_ref, go_ref, keep0, keep1, send0, send1):
    low, core = place[0], place[1]
    width = go_ref.shape[1] // 2
    mine = nb_ref[...]
    theirs = nbo_ref[...].astype(BF16)
    for c, keep, send in ((0, keep0, send0), (1, keep1, send1)):
        ours = g_ref[:, at(core * 2 + c, width)]
        other = go_ref[:, c * width : (c + 1) * width].astype(BF16)
        product = dot(mine, ours, TN) + dot(theirs, other, TN)
        for i in range(2):
            first = product[2 * i * HD : (2 * i + 1) * HD]
            second = product[(2 * i + 1) * HD : (2 * i + 2) * HD]
            keep[i] = jnp.where(low == 0, first, second)
            send[i] = jnp.where(low == 0, second, first)


def output_body(far_ref, near_ref, w_ref, out_ref):
    size = 2 * PAIR

    @pl.loop(0, out_ref.shape[1] // size)
    def _(c):
        total = dot(near_ref[...], w_ref[PAIR : 3 * PAIR, at(c, size)], NN)
        total += dot(far_ref[:, :PAIR], w_ref[:PAIR, at(c, size)], NN)
        total += dot(far_ref[:, PAIR:], w_ref[3 * PAIR :, at(c, size)], NN)
        out_ref[:, at(c, size)] = total.astype(BF16)


def exclusive(states, count, low, reverse, pins):
    swap = [(s, s ^ 1) for s in range(count)]
    sign = -2 if reverse else 2
    pairs = count // 2
    first = low == (1 if reverse else 0)

    def links(step):
        return [(s, s + sign * step) for s in range(count) if 0 <= s + sign * step < count]

    received = [lax.ppermute(send, "seq", swap) for _, send in states]
    total = [keep + got for (keep, _), got in zip(states, received)]
    outside = [None for _ in states]
    step = 1
    while step < pairs:
        pinned = pins.pop(0) if pins else ()
        for i in range(len(states)):
            total[i] = after(total[i], *pinned)
            got = lax.ppermute(total[i], "seq", links(step))
            outside[i] = got if step == 1 else outside[i] + got
            total[i] = total[i] + got
        step *= 2
    pinned = pins.pop(0) if pins else ()
    results = []
    for (keep, _), got, sums in zip(states, received, outside):
        mine = jnp.where(first, sums, sums + got)
        theirs = after(jnp.where(first, sums + keep, sums), *pinned)
        results.append((mine, lax.ppermute(theirs, "seq", swap)))
    return results


def per_device(queries, keys, values, out_weight, out_grad):
    count = lax.axis_size("seq")
    cores = lax.axis_size("dp")
    spot = lax.axis_index("seq")
    core = lax.axis_index("dp")
    low, level = spot % 2, spot // 2
    q, k, v, g = queries[0], keys[0], values[0], out_grad[0]
    length, features = q.shape
    width = g.shape[1]
    place = jnp.stack([low, core]).astype(jnp.int32)
    part = features // 2
    state = shape((2, HD, HD), F32)
    unit = 2 * H * length * HD

    flat = call(state_body, (state,) * 4, (place, k, v), unit * HD, "state")
    states = [(flat[0], flat[1]), (flat[2], flat[3])]

    fast = count == 8 and cores == 2
    half = width // 2
    swap = [(0, 1), (1, 0)]
    away = g
    if fast:
        away = lax.dynamic_slice_in_dim(g, (1 - core) * half, half, axis=1).astype(F32)
        go = lax.ppermute(away, "dp", swap)
    (att,) = call(local_body, (shape((length, features), F32),), (q, k, v), 3 * unit * length, "local")
    (d_normed,) = call(
        d_normed_body,
        (shape((length, features), F32),),
        (g, out_weight),
        2 * length * features * width,
        "d_normed",
    )
    priors = exclusive(states, count, low, False, [(away,), (att,), (d_normed,)])

    normed, d_atts, grad_states = [], [], []
    for rows, (own, other) in zip(GROUPS, priors):
        nb, nb32, da, keep, send = call(
            functools.partial(norm_body, rows),
            (
                shape((length, part), BF16),
                shape((length, part), F32),
                shape((length, part), BF16),
                state,
                state,
            ),
            (place, q, att, d_normed, own, other),
            2 * unit * HD,
            "norm",
        )
        normed.append((nb, nb32))
        d_atts.append(da)
        grad_states.append((keep, send))

    scale = 1.0 / math.sqrt(length * count * cores)
    if fast:
        block = shape((2, HD, half // 2), F32)
        chunks = []
        for nb, nb32 in normed:
            nbo = lax.ppermute(nb32, "dp", swap)
            out = call(
                weight_body, (block,) * 4, (place, nb, g, nbo, go), 2 * length * features * half, "weight"
            )
            chunks.append([(out[0], out[2]), (out[1], out[3])])
        ready = (chunks[1][0][1],)
        pins = [(chunks[0][0][1],), ready]
        weight_grad = scatter(chunks, level) * scale
    else:
        far, near = normed[0][0], normed[1][0]
        nb = jnp.concatenate([far[:, :PAIR], near, far[:, PAIR:]], axis=1)
        product = lax.dot_general(nb, g, TN, preferred_element_type=F32)
        product = lax.psum_scatter(product, "dp", scatter_dimension=1, tiled=True)
        weight_grad = lax.psum_scatter(product, "seq", scatter_dimension=0, tiled=True) * scale
        ready, pins = (), []

    laters = exclusive(grad_states, count, low, True, pins)

    pieces = []
    for rows, da, (own, other) in zip(GROUPS, d_atts, priors):
        pieces.append(
            call(
                functools.partial(grads_body, rows),
                (shape((length, part), BF16), shape((length, part), F32), shape((length, part), F32)),
                (place, q, k, v, after(da, *ready), own, other),
                5 * unit * length,
                "grads",
            )
        )
    (output,) = call(
        output_body,
        (shape((length, width), BF16),),
        (after(normed[0][0], *ready), normed[1][0], out_weight),
        2 * length * features * width,
        "output",
    )
    far, near = pieces[0][0], pieces[1][0]
    query_grad = jnp.concatenate([far[:, :PAIR], near, far[:, PAIR:]], axis=1)
    operands = [place, k, v]
    for piece, later in zip(pieces, laters):
        operands += [piece[1], piece[2], later[0], later[1]]
    key_grad, value_grad = call(
        final_body, (shape((length, features), BF16),) * 2, tuple(operands), 4 * unit * HD, "final"
    )
    return output[None], query_grad[None], key_grad[None], value_grad[None], weight_grad


def scatter(chunks, level):
    swap = [(s, s ^ 1) for s in range(8)]

    def on(links):
        return [(2 * a + i, 2 * b + i) for a, b in links for i in range(2)]

    inward = on([(0, 1), (3, 2)])
    middle = on([(1, 2), (2, 1)])
    outward = on([(2, 3), (1, 0)])
    lower = level < 2

    def paired(chunk, *pinned):
        keep, send = chunk
        base = keep + lax.ppermute(after(send, *pinned), "seq", swap)
        return jnp.where(lower, base[1], base[0]), jnp.where(lower, base[0], base[1])

    far0 = paired(chunks[0][0])
    far1 = paired(chunks[0][1])
    near0 = paired(chunks[1][0], far0[0])
    near1 = paired(chunks[1][1], far1[0])
    parts = []
    for far, near in ((far0, near0), (far1, near1)):
        up, down = far
        got = lax.ppermute(up, "seq", inward)
        got = lax.ppermute(up + got, "seq", middle)
        got = lax.ppermute(down + got, "seq", outward)
        outer_sum = down + got
        up, down = near
        got = lax.ppermute(up, "seq", inward)
        direct = lax.ppermute(down, "seq", inward)
        got = lax.ppermute(up + got, "seq", middle)
        inner_sum = (down + direct) + got
        outer = (level == 0) | (level == 3)
        parts.append(jnp.where(outer, outer_sum, inner_sum))
    return jnp.concatenate(parts, axis=1)


def solution(mesh):
    rows = P(("parts", "dp"), "seq", None)
    return jax.shard_map(
        per_device,
        mesh=mesh,
        in_specs=(rows, rows, rows, P(), rows),
        out_specs=(rows, rows, rows, rows, P(("parts", "seq"), "dp")),
        check_vma=False,
    )
```

time: 169 us -> 146 us (0.86)
  waiting for transfers between devices: 69.1 us -> 24.9 us
  starting transfers between devices: 45.3 us -> 61.3 us
  matrix products: 10.6 us -> 0 us
  other arithmetic: 5.61 us -> 12.1 us
  local copies, waits for them, and re-layouts: 5.95 us -> 11.6 us
  Pallas kernels: 28.7 us -> 33.2 us
    ppermute x12 -> x20, waiting for transfers between devices: 60.4 us -> 12.6 us  [the longest x4 4.99 us: exclusive(): received = [lax.ppermute(send, 'seq', swap) for _, send in states]]
    ppermute x12 -> x20, starting transfers between devices: 20.1 us -> 32.9 us  [the longest x8 19.3 us: exclusive(): got = lax.ppermute(total[i], 'seq', links(step))]
    dot_general x2 -> x0, matrix products: 10.6 us -> none  [the longest x1 5.43 us: per_device(): output = jnp.dot(nb, out_weight, preferred_element_type=F32).astype(BF16)]
    unnamed x38 -> x60, local copies, waits for them, and re-layouts: 5.95 us -> 11.6 us
    ppermute x4, waiting for transfers between devices: 0.97 us -> 5.89 us  [scatter(): got = lax.ppermute(up, 'seq', inward)]
    pallas_call x7 -> x11, Pallas kernels: 28.7 us -> 33.2 us  [call(): pl.pallas_call(body, out_shape=tuple(out_shapes), in_specs=specs, out_spe...]
    ppermute x4, waiting for transfers between devices: 7.16 us -> 3.64 us  [scatter(): got = lax.ppermute(up + got, 'seq', middle)]
    add x8 -> x12, other arithmetic: 1.48 us -> 4.11 us  [the longest x4 1.7 us: exclusive(): total = [keep + got for (keep, _), got in zip(states, received)]]
  transfers between devices with their start and end apart: 26 -> 35, of which waited for: 12 -> 13; matrix products, arithmetic and copies ran while one was open for 9% -> 8% of each run, Pallas kernels for 17% -> 22%
where the time goes in v2:
time: 146 us; the launch traced here: 144 us
  starting transfers between devices  61.3 us (42%)
  Pallas kernels  33.2 us (23%)
  waiting for transfers between devices  24.9 us (17%)
  other arithmetic  12.1 us (8%)
  local copies, waits for them, and re-layouts  11.6 us (8%)
    pallas_call x11, Pallas kernels, call(): pl.pallas_call(body, out_shape=tuple(out_shapes), in_specs=specs, out_spe...  33.2 us
    ppermute x8, starting transfers between devices, exclusive(): got = lax.ppermute(total[i], 'seq', links(step))  19.3 us
    ppermute x4, starting transfers between devices, scatter(): got = lax.ppermute(up + got, 'seq', middle)  15.8 us
    unnamed x60, local copies, waits for them, and re-layouts  11.6 us
    ppermute x4, starting transfers between devices, exclusive(): results.append((mine, lax.ppermute(theirs, 'seq', swap)))  5.99 us
    ppermute x4, waiting for transfers between devices, scatter(): got = lax.ppermute(up, 'seq', inward)  5.89 us
    ppermute x4, starting transfers between devices, scatter(): got = lax.ppermute(up, 'seq', inward)  5.16 us
    ppermute x4, waiting for transfers between devices, exclusive(): received = [lax.ppermute(send, 'seq', swap) for _, send in states]  4.99 us
  transfers between devices with their start and end apart: 35, of which 13 were waited for; matrix products, arithmetic and copies ran while one was open for 8% of the time, Pallas kernels for 22%

profile of v2, /device:TPU:12, one launch (start us, length us, event | category | flops | bytes accessed | tf_op | source)
XLA Modules:
  0.0 144.4 jit_solution(13251056159381667275)
XLA Ops:
  0.7 1.1 copy-done.1
  1.9 1.1 copy-done.3
  3.0 1.1 state.1
  4.1 1.6 %collective-permute-start = (f32[2,128,128]{2,1,0:T(8,128)S(1)}, f32[2,128,128]{2,1,0:T(8,128)S(1)}, u32[]{:S(2)}, u32[]{:S(2)}) collective-permute-start(f32[2,128,128]{2,1,0:T(8,128)S(1)} %get-tuple-element.51), channel_id=1, source_target_pairs={{0,2},{2,0},{4,6},{6,4},{8,10},{10,8},{12,14},{14,12},{1,3},{3,1},... | collective-permute-start | bytes 393224 | tf_op jit(solution)/shard_map/ppermute | solution.py:196
  5.7 2.5 %bitcast_convert_fusion = f32[384,1024]{1,0:T(8,128)} fusion(bf16[1,384,2048]{2,1,0:T(8,128)(2,1)} %param.9, s32[]{:T(128)S(6)} %select_n.124), kind=kLoop, calls=%fused_computation.1 | loop fusion | flops 393216 | bytes 2359300 | tf_op jit(solution)/shard_map/convert_element_type | solution.py:239
  9.5 3.5 %collective-permute-start.1 = (f32[2,128,128]{2,1,0:T(8,128)S(1)}, f32[2,128,128]{2,1,0:T(8,128)S(1)}, u32[]{:S(2)}, u32[]{:S(2)}) collective-permute-start(f32[2,128,128]{2,1,0:T(8,128)S(1)} %add.117), channel_id=1, source_target_pairs={{0,4},{2,6},{4,8},{6,10},{8,12},{10,14},{1,5},{3,7},{5,9},{7,11},{... | collective-permute-start | bytes 393224 | tf_op jit(solution)/shard_map/ppermute | solution.py:204
  13.0 2.4 %local.1.att_ref = f32[384,1024]{1,0:T(8,128)S(1)} custom-call(bf16[384,1024]{1,0:T(8,128)(2,1)S(1)} %bitcast.40, bf16[384,1024]{1,0:T(8,128)(2,1)S(1)} %bitcast.46, bf16[384,1024]{1,0:T(8,128)(2,1)S(1)} %bitcast.51), custom_call_target="tpu_custom_call" | custom-call | flops 56623104 | tf_op jit(solution)/shard_map/local/pallas_call | solution.py:67
  15.4 1.1 copy-done.10
  16.6 3.5 %collective-permute-start.5 = (f32[2,128,128]{2,1,0:T(8,128)S(1)}, f32[2,128,128]{2,1,0:T(8,128)S(1)}, u32[]{:S(2)}, u32[]{:S(2)}) collective-permute-start(f32[2,128,128]{2,1,0:T(8,128)S(1)} %add.123), channel_id=1, source_target_pairs={{0,4},{2,6},{4,8},{6,10},{8,12},{10,14},{1,5},{3,7},{5,9},{7,11},{... | collective-permute-start | bytes 393224 | tf_op jit(solution)/shard_map/ppermute | solution.py:204
  20.1 1.9 %collective-permute-start.2 = (f32[2,128,128]{2,1,0:T(8,128)S(1)}, f32[2,128,128]{2,1,0:T(8,128)}, u32[]{:S(2)}, u32[]{:S(2)}) collective-permute-start(f32[2,128,128]{2,1,0:T(8,128)S(1)} %add.119), channel_id=1, source_target_pairs={{0,8},{2,10},{4,12},{6,14},{1,9},{3,11},{5,13},{7,15},{16,24},{18,... | collective-permute-start | bytes 393224 | tf_op jit(solution)/shard_map/ppermute | solution.py:204
  22.1 1.4 copy-done.5
  23.5 2.2 %copy-done.8 = bf16[1024,2048]{1,0:T(8,128)(2,1)S(1)} copy-done((bf16[1024,2048]{1,0:T(8,128)(2,1)S(1)}, bf16[1024,2048]{1,0:T(8,128)(2,1)}, u32[]{:S(2)}) %copy-start.8) | copy-done | bytes 4194328
  25.7 2.4 %d_normed.1.dn_ref = f32[384,1024]{1,0:T(8,128)S(1)} custom-call(bf16[384,2048]{1,0:T(8,128)(2,1)S(1)} %bitcast.55, bf16[1024,2048]{1,0:T(8,128)(2,1)S(1)} %copy-done.8), custom_call_target="tpu_custom_call" | custom-call | flops 100663296 | tf_op jit(solution)/shard_map/d_normed/pallas_call | solution.py:67
  28.1 1.4 collective-permute-start.6
  29.6 0.9 add_select_fusion.6
  30.5 1.6 %collective-permute-start.3 = (f32[2,128,128]{2,1,0:T(8,128)S(1)}, f32[2,128,128]{2,1,0:T(8,128)S(1)}, u32[]{:S(2)}, u32[]{:S(2)}) collective-permute-start(f32[2,128,128]{2,1,0:T(8,128)S(1)} %get-tuple-element.54), channel_id=1, source_target_pairs={{0,2},{2,0},{4,6},{6,4},{8,10},{10,8},{12,14},{14,12},{1,3},{3,1},... | collective-permute-start | bytes 393224 | tf_op jit(solution)/shard_map/ppermute | solution.py:213
  32.1 2.6 %collective-permute-done.6 = f32[2,128,128]{2,1,0:T(8,128)S(1)} collective-permute-done((f32[2,128,128]{2,1,0:T(8,128)S(1)}, f32[2,128,128]{2,1,0:T(8,128)S(1)}, u32[]{:S(2)}, u32[]{:S(2)}) %collective-permute-start.6) | collective-permute-done | bytes 131104 | tf_op jit(solution)/shard_map/ppermute | solution.py:204
  34.8 1.5 %collective-permute-start.7 = (f32[2,128,128]{2,1,0:T(8,128)S(1)}, f32[2,128,128]{2,1,0:T(8,128)S(1)}, u32[]{:S(2)}, u32[]{:S(2)}) collective-permute-start(f32[2,128,128]{2,1,0:T(8,128)S(1)} %get-tuple-element.60), channel_id=1, source_target_pairs={{0,2},{2,0},{4,6},{6,4},{8,10},{10,8},{12,14},{14,12},{1,3},{3,1},... | collective-permute-start | bytes 393224 | tf_op jit(solution)/shard_map/ppermute | solution.py:213
  36.4 2.5 %norm.2 = (bf16[384,512]{1,0:T(8,128)(2,1)S(1)}, f32[384,512]{1,0:T(8,128)S(1)}, bf16[384,512]{1,0:T(8,128)(2,1)S(1)}, f32[2,128,128]{2,1,0:T(8,128)S(1)}, f32[2,128,128]{2,1,0:T(8,128)S(1)}) custom-call(s32[2]{0:T(128)S(1)} %pad_add_fusion.place, bf16[384,1024]{1,0:T(8,128)(2,1)S(1)} %bitcast.41, f32[384,1024]{1,0:T(8,128)S(1)} %copy-done.11, ...), custom_call_target="tpu_custom_call" | custom-call | flops 12582912 | tf_op jit(solution)/shard_map/norm/pallas_call | solution.py:67
  39.8 3.2 %norm.3 = (bf16[384,512]{1,0:T(8,128)(2,1)S(1)}, f32[384,512]{1,0:T(8,128)}, bf16[384,512]{1,0:T(8,128)(2,1)S(1)}, f32[2,128,128]{2,1,0:T(8,128)S(1)}, f32[2,128,128]{2,1,0:T(8,128)}) custom-call(s32[2]{0:T(128)S(1)} %pad_add_fusion.place, bf16[384,1024]{1,0:T(8,128)(2,1)S(1)} %bitcast.42, f32[384,1024]{1,0:T(8,128)S(1)} %copy-done.11, ...), custom_call_target="tpu_custom_call" | custom-call | flops 12582912 | tf_op jit(solution)/shard_map/norm/pallas_call | solution.py:67
  43.4 1.4 collective-permute-start.10
  45.5 4.3 %collective-permute-done.10 = f32[2,128,128]{2,1,0:T(8,128)S(1)} collective-permute-done((f32[2,128,128]{2,1,0:T(8,128)S(1)}, f32[2,128,128]{2,1,0:T(8,128)S(1)}, u32[]{:S(2)}, u32[]{:S(2)}) %collective-permute-start.10) | collective-permute-done | bytes 131104 | tf_op jit(solution)/shard_map/ppermute | solution.py:196
  50.5 3.5 %weight.3 = (f32[2,128,512]{2,1,0:T(8,128)S(1)}, f32[2,128,512]{2,1,0:T(8,128)S(1)}, f32[2,128,512]{2,1,0:T(8,128)S(1)}, f32[2,128,512]{2,1,0:T(8,128)}) custom-call(s32[2]{0:T(128)S(1)} %pad_add_fusion.place, bf16[384,512]{1,0:T(8,128)(2,1)S(1)} %get-tuple-element.64.far_ref.nb_ref, bf16[384,2048]{1,0:T(8,128)(2,1)S(1)} %bitcast.56, ...), custom_call_target="tpu_custom_call" | custom-call | flops 50331648 | tf_op jit(solution)/shard_map/weight/pallas_call | solution.py:67
  54.0 0.8 copy-done.12
  54.8 0.8 copy-done.14
  55.6 0.8 copy-done.26
  56.4 4.0 %collective-permute-start.12 = (f32[2,128,128]{2,1,0:T(8,128)}, f32[2,128,128]{2,1,0:T(8,128)}, u32[]{:S(2)}, u32[]{:S(2)}) collective-permute-start(f32[2,128,128]{2,1,0:T(8,128)} %add.128), channel_id=1, source_target_pairs={{4,0},{6,2},{8,4},{10,6},{12,8},{14,10},{5,1},{7,3},{9,5},{11,7},{... | collective-permute-start | bytes 393224 | tf_op jit(solution)/shard_map/ppermute | solution.py:204
  60.4 1.5 %collective-permute-start.27 = (f32[2,128,512]{2,1,0:T(8,128)}, f32[2,128,512]{2,1,0:T(8,128)}, u32[]{:S(2)}, u32[]{:S(2)}) collective-permute-start(f32[2,128,512]{2,1,0:T(8,128)} %get-tuple-element.91), channel_id=1, source_target_pairs={{0,2},{2,0},{4,6},{6,4},{8,10},{10,8},{12,14},{14,12},{1,3},{3,1},... | collective-permute-start | bytes 1572872 | tf_op jit(solution)/shard_map/ppermute | solution.py:335
  61.9 1.0 add.133
  62.9 1.4 copy-done.7
  64.3 3.0 %weight.2 = (f32[2,128,512]{2,1,0:T(8,128)S(1)}, f32[2,128,512]{2,1,0:T(8,128)S(1)}, f32[2,128,512]{2,1,0:T(8,128)S(1)}, f32[2,128,512]{2,1,0:T(8,128)S(1)}) custom-call(s32[2]{0:T(128)S(1)} %pad_add_fusion.place, bf16[384,512]{1,0:T(8,128)(2,1)S(1)} %get-tuple-element.61.nb_ref.near_ref, bf16[384,2048]{1,0:T(8,128)(2,1)S(1)} %bitcast.57, ...), custom_call_target="tpu_custom_call" | custom-call | flops 50331648 | tf_op jit(solution)/shard_map/weight/pallas_call | solution.py:67
  67.3 2.2 %collective-permute-start.16 = (f32[2,128,128]{2,1,0:T(8,128)S(1)}, f32[2,128,128]{2,1,0:T(8,128)S(1)}, u32[]{:S(2)}, u32[]{:S(2)}) collective-permute-start(f32[2,128,128]{2,1,0:T(8,128)S(1)} %add.133), channel_id=1, source_target_pairs={{4,0},{6,2},{8,4},{10,6},{12,8},{14,10},{5,1},{7,3},{9,5},{11,7},{... | collective-permute-start | bytes 393224 | tf_op jit(solution)/shard_map/ppermute | solution.py:204
  70.3 4.3 %grads.2 = (bf16[384,512]{1,0:T(8,128)(2,1)S(1)}, f32[384,512]{1,0:T(8,128)S(1)}, f32[384,512]{1,0:T(8,128)S(1)}) custom-call(s32[2]{0:T(128)S(1)} %pad_add_fusion.place, bf16[384,1024]{1,0:T(8,128)(2,1)S(1)} %bitcast.43, bf16[384,1024]{1,0:T(8,128)(2,1)S(1)} %bitcast.47, bf16[384,1024]{1,0:T(8,128)(2,1)S(1)} %bitcast.52, bf16[384,512]{1,0:T(8,128)(2,1)S(1)} %copy-done.25, ...), custom_call_target="tpu_custom_call" | custom-call | flops 94371840 | tf_op jit(solution)/shard_map/grads/pallas_call | solution.py:67
  74.6 1.0 add.129
  75.6 1.3 collective-permute-start.13
  77.0 4.4 %grads.3 = (bf16[384,512]{1,0:T(8,128)(2,1)S(1)}, f32[384,512]{1,0:T(8,128)S(1)}, f32[384,512]{1,0:T(8,128)S(1)}) custom-call(s32[2]{0:T(128)S(1)} %pad_add_fusion.place, bf16[384,1024]{1,0:T(8,128)(2,1)S(1)} %bitcast.44, bf16[384,1024]{1,0:T(8,128)(2,1)S(1)} %bitcast.48, bf16[384,1024]{1,0:T(8,128)(2,1)S(1)} %bitcast.53, bf16[384,512]{1,0:T(8,128)(2,1)S(1)} %copy-done.23, ...), custom_call_target="tpu_custom_call" | custom-call | flops 94371840 | tf_op jit(solution)/shard_map/grads/pallas_call | solution.py:67
  81.4 1.4 collective-permute-start.17
  83.4 0.9 add_select_fusion.2
  84.4 1.5 %collective-permute-start.14 = (f32[2,128,128]{2,1,0:T(8,128)S(1)}, f32[2,128,128]{2,1,0:T(8,128)S(1)}, u32[]{:S(2)}, u32[]{:S(2)}) collective-permute-start(f32[2,128,128]{2,1,0:T(8,128)S(1)} %get-tuple-element.103), channel_id=1, source_target_pairs={{0,2},{2,0},{4,6},{6,4},{8,10},{10,8},{12,14},{14,12},{1,3},{3,1},... | collective-permute-start | bytes 393224 | tf_op jit(solution)/shard_map/ppermute | solution.py:213
  85.8 1.1 add.146
  87.0 1.3 collective-permute-start.28
  89.1 1.3 collective-permute-start.20
  90.5 0.9 add_select_fusion
  91.4 1.5 %collective-permute-start.18 = (f32[2,128,128]{2,1,0:T(8,128)S(1)}, f32[2,128,128]{2,1,0:T(8,128)S(1)}, u32[]{:S(2)}, u32[]{:S(2)}) collective-permute-start(f32[2,128,128]{2,1,0:T(8,128)S(1)} %get-tuple-element.101), channel_id=1, source_target_pairs={{0,2},{2,0},{4,6},{6,4},{8,10},{10,8},{12,14},{14,12},{1,3},{3,1},... | collective-permute-start | bytes 393224 | tf_op jit(solution)/shard_map/ppermute | solution.py:213
  92.9 3.7 %collective-permute-done.28 = f32[128,512]{1,0:T(8,128)S(1)} collective-permute-done((f32[128,512]{1,0:T(8,128)S(1)}, f32[128,512]{1,0:T(8,128)S(1)}, u32[]{:S(2)}, u32[]{:S(2)}) %collective-permute-start.28) | collective-permute-done | bytes 262176 | tf_op jit(solution)/shard_map/ppermute | solution.py:345
  97.3 2.1 %collective-permute-done.20 = f32[128,512]{1,0:T(8,128)S(1)} collective-permute-done((f32[128,512]{1,0:T(8,128)S(1)}, f32[128,512]{1,0:T(8,128)S(1)}, u32[]{:S(2)}, u32[]{:S(2)}) %collective-permute-start.20) | collective-permute-done | bytes 262176 | tf_op jit(solution)/shard_map/ppermute | solution.py:345
  99.4 3.6 %collective-permute-start.29 = (f32[128,512]{1,0:T(8,128)S(1)}, f32[128,512]{1,0:T(8,128)S(1)}, u32[]{:S(2)}, u32[]{:S(2)}) collective-permute-start(f32[128,512]{1,0:T(8,128)S(1)} %fusion.4), channel_id=1, source_target_pairs={{4,8},{6,10},{8,4},{10,6},{5,9},{7,11},{9,5},{11,7},{20,24},{22,26... | collective-permute-start | bytes 786440 | tf_op jit(solution)/shard_map/ppermute | solution.py:346
  103.2 3.4 %collective-permute-start.21 = (f32[128,512]{1,0:T(8,128)S(1)}, f32[128,512]{1,0:T(8,128)S(1)}, u32[]{:S(2)}, u32[]{:S(2)}) collective-permute-start(f32[128,512]{1,0:T(8,128)S(1)} %fusion.3), channel_id=1, source_target_pairs={{4,8},{6,10},{8,4},{10,6},{5,9},{7,11},{9,5},{11,7},{20,24},{22,26... | collective-permute-start | bytes 786440 | tf_op jit(solution)/shard_map/ppermute | solution.py:346
  106.8 2.2 %collective-permute-done.29 = f32[128,512]{1,0:T(8,128)S(1)} collective-permute-done((f32[128,512]{1,0:T(8,128)S(1)}, f32[128,512]{1,0:T(8,128)S(1)}, u32[]{:S(2)}, u32[]{:S(2)}) %collective-permute-start.29) | collective-permute-done | bytes 262176 | tf_op jit(solution)/shard_map/ppermute | solution.py:346
  109.0 1.3 collective-permute-start.33
  110.4 4.0 %collective-permute-done.23 = f32[2,128,512]{2,1,0:T(8,128)S(1)} collective-permute-done((f32[2,128,512]{2,1,0:T(8,128)S(1)}, f32[2,128,512]{2,1,0:T(8,128)S(1)}, u32[]{:S(2)}, u32[]{:S(2)}) %collective-permute-start.23) | collective-permute-done | bytes 524320 | tf_op jit(solution)/shard_map/ppermute | solution.py:335
  114.4 2.9 %collective-permute-start.30 = (f32[128,512]{1,0:T(8,128)S(1)}, f32[128,512]{1,0:T(8,128)S(1)}, u32[]{:S(2)}, u32[]{:S(2)}) collective-permute-start(f32[128,512]{1,0:T(8,128)S(1)} %bitcast_add_fusion.1), channel_id=1, source_target_pairs={{8,12},{10,14},{4,0},{6,2},{9,13},{11,15},{5,1},{7,3},{24,28},{26,... | collective-permute-start | bytes 786440 | tf_op jit(solution)/shard_map/ppermute | solution.py:347
  117.4 1.6 %collective-permute-start.32 = (f32[128,512]{1,0:T(8,128)S(1)}, f32[128,512]{1,0:T(8,128)S(1)}, u32[]{:S(2)}, u32[]{:S(2)}) collective-permute-start(f32[128,512]{1,0:T(8,128)S(1)} %get-tuple-element.97), channel_id=1, source_target_pairs={{0,4},{2,6},{12,8},{14,10},{1,5},{3,7},{13,9},{15,11},{16,20},{18,... | collective-permute-start | bytes 786440 | tf_op jit(solution)/shard_map/ppermute | solution.py:351
  119.0 1.3 collective-permute-start.25
  120.3 4.8 %collective-permute-start.34 = (f32[128,512]{1,0:T(8,128)S(1)}, f32[128,512]{1,0:T(8,128)S(1)}, u32[]{:S(2)}, u32[]{:S(2)}) collective-permute-start(f32[128,512]{1,0:T(8,128)S(1)} %add.152), channel_id=1, source_target_pairs={{4,8},{6,10},{8,4},{10,6},{5,9},{7,11},{9,5},{11,7},{20,24},{22,26... | collective-permute-start | bytes 786440 | tf_op jit(solution)/shard_map/ppermute | solution.py:352
  125.2 1.0 maximum_bitcast_fusion
  126.1 3.4 %output.1 = bf16[384,2048]{1,0:T(8,128)(2,1)} custom-call(bf16[384,512]{1,0:T(8,128)(2,1)S(1)} %get-tuple-element.64.far_ref.nb_ref, bf16[384,512]{1,0:T(8,128)(2,1)S(1)} %get-tuple-element.61.nb_ref.near_ref, bf16[1024,2048]{1,0:T(8,128)(2,1)S(1)} %copy-done.9), custom_call_target="tpu_custom_call" | custom-call | flops 100663296 | tf_op jit(solution)/shard_map/output/pallas_call | solution.py:67
  129.6 2.8 %final.1 = (bf16[384,1024]{1,0:T(8,128)(2,1)}, bf16[384,1024]{1,0:T(8,128)(2,1)}) custom-call(s32[2]{0:T(128)S(1)} %pad_add_fusion.place, bf16[384,1024]{1,0:T(8,128)(2,1)S(1)} %bitcast.49, bf16[384,1024]{1,0:T(8,128)(2,1)S(1)} %bitcast.54, f32[384,512]{1,0:T(8,128)S(1)} %get-tuple-element.71.refs_0_, f32[384,512]{1,0:T(8,128)S(1)} %get-tuple-element.72.refs_1_, ...), custom_call_target="tpu_custom_call" | custom-call | flops 25165824 | tf_op jit(solution)/shard_map/final/pallas_call | solution.py:67
  132.4 1.3 collective-permute-start.22
  133.7 1.3 collective-permute-start.24
  135.1 4.0 %collective-permute-start.26 = (f32[128,512]{1,0:T(8,128)S(1)}, f32[128,512]{1,0:T(8,128)S(1)}, u32[]{:S(2)}, u32[]{:S(2)}) collective-permute-start(f32[128,512]{1,0:T(8,128)S(1)} %add.144), channel_id=1, source_target_pairs={{4,8},{6,10},{8,4},{10,6},{5,9},{7,11},{9,5},{11,7},{20,24},{22,26... | collective-permute-start | bytes 786440 | tf_op jit(solution)/shard_map/ppermute | solution.py:352
  139.3 2.7 %collective-permute-done.24 = f32[128,512]{1,0:T(8,128)S(1)} collective-permute-done((f32[128,512]{1,0:T(8,128)S(1)}, f32[128,512]{1,0:T(8,128)S(1)}, u32[]{:S(2)}, u32[]{:S(2)}) %collective-permute-start.24) | collective-permute-done | bytes 262176 | tf_op jit(solution)/shard_map/ppermute | solution.py:351
  142.0 1.4 collective-permute-done.26
  143.6 0.8 maximum_multiply_fusion
  (110 shorter events, 8.1 us)
Async XLA Ops:
  0.7 1.1 copy-start.1
  1.9 1.1 copy-start.3
  4.1 8.9 %copy-start = (bf16[1,384,1024]{2,1,0:T(8,128)(2,1)S(1)}, bf16[1,384,1024]{2,1,0:T(8,128)(2,1)}, u32[]{:S(2)}) copy-start(bf16[1,384,1024]{2,1,0:T(8,128)(2,1)} %param.5) | copy-start | bytes 2359300
  4.1 8.9 %copy-start.2 = (bf16[1,384,1024]{2,1,0:T(8,128)(2,1)S(1)}, bf16[1,384,1024]{2,1,0:T(8,128)(2,1)}, u32[]{:S(2)}) copy-start(bf16[1,384,1024]{2,1,0:T(8,128)(2,1)} %param.6) | copy-start | bytes 2359300
  4.1 8.8 %copy-start.4 = (bf16[1,384,1024]{2,1,0:T(8,128)(2,1)S(1)}, bf16[1,384,1024]{2,1,0:T(8,128)(2,1)}, u32[]{:S(2)}) copy-start(bf16[1,384,1024]{2,1,0:T(8,128)(2,1)} %param.7) | copy-start | bytes 2359300
  4.1 5.3 %collective-permute-start = (f32[2,128,128]{2,1,0:T(8,128)S(1)}, f32[2,128,128]{2,1,0:T(8,128)S(1)}, u32[]{:S(2)}, u32[]{:S(2)}) collective-permute-start(f32[2,128,128]{2,1,0:T(8,128)S(1)} %get-tuple-element.51), channel_id=1, source_target_pairs={{0,2},{2,0},{4,6},{6,4},{8,10},{10,8},{12,14},{14,12},{1,3},{3,1},... | collective-permute-start | bytes 393224 | tf_op jit(solution)/shard_map/ppermute | solution.py:196
  8.2 42.3 %collective-permute-start.9 = (f32[384,1024]{1,0:T(8,128)}, f32[384,1024]{1,0:T(8,128)}, u32[]{:S(2)}, u32[]{:S(2)}) collective-permute-start(f32[384,1024]{1,0:T(8,128)} %bitcast_convert_fusion), channel_id=1, source_target_pairs={{0,1},{1,0},{2,3},{3,2},{4,5},{5,4},{6,7},{7,6},{8,9},{9,8},{10,11... | collective-permute-start | bytes 4718600 | tf_op jit(solution)/shard_map/ppermute | solution.py:240
  8.2 8.4 %collective-permute-start.4 = (f32[2,128,128]{2,1,0:T(8,128)S(1)}, f32[2,128,128]{2,1,0:T(8,128)S(1)}, u32[]{:S(2)}, u32[]{:S(2)}) collective-permute-start(f32[2,128,128]{2,1,0:T(8,128)S(1)} %get-tuple-element.57), channel_id=1, source_target_pairs={{0,2},{2,0},{4,6},{6,4},{8,10},{10,8},{12,14},{14,12},{1,3},{3,1},... | collective-permute-start | bytes 393224 | tf_op jit(solution)/shard_map/ppermute | solution.py:196
  9.5 10.6 %collective-permute-start.1 = (f32[2,128,128]{2,1,0:T(8,128)S(1)}, f32[2,128,128]{2,1,0:T(8,128)S(1)}, u32[]{:S(2)}, u32[]{:S(2)}) collective-permute-start(f32[2,128,128]{2,1,0:T(8,128)S(1)} %add.117), channel_id=1, source_target_pairs={{0,4},{2,6},{4,8},{6,10},{8,12},{10,14},{1,5},{3,7},{5,9},{7,11},{... | collective-permute-start | bytes 393224 | tf_op jit(solution)/shard_map/ppermute | solution.py:204
  15.4 1.1 copy-start.10
  16.6 11.5 %collective-permute-start.5 = (f32[2,128,128]{2,1,0:T(8,128)S(1)}, f32[2,128,128]{2,1,0:T(8,128)S(1)}, u32[]{:S(2)}, u32[]{:S(2)}) collective-permute-start(f32[2,128,128]{2,1,0:T(8,128)S(1)} %add.123), channel_id=1, source_target_pairs={{0,4},{2,6},{4,8},{6,10},{8,12},{10,14},{1,5},{3,7},{5,9},{7,11},{... | collective-permute-start | bytes 393224 | tf_op jit(solution)/shard_map/ppermute | solution.py:204
  20.1 9.5 %collective-permute-start.2 = (f32[2,128,128]{2,1,0:T(8,128)S(1)}, f32[2,128,128]{2,1,0:T(8,128)}, u32[]{:S(2)}, u32[]{:S(2)}) collective-permute-start(f32[2,128,128]{2,1,0:T(8,128)S(1)} %add.119), channel_id=1, source_target_pairs={{0,8},{2,10},{4,12},{6,14},{1,9},{3,11},{5,13},{7,15},{16,24},{18,... | collective-permute-start | bytes 393224 | tf_op jit(solution)/shard_map/ppermute | solution.py:204
  22.1 1.4 copy-start.5
  23.5 2.2 %copy-start.8 = (bf16[1024,2048]{1,0:T(8,128)(2,1)S(1)}, bf16[1024,2048]{1,0:T(8,128)(2,1)}, u32[]{:S(2)}) copy-start(bf16[1024,2048]{1,0:T(8,128)(2,1)} %w_ref.3) | copy-start | bytes 12582916
  28.1 8.3 %copy-start.11 = (f32[384,1024]{1,0:T(8,128)S(1)}, f32[384,1024]{1,0:T(8,128)}, u32[]{:S(2)}) copy-start(f32[384,1024]{1,0:T(8,128)} %copy-done.10) | copy-start | bytes 4718596
  28.1 6.6 %collective-permute-start.6 = (f32[2,128,128]{2,1,0:T(8,128)S(1)}, f32[2,128,128]{2,1,0:T(8,128)S(1)}, u32[]{:S(2)}, u32[]{:S(2)}) collective-permute-start(f32[2,128,128]{2,1,0:T(8,128)S(1)} %add.124), channel_id=1, source_target_pairs={{0,8},{2,10},{4,12},{6,14},{1,9},{3,11},{5,13},{7,15},{16,24},{18,... | collective-permute-start | bytes 393224 | tf_op jit(solution)/shard_map/ppermute | solution.py:204
  30.5 5.9 %collective-permute-start.3 = (f32[2,128,128]{2,1,0:T(8,128)S(1)}, f32[2,128,128]{2,1,0:T(8,128)S(1)}, u32[]{:S(2)}, u32[]{:S(2)}) collective-permute-start(f32[2,128,128]{2,1,0:T(8,128)S(1)} %get-tuple-element.54), channel_id=1, source_target_pairs={{0,2},{2,0},{4,6},{6,4},{8,10},{10,8},{12,14},{14,12},{1,3},{3,1},... | collective-permute-start | bytes 393224 | tf_op jit(solution)/shard_map/ppermute | solution.py:213
  34.8 5.0 %collective-permute-start.7 = (f32[2,128,128]{2,1,0:T(8,128)S(1)}, f32[2,128,128]{2,1,0:T(8,128)S(1)}, u32[]{:S(2)}, u32[]{:S(2)}) collective-permute-start(f32[2,128,128]{2,1,0:T(8,128)S(1)} %get-tuple-element.60), channel_id=1, source_target_pairs={{0,2},{2,0},{4,6},{6,4},{8,10},{10,8},{12,14},{14,12},{1,3},{3,1},... | collective-permute-start | bytes 393224 | tf_op jit(solution)/shard_map/ppermute | solution.py:213
  36.4 2.6 %copy-start.16 = (f32[2,128,128]{2,1,0:T(8,128)}, f32[2,128,128]{2,1,0:T(8,128)S(1)}, u32[]{:S(2)}) copy-start(f32[2,128,128]{2,1,0:T(8,128)S(1)} %collective-permute-done.3.other_ref) | copy-start | bytes 393220
  39.7 10.1 %copy-start.20 = (f32[2,128,128]{2,1,0:T(8,128)}, f32[2,128,128]{2,1,0:T(8,128)S(1)}, u32[]{:S(2)}) copy-start(f32[2,128,128]{2,1,0:T(8,128)S(1)} %get-tuple-element.73) | copy-start | bytes 393220
  39.7 10.8 %collective-permute-start.11 = (f32[384,512]{1,0:T(8,128)S(1)}, f32[384,512]{1,0:T(8,128)S(1)}, u32[]{:S(2)}, u32[]{:S(2)}) collective-permute-start(f32[384,512]{1,0:T(8,128)S(1)} %get-tuple-element.75), channel_id=1, source_target_pairs={{0,1},{1,0},{2,3},{3,2},{4,5},{5,4},{6,7},{7,6},{8,9},{9,8},{10,11... | collective-permute-start | bytes 2359304 | tf_op jit(solution)/shard_map/ppermute | solution.py:275
  39.8 10.7 %copy-start.6 = (bf16[1,384,2048]{2,1,0:T(8,128)(2,1)S(1)}, bf16[1,384,2048]{2,1,0:T(8,128)(2,1)}, u32[]{:S(2)}) copy-start(bf16[1,384,2048]{2,1,0:T(8,128)(2,1)} %param.9) | copy-start | bytes 4718596
  43.0 11.0 %copy-start.18 = (f32[2,128,128]{2,1,0:T(8,128)}, f32[2,128,128]{2,1,0:T(8,128)S(1)}, u32[]{:S(2)}) copy-start(f32[2,128,128]{2,1,0:T(8,128)S(1)} %get-tuple-element.81) | copy-start | bytes 393220
  43.0 11.0 %copy-start.22 = (bf16[384,512]{1,0:T(8,128)(2,1)}, bf16[384,512]{1,0:T(8,128)(2,1)S(1)}, u32[]{:S(2)}) copy-start(bf16[384,512]{1,0:T(8,128)(2,1)S(1)} %get-tuple-element.69.da_ref) | copy-start | bytes 1179652
  43.0 19.9 %collective-permute-start.8 = (f32[384,512]{1,0:T(8,128)}, f32[384,512]{1,0:T(8,128)}, u32[]{:S(2)}, u32[]{:S(2)}) collective-permute-start(f32[384,512]{1,0:T(8,128)} %get-tuple-element.62), channel_id=1, source_target_pairs={{0,1},{1,0},{2,3},{3,2},{4,5},{5,4},{6,7},{7,6},{8,9},{9,8},{10,11... | collective-permute-start | bytes 2359304 | tf_op jit(solution)/shard_map/ppermute | solution.py:275
  43.4 6.4 %collective-permute-start.10 = (f32[2,128,128]{2,1,0:T(8,128)S(1)}, f32[2,128,128]{2,1,0:T(8,128)S(1)}, u32[]{:S(2)}, u32[]{:S(2)}) collective-permute-start(f32[2,128,128]{2,1,0:T(8,128)S(1)} %get-tuple-element.74), channel_id=1, source_target_pairs={{0,2},{2,0},{4,6},{6,4},{8,10},{10,8},{12,14},{14,12},{1,3},{3,1},... | collective-permute-start | bytes 393224 | tf_op jit(solution)/shard_map/ppermute | solution.py:196
  44.9 17.0 %collective-permute-start.15 = (f32[2,128,128]{2,1,0:T(8,128)}, f32[2,128,128]{2,1,0:T(8,128)}, u32[]{:S(2)}, u32[]{:S(2)}) collective-permute-start(f32[2,128,128]{2,1,0:T(8,128)} %get-tuple-element.82), channel_id=1, source_target_pairs={{0,2},{2,0},{4,6},{6,4},{8,10},{10,8},{12,14},{14,12},{1,3},{3,1},... | collective-permute-start | bytes 393224 | tf_op jit(solution)/shard_map/ppermute | solution.py:196
  49.8 4.2 %copy-start.28 = (f32[2,128,128]{2,1,0:T(8,128)}, f32[2,128,128]{2,1,0:T(8,128)S(1)}, u32[]{:S(2)}) copy-start(f32[2,128,128]{2,1,0:T(8,128)S(1)} %collective-permute-done.10) | copy-start | bytes 393220
  54.0 0.8 copy-start.12
  54.8 0.8 copy-start.14
  55.6 0.8 copy-start.26
  56.4 18.2 %collective-permute-start.12 = (f32[2,128,128]{2,1,0:T(8,128)}, f32[2,128,128]{2,1,0:T(8,128)}, u32[]{:S(2)}, u32[]{:S(2)}) collective-permute-start(f32[2,128,128]{2,1,0:T(8,128)} %add.128), channel_id=1, source_target_pairs={{4,0},{6,2},{8,4},{10,6},{12,8},{14,10},{5,1},{7,3},{9,5},{11,7},{... | collective-permute-start | bytes 393224 | tf_op jit(solution)/shard_map/ppermute | solution.py:204
  60.4 25.5 %collective-permute-start.27 = (f32[2,128,512]{2,1,0:T(8,128)}, f32[2,128,512]{2,1,0:T(8,128)}, u32[]{:S(2)}, u32[]{:S(2)}) collective-permute-start(f32[2,128,512]{2,1,0:T(8,128)} %get-tuple-element.91), channel_id=1, source_target_pairs={{0,2},{2,0},{4,6},{6,4},{8,10},{10,8},{12,14},{14,12},{1,3},{3,1},... | collective-permute-start | bytes 1572872 | tf_op jit(solution)/shard_map/ppermute | solution.py:335
  62.9 1.4 copy-start.7
  64.3 5.3 %copy-start.27 = (f32[2,128,512]{2,1,0:T(8,128)S(1)}, f32[2,128,512]{2,1,0:T(8,128)}, u32[]{:S(2)}) copy-start(f32[2,128,512]{2,1,0:T(8,128)} %copy-done.26) | copy-start | bytes 1572868
  64.3 6.0 %copy-start.17 = (f32[2,128,128]{2,1,0:T(8,128)S(1)}, f32[2,128,128]{2,1,0:T(8,128)}, u32[]{:S(2)}) copy-start(f32[2,128,128]{2,1,0:T(8,128)} %copy-done.16) | copy-start | bytes 393220
  64.3 6.0 %copy-start.25 = (bf16[384,512]{1,0:T(8,128)(2,1)S(1)}, bf16[384,512]{1,0:T(8,128)(2,1)}, u32[]{:S(2)}) copy-start(bf16[384,512]{1,0:T(8,128)(2,1)} %copy-done.24) | copy-start | bytes 1179652
  67.3 9.6 %copy-start.23 = (bf16[384,512]{1,0:T(8,128)(2,1)S(1)}, bf16[384,512]{1,0:T(8,128)(2,1)}, u32[]{:S(2)}) copy-start(bf16[384,512]{1,0:T(8,128)(2,1)} %copy-done.22) | copy-start | bytes 1179652
  67.3 14.0 %collective-permute-start.16 = (f32[2,128,128]{2,1,0:T(8,128)S(1)}, f32[2,128,128]{2,1,0:T(8,128)S(1)}, u32[]{:S(2)}, u32[]{:S(2)}) collective-permute-start(f32[2,128,128]{2,1,0:T(8,128)S(1)} %add.133), channel_id=1, source_target_pairs={{4,0},{6,2},{8,4},{10,6},{12,8},{14,10},{5,1},{7,3},{9,5},{11,7},{... | collective-permute-start | bytes 393224 | tf_op jit(solution)/shard_map/ppermute | solution.py:204
  69.6 19.4 %collective-permute-start.19 = (f32[2,128,512]{2,1,0:T(8,128)S(1)}, f32[2,128,512]{2,1,0:T(8,128)S(1)}, u32[]{:S(2)}, u32[]{:S(2)}) collective-permute-start(f32[2,128,512]{2,1,0:T(8,128)S(1)} %copy-done.27), channel_id=1, source_target_pairs={{0,2},{2,0},{4,6},{6,4},{8,10},{10,8},{12,14},{14,12},{1,3},{3,1},... | collective-permute-start | bytes 1572872 | tf_op jit(solution)/shard_map/ppermute | solution.py:335
  75.6 7.8 %collective-permute-start.13 = (f32[2,128,128]{2,1,0:T(8,128)S(1)}, f32[2,128,128]{2,1,0:T(8,128)S(1)}, u32[]{:S(2)}, u32[]{:S(2)}) collective-permute-start(f32[2,128,128]{2,1,0:T(8,128)S(1)} %add.129), channel_id=1, source_target_pairs={{8,0},{10,2},{12,4},{14,6},{9,1},{11,3},{13,5},{15,7},{24,16},{26,... | collective-permute-start | bytes 393224 | tf_op jit(solution)/shard_map/ppermute | solution.py:204
  77.0 6.5 %copy-start.21 = (f32[2,128,128]{2,1,0:T(8,128)S(1)}, f32[2,128,128]{2,1,0:T(8,128)}, u32[]{:S(2)}) copy-start(f32[2,128,128]{2,1,0:T(8,128)} %copy-done.20) | copy-start | bytes 393220
  77.0 6.5 %copy-start.29 = (f32[2,128,128]{2,1,0:T(8,128)S(1)}, f32[2,128,128]{2,1,0:T(8,128)}, u32[]{:S(2)}) copy-start(f32[2,128,128]{2,1,0:T(8,128)} %copy-done.28) | copy-start | bytes 393220
  77.0 8.9 %copy-start.15 = (f32[2,128,512]{2,1,0:T(8,128)S(1)}, f32[2,128,512]{2,1,0:T(8,128)}, u32[]{:S(2)}) copy-start(f32[2,128,512]{2,1,0:T(8,128)} %copy-done.14) | copy-start | bytes 1572868
  81.4 7.6 %copy-start.13 = (f32[2,128,512]{2,1,0:T(8,128)S(1)}, f32[2,128,512]{2,1,0:T(8,128)}, u32[]{:S(2)}) copy-start(f32[2,128,512]{2,1,0:T(8,128)} %copy-done.12) | copy-start | bytes 1572868
  81.4 9.0 %collective-permute-start.17 = (f32[2,128,128]{2,1,0:T(8,128)S(1)}, f32[2,128,128]{2,1,0:T(8,128)S(1)}, u32[]{:S(2)}, u32[]{:S(2)}) collective-permute-start(f32[2,128,128]{2,1,0:T(8,128)S(1)} %add.134), channel_id=1, source_target_pairs={{8,0},{10,2},{12,4},{14,6},{9,1},{11,3},{13,5},{15,7},{24,16},{26,... | collective-permute-start | bytes 393224 | tf_op jit(solution)/shard_map/ppermute | solution.py:204
  84.4 34.7 %collective-permute-start.14 = (f32[2,128,128]{2,1,0:T(8,128)S(1)}, f32[2,128,128]{2,1,0:T(8,128)S(1)}, u32[]{:S(2)}, u32[]{:S(2)}) collective-permute-start(f32[2,128,128]{2,1,0:T(8,128)S(1)} %get-tuple-element.103), channel_id=1, source_target_pairs={{0,2},{2,0},{4,6},{6,4},{8,10},{10,8},{12,14},{14,12},{1,3},{3,1},... | collective-permute-start | bytes 393224 | tf_op jit(solution)/shard_map/ppermute | solution.py:213
  87.0 3.5 %copy-start.19 = (f32[2,128,128]{2,1,0:T(8,128)S(1)}, f32[2,128,128]{2,1,0:T(8,128)}, u32[]{:S(2)}) copy-start(f32[2,128,128]{2,1,0:T(8,128)} %copy-done.18) | copy-start | bytes 393220
  87.0 9.6 %collective-permute-start.28 = (f32[128,512]{1,0:T(8,128)S(1)}, f32[128,512]{1,0:T(8,128)S(1)}, u32[]{:S(2)}, u32[]{:S(2)}) collective-permute-start(f32[128,512]{1,0:T(8,128)S(1)} %select_bitcast_fusion.2), channel_id=1, source_target_pairs={{0,4},{2,6},{12,8},{14,10},{1,5},{3,7},{13,9},{15,11},{16,20},{18,... | collective-permute-start | bytes 786440 | tf_op jit(solution)/shard_map/ppermute | solution.py:345
  88.3 14.9 %collective-permute-start.31 = (f32[2,128,512]{2,1,0:T(8,128)S(1)}, f32[2,128,512]{2,1,0:T(8,128)S(1)}, u32[]{:S(2)}, u32[]{:S(2)}) collective-permute-start(f32[2,128,512]{2,1,0:T(8,128)S(1)} %get-tuple-element.94), channel_id=1, source_target_pairs={{0,2},{2,0},{4,6},{6,4},{8,10},{10,8},{12,14},{14,12},{1,3},{3,1},... | collective-permute-start | bytes 1572872 | tf_op jit(solution)/shard_map/ppermute | solution.py:335
  89.1 10.3 %collective-permute-start.20 = (f32[128,512]{1,0:T(8,128)S(1)}, f32[128,512]{1,0:T(8,128)S(1)}, u32[]{:S(2)}, u32[]{:S(2)}) collective-permute-start(f32[128,512]{1,0:T(8,128)S(1)} %select_bitcast_fusion.5), channel_id=1, source_target_pairs={{0,4},{2,6},{12,8},{14,10},{1,5},{3,7},{13,9},{15,11},{16,20},{18,... | collective-permute-start | bytes 786440 | tf_op jit(solution)/shard_map/ppermute | solution.py:345
  91.4 28.9 %collective-permute-start.18 = (f32[2,128,128]{2,1,0:T(8,128)S(1)}, f32[2,128,128]{2,1,0:T(8,128)S(1)}, u32[]{:S(2)}, u32[]{:S(2)}) collective-permute-start(f32[2,128,128]{2,1,0:T(8,128)S(1)} %get-tuple-element.101), channel_id=1, source_target_pairs={{0,2},{2,0},{4,6},{6,4},{8,10},{10,8},{12,14},{14,12},{1,3},{3,1},... | collective-permute-start | bytes 393224 | tf_op jit(solution)/shard_map/ppermute | solution.py:213
  96.6 17.7 %collective-permute-start.23 = (f32[2,128,512]{2,1,0:T(8,128)S(1)}, f32[2,128,512]{2,1,0:T(8,128)S(1)}, u32[]{:S(2)}, u32[]{:S(2)}) collective-permute-start(f32[2,128,512]{2,1,0:T(8,128)S(1)} %get-tuple-element.89), channel_id=1, source_target_pairs={{0,2},{2,0},{4,6},{6,4},{8,10},{10,8},{12,14},{14,12},{1,3},{3,1},... | collective-permute-start | bytes 1572872 | tf_op jit(solution)/shard_map/ppermute | solution.py:335
  99.4 9.6 %collective-permute-start.29 = (f32[128,512]{1,0:T(8,128)S(1)}, f32[128,512]{1,0:T(8,128)S(1)}, u32[]{:S(2)}, u32[]{:S(2)}) collective-permute-start(f32[128,512]{1,0:T(8,128)S(1)} %fusion.4), channel_id=1, source_target_pairs={{4,8},{6,10},{8,4},{10,6},{5,9},{7,11},{9,5},{11,7},{20,24},{22,26... | collective-permute-start | bytes 786440 | tf_op jit(solution)/shard_map/ppermute | solution.py:346
  103.2 29.1 %collective-permute-start.21 = (f32[128,512]{1,0:T(8,128)S(1)}, f32[128,512]{1,0:T(8,128)S(1)}, u32[]{:S(2)}, u32[]{:S(2)}) collective-permute-start(f32[128,512]{1,0:T(8,128)S(1)} %fusion.3), channel_id=1, source_target_pairs={{4,8},{6,10},{8,4},{10,6},{5,9},{7,11},{9,5},{11,7},{20,24},{22,26... | collective-permute-start | bytes 786440 | tf_op jit(solution)/shard_map/ppermute | solution.py:346
  109.0 8.4 %collective-permute-start.33 = (f32[128,512]{1,0:T(8,128)S(1)}, f32[128,512]{1,0:T(8,128)S(1)}, u32[]{:S(2)}, u32[]{:S(2)}) collective-permute-start(f32[128,512]{1,0:T(8,128)S(1)} %get-tuple-element.98), channel_id=1, source_target_pairs={{0,4},{2,6},{12,8},{14,10},{1,5},{3,7},{13,9},{15,11},{16,20},{18,... | collective-permute-start | bytes 786440 | tf_op jit(solution)/shard_map/ppermute | solution.py:350
  114.4 20.7 %collective-permute-start.30 = (f32[128,512]{1,0:T(8,128)S(1)}, f32[128,512]{1,0:T(8,128)S(1)}, u32[]{:S(2)}, u32[]{:S(2)}) collective-permute-start(f32[128,512]{1,0:T(8,128)S(1)} %bitcast_add_fusion.1), channel_id=1, source_target_pairs={{8,12},{10,14},{4,0},{6,2},{9,13},{11,15},{5,1},{7,3},{24,28},{26,... | collective-permute-start | bytes 786440 | tf_op jit(solution)/shard_map/ppermute | solution.py:347
  117.2 8.9 %copy-start.9 = (bf16[1024,2048]{1,0:T(8,128)(2,1)S(1)}, bf16[1024,2048]{1,0:T(8,128)(2,1)}, u32[]{:S(2)}) copy-start(bf16[1024,2048]{1,0:T(8,128)(2,1)} %w_ref.3) | copy-start | bytes 12582916
  117.4 21.7 %collective-permute-start.32 = (f32[128,512]{1,0:T(8,128)S(1)}, f32[128,512]{1,0:T(8,128)S(1)}, u32[]{:S(2)}, u32[]{:S(2)}) collective-permute-start(f32[128,512]{1,0:T(8,128)S(1)} %get-tuple-element.97), channel_id=1, source_target_pairs={{0,4},{2,6},{12,8},{14,10},{1,5},{3,7},{13,9},{15,11},{16,20},{18,... | collective-permute-start | bytes 786440 | tf_op jit(solution)/shard_map/ppermute | solution.py:351
  119.0 14.7 %collective-permute-start.25 = (f32[128,512]{1,0:T(8,128)S(1)}, f32[128,512]{1,0:T(8,128)S(1)}, u32[]{:S(2)}, u32[]{:S(2)}) collective-permute-start(f32[128,512]{1,0:T(8,128)S(1)} %get-tuple-element.96), channel_id=1, source_target_pairs={{0,4},{2,6},{12,8},{14,10},{1,5},{3,7},{13,9},{15,11},{16,20},{18,... | collective-permute-start | bytes 786440 | tf_op jit(solution)/shard_map/ppermute | solution.py:350
  120.3 18.7 %collective-permute-start.34 = (f32[128,512]{1,0:T(8,128)S(1)}, f32[128,512]{1,0:T(8,128)S(1)}, u32[]{:S(2)}, u32[]{:S(2)}) collective-permute-start(f32[128,512]{1,0:T(8,128)S(1)} %add.152), channel_id=1, source_target_pairs={{4,8},{6,10},{8,4},{10,6},{5,9},{7,11},{9,5},{11,7},{20,24},{22,26... | collective-permute-start | bytes 786440 | tf_op jit(solution)/shard_map/ppermute | solution.py:352
  132.4 6.8 %collective-permute-start.22 = (f32[128,512]{1,0:T(8,128)S(1)}, f32[128,512]{1,0:T(8,128)S(1)}, u32[]{:S(2)}, u32[]{:S(2)}) collective-permute-start(f32[128,512]{1,0:T(8,128)S(1)} %bitcast_add_fusion.3), channel_id=1, source_target_pairs={{8,12},{10,14},{4,0},{6,2},{9,13},{11,15},{5,1},{7,3},{24,28},{26,... | collective-permute-start | bytes 786440 | tf_op jit(solution)/shard_map/ppermute | solution.py:347
  133.7 8.3 %collective-permute-start.24 = (f32[128,512]{1,0:T(8,128)S(1)}, f32[128,512]{1,0:T(8,128)S(1)}, u32[]{:S(2)}, u32[]{:S(2)}) collective-permute-start(f32[128,512]{1,0:T(8,128)S(1)} %get-tuple-element.95), channel_id=1, source_target_pairs={{0,4},{2,6},{12,8},{14,10},{1,5},{3,7},{13,9},{15,11},{16,20},{18,... | collective-permute-start | bytes 786440 | tf_op jit(solution)/shard_map/ppermute | solution.py:351
  135.1 8.3 %collective-permute-start.26 = (f32[128,512]{1,0:T(8,128)S(1)}, f32[128,512]{1,0:T(8,128)S(1)}, u32[]{:S(2)}, u32[]{:S(2)}) collective-permute-start(f32[128,512]{1,0:T(8,128)S(1)} %add.144), channel_id=1, source_target_pairs={{4,8},{6,10},{8,4},{10,6},{5,9},{7,11},{9,5},{11,7},{20,24},{22,26... | collective-permute-start | bytes 786440 | tf_op jit(solution)/shard_map/ppermute | solution.py:352
  (1 other events, 0.7 us)

commit v3 on v2

v3 whole, which is shorter than its diff:
```python
import functools
import math

import jax
import jax.numpy as jnp
from jax import lax
from jax.experimental import pallas as pl
from jax.experimental.pallas import tpu as pltpu
from jax.sharding import PartitionSpec as P

H = 8
HD = 128
PAIR = 2 * HD
PAIRS = H // 2
FAR = (0, 3)
NEAR = (1, 2)
WIDTHS = ((4, 4), (5, 3))
EPSILON = 1e-06
F32 = jnp.float32
BF16 = jnp.bfloat16
VMEM = pltpu.VMEM
VMEM_LIMIT = 16 << 20
COST = 16

NN = (((1,), (0,)), ((), ()))
NT = (((1,), (1,)), ((), ()))
TN = (((0,), (0,)), ((), ()))


def dot(a, b, dims):
    return lax.dot_general(a, b, dims, preferred_element_type=F32)


def halves(a):
    high = a.astype(BF16)
    return high, (a - high.astype(F32)).astype(BF16)


def two_pass(a, b, dims):
    high, low = halves(a)
    return dot(high, b, dims) + dot(low, b, dims)


def two_pass_right(a, b, dims):
    high, low = halves(b)
    return dot(a, high, dims) + dot(a, low, dims)


def causal(length, lower):
    rows = lax.broadcasted_iota(jnp.int32, (length, length), 0)
    cols = lax.broadcasted_iota(jnp.int32, (length, length), 1)
    return rows >= cols if lower else rows <= cols


def at(position, size=HD):
    if isinstance(position, int):
        return pl.ds(position * size, size)
    return pl.ds(pl.multiple_of(position * size, size), size)


def shape(dims, dtype):
    return jax.ShapeDtypeStruct(dims, dtype)


def call(body, out_shapes, operands, flops, name):
    specs = []
    for operand in operands:
        space = pltpu.SMEM if operand.dtype == jnp.int32 else VMEM
        specs.append(pl.BlockSpec(memory_space=space))
    return pl.pallas_call(
        body,
        out_shape=tuple(out_shapes),
        in_specs=specs,
        out_specs=tuple(pl.BlockSpec(memory_space=VMEM) for _ in out_shapes),
        compiler_params=pltpu.CompilerParams(vmem_limit_bytes=VMEM_LIMIT),
        cost_estimate=pl.CostEstimate(flops=flops // COST, bytes_accessed=0, transcendentals=0),
        name=name,
    )(*operands)


def after(value, *others):
    return lax.optimization_barrier((value, *others))[0]


def state_body(place, k_ref, v_ref, keep_ref, send_ref):
    low = place[0]
    for j in range(PAIRS):
        for out, head in ((send_ref, 2 * j + 1 - low), (keep_ref, 2 * j + low)):
            out[j] = dot(k_ref[:, at(head)], v_ref[:, at(head)], TN)


def away_body(place, g_ref, out_ref):
    half = out_ref.shape[1]
    out_ref[...] = g_ref[:, at(1 - place[1], half)].astype(F32)


def local_body(q_ref, k_ref, v_ref, out_ref):
    mask = causal(q_ref.shape[0], True)
    for h in range(H):
        scores = dot(q_ref[:, at(h)], k_ref[:, at(h)], NT)
        scores = jnp.where(mask, scores, 0.0)
        out_ref[:, at(h)] = two_pass(scores, v_ref[:, at(h)], NN)


def d_normed_body(g_ref, w_ref, out_ref):
    @pl.loop(0, PAIRS)
    def _(j):
        out_ref[:, at(j, PAIR)] = dot(g_ref[...], w_ref[at(j, PAIR), :], NT)


def norm_body(rows, place, q_ref, att_ref, dn_ref, own_ref, other_ref, *refs):
    low = place[0]
    nb_ref, nb32_ref, da_ref, keep_ref, send_ref = refs[-5:]
    whole = keep_ref.shape[0] == PAIRS
    if whole:
        for i, j in enumerate(FAR):
            keep_ref[j] = refs[0][i]
            send_ref[j] = refs[1][i]
    for i, j in enumerate(rows):
        for prior, out, part in ((own_ref, keep_ref, low), (other_ref, send_ref, 1 - low)):
            here, there = at(2 * j + part), at(2 * i + part)
            q = q_ref[:, here]
            attended = att_ref[:, here] + two_pass_right(q, prior[j], NN)
            inverse = lax.rsqrt(jnp.mean(attended * attended, axis=-1, keepdims=True) + EPSILON)
            normed = attended * inverse
            rounded = normed.astype(BF16)
            nb_ref[:, there] = rounded
            nb32_ref[:, there] = rounded.astype(F32)
            d_normed = dn_ref[:, here]
            mean = jnp.mean(d_normed * normed, axis=-1, keepdims=True)
            d_att = (inverse * (d_normed - normed * mean)).astype(BF16)
            da_ref[:, there] = d_att
            out[j if whole else i] = dot(q, d_att, TN)


def grads_body(
    place, q_ref, k_ref, v_ref, far_ref, near_ref, own_ref, other_ref, qg_ref, kl_ref, vl_ref
):
    low = place[0]
    lower = causal(q_ref.shape[0], True)
    upper = causal(q_ref.shape[0], False)
    for da_ref, rows in ((far_ref, FAR), (near_ref, NEAR)):
        for i, j in enumerate(rows):
            for prior, part in ((own_ref, low), (other_ref, 1 - low)):
                here, there = at(2 * j + part), at(2 * i + part)
                q, k, v, d_att = q_ref[:, here], k_ref[:, here], v_ref[:, here], da_ref[:, there]
                cross = jnp.where(lower, dot(d_att, v, NT), 0.0)
                part_sum = two_pass(cross, k, NN) + two_pass_right(d_att, prior[j], NT)
                qg_ref[:, here] = part_sum.astype(BF16)
                cross = jnp.where(upper, dot(v, d_att, NT), 0.0)
                kl_ref[:, here] = two_pass(cross, q, NN)
                scores = jnp.where(upper, dot(k, q, NT), 0.0)
                vl_ref[:, here] = two_pass(scores, d_att, NN)


def final_body(place, k_ref, v_ref, kl_ref, vl_ref, own_ref, other_ref, kg_ref, vg_ref):
    low = place[0]
    for j in range(PAIRS):
        for later, part in ((own_ref, low), (other_ref, 1 - low)):
            here = at(2 * j + part)
            high, rest = halves(later[j])
            v, k = v_ref[:, here], k_ref[:, here]
            kg_ref[:, here] = (kl_ref[:, here] + (dot(v, high, NT) + dot(v, rest, NT))).astype(BF16)
            vg_ref[:, here] = (vl_ref[:, here] + (dot(k, high, NN) + dot(k, rest, NN))).astype(BF16)


def weight_body(place, nb_ref, g_ref, nbo_ref, go_ref, *outs):
    low, core = place[0], place[1]
    half = go_ref.shape[1]
    mine = nb_ref[...]
    theirs = nbo_ref[...].astype(BF16)
    start = 0
    for keep, send in zip(outs[::2], outs[1::2]):
        width = keep.shape[2]
        ours = g_ref[:, pl.ds(pl.multiple_of(core * half + start, HD), width)]
        other = go_ref[:, start : start + width].astype(BF16)
        start += width
        product = dot(mine, ours, TN) + dot(theirs, other, TN)
        for i in range(2):
            first = product[2 * i * HD : (2 * i + 1) * HD]
            second = product[(2 * i + 1) * HD : (2 * i + 2) * HD]
            keep[i] = jnp.where(low == 0, first, second)
            send[i] = jnp.where(low == 0, second, first)


def output_body(far_ref, near_ref, w_ref, out_ref):
    size = 2 * PAIR

    @pl.loop(0, out_ref.shape[1] // size)
    def _(c):
        total = dot(near_ref[...], w_ref[PAIR : 3 * PAIR, at(c, size)], NN)
        total += dot(far_ref[:, :PAIR], w_ref[:PAIR, at(c, size)], NN)
        total += dot(far_ref[:, PAIR:], w_ref[3 * PAIR :, at(c, size)], NN)
        out_ref[:, at(c, size)] = total.astype(BF16)


def exclusive(keep, send, count, even, reverse, pins):
    swap = [(s, s ^ 1) for s in range(count)]
    sign = -2 if reverse else 2
    pairs = count // 2

    def first(here, there):
        return jnp.where(even, there, here) if reverse else jnp.where(even, here, there)

    def links(step):
        return [(s, s + sign * step) for s in range(count) if 0 <= s + sign * step < count]

    received = lax.ppermute(send, "seq", swap)
    total = keep + received
    outside = None
    step = 1
    while step < pairs:
        pinned = pins.pop(0) if pins else ()
        total = after(total, *pinned)
        got = lax.ppermute(total, "seq", links(step))
        outside = got if step == 1 else outside + got
        total = total + got
        step *= 2
    pinned = pins.pop(0) if pins else ()
    mine = first(outside, outside + received)
    theirs = after(first(outside + keep, outside), *pinned)
    return mine, lax.ppermute(theirs, "seq", swap)


def per_device(queries, keys, values, out_weight, out_grad):
    count = lax.axis_size("seq")
    cores = lax.axis_size("dp")
    spot = lax.axis_index("seq")
    core = lax.axis_index("dp")
    low, level = spot & 1, spot >> 1
    place = jnp.stack([low, core]).astype(jnp.int32)
    place, even, lower, outer = lax.optimization_barrier(
        (place, low == 0, level < 2, (level == 0) | (level == 3))
    )
    q, k, v, g = queries[0], keys[0], values[0], out_grad[0]
    length, features = q.shape
    width = g.shape[1]
    part = features // 2
    half = width // 2
    state = shape((PAIRS, HD, HD), F32)
    rows32 = shape((length, features), F32)
    rows16 = shape((length, features), BF16)
    unit = 2 * H * length * HD
    fast = count == 8 and cores == 2
    swap = [(0, 1), (1, 0)]

    keep, send = call(state_body, (state, state), (place, k, v), unit * HD, "state")
    away = g
    if fast:
        (away,) = call(away_body, (shape((length, half), F32),), (place, g), unit, "away")
        go = lax.ppermute(away, "dp", swap)
    (att,) = call(local_body, (rows32,), (q, k, v), 3 * unit * length, "local")
    (d_normed,) = call(d_normed_body, (rows32,), (g, out_weight), unit * width, "d_normed")
    own, other = exclusive(keep, send, count, even, False, [(away, att), (d_normed,)])

    pieces = (shape((length, part), BF16), shape((length, part), F32), shape((length, part), BF16))
    some = shape((2, HD, HD), F32)
    far, far32, far_att, *some_states = call(
        functools.partial(norm_body, FAR),
        pieces + (some, some),
        (place, q, att, d_normed, own, other),
        unit * HD,
        "norm_far",
    )
    near, near32, near_att, keep, send = call(
        functools.partial(norm_body, NEAR),
        pieces + (state, state),
        (place, q, att, d_normed, own, other, *some_states),
        unit * HD * 64,
        "norm_near",
    )

    scale = 1.0 / math.sqrt(length * count * cores)
    if fast:
        chunks = []
        for nb, nb32, widths in ((far, far32, WIDTHS[0]), (near, near32, WIDTHS[1])):
            nbo = lax.ppermute(nb32, "dp", swap)
            blocks = []
            for w in widths:
                block = shape((2, HD, w * half // sum(widths)), F32)
                blocks += [block, block]
            if chunks:
                nb = after(nb, chunks[0][1][1])
            out = call(weight_body, tuple(blocks), (place, nb, g, nbo, go), unit * half, "weight")
            chunks.append([(out[0], out[1]), (out[2], out[3])])
        ready = (chunks[1][0][1],)
        early = chunks[0][0][1]
        weight_grad, landed = scatter(chunks, lower, outer)
        weight_grad = weight_grad * scale
    else:
        nb = jnp.concatenate([far[:, :PAIR], near, far[:, PAIR:]], axis=1)
        product = lax.dot_general(nb, g, TN, preferred_element_type=F32)
        product = lax.psum_scatter(product, "dp", scatter_dimension=1, tiled=True)
        weight_grad = lax.psum_scatter(product, "seq", scatter_dimension=0, tiled=True) * scale
        ready, early, landed = (), near, near

    query_grad, key_local, value_local = call(
        grads_body,
        (rows16, rows32, rows32),
        (place, q, k, v, after(far_att, landed), near_att, own, other),
        9 * unit * length,
        "grads",
    )
    (output,) = call(
        output_body,
        (shape((length, width), BF16),),
        (after(far, *ready), near, out_weight),
        unit * width,
        "output",
    )
    pins = [(early,), (output,), (key_local,)]
    own_later, other_later = exclusive(keep, send, count, even, True, pins)

    key_grad, value_grad = call(
        final_body,
        (rows16, rows16),
        (place, k, v, key_local, value_local, own_later, other_later),
        4 * unit * HD,
        "final",
    )
    return output[None], query_grad[None], key_grad[None], value_grad[None], weight_grad


def scatter(chunks, lower, outer):
    swap = [(s, s ^ 1) for s in range(8)]

    def on(links):
        return [(2 * a + i, 2 * b + i) for a, b in links for i in range(2)]

    inward = on([(0, 1), (3, 2)])
    middle = on([(1, 2), (2, 1)])
    outward = on([(2, 3), (1, 0)])

    def paired(chunk, *pinned):
        keep, send = chunk
        base = keep + lax.ppermute(after(send, *pinned), "seq", swap)
        return jnp.where(lower, base[1], base[0]), jnp.where(lower, base[0], base[1])

    far, near, pins = [], [], []
    for chunk in chunks[0]:
        up, down = paired(chunk)
        pins.append(up)
        got = lax.ppermute(up, "seq", inward)
        got = lax.ppermute(up + got, "seq", middle)
        got = lax.ppermute(down + got, "seq", outward)
        far.append(down + got)
    for chunk, pin in zip(chunks[1], ((), pins[:1])):
        up, down = paired(chunk, *pin)
        got = lax.ppermute(up, "seq", inward)
        direct = lax.ppermute(down, "seq", inward)
        got = lax.ppermute(up + got, "seq", middle)
        near.append((down + direct) + got)
    total = jnp.where(outer, jnp.concatenate(far, axis=1), jnp.concatenate(near, axis=1))
    return total, pins[0]


def solution(mesh):
    rows = P(("parts", "dp"), "seq", None)
    return jax.shard_map(
        per_device,
        mesh=mesh,
        in_specs=(rows, rows, rows, P(), rows),
        out_specs=(rows, rows, rows, rows, P(("parts", "seq"), "dp")),
        check_vma=False,
    )
```

time: 146 us -> 136 us (0.932); the launches traced: 144 us -> 136 us
  waiting for transfers between devices: 24.9 us -> 51.8 us
  starting transfers between devices: 61.3 us -> 47.6 us
  other arithmetic: 12.1 us -> 2.2 us
  local copies, waits for them, and re-layouts: 11.6 us -> 2.85 us
  Pallas kernels: 33.2 us -> 30.4 us
    ppermute x16 -> x8, waiting for transfers between devices: 8.47 us -> 38.8 us  [the longest x4 20.2 us: exclusive(): got = lax.ppermute(total, 'seq', links(step))]
    ppermute x16 -> x8, starting transfers between devices: 29.5 us -> 17.3 us  [the longest x4 11.2 us: exclusive(): got = lax.ppermute(total, 'seq', links(step))]
    unnamed x60 -> x10, local copies, waits for them, and re-layouts: 11.6 us -> 2.85 us
    select_n x6 -> x2, other arithmetic: 3.17 us -> 0.15 us  [the longest x1 0.08 us: first(): jnp.where(even, there, here)]
    pallas_call x11, Pallas kernels: 33.2 us -> 30.4 us  [call(): pl.pallas_call(body, out_shape=tuple(out_shapes), in_specs=specs, out_spe...]
    ppermute x2, waiting for transfers between devices: 2.75 us -> 0.01 us  [scatter(): direct = lax.ppermute(down, 'seq', inward)]
    convert_element_type x1 -> x0, other arithmetic: 2.47 us -> none  [per_device(): lax.dynamic_slice_in_dim(g, (1 - core) * half, half, axis=1).astype(F32)]
    add x8, other arithmetic: 2.74 us -> 0.36 us  [the longest x2 0.12 us: scatter(): far.append(down + got)]
  transfers between devices with their start and end apart: 35 -> 27, of which waited for: 13 -> 13; matrix products, arithmetic and copies ran while one was open for 8% -> 1% of each run, Pallas kernels for 22% -> 22%
where the time goes in v3:
time: 136 us
  waiting for transfers between devices  51.8 us (38%)
  starting transfers between devices  47.6 us (35%)
  Pallas kernels  30.4 us (22%)
  local copies, waits for them, and re-layouts  2.85 us (2%)
  other arithmetic  2.2 us (2%)
    pallas_call x11, Pallas kernels, call(): pl.pallas_call(body, out_shape=tuple(out_shapes), in_specs=specs, out_spe...  30.4 us
    ppermute x4, waiting for transfers between devices, exclusive(): got = lax.ppermute(total, 'seq', links(step))  20.2 us
    ppermute x4, starting transfers between devices, scatter(): got = lax.ppermute(up + got, 'seq', middle)  14.7 us
    ppermute x4, starting transfers between devices, exclusive(): got = lax.ppermute(total, 'seq', links(step))  11.2 us
    ppermute x2, waiting for transfers between devices, exclusive(): return (mine, lax.ppermute(theirs, 'seq', swap))  10.4 us
    ppermute x2, waiting for transfers between devices, exclusive(): received = lax.ppermute(send, 'seq', swap)  8.2 us
    ppermute x4, starting transfers between devices, scatter(): got = lax.ppermute(up, 'seq', inward)  5.35 us
    ppermute x4, waiting for transfers between devices, paired(): base = keep + lax.ppermute(after(send, *pinned), 'seq', swap)  5.24 us
  transfers between devices with their start and end apart: 27, of which 13 were waited for; matrix products, arithmetic and copies ran while one was open for 1% of the time, Pallas kernels for 22%

profile of v3, /device:TPU:12, one launch (start us, length us, event | category | flops | bytes accessed | tf_op | source)
XLA Modules:
  0.0 136.0 jit_solution(16244800106918265247)
XLA Ops:
  0.7 0.1 pad_add_fusion.place
  0.7 1.2 copy-done.3
  2.0 1.1 copy-done.4
  3.1 1.1 state.1
  4.2 1.6 %collective-permute-start = (f32[4,128,128]{2,1,0:T(8,128)S(1)}, f32[4,128,128]{2,1,0:T(8,128)S(1)}, u32[]{:S(2)}, u32[]{:S(2)}) collective-permute-start(f32[4,128,128]{2,1,0:T(8,128)S(1)} %get-tuple-element.46), channel_id=1, source_target_pairs={{0,2},{2,0},{4,6},{6,4},{8,10},{10,8},{12,14},{14,12},{1,3},{3,1},... | collective-permute-start | bytes 786440 | tf_op jit(solution)/shard_map/ppermute | solution.py:208
  5.8 0.6 away.1
  6.4 0.5 copy-done.2
  6.9 2.4 %local.1.att_ref = f32[384,1024]{1,0:T(8,128)S(1)} custom-call(bf16[384,1024]{1,0:T(8,128)(2,1)S(1)} %bitcast.36, bf16[384,1024]{1,0:T(8,128)(2,1)S(1)} %bitcast.41, bf16[384,1024]{1,0:T(8,128)(2,1)S(1)} %bitcast.45), custom_call_target="tpu_custom_call" | custom-call | flops 56623104 | tf_op jit(solution)/shard_map/local/pallas_call | solution.py:70
  9.3 3.0 %collective-permute-done = f32[4,128,128]{2,1,0:T(8,128)S(1)} collective-permute-done((f32[4,128,128]{2,1,0:T(8,128)S(1)}, f32[4,128,128]{2,1,0:T(8,128)S(1)}, u32[]{:S(2)}, u32[]{:S(2)}) %collective-permute-start) | collective-permute-done | bytes 262176 | tf_op jit(solution)/shard_map/ppermute | solution.py:208
  12.4 3.5 %collective-permute-start.1 = (f32[4,128,128]{2,1,0:T(8,128)S(1)}, f32[4,128,128]{2,1,0:T(8,128)S(1)}, u32[]{:S(2)}, u32[]{:S(2)}) collective-permute-start(f32[4,128,128]{2,1,0:T(8,128)S(1)} %add.78), channel_id=1, source_target_pairs={{0,4},{2,6},{4,8},{6,10},{8,12},{10,14},{1,5},{3,7},{5,9},{7,11},{... | collective-permute-start | bytes 786440 | tf_op jit(solution)/shard_map/ppermute | solution.py:215
  15.9 2.4 %d_normed.1.dn_ref = f32[384,1024]{1,0:T(8,128)S(1)} custom-call(bf16[384,2048]{1,0:T(8,128)(2,1)S(1)} %bitcast.33, bf16[1024,2048]{1,0:T(8,128)(2,1)S(1)} %copy-done.1), custom_call_target="tpu_custom_call" | custom-call | flops 100663296 | tf_op jit(solution)/shard_map/d_normed/pallas_call | solution.py:70
  18.3 3.1 %collective-permute-done.1 = f32[4,128,128]{2,1,0:T(8,128)S(1)} collective-permute-done((f32[4,128,128]{2,1,0:T(8,128)S(1)}, f32[4,128,128]{2,1,0:T(8,128)S(1)}, u32[]{:S(2)}, u32[]{:S(2)}) %collective-permute-start.1) | collective-permute-done | bytes 262176 | tf_op jit(solution)/shard_map/ppermute | solution.py:215
  21.5 4.5 %collective-permute-start.2 = (f32[4,128,128]{2,1,0:T(8,128)S(1)}, f32[4,128,128]{2,1,0:T(8,128)S(1)}, u32[]{:S(2)}, u32[]{:S(2)}) collective-permute-start(f32[4,128,128]{2,1,0:T(8,128)S(1)} %add.79), channel_id=1, source_target_pairs={{0,8},{2,10},{4,12},{6,14},{1,9},{3,11},{5,13},{7,15},{16,24},{18,... | collective-permute-start | bytes 786440 | tf_op jit(solution)/shard_map/ppermute | solution.py:215
  26.0 0.1 collective-permute-start.5
  26.1 9.2 %collective-permute-done.2 = f32[4,128,128]{2,1,0:T(8,128)S(1)} collective-permute-done((f32[4,128,128]{2,1,0:T(8,128)S(1)}, f32[4,128,128]{2,1,0:T(8,128)S(1)}, u32[]{:S(2)}, u32[]{:S(2)}) %collective-permute-start.2) | collective-permute-done | bytes 262176 | tf_op jit(solution)/shard_map/ppermute | solution.py:215
  35.2 0.1 add_select_fusion.2
  35.3 1.6 %collective-permute-start.3 = (f32[4,128,128]{2,1,0:T(8,128)S(1)}, f32[4,128,128]{2,1,0:T(8,128)S(1)}, u32[]{:S(2)}, u32[]{:S(2)}) collective-permute-start(f32[4,128,128]{2,1,0:T(8,128)S(1)} %get-tuple-element.85), channel_id=1, source_target_pairs={{0,2},{2,0},{4,6},{6,4},{8,10},{10,8},{12,14},{14,12},{1,3},{3,1},... | collective-permute-start | bytes 786440 | tf_op jit(solution)/shard_map/ppermute | solution.py:222
  36.9 6.7 %collective-permute-done.3.other_ref = f32[4,128,128]{2,1,0:T(8,128)S(1)} collective-permute-done((f32[4,128,128]{2,1,0:T(8,128)S(1)}, f32[4,128,128]{2,1,0:T(8,128)S(1)}, u32[]{:S(2)}, u32[]{:S(2)}) %collective-permute-start.3) | collective-permute-done | bytes 262176 | tf_op jit(solution)/shard_map/ppermute | solution.py:222
  43.6 2.5 %norm_far.1 = (bf16[384,512]{1,0:T(8,128)(2,1)S(1)}, f32[384,512]{1,0:T(8,128)S(1)}, bf16[384,512]{1,0:T(8,128)(2,1)S(1)}, f32[2,128,128]{2,1,0:T(8,128)S(1)}, f32[2,128,128]{2,1,0:T(8,128)S(1)}) custom-call(s32[2]{0:T(128)S(1)} %pad_add_fusion.place, bf16[384,1024]{1,0:T(8,128)(2,1)S(1)} %bitcast.37, f32[384,1024]{1,0:T(8,128)S(1)} %local.1.att_ref, ...), custom_call_target="tpu_custom_call" | custom-call | flops 6291456 | tf_op jit(solution)/shard_map/norm_far/pallas_call | solution.py:70
  46.1 0.1 collective-permute-start.4
  46.2 2.6 %norm_near.1 = (bf16[384,512]{1,0:T(8,128)(2,1)S(1)}, f32[384,512]{1,0:T(8,128)S(1)}, bf16[384,512]{1,0:T(8,128)(2,1)S(1)}, f32[4,128,128]{2,1,0:T(8,128)S(1)}, f32[4,128,128]{2,1,0:T(8,128)S(1)}) custom-call(s32[2]{0:T(128)S(1)} %pad_add_fusion.place, bf16[384,1024]{1,0:T(8,128)(2,1)S(1)} %bitcast.38, f32[384,1024]{1,0:T(8,128)S(1)} %local.1.att_ref, ...), custom_call_target="tpu_custom_call" | custom-call | flops 402653184 | tf_op jit(solution)/shard_map/norm_near/pallas_call | solution.py:70
  48.8 0.6 collective-permute-start.6
  49.3 1.5 %collective-permute-start.8 = (f32[4,128,128]{2,1,0:T(8,128)S(1)}, f32[4,128,128]{2,1,0:T(8,128)S(1)}, u32[]{:S(2)}, u32[]{:S(2)}) collective-permute-start(f32[4,128,128]{2,1,0:T(8,128)S(1)} %get-tuple-element.69), channel_id=1, source_target_pairs={{0,2},{2,0},{4,6},{6,4},{8,10},{10,8},{12,14},{14,12},{1,3},{3,1},... | collective-permute-start | bytes 786440 | tf_op jit(solution)/shard_map/ppermute | solution.py:208
  50.8 1.8 %weight.2 = (f32[2,128,512]{2,1,0:T(8,128)S(1)}, f32[2,128,512]{2,1,0:T(8,128)S(1)}, f32[2,128,512]{2,1,0:T(8,128)S(1)}, f32[2,128,512]{2,1,0:T(8,128)S(1)}) custom-call(s32[2]{0:T(128)S(1)} %pad_add_fusion.place, bf16[384,512]{1,0:T(8,128)(2,1)S(1)} %get-tuple-element.58.nb_ref.far_ref, bf16[384,2048]{1,0:T(8,128)(2,1)S(1)} %bitcast.34, ...), custom_call_target="tpu_custom_call" | custom-call | flops 50331648 | tf_op jit(solution)/shard_map/weight/pallas_call | solution.py:70
  52.7 0.6 collective-permute-start.7
  53.3 5.2 %collective-permute-done.8 = f32[4,128,128]{2,1,0:T(8,128)S(1)} collective-permute-done((f32[4,128,128]{2,1,0:T(8,128)S(1)}, f32[4,128,128]{2,1,0:T(8,128)S(1)}, u32[]{:S(2)}, u32[]{:S(2)}) %collective-permute-start.8) | collective-permute-done | bytes 262176 | tf_op jit(solution)/shard_map/ppermute | solution.py:208
  58.5 1.9 %collective-permute-start.9 = (f32[4,128,128]{2,1,0:T(8,128)S(1)}, f32[4,128,128]{2,1,0:T(8,128)S(1)}, u32[]{:S(2)}, u32[]{:S(2)}) collective-permute-start(f32[4,128,128]{2,1,0:T(8,128)S(1)} %add.84), channel_id=1, source_target_pairs={{4,0},{6,2},{8,4},{10,6},{12,8},{14,10},{5,1},{7,3},{9,5},{11,7},{... | collective-permute-start | bytes 786440 | tf_op jit(solution)/shard_map/ppermute | solution.py:215
  60.5 2.0 %weight.3 = (f32[2,128,640]{2,1,0:T(8,128)S(1)}, f32[2,128,640]{2,1,0:T(8,128)S(1)}, f32[2,128,384]{2,1,0:T(8,128)S(1)}, f32[2,128,384]{2,1,0:T(8,128)S(1)}) custom-call(s32[2]{0:T(128)S(1)} %pad_add_fusion.place, bf16[384,512]{1,0:T(8,128)(2,1)S(1)} %get-tuple-element.55.nb_ref.near_ref, bf16[384,2048]{1,0:T(8,128)(2,1)S(1)} %bitcast.35, ...), custom_call_target="tpu_custom_call" | custom-call | flops 50331648 | tf_op jit(solution)/shard_map/weight/pallas_call | solution.py:70
  62.5 3.5 %output.1 = bf16[384,2048]{1,0:T(8,128)(2,1)} custom-call(bf16[384,512]{1,0:T(8,128)(2,1)S(1)} %get-tuple-element.58.nb_ref.far_ref, bf16[384,512]{1,0:T(8,128)(2,1)S(1)} %get-tuple-element.55.nb_ref.near_ref, bf16[1024,2048]{1,0:T(8,128)(2,1)S(1)} %copy-done.1), custom_call_target="tpu_custom_call" | custom-call | flops 100663296 | tf_op jit(solution)/shard_map/output/pallas_call | solution.py:70
  66.0 1.0 collective-permute-done.9
  67.0 1.3 collective-permute-start.10
  68.3 1.6 %collective-permute-start.15 = (f32[2,128,512]{2,1,0:T(8,128)S(1)}, f32[2,128,512]{2,1,0:T(8,128)S(1)}, u32[]{:S(2)}, u32[]{:S(2)}) collective-permute-start(f32[2,128,512]{2,1,0:T(8,128)S(1)} %get-tuple-element.54), channel_id=1, source_target_pairs={{0,2},{2,0},{4,6},{6,4},{8,10},{10,8},{12,14},{14,12},{1,3},{3,1},... | collective-permute-start | bytes 1572872 | tf_op jit(solution)/shard_map/ppermute | solution.py:336
  69.9 0.5 collective-permute-start.19
  70.4 0.1 add.83
  70.6 1.3 collective-permute-start.12
  71.9 6.9 %collective-permute-done.10 = f32[4,128,128]{2,1,0:T(8,128)S(1)} collective-permute-done((f32[4,128,128]{2,1,0:T(8,128)S(1)}, f32[4,128,128]{2,1,0:T(8,128)S(1)}, u32[]{:S(2)}, u32[]{:S(2)}) %collective-permute-start.10) | collective-permute-done | bytes 262176 | tf_op jit(solution)/shard_map/ppermute | solution.py:215
  78.8 0.1 add_select_fusion
  78.8 1.6 %collective-permute-start.23 = (f32[2,128,384]{2,1,0:T(8,128)S(1)}, f32[2,128,384]{2,1,0:T(8,128)S(1)}, u32[]{:S(2)}, u32[]{:S(2)}) collective-permute-start(f32[2,128,384]{2,1,0:T(8,128)S(1)} %get-tuple-element.80), channel_id=1, source_target_pairs={{0,2},{2,0},{4,6},{6,4},{8,10},{10,8},{12,14},{14,12},{1,3},{3,1},... | collective-permute-start | bytes 1179656 | tf_op jit(solution)/shard_map/ppermute | solution.py:336
  80.4 2.9 %collective-permute-done.15 = f32[2,128,512]{2,1,0:T(8,128)S(1)} collective-permute-done((f32[2,128,512]{2,1,0:T(8,128)S(1)}, f32[2,128,512]{2,1,0:T(8,128)S(1)}, u32[]{:S(2)}, u32[]{:S(2)}) %collective-permute-start.15) | collective-permute-done | bytes 524320 | tf_op jit(solution)/shard_map/ppermute | solution.py:336
  83.3 0.1 add.92
  83.4 1.5 %collective-permute-start.16 = (f32[128,512]{1,0:T(8,128)S(1)}, f32[128,512]{1,0:T(8,128)S(1)}, u32[]{:S(2)}, u32[]{:S(2)}) collective-permute-start(f32[128,512]{1,0:T(8,128)S(1)} %select_bitcast_fusion.2), channel_id=1, source_target_pairs={{0,4},{2,6},{12,8},{14,10},{1,5},{3,7},{13,9},{15,11},{16,20},{18,... | collective-permute-start | bytes 786440 | tf_op jit(solution)/shard_map/ppermute | solution.py:343
  84.9 8.6 %grads.1 = (bf16[384,1024]{1,0:T(8,128)(2,1)}, f32[384,1024]{1,0:T(8,128)S(1)}, f32[384,1024]{1,0:T(8,128)S(1)}) custom-call(s32[2]{0:T(128)S(1)} %pad_add_fusion.place, bf16[384,1024]{1,0:T(8,128)(2,1)S(1)} %bitcast.39, bf16[384,1024]{1,0:T(8,128)(2,1)S(1)} %bitcast.42, bf16[384,1024]{1,0:T(8,128)(2,1)S(1)} %bitcast.46, ...), custom_call_target="tpu_custom_call" | custom-call | flops 169869312 | tf_op jit(solution)/shard_map/grads/pallas_call | solution.py:70
  93.5 1.5 %collective-permute-start.11 = (f32[4,128,128]{2,1,0:T(8,128)S(1)}, f32[4,128,128]{2,1,0:T(8,128)S(1)}, u32[]{:S(2)}, u32[]{:S(2)}) collective-permute-start(f32[4,128,128]{2,1,0:T(8,128)S(1)} %get-tuple-element.72), channel_id=1, source_target_pairs={{0,2},{2,0},{4,6},{6,4},{8,10},{10,8},{12,14},{14,12},{1,3},{3,1},... | collective-permute-start | bytes 786440 | tf_op jit(solution)/shard_map/ppermute | solution.py:222
  95.0 2.4 %collective-permute-done.19 = f32[2,128,640]{2,1,0:T(8,128)S(1)} collective-permute-done((f32[2,128,640]{2,1,0:T(8,128)S(1)}, f32[2,128,640]{2,1,0:T(8,128)S(1)}, u32[]{:S(2)}, u32[]{:S(2)}) %collective-permute-start.19) | collective-permute-done | bytes 655392 | tf_op jit(solution)/shard_map/ppermute | solution.py:336
  97.3 0.1 add.96
  97.4 0.1 fusion.1
  97.5 4.3 %collective-permute-start.13 = (f32[128,512]{1,0:T(8,128)S(1)}, f32[128,512]{1,0:T(8,128)S(1)}, u32[]{:S(2)}, u32[]{:S(2)}) collective-permute-start(f32[128,512]{1,0:T(8,128)S(1)} %fusion.1), channel_id=1, source_target_pairs={{4,8},{6,10},{8,4},{10,6},{5,9},{7,11},{9,5},{11,7},{20,24},{22,26... | collective-permute-start | bytes 786440 | tf_op jit(solution)/shard_map/ppermute | solution.py:344
  101.8 1.3 collective-permute-start.20
  103.1 1.3 collective-permute-start.21
  104.4 0.1 fusion.2
  104.5 3.7 %collective-permute-done.11.other_ref = f32[4,128,128]{2,1,0:T(8,128)S(1)} collective-permute-done((f32[4,128,128]{2,1,0:T(8,128)S(1)}, f32[4,128,128]{2,1,0:T(8,128)S(1)}, u32[]{:S(2)}, u32[]{:S(2)}) %collective-permute-start.11) | collective-permute-done | bytes 262176 | tf_op jit(solution)/shard_map/ppermute | solution.py:222
  108.2 3.9 %collective-permute-start.17 = (f32[128,512]{1,0:T(8,128)S(1)}, f32[128,512]{1,0:T(8,128)S(1)}, u32[]{:S(2)}, u32[]{:S(2)}) collective-permute-start(f32[128,512]{1,0:T(8,128)S(1)} %fusion.2), channel_id=1, source_target_pairs={{4,8},{6,10},{8,4},{10,6},{5,9},{7,11},{9,5},{11,7},{20,24},{22,26... | collective-permute-start | bytes 786440 | tf_op jit(solution)/shard_map/ppermute | solution.py:344
  112.1 2.8 %final.1 = (bf16[384,1024]{1,0:T(8,128)(2,1)}, bf16[384,1024]{1,0:T(8,128)(2,1)}) custom-call(s32[2]{0:T(128)S(1)} %pad_add_fusion.place, bf16[384,1024]{1,0:T(8,128)(2,1)S(1)} %bitcast.43, bf16[384,1024]{1,0:T(8,128)(2,1)S(1)} %bitcast.47, f32[384,1024]{1,0:T(8,128)S(1)} %get-tuple-element.66.kl_ref, f32[384,1024]{1,0:T(8,128)S(1)} %get-tuple-element.67.vl_ref, ...), custom_call_target="tpu_custom_call" | custom-call | flops 25165824 | tf_op jit(solution)/shard_map/final/pallas_call | solution.py:70
  115.0 1.3 collective-permute-start.14
  116.3 1.3 collective-permute-start.24
  117.6 1.3 collective-permute-start.25
  119.0 3.3 %collective-permute-start.22 = (f32[128,640]{1,0:T(8,128)S(1)}, f32[128,640]{1,0:T(8,128)S(1)}, u32[]{:S(2)}, u32[]{:S(2)}) collective-permute-start(f32[128,640]{1,0:T(8,128)S(1)} %add.98), channel_id=1, source_target_pairs={{4,8},{6,10},{8,4},{10,6},{5,9},{7,11},{9,5},{11,7},{20,24},{22,26... | collective-permute-start | bytes 983048 | tf_op jit(solution)/shard_map/ppermute | solution.py:351
  122.3 3.7 %collective-permute-done.25 = f32[128,384]{1,0:T(8,128)S(1)} collective-permute-done((f32[128,384]{1,0:T(8,128)S(1)}, f32[128,384]{1,0:T(8,128)S(1)}, u32[]{:S(2)}, u32[]{:S(2)}) %collective-permute-start.25) | collective-permute-done | bytes 196640 | tf_op jit(solution)/shard_map/ppermute | solution.py:349
  126.0 1.5 %collective-permute-start.18 = (f32[128,512]{1,0:T(8,128)S(1)}, f32[128,512]{1,0:T(8,128)S(1)}, u32[]{:S(2)}, u32[]{:S(2)}) collective-permute-start(f32[128,512]{1,0:T(8,128)S(1)} %bitcast_add_fusion.1), channel_id=1, source_target_pairs={{8,12},{10,14},{4,0},{6,2},{9,13},{11,15},{5,1},{7,3},{24,28},{26,... | collective-permute-start | bytes 786440 | tf_op jit(solution)/shard_map/ppermute | solution.py:345
  127.5 3.3 %collective-permute-start.26 = (f32[128,384]{1,0:T(8,128)S(1)}, f32[128,384]{1,0:T(8,128)S(1)}, u32[]{:S(2)}, u32[]{:S(2)}) collective-permute-start(f32[128,384]{1,0:T(8,128)S(1)} %add.102), channel_id=1, source_target_pairs={{4,8},{6,10},{8,4},{10,6},{5,9},{7,11},{9,5},{11,7},{20,24},{22,26... | collective-permute-start | bytes 589832 | tf_op jit(solution)/shard_map/ppermute | solution.py:351
  130.8 0.1 bitcast_add_fusion.2
  130.9 0.4 collective-permute-done.18
  131.4 3.7 %collective-permute-done.26 = f32[128,384]{1,0:T(8,128)S(1)} collective-permute-done((f32[128,384]{1,0:T(8,128)S(1)}, f32[128,384]{1,0:T(8,128)S(1)}, u32[]{:S(2)}, u32[]{:S(2)}) %collective-permute-start.26) | collective-permute-done | bytes 196640 | tf_op jit(solution)/shard_map/ppermute | solution.py:351
  135.1 0.9 fusion
  (37 shorter events, 0.7 us)
Async XLA Ops:
  0.6 5.1 %copy-start = (bf16[1,384,2048]{2,1,0:T(8,128)(2,1)S(1)}, bf16[1,384,2048]{2,1,0:T(8,128)(2,1)}, u32[]{:S(2)}) copy-start(bf16[1,384,2048]{2,1,0:T(8,128)(2,1)} %param.9) | copy-start | bytes 4718596
  0.7 1.2 copy-start.3
  2.0 1.1 copy-start.4
  4.2 8.1 %collective-permute-start = (f32[4,128,128]{2,1,0:T(8,128)S(1)}, f32[4,128,128]{2,1,0:T(8,128)S(1)}, u32[]{:S(2)}, u32[]{:S(2)}) collective-permute-start(f32[4,128,128]{2,1,0:T(8,128)S(1)} %get-tuple-element.46), channel_id=1, source_target_pairs={{0,2},{2,0},{4,6},{6,4},{8,10},{10,8},{12,14},{14,12},{1,3},{3,1},... | collective-permute-start | bytes 786440 | tf_op jit(solution)/shard_map/ppermute | solution.py:208
  5.8 1.1 copy-start.2
  6.9 9.0 %copy-start.1 = (bf16[1024,2048]{1,0:T(8,128)(2,1)S(1)}, bf16[1024,2048]{1,0:T(8,128)(2,1)}, u32[]{:S(2)}) copy-start(bf16[1024,2048]{1,0:T(8,128)(2,1)} %w_ref.3) | copy-start | bytes 12582916
  12.4 9.1 %collective-permute-start.1 = (f32[4,128,128]{2,1,0:T(8,128)S(1)}, f32[4,128,128]{2,1,0:T(8,128)S(1)}, u32[]{:S(2)}, u32[]{:S(2)}) collective-permute-start(f32[4,128,128]{2,1,0:T(8,128)S(1)} %add.78), channel_id=1, source_target_pairs={{0,4},{2,6},{4,8},{6,10},{8,12},{10,14},{1,5},{3,7},{5,9},{7,11},{... | collective-permute-start | bytes 786440 | tf_op jit(solution)/shard_map/ppermute | solution.py:215
  21.5 13.8 %collective-permute-start.2 = (f32[4,128,128]{2,1,0:T(8,128)S(1)}, f32[4,128,128]{2,1,0:T(8,128)S(1)}, u32[]{:S(2)}, u32[]{:S(2)}) collective-permute-start(f32[4,128,128]{2,1,0:T(8,128)S(1)} %add.79), channel_id=1, source_target_pairs={{0,8},{2,10},{4,12},{6,14},{1,9},{3,11},{5,13},{7,15},{16,24},{18,... | collective-permute-start | bytes 786440 | tf_op jit(solution)/shard_map/ppermute | solution.py:215
  26.0 24.8 %collective-permute-start.5 = (f32[384,1024]{1,0:T(8,128)S(1)}, f32[384,1024]{1,0:T(8,128)S(1)}, u32[]{:S(2)}, u32[]{:S(2)}) collective-permute-start(f32[384,1024]{1,0:T(8,128)S(1)} %away.1), channel_id=1, source_target_pairs={{0,1},{1,0},{2,3},{3,2},{4,5},{5,4},{6,7},{7,6},{8,9},{9,8},{10,11... | collective-permute-start | bytes 4718600 | tf_op jit(solution)/shard_map/ppermute | solution.py:251
  35.3 8.3 %collective-permute-start.3 = (f32[4,128,128]{2,1,0:T(8,128)S(1)}, f32[4,128,128]{2,1,0:T(8,128)S(1)}, u32[]{:S(2)}, u32[]{:S(2)}) collective-permute-start(f32[4,128,128]{2,1,0:T(8,128)S(1)} %get-tuple-element.85), channel_id=1, source_target_pairs={{0,2},{2,0},{4,6},{6,4},{8,10},{10,8},{12,14},{14,12},{1,3},{3,1},... | collective-permute-start | bytes 786440 | tf_op jit(solution)/shard_map/ppermute | solution.py:222
  46.1 4.7 %collective-permute-start.4 = (f32[384,512]{1,0:T(8,128)S(1)}, f32[384,512]{1,0:T(8,128)S(1)}, u32[]{:S(2)}, u32[]{:S(2)}) collective-permute-start(f32[384,512]{1,0:T(8,128)S(1)} %get-tuple-element.53), channel_id=1, source_target_pairs={{0,1},{1,0},{2,3},{3,2},{4,5},{5,4},{6,7},{7,6},{8,9},{9,8},{10,11... | collective-permute-start | bytes 2359304 | tf_op jit(solution)/shard_map/ppermute | solution.py:277
  48.8 11.7 %collective-permute-start.6 = (f32[384,512]{1,0:T(8,128)S(1)}, f32[384,512]{1,0:T(8,128)S(1)}, u32[]{:S(2)}, u32[]{:S(2)}) collective-permute-start(f32[384,512]{1,0:T(8,128)S(1)} %get-tuple-element.56), channel_id=1, source_target_pairs={{0,1},{1,0},{2,3},{3,2},{4,5},{5,4},{6,7},{7,6},{8,9},{9,8},{10,11... | collective-permute-start | bytes 2359304 | tf_op jit(solution)/shard_map/ppermute | solution.py:277
  49.3 9.2 %collective-permute-start.8 = (f32[4,128,128]{2,1,0:T(8,128)S(1)}, f32[4,128,128]{2,1,0:T(8,128)S(1)}, u32[]{:S(2)}, u32[]{:S(2)}) collective-permute-start(f32[4,128,128]{2,1,0:T(8,128)S(1)} %get-tuple-element.69), channel_id=1, source_target_pairs={{0,2},{2,0},{4,6},{6,4},{8,10},{10,8},{12,14},{14,12},{1,3},{3,1},... | collective-permute-start | bytes 786440 | tf_op jit(solution)/shard_map/ppermute | solution.py:208
  52.7 17.8 %collective-permute-start.7 = (f32[2,128,512]{2,1,0:T(8,128)S(1)}, f32[2,128,512]{2,1,0:T(8,128)S(1)}, u32[]{:S(2)}, u32[]{:S(2)}) collective-permute-start(f32[2,128,512]{2,1,0:T(8,128)S(1)} %get-tuple-element.62), channel_id=1, source_target_pairs={{0,2},{2,0},{4,6},{6,4},{8,10},{10,8},{12,14},{14,12},{1,3},{3,1},... | collective-permute-start | bytes 1572872 | tf_op jit(solution)/shard_map/ppermute | solution.py:336
  58.5 8.5 %collective-permute-start.9 = (f32[4,128,128]{2,1,0:T(8,128)S(1)}, f32[4,128,128]{2,1,0:T(8,128)S(1)}, u32[]{:S(2)}, u32[]{:S(2)}) collective-permute-start(f32[4,128,128]{2,1,0:T(8,128)S(1)} %add.84), channel_id=1, source_target_pairs={{4,0},{6,2},{8,4},{10,6},{12,8},{14,10},{5,1},{7,3},{9,5},{11,7},{... | collective-permute-start | bytes 786440 | tf_op jit(solution)/shard_map/ppermute | solution.py:215
  67.0 11.7 %collective-permute-start.10 = (f32[4,128,128]{2,1,0:T(8,128)S(1)}, f32[4,128,128]{2,1,0:T(8,128)S(1)}, u32[]{:S(2)}, u32[]{:S(2)}) collective-permute-start(f32[4,128,128]{2,1,0:T(8,128)S(1)} %add.85), channel_id=1, source_target_pairs={{8,0},{10,2},{12,4},{14,6},{9,1},{11,3},{13,5},{15,7},{24,16},{26,... | collective-permute-start | bytes 786440 | tf_op jit(solution)/shard_map/ppermute | solution.py:215
  68.3 14.9 %collective-permute-start.15 = (f32[2,128,512]{2,1,0:T(8,128)S(1)}, f32[2,128,512]{2,1,0:T(8,128)S(1)}, u32[]{:S(2)}, u32[]{:S(2)}) collective-permute-start(f32[2,128,512]{2,1,0:T(8,128)S(1)} %get-tuple-element.54), channel_id=1, source_target_pairs={{0,2},{2,0},{4,6},{6,4},{8,10},{10,8},{12,14},{14,12},{1,3},{3,1},... | collective-permute-start | bytes 1572872 | tf_op jit(solution)/shard_map/ppermute | solution.py:336
  69.9 27.4 %collective-permute-start.19 = (f32[2,128,640]{2,1,0:T(8,128)S(1)}, f32[2,128,640]{2,1,0:T(8,128)S(1)}, u32[]{:S(2)}, u32[]{:S(2)}) collective-permute-start(f32[2,128,640]{2,1,0:T(8,128)S(1)} %get-tuple-element.57), channel_id=1, source_target_pairs={{0,2},{2,0},{4,6},{6,4},{8,10},{10,8},{12,14},{14,12},{1,3},{3,1},... | collective-permute-start | bytes 1966088 | tf_op jit(solution)/shard_map/ppermute | solution.py:336
  70.6 26.8 %collective-permute-start.12 = (f32[128,512]{1,0:T(8,128)S(1)}, f32[128,512]{1,0:T(8,128)S(1)}, u32[]{:S(2)}, u32[]{:S(2)}) collective-permute-start(f32[128,512]{1,0:T(8,128)S(1)} %select_bitcast_fusion.3), channel_id=1, source_target_pairs={{0,4},{2,6},{12,8},{14,10},{1,5},{3,7},{13,9},{15,11},{16,20},{18,... | collective-permute-start | bytes 786440 | tf_op jit(solution)/shard_map/ppermute | solution.py:343
  78.8 36.0 %collective-permute-start.23 = (f32[2,128,384]{2,1,0:T(8,128)S(1)}, f32[2,128,384]{2,1,0:T(8,128)S(1)}, u32[]{:S(2)}, u32[]{:S(2)}) collective-permute-start(f32[2,128,384]{2,1,0:T(8,128)S(1)} %get-tuple-element.80), channel_id=1, source_target_pairs={{0,2},{2,0},{4,6},{6,4},{8,10},{10,8},{12,14},{14,12},{1,3},{3,1},... | collective-permute-start | bytes 1179656 | tf_op jit(solution)/shard_map/ppermute | solution.py:336
  83.4 19.7 %collective-permute-start.16 = (f32[128,512]{1,0:T(8,128)S(1)}, f32[128,512]{1,0:T(8,128)S(1)}, u32[]{:S(2)}, u32[]{:S(2)}) collective-permute-start(f32[128,512]{1,0:T(8,128)S(1)} %select_bitcast_fusion.2), channel_id=1, source_target_pairs={{0,4},{2,6},{12,8},{14,10},{1,5},{3,7},{13,9},{15,11},{16,20},{18,... | collective-permute-start | bytes 786440 | tf_op jit(solution)/shard_map/ppermute | solution.py:343
  93.5 14.7 %collective-permute-start.11 = (f32[4,128,128]{2,1,0:T(8,128)S(1)}, f32[4,128,128]{2,1,0:T(8,128)S(1)}, u32[]{:S(2)}, u32[]{:S(2)}) collective-permute-start(f32[4,128,128]{2,1,0:T(8,128)S(1)} %get-tuple-element.72), channel_id=1, source_target_pairs={{0,2},{2,0},{4,6},{6,4},{8,10},{10,8},{12,14},{14,12},{1,3},{3,1},... | collective-permute-start | bytes 786440 | tf_op jit(solution)/shard_map/ppermute | solution.py:222
  97.5 17.4 %collective-permute-start.13 = (f32[128,512]{1,0:T(8,128)S(1)}, f32[128,512]{1,0:T(8,128)S(1)}, u32[]{:S(2)}, u32[]{:S(2)}) collective-permute-start(f32[128,512]{1,0:T(8,128)S(1)} %fusion.1), channel_id=1, source_target_pairs={{4,8},{6,10},{8,4},{10,6},{5,9},{7,11},{9,5},{11,7},{20,24},{22,26... | collective-permute-start | bytes 786440 | tf_op jit(solution)/shard_map/ppermute | solution.py:344
  101.8 29.0 %collective-permute-start.20 = (f32[128,640]{1,0:T(8,128)S(1)}, f32[128,640]{1,0:T(8,128)S(1)}, u32[]{:S(2)}, u32[]{:S(2)}) collective-permute-start(f32[128,640]{1,0:T(8,128)S(1)} %get-tuple-element.81), channel_id=1, source_target_pairs={{0,4},{2,6},{12,8},{14,10},{1,5},{3,7},{13,9},{15,11},{16,20},{18,... | collective-permute-start | bytes 983048 | tf_op jit(solution)/shard_map/ppermute | solution.py:350
  103.1 14.5 %collective-permute-start.21 = (f32[128,640]{1,0:T(8,128)S(1)}, f32[128,640]{1,0:T(8,128)S(1)}, u32[]{:S(2)}, u32[]{:S(2)}) collective-permute-start(f32[128,640]{1,0:T(8,128)S(1)} %get-tuple-element.82), channel_id=1, source_target_pairs={{0,4},{2,6},{12,8},{14,10},{1,5},{3,7},{13,9},{15,11},{16,20},{18,... | collective-permute-start | bytes 983048 | tf_op jit(solution)/shard_map/ppermute | solution.py:349
  108.2 10.8 %collective-permute-start.17 = (f32[128,512]{1,0:T(8,128)S(1)}, f32[128,512]{1,0:T(8,128)S(1)}, u32[]{:S(2)}, u32[]{:S(2)}) collective-permute-start(f32[128,512]{1,0:T(8,128)S(1)} %fusion.2), channel_id=1, source_target_pairs={{4,8},{6,10},{8,4},{10,6},{5,9},{7,11},{9,5},{11,7},{20,24},{22,26... | collective-permute-start | bytes 786440 | tf_op jit(solution)/shard_map/ppermute | solution.py:344
  115.0 12.5 %collective-permute-start.14 = (f32[128,512]{1,0:T(8,128)S(1)}, f32[128,512]{1,0:T(8,128)S(1)}, u32[]{:S(2)}, u32[]{:S(2)}) collective-permute-start(f32[128,512]{1,0:T(8,128)S(1)} %bitcast_add_fusion.3), channel_id=1, source_target_pairs={{8,12},{10,14},{4,0},{6,2},{9,13},{11,15},{5,1},{7,3},{24,28},{26,... | collective-permute-start | bytes 786440 | tf_op jit(solution)/shard_map/ppermute | solution.py:345
  116.3 15.0 %collective-permute-start.24 = (f32[128,384]{1,0:T(8,128)S(1)}, f32[128,384]{1,0:T(8,128)S(1)}, u32[]{:S(2)}, u32[]{:S(2)}) collective-permute-start(f32[128,384]{1,0:T(8,128)S(1)} %get-tuple-element.87), channel_id=1, source_target_pairs={{0,4},{2,6},{12,8},{14,10},{1,5},{3,7},{13,9},{15,11},{16,20},{18,... | collective-permute-start | bytes 589832 | tf_op jit(solution)/shard_map/ppermute | solution.py:350
  117.6 8.4 %collective-permute-start.25 = (f32[128,384]{1,0:T(8,128)S(1)}, f32[128,384]{1,0:T(8,128)S(1)}, u32[]{:S(2)}, u32[]{:S(2)}) collective-permute-start(f32[128,384]{1,0:T(8,128)S(1)} %get-tuple-element.88), channel_id=1, source_target_pairs={{0,4},{2,6},{12,8},{14,10},{1,5},{3,7},{13,9},{15,11},{16,20},{18,... | collective-permute-start | bytes 589832 | tf_op jit(solution)/shard_map/ppermute | solution.py:349
  119.0 11.8 %collective-permute-start.22 = (f32[128,640]{1,0:T(8,128)S(1)}, f32[128,640]{1,0:T(8,128)S(1)}, u32[]{:S(2)}, u32[]{:S(2)}) collective-permute-start(f32[128,640]{1,0:T(8,128)S(1)} %add.98), channel_id=1, source_target_pairs={{4,8},{6,10},{8,4},{10,6},{5,9},{7,11},{9,5},{11,7},{20,24},{22,26... | collective-permute-start | bytes 983048 | tf_op jit(solution)/shard_map/ppermute | solution.py:351
  126.0 5.3 %collective-permute-start.18 = (f32[128,512]{1,0:T(8,128)S(1)}, f32[128,512]{1,0:T(8,128)S(1)}, u32[]{:S(2)}, u32[]{:S(2)}) collective-permute-start(f32[128,512]{1,0:T(8,128)S(1)} %bitcast_add_fusion.1), channel_id=1, source_target_pairs={{8,12},{10,14},{4,0},{6,2},{9,13},{11,15},{5,1},{7,3},{24,28},{26,... | collective-permute-start | bytes 786440 | tf_op jit(solution)/shard_map/ppermute | solution.py:345
  127.5 7.6 %collective-permute-start.26 = (f32[128,384]{1,0:T(8,128)S(1)}, f32[128,384]{1,0:T(8,128)S(1)}, u32[]{:S(2)}, u32[]{:S(2)}) collective-permute-start(f32[128,384]{1,0:T(8,128)S(1)} %add.102), channel_id=1, source_target_pairs={{4,8},{6,10},{8,4},{10,6},{5,9},{7,11},{9,5},{11,7},{20,24},{22,26... | collective-permute-start | bytes 589832 | tf_op jit(solution)/shard_map/ppermute | solution.py:351

commit v4 on v3

--- a/solution.py
+++ b/solution.py
@@ -82,11 +82,12 @@
     return lax.optimization_barrier((value, *others))[0]
 
 
-def state_body(place, k_ref, v_ref, keep_ref, send_ref):
+def state_body(place, k_ref, v_ref, *outs):
     low = place[0]
-    for j in range(PAIRS):
-        for out, head in ((send_ref, 2 * j + 1 - low), (keep_ref, 2 * j + low)):
-            out[j] = dot(k_ref[:, at(head)], v_ref[:, at(head)], TN)
+    for rows, keep_ref, send_ref in ((FAR, outs[0], outs[1]), (NEAR, outs[2], outs[3])):
+        for i, j in enumerate(rows):
+            for out, head in ((send_ref, 2 * j + 1 - low), (keep_ref, 2 * j + low)):
+                out[i] = dot(k_ref[:, at(head)], v_ref[:, at(head)], TN)
 
 
 def away_body(place, g_ref, out_ref):
@@ -120,7 +121,7 @@
         for prior, out, part in ((own_ref, keep_ref, low), (other_ref, send_ref, 1 - low)):
             here, there = at(2 * j + part), at(2 * i + part)
             q = q_ref[:, here]
-            attended = att_ref[:, here] + two_pass_right(q, prior[j], NN)
+            attended = att_ref[:, here] + two_pass_right(q, prior[i], NN)
             inverse = lax.rsqrt(jnp.mean(attended * attended, axis=-1, keepdims=True) + EPSILON)
             normed = attended * inverse
             rounded = normed.astype(BF16)
@@ -133,19 +134,18 @@
             out[j if whole else i] = dot(q, d_att, TN)
 
 
-def grads_body(
-    place, q_ref, k_ref, v_ref, far_ref, near_ref, own_ref, other_ref, qg_ref, kl_ref, vl_ref
-):
+def grads_body(place, q_ref, k_ref, v_ref, *refs):
     low = place[0]
+    qg_ref, kl_ref, vl_ref = refs[-3:]
     lower = causal(q_ref.shape[0], True)
     upper = causal(q_ref.shape[0], False)
-    for da_ref, rows in ((far_ref, FAR), (near_ref, NEAR)):
+    for rows, (da_ref, own_ref, other_ref) in ((FAR, refs[:3]), (NEAR, refs[3:6])):
         for i, j in enumerate(rows):
             for prior, part in ((own_ref, low), (other_ref, 1 - low)):
                 here, there = at(2 * j + part), at(2 * i + part)
                 q, k, v, d_att = q_ref[:, here], k_ref[:, here], v_ref[:, here], da_ref[:, there]
                 cross = jnp.where(lower, dot(d_att, v, NT), 0.0)
-                part_sum = two_pass(cross, k, NN) + two_pass_right(d_att, prior[j], NT)
+                part_sum = two_pass(cross, k, NN) + two_pass_right(d_att, prior[i], NT)
                 qg_ref[:, here] = part_sum.astype(BF16)
                 cross = jnp.where(upper, dot(v, d_att, NT), 0.0)
                 kl_ref[:, here] = two_pass(cross, q, NN)
@@ -194,7 +194,7 @@
         out_ref[:, at(c, size)] = total.astype(BF16)
 
 
-def exclusive(keep, send, count, even, reverse, pins):
+def exclusive(states, count, even, reverse, pins):
     swap = [(s, s ^ 1) for s in range(count)]
     sign = -2 if reverse else 2
     pairs = count // 2
@@ -205,21 +205,29 @@
     def links(step):
         return [(s, s + sign * step) for s in range(count) if 0 <= s + sign * step < count]
 
-    received = lax.ppermute(send, "seq", swap)
-    total = keep + received
-    outside = None
+    received = [got for _, got in states]
+    totals = [keep + got for keep, got in states]
+    sums = [None for _ in states]
+    trail = ()
     step = 1
     while step < pairs:
-        pinned = pins.pop(0) if pins else ()
-        total = after(total, *pinned)
-        got = lax.ppermute(total, "seq", links(step))
-        outside = got if step == 1 else outside + got
-        total = total + got
+        pinned = (*trail, *(pins.pop(0) if pins else ()))
+        for i, total in enumerate(totals):
+            total = after(total, *pinned)
+            pinned = (total,)
+            trail = (total,) if i else ()
+            got = lax.ppermute(total, "seq", links(step))
+            sums[i] = got if step == 1 else sums[i] + got
+            totals[i] = total + got
         step *= 2
-    pinned = pins.pop(0) if pins else ()
-    mine = first(outside, outside + received)
-    theirs = after(first(outside + keep, outside), *pinned)
-    return mine, lax.ppermute(theirs, "seq", swap)
+    pinned = (*trail, *(pins.pop(0) if pins else ()))
+    results = []
+    for (keep, _), got, before in zip(states, received, sums):
+        mine = first(before, before + got)
+        theirs = after(first(before + keep, before), *pinned)
+        pinned = ()
+        results.append((mine, lax.ppermute(theirs, "seq", swap)))
+    return results
 
 
 def per_device(queries, keys, values, out_weight, out_grad):
@@ -229,8 +237,8 @@
     core = lax.axis_index("dp")
     low, level = spot & 1, spot >> 1
     place = jnp.stack([low, core]).astype(jnp.int32)
-    place, even, lower, outer = lax.optimization_barrier(
-        (place, low == 0, level < 2, (level == 0) | (level == 3))
+    place, even, lower, outer, odd = lax.optimization_barrier(
+        (place, low == 0, level < 2, (level == 0) | (level == 3), (level & 1) == 1)
     )
     q, k, v, g = queries[0], keys[0], values[0], out_grad[0]
     length, features = q.shape
@@ -238,78 +246,92 @@
     part = features // 2
     half = width // 2
     state = shape((PAIRS, HD, HD), F32)
+    some = shape((2, HD, HD), F32)
     rows32 = shape((length, features), F32)
     rows16 = shape((length, features), BF16)
     unit = 2 * H * length * HD
     fast = count == 8 and cores == 2
     swap = [(0, 1), (1, 0)]
 
-    keep, send = call(state_body, (state, state), (place, k, v), unit * HD, "state")
+    def trade(send):
+        return lax.ppermute(send, "seq", [(s, s ^ 1) for s in range(count)])
+
+    states = call(state_body, (some,) * 4, (place, k, v), unit * HD, "state")
     away = g
     if fast:
-        (away,) = call(away_body, (shape((length, half), F32),), (place, g), unit, "away")
+        (away,) = call(away_body, (shape((length, half), F32),), (place, after(g, states[0])), unit, "away")
         go = lax.ppermute(away, "dp", swap)
     (att,) = call(local_body, (rows32,), (q, k, v), 3 * unit * length, "local")
     (d_normed,) = call(d_normed_body, (rows32,), (g, out_weight), unit * width, "d_normed")
-    own, other = exclusive(keep, send, count, even, False, [(away, att), (d_normed,)])
+    far_prior, near_prior = exclusive(
+        [(states[0], trade(states[1])), (states[2], trade(states[3]))], count, even, False, [(away,), (att,), (d_normed,)]
+    )
 
     pieces = (shape((length, part), BF16), shape((length, part), F32), shape((length, part), BF16))
-    some = shape((2, HD, HD), F32)
     far, far32, far_att, *some_states = call(
         functools.partial(norm_body, FAR),
         pieces + (some, some),
-        (place, q, att, d_normed, own, other),
+        (place, q, att, d_normed, after(far_prior[0], near_prior[0]), far_prior[1]),
         unit * HD,
         "norm_far",
     )
+
+    def product(nb, nbo, widths):
+        blocks = []
+        for w in widths:
+            block = shape((2, HD, w * half // sum(widths)), F32)
+            blocks += [block, block]
+        out = call(weight_body, tuple(blocks), (place, nb, g, nbo, go), unit * half, "weight")
+        return list(zip(out[::2], out[1::2]))
+
+    near_own, near_other = near_prior
+    if fast:
+        chunks = product(far, lax.ppermute(far32, "dp", swap), WIDTHS[0])
+        near_own = after(near_own, chunks[0][1])
+        landed = chunks[0][0] + trade(after(chunks[0][1], near_other))
     near, near32, near_att, keep, send = call(
         functools.partial(norm_body, NEAR),
         pieces + (state, state),
-        (place, q, att, d_normed, own, other, *some_states),
+        (place, q, att, d_normed, near_own, near_other, *some_states),
         unit * HD * 64,
         "norm_near",
     )
 
     scale = 1.0 / math.sqrt(length * count * cores)
+    received = trade(send)
     if fast:
-        chunks = []
-        for nb, nb32, widths in ((far, far32, WIDTHS[0]), (near, near32, WIDTHS[1])):
-            nbo = lax.ppermute(nb32, "dp", swap)
-            blocks = []
-            for w in widths:
-                block = shape((2, HD, w * half // sum(widths)), F32)
-                blocks += [block, block]
-            if chunks:
-                nb = after(nb, chunks[0][1][1])
-            out = call(weight_body, tuple(blocks), (place, nb, g, nbo, go), unit * half, "weight")
-            chunks.append([(out[0], out[1]), (out[2], out[3])])
-        ready = (chunks[1][0][1],)
-        early = chunks[0][0][1]
-        weight_grad, landed = scatter(chunks, lower, outer)
-        weight_grad = weight_grad * scale
+        others = [(kept, trade(after(sent, landed))) for kept, sent in chunks[1:]]
+        lines = [toward(landed, lower, odd)]
+        nbo = lax.ppermute(after(near32, landed, received), "dp", swap)
+        chunks = product(after(near, lines[0][0]), nbo, WIDTHS[1])
+        ready = chunks[0][1]
+        near_bases = [kept + trade(sent) for kept, sent in chunks]
+        lines += [toward(kept + after(got, ready), lower, odd) for kept, got in others]
+        weight_grad = scatter(lines, near_bases, lower, outer) * scale
     else:
         nb = jnp.concatenate([far[:, :PAIR], near, far[:, PAIR:]], axis=1)
-        product = lax.dot_general(nb, g, TN, preferred_element_type=F32)
-        product = lax.psum_scatter(product, "dp", scatter_dimension=1, tiled=True)
-        weight_grad = lax.psum_scatter(product, "seq", scatter_dimension=0, tiled=True) * scale
-        ready, early, landed = (), near, near
+        weight = lax.dot_general(nb, g, TN, preferred_element_type=F32)
+        weight = lax.psum_scatter(weight, "dp", scatter_dimension=1, tiled=True)
+        weight_grad = lax.psum_scatter(weight, "seq", scatter_dimension=0, tiled=True) * scale
+        ready = near
 
     query_grad, key_local, value_local = call(
         grads_body,
         (rows16, rows32, rows32),
-        (place, q, k, v, after(far_att, landed), near_att, own, other),
+        (place, q, k, v, after(far_att, ready), *far_prior, near_att, *near_prior),
         9 * unit * length,
         "grads",
     )
     (output,) = call(
         output_body,
         (shape((length, width), BF16),),
-        (after(far, *ready), near, out_weight),
+        (after(far, ready), near, out_weight),
         unit * width,
         "output",
     )
-    pins = [(early,), (output,), (key_local,)]
-    own_later, other_later = exclusive(keep, send, count, even, True, pins)
+    ((own_later, other_later),) = exclusive(
+        [(keep, received)], count, even, True, [(), (output,), (key_local,)]
+    )
 
     key_grad, value_grad = call(
         final_body,
@@ -321,37 +343,28 @@
     return output[None], query_grad[None], key_grad[None], value_grad[None], weight_grad
 
 
-def scatter(chunks, lower, outer):
-    swap = [(s, s ^ 1) for s in range(8)]
-
-    def on(links):
-        return [(2 * a + i, 2 * b + i) for a, b in links for i in range(2)]
-
-    inward = on([(0, 1), (3, 2)])
-    middle = on([(1, 2), (2, 1)])
-    outward = on([(2, 3), (1, 0)])
-
-    def paired(chunk, *pinned):
-        keep, send = chunk
-        base = keep + lax.ppermute(after(send, *pinned), "seq", swap)
-        return jnp.where(lower, base[1], base[0]), jnp.where(lower, base[0], base[1])
-
-    far, near, pins = [], [], []
-    for chunk in chunks[0]:
-        up, down = paired(chunk)
-        pins.append(up)
-        got = lax.ppermute(up, "seq", inward)
-        got = lax.ppermute(up + got, "seq", middle)
-        got = lax.ppermute(down + got, "seq", outward)
-        far.append(down + got)
-    for chunk, pin in zip(chunks[1], ((), pins[:1])):
-        up, down = paired(chunk, *pin)
-        got = lax.ppermute(up, "seq", inward)
-        direct = lax.ppermute(down, "seq", inward)
-        got = lax.ppermute(up + got, "seq", middle)
-        near.append((down + direct) + got)
-    total = jnp.where(outer, jnp.concatenate(far, axis=1), jnp.concatenate(near, axis=1))
-    return total, pins[0]
+def along(links):
+    return [(2 * a + i, 2 * b + i) for a, b in links for i in range(2)]
+
+
+def toward(base, lower, odd):
+    out = jnp.where(odd, base[0], base[1])
+    got = lax.ppermute(out, "seq", along([(0, 1), (1, 0), (2, 3), (3, 2)]))
+    return jnp.where(lower, base[1], base[0]) + got, jnp.where(lower, base[0], base[1]) + got
+
+
+def scatter(lines, near_bases, lower, outer):
+    far, near = [], []
+    for half, rest in lines:
+        pin = half
+        far.append(rest + lax.ppermute(half, "seq", along([(1, 3), (2, 0)])))
+    for base in near_bases:
+        base = after(base, pin)
+        got = lax.ppermute(base, "seq", along([(0, 1), (3, 2)]))
+        pin = jnp.where(lower, base[1] + got[1], base[0] + got[0])
+        final = lax.ppermute(pin, "seq", along([(1, 2), (2, 1)]))
+        near.append(jnp.where(lower, base[0] + got[0], base[1] + got[1]) + final)
+    return jnp.where(outer, jnp.concatenate(far, axis=1), jnp.concatenate(near, axis=1))
 
 
 def solution(mesh):

time: 136 us -> 137 us (level)
    ppermute x22 -> x20, waiting for transfers between devices: 31.6 us -> 47 us  [the longest x7 20.8 us: trade(): return lax.ppermute(send, 'seq', [(s, s ^ 1) for s in range(count)])]
    ppermute x4 -> x6, waiting for transfers between devices: 20.2 us -> 5.91 us  [exclusive(): got = lax.ppermute(total, 'seq', links(step))]
    ppermute x4 -> x6, starting transfers between devices: 11.2 us -> 13.3 us  [exclusive(): got = lax.ppermute(total, 'seq', links(step))]
    ppermute x22 -> x20, starting transfers between devices: 36.3 us -> 34.6 us  [the longest x7 9.07 us: trade(): return lax.ppermute(send, 'seq', [(s, s ^ 1) for s in range(count)])]
  transfers between devices with their start and end apart: 27 -> 27, of which waited for: 13 -> 16; matrix products, arithmetic and copies ran while one was open for 1% -> 1% of each run, Pallas kernels for 22% -> 21%
where the time goes in v4:
time: 137 us
  waiting for transfers between devices  52.9 us (39%)
  starting transfers between devices  48 us (35%)
  Pallas kernels  30.4 us (22%)
  local copies, waits for them, and re-layouts  2.38 us (2%)
  other arithmetic  2.16 us (2%)
    pallas_call x11, Pallas kernels, call(): pl.pallas_call(body, out_shape=tuple(out_shapes), in_specs=specs, out_spe...  30.4 us
    ppermute x7, waiting for transfers between devices, trade(): return lax.ppermute(send, 'seq', [(s, s ^ 1) for s in range(count)])  20.8 us
    ppermute x6, starting transfers between devices, exclusive(): got = lax.ppermute(total, 'seq', links(step))  13.3 us
    ppermute x2, waiting for transfers between devices, toward(): got = lax.ppermute(out, 'seq', along([(0, 1), (1, 0), (2, 3), (3, 2)]))  11.5 us
    ppermute x7, starting transfers between devices, trade(): return lax.ppermute(send, 'seq', [(s, s ^ 1) for s in range(count)])  9.07 us
    ppermute x2, starting transfers between devices, scatter(): far.append(rest + lax.ppermute(half, 'seq', along([(1, 3), (2, 0)])))  6.93 us
    ppermute x2, starting transfers between devices, toward(): got = lax.ppermute(out, 'seq', along([(0, 1), (1, 0), (2, 3), (3, 2)]))  6.24 us
    ppermute x6, waiting for transfers between devices, exclusive(): got = lax.ppermute(total, 'seq', links(step))  5.91 us
  transfers between devices with their start and end apart: 27, of which 16 were waited for; matrix products, arithmetic and copies ran while one was open for 1% of the time, Pallas kernels for 21%

profile of v4, /device:TPU:12, one launch (start us, length us, event | category | flops | bytes accessed | tf_op | source)
XLA Modules:
  0.0 136.9 jit_solution(5754198706012633698)
XLA Ops:
  0.7 0.1 pad_add_fusion.place
  0.7 1.2 copy-done.3
  2.0 1.1 copy-done.4
  3.1 1.1 state.1
  4.2 1.6 %collective-permute-start = (f32[2,128,128]{2,1,0:T(8,128)S(1)}, f32[2,128,128]{2,1,0:T(8,128)S(1)}, u32[]{:S(2)}, u32[]{:S(2)}) collective-permute-start(f32[2,128,128]{2,1,0:T(8,128)S(1)} %get-tuple-element.59), channel_id=1, source_target_pairs={{0,2},{2,0},{4,6},{6,4},{8,10},{10,8},{12,14},{14,12},{1,3},{3,1},... | collective-permute-start | bytes 393224 | tf_op jit(solution)/shard_map/ppermute | solution.py:257
  5.8 0.6 away.1
  6.4 0.1 collective-permute-start.8
  6.5 0.6 collective-permute-start.2
  7.1 2.4 %collective-permute-done = f32[2,128,128]{2,1,0:T(8,128)S(1)} collective-permute-done((f32[2,128,128]{2,1,0:T(8,128)S(1)}, f32[2,128,128]{2,1,0:T(8,128)S(1)}, u32[]{:S(2)}, u32[]{:S(2)}) %collective-permute-start) | collective-permute-done | bytes 131104 | tf_op jit(solution)/shard_map/ppermute | solution.py:257
  9.5 3.5 %collective-permute-start.1 = (f32[2,128,128]{2,1,0:T(8,128)S(1)}, f32[2,128,128]{2,1,0:T(8,128)S(1)}, u32[]{:S(2)}, u32[]{:S(2)}) collective-permute-start(f32[2,128,128]{2,1,0:T(8,128)S(1)} %add.101), channel_id=1, source_target_pairs={{0,4},{2,6},{4,8},{6,10},{8,12},{10,14},{1,5},{3,7},{5,9},{7,11},{... | collective-permute-start | bytes 393224 | tf_op jit(solution)/shard_map/ppermute | solution.py:219
  13.1 2.4 %local.1.att_ref = f32[384,1024]{1,0:T(8,128)S(1)} custom-call(bf16[384,1024]{1,0:T(8,128)(2,1)S(1)} %bitcast.38, bf16[384,1024]{1,0:T(8,128)(2,1)S(1)} %bitcast.43, bf16[384,1024]{1,0:T(8,128)(2,1)S(1)} %bitcast.47), custom_call_target="tpu_custom_call" | custom-call | flops 56623104 | tf_op jit(solution)/shard_map/local/pallas_call | solution.py:70
  15.5 3.5 %collective-permute-start.4 = (f32[2,128,128]{2,1,0:T(8,128)S(1)}, f32[2,128,128]{2,1,0:T(8,128)S(1)}, u32[]{:S(2)}, u32[]{:S(2)}) collective-permute-start(f32[2,128,128]{2,1,0:T(8,128)S(1)} %add.103), channel_id=1, source_target_pairs={{0,4},{2,6},{4,8},{6,10},{8,12},{10,14},{1,5},{3,7},{5,9},{7,11},{... | collective-permute-start | bytes 393224 | tf_op jit(solution)/shard_map/ppermute | solution.py:219
  19.1 1.9 %collective-permute-start.3 = (f32[2,128,128]{2,1,0:T(8,128)S(1)}, f32[2,128,128]{2,1,0:T(8,128)S(1)}, u32[]{:S(2)}, u32[]{:S(2)}) collective-permute-start(f32[2,128,128]{2,1,0:T(8,128)S(1)} %add.102), channel_id=1, source_target_pairs={{0,8},{2,10},{4,12},{6,14},{1,9},{3,11},{5,13},{7,15},{16,24},{18,... | collective-permute-start | bytes 393224 | tf_op jit(solution)/shard_map/ppermute | solution.py:219
  20.9 2.4 %d_normed.1.dn_ref = f32[384,1024]{1,0:T(8,128)S(1)} custom-call(bf16[384,2048]{1,0:T(8,128)(2,1)S(1)} %bitcast.35, bf16[1024,2048]{1,0:T(8,128)(2,1)S(1)} %copy-done.1), custom_call_target="tpu_custom_call" | custom-call | flops 100663296 | tf_op jit(solution)/shard_map/d_normed/pallas_call | solution.py:70
  23.4 3.3 %collective-permute-done.4 = f32[2,128,128]{2,1,0:T(8,128)S(1)} collective-permute-done((f32[2,128,128]{2,1,0:T(8,128)S(1)}, f32[2,128,128]{2,1,0:T(8,128)S(1)}, u32[]{:S(2)}, u32[]{:S(2)}) %collective-permute-start.4) | collective-permute-done | bytes 131104 | tf_op jit(solution)/shard_map/ppermute | solution.py:219
  26.7 1.3 collective-permute-start.5
  28.0 1.1 collective-permute-done.3
  29.1 1.6 %collective-permute-start.6 = (f32[2,128,128]{2,1,0:T(8,128)S(1)}, f32[2,128,128]{2,1,0:T(8,128)S(1)}, u32[]{:S(2)}, u32[]{:S(2)}) collective-permute-start(f32[2,128,128]{2,1,0:T(8,128)S(1)} %get-tuple-element.68), channel_id=1, source_target_pairs={{0,2},{2,0},{4,6},{6,4},{8,10},{10,8},{12,14},{14,12},{1,3},{3,1},... | collective-permute-start | bytes 393224 | tf_op jit(solution)/shard_map/ppermute | solution.py:229
  30.8 3.4 %collective-permute-done.6.other_ref.refs_2_ = f32[2,128,128]{2,1,0:T(8,128)S(1)} collective-permute-done((f32[2,128,128]{2,1,0:T(8,128)S(1)}, f32[2,128,128]{2,1,0:T(8,128)S(1)}, u32[]{:S(2)}, u32[]{:S(2)}) %collective-permute-start.6) | collective-permute-done | bytes 131104 | tf_op jit(solution)/shard_map/ppermute | solution.py:229
  34.1 2.5 %norm_far.1 = (bf16[384,512]{1,0:T(8,128)(2,1)S(1)}, f32[384,512]{1,0:T(8,128)S(1)}, bf16[384,512]{1,0:T(8,128)(2,1)S(1)}, f32[2,128,128]{2,1,0:T(8,128)S(1)}, f32[2,128,128]{2,1,0:T(8,128)S(1)}) custom-call(s32[2]{0:T(128)S(1)} %pad_add_fusion.place, bf16[384,1024]{1,0:T(8,128)(2,1)S(1)} %bitcast.39, f32[384,1024]{1,0:T(8,128)S(1)} %local.1.att_ref, ...), custom_call_target="tpu_custom_call" | custom-call | flops 6291456 | tf_op jit(solution)/shard_map/norm_far/pallas_call | solution.py:70
  36.7 0.1 collective-permute-start.7
  36.8 1.6 %collective-permute-start.9 = (f32[2,128,128]{2,1,0:T(8,128)S(1)}, f32[2,128,128]{2,1,0:T(8,128)S(1)}, u32[]{:S(2)}, u32[]{:S(2)}) collective-permute-start(f32[2,128,128]{2,1,0:T(8,128)S(1)} %get-tuple-element.109), channel_id=1, source_target_pairs={{0,2},{2,0},{4,6},{6,4},{8,10},{10,8},{12,14},{14,12},{1,3},{3,1},... | collective-permute-start | bytes 393224 | tf_op jit(solution)/shard_map/ppermute | solution.py:229
  38.4 0.6 collective-permute-done.7.nbo_ref
  39.0 1.8 %weight.2 = (f32[2,128,512]{2,1,0:T(8,128)S(1)}, f32[2,128,512]{2,1,0:T(8,128)S(1)}, f32[2,128,512]{2,1,0:T(8,128)S(1)}, f32[2,128,512]{2,1,0:T(8,128)S(1)}) custom-call(s32[2]{0:T(128)S(1)} %pad_add_fusion.place, bf16[384,512]{1,0:T(8,128)(2,1)S(1)} %get-tuple-element.85.nb_ref.far_ref, bf16[384,2048]{1,0:T(8,128)(2,1)S(1)} %bitcast.36, ...), custom_call_target="tpu_custom_call" | custom-call | flops 50331648 | tf_op jit(solution)/shard_map/weight/pallas_call | solution.py:70
  40.9 1.8 %collective-permute-done.9.other_ref.refs_5_ = f32[2,128,128]{2,1,0:T(8,128)S(1)} collective-permute-done((f32[2,128,128]{2,1,0:T(8,128)S(1)}, f32[2,128,128]{2,1,0:T(8,128)S(1)}, u32[]{:S(2)}, u32[]{:S(2)}) %collective-permute-start.9) | collective-permute-done | bytes 131104 | tf_op jit(solution)/shard_map/ppermute | solution.py:229
  42.7 1.6 %collective-permute-start.10 = (f32[2,128,512]{2,1,0:T(8,128)S(1)}, f32[2,128,512]{2,1,0:T(8,128)S(1)}, u32[]{:S(2)}, u32[]{:S(2)}) collective-permute-start(f32[2,128,512]{2,1,0:T(8,128)S(1)} %get-tuple-element.78), channel_id=1, source_target_pairs={{0,2},{2,0},{4,6},{6,4},{8,10},{10,8},{12,14},{14,12},{1,3},{3,1},... | collective-permute-start | bytes 1572872 | tf_op jit(solution)/shard_map/ppermute | solution.py:257
  44.2 2.6 %norm_near.1 = (bf16[384,512]{1,0:T(8,128)(2,1)S(1)}, f32[384,512]{1,0:T(8,128)S(1)}, bf16[384,512]{1,0:T(8,128)(2,1)S(1)}, f32[4,128,128]{2,1,0:T(8,128)S(1)}, f32[4,128,128]{2,1,0:T(8,128)S(1)}) custom-call(s32[2]{0:T(128)S(1)} %pad_add_fusion.place, bf16[384,1024]{1,0:T(8,128)(2,1)S(1)} %bitcast.40, f32[384,1024]{1,0:T(8,128)S(1)} %local.1.att_ref, ...), custom_call_target="tpu_custom_call" | custom-call | flops 402653184 | tf_op jit(solution)/shard_map/norm_near/pallas_call | solution.py:70
  46.8 0.5 collective-permute-start.12
  47.3 10.2 %collective-permute-done.10 = f32[2,128,512]{2,1,0:T(8,128)S(1)} collective-permute-done((f32[2,128,512]{2,1,0:T(8,128)S(1)}, f32[2,128,512]{2,1,0:T(8,128)S(1)}, u32[]{:S(2)}, u32[]{:S(2)}) %collective-permute-start.10) | collective-permute-done | bytes 524320 | tf_op jit(solution)/shard_map/ppermute | solution.py:257
  57.5 0.1 add.111
  57.6 4.2 %collective-permute-done.12 = f32[4,128,128]{2,1,0:T(8,128)S(1)} collective-permute-done((f32[4,128,128]{2,1,0:T(8,128)S(1)}, f32[4,128,128]{2,1,0:T(8,128)S(1)}, u32[]{:S(2)}, u32[]{:S(2)}) %collective-permute-start.12) | collective-permute-done | bytes 262176 | tf_op jit(solution)/shard_map/ppermute | solution.py:257
  61.8 1.6 %collective-permute-start.18 = (f32[2,128,512]{2,1,0:T(8,128)S(1)}, f32[2,128,512]{2,1,0:T(8,128)S(1)}, u32[]{:S(2)}, u32[]{:S(2)}) collective-permute-start(f32[2,128,512]{2,1,0:T(8,128)S(1)} %get-tuple-element.100), channel_id=1, source_target_pairs={{0,2},{2,0},{4,6},{6,4},{8,10},{10,8},{12,14},{14,12},{1,3},{3,1},... | collective-permute-start | bytes 1572872 | tf_op jit(solution)/shard_map/ppermute | solution.py:257
  63.4 2.4 %collective-permute-start.11 = (f32[128,512]{1,0:T(8,128)S(1)}, f32[128,512]{1,0:T(8,128)S(1)}, u32[]{:S(2)}, u32[]{:S(2)}) collective-permute-start(f32[128,512]{1,0:T(8,128)S(1)} %select_bitcast_fusion.2), channel_id=1, source_target_pairs={{0,4},{2,6},{4,0},{6,2},{8,12},{10,14},{12,8},{14,10},{1,5},{3,7},... | collective-permute-start | bytes 786440 | tf_op jit(solution)/shard_map/ppermute | solution.py:352
  65.8 6.7 %collective-permute-done.11 = f32[128,512]{1,0:T(8,128)S(1)} collective-permute-done((f32[128,512]{1,0:T(8,128)S(1)}, f32[128,512]{1,0:T(8,128)S(1)}, u32[]{:S(2)}, u32[]{:S(2)}) %collective-permute-start.11) | collective-permute-done | bytes 262176 | tf_op jit(solution)/shard_map/ppermute | solution.py:352
  72.6 2.0 %weight.3 = (f32[2,128,640]{2,1,0:T(8,128)S(1)}, f32[2,128,640]{2,1,0:T(8,128)S(1)}, f32[2,128,384]{2,1,0:T(8,128)S(1)}, f32[2,128,384]{2,1,0:T(8,128)S(1)}) custom-call(s32[2]{0:T(128)S(1)} %pad_add_fusion.place, bf16[384,512]{1,0:T(8,128)(2,1)S(1)} %get-tuple-element.80.nb_ref.near_ref, bf16[384,2048]{1,0:T(8,128)(2,1)S(1)} %bitcast.37, ...), custom_call_target="tpu_custom_call" | custom-call | flops 50331648 | tf_op jit(solution)/shard_map/weight/pallas_call | solution.py:70
  74.6 1.6 %collective-permute-start.21 = (f32[2,128,640]{2,1,0:T(8,128)S(1)}, f32[2,128,640]{2,1,0:T(8,128)S(1)}, u32[]{:S(2)}, u32[]{:S(2)}) collective-permute-start(f32[2,128,640]{2,1,0:T(8,128)S(1)} %get-tuple-element.84), channel_id=1, source_target_pairs={{0,2},{2,0},{4,6},{6,4},{8,10},{10,8},{12,14},{14,12},{1,3},{3,1},... | collective-permute-start | bytes 1966088 | tf_op jit(solution)/shard_map/ppermute | solution.py:257
  76.3 0.1 add.120
  76.4 3.8 %collective-permute-start.19 = (f32[128,512]{1,0:T(8,128)S(1)}, f32[128,512]{1,0:T(8,128)S(1)}, u32[]{:S(2)}, u32[]{:S(2)}) collective-permute-start(f32[128,512]{1,0:T(8,128)S(1)} %select_bitcast_fusion.1), channel_id=1, source_target_pairs={{0,4},{2,6},{4,0},{6,2},{8,12},{10,14},{12,8},{14,10},{1,5},{3,7},... | collective-permute-start | bytes 786440 | tf_op jit(solution)/shard_map/ppermute | solution.py:352
  80.2 1.9 %collective-permute-start.14 = (f32[4,128,128]{2,1,0:T(8,128)S(1)}, f32[4,128,128]{2,1,0:T(8,128)S(1)}, u32[]{:S(2)}, u32[]{:S(2)}) collective-permute-start(f32[4,128,128]{2,1,0:T(8,128)S(1)} %add.113), channel_id=1, source_target_pairs={{4,0},{6,2},{8,4},{10,6},{12,8},{14,10},{5,1},{7,3},{9,5},{11,7},{... | collective-permute-start | bytes 786440 | tf_op jit(solution)/shard_map/ppermute | solution.py:219
  82.2 4.8 %collective-permute-done.19 = f32[128,512]{1,0:T(8,128)S(1)} collective-permute-done((f32[128,512]{1,0:T(8,128)S(1)}, f32[128,512]{1,0:T(8,128)S(1)}, u32[]{:S(2)}, u32[]{:S(2)}) %collective-permute-start.19) | collective-permute-done | bytes 262176 | tf_op jit(solution)/shard_map/ppermute | solution.py:352
  87.0 4.0 %collective-permute-done.21 = f32[2,128,640]{2,1,0:T(8,128)S(1)} collective-permute-done((f32[2,128,640]{2,1,0:T(8,128)S(1)}, f32[2,128,640]{2,1,0:T(8,128)S(1)}, u32[]{:S(2)}, u32[]{:S(2)}) %collective-permute-start.21) | collective-permute-done | bytes 655392 | tf_op jit(solution)/shard_map/ppermute | solution.py:257
  91.1 0.1 add.124
  91.1 1.3 collective-permute-start.22
  92.5 3.5 %output.1 = bf16[384,2048]{1,0:T(8,128)(2,1)} custom-call(bf16[384,512]{1,0:T(8,128)(2,1)S(1)} %get-tuple-element.85.nb_ref.far_ref, bf16[384,512]{1,0:T(8,128)(2,1)S(1)} %get-tuple-element.80.nb_ref.near_ref, bf16[1024,2048]{1,0:T(8,128)(2,1)S(1)} %copy-done.1), custom_call_target="tpu_custom_call" | custom-call | flops 100663296 | tf_op jit(solution)/shard_map/output/pallas_call | solution.py:70
  96.0 1.3 collective-permute-start.15
  97.3 1.6 %collective-permute-start.24 = (f32[2,128,384]{2,1,0:T(8,128)S(1)}, f32[2,128,384]{2,1,0:T(8,128)S(1)}, u32[]{:S(2)}, u32[]{:S(2)}) collective-permute-start(f32[2,128,384]{2,1,0:T(8,128)S(1)} %get-tuple-element.105), channel_id=1, source_target_pairs={{0,2},{2,0},{4,6},{6,4},{8,10},{10,8},{12,14},{14,12},{1,3},{3,1},... | collective-permute-start | bytes 1179656 | tf_op jit(solution)/shard_map/ppermute | solution.py:257
  98.9 5.6 %collective-permute-start.17 = (f32[128,512]{1,0:T(8,128)S(1)}, f32[128,512]{1,0:T(8,128)S(1)}, u32[]{:S(2)}, u32[]{:S(2)}) collective-permute-start(f32[128,512]{1,0:T(8,128)S(1)} %bitcast_add_fusion.4), channel_id=1, source_target_pairs={{4,12},{6,14},{8,0},{10,2},{5,13},{7,15},{9,1},{11,3},{20,28},{22,... | collective-permute-start | bytes 786440 | tf_op jit(solution)/shard_map/ppermute | solution.py:360
  104.5 8.6 %grads.1 = (bf16[384,1024]{1,0:T(8,128)(2,1)}, f32[384,1024]{1,0:T(8,128)S(1)}, f32[384,1024]{1,0:T(8,128)S(1)}) custom-call(s32[2]{0:T(128)S(1)} %pad_add_fusion.place, bf16[384,1024]{1,0:T(8,128)(2,1)S(1)} %bitcast.41, bf16[384,1024]{1,0:T(8,128)(2,1)S(1)} %bitcast.44, bf16[384,1024]{1,0:T(8,128)(2,1)S(1)} %bitcast.48, ...), custom_call_target="tpu_custom_call" | custom-call | flops 169869312 | tf_op jit(solution)/shard_map/grads/pallas_call | solution.py:70
  113.1 1.3 collective-permute-start.20
  114.4 1.5 %collective-permute-done.15 = f32[4,128,128]{2,1,0:T(8,128)S(1)} collective-permute-done((f32[4,128,128]{2,1,0:T(8,128)S(1)}, f32[4,128,128]{2,1,0:T(8,128)S(1)}, u32[]{:S(2)}, u32[]{:S(2)}) %collective-permute-start.15) | collective-permute-done | bytes 262176 | tf_op jit(solution)/shard_map/ppermute | solution.py:219
  116.0 0.1 add_select_fusion
  116.0 0.9 collective-permute-start.16
  117.1 1.3 collective-permute-start.25
  118.4 0.1 fusion.2
  118.5 3.5 %collective-permute-start.23 = (f32[128,640]{1,0:T(8,128)S(1)}, f32[128,640]{1,0:T(8,128)S(1)}, u32[]{:S(2)}, u32[]{:S(2)}) collective-permute-start(f32[128,640]{1,0:T(8,128)S(1)} %select_bitcast_fusion), channel_id=1, source_target_pairs={{4,8},{6,10},{8,4},{10,6},{5,9},{7,11},{9,5},{11,7},{20,24},{22,26... | collective-permute-start | bytes 983048 | tf_op jit(solution)/shard_map/ppermute | solution.py:365
  122.0 0.1 fusion.1
  122.1 0.5 collective-permute-done.16.other_ref
  122.5 2.8 %final.1 = (bf16[384,1024]{1,0:T(8,128)(2,1)}, bf16[384,1024]{1,0:T(8,128)(2,1)}) custom-call(s32[2]{0:T(128)S(1)} %pad_add_fusion.place, bf16[384,1024]{1,0:T(8,128)(2,1)S(1)} %bitcast.45, bf16[384,1024]{1,0:T(8,128)(2,1)S(1)} %bitcast.49, f32[384,1024]{1,0:T(8,128)S(1)} %get-tuple-element.90.kl_ref, f32[384,1024]{1,0:T(8,128)S(1)} %get-tuple-element.91.vl_ref, ...), custom_call_target="tpu_custom_call" | custom-call | flops 25165824 | tf_op jit(solution)/shard_map/final/pallas_call | solution.py:70
  125.3 3.0 %collective-permute-done.25 = f32[2,128,384]{2,1,0:T(8,128)S(1)} collective-permute-done((f32[2,128,384]{2,1,0:T(8,128)S(1)}, f32[2,128,384]{2,1,0:T(8,128)S(1)}, u32[]{:S(2)}, u32[]{:S(2)}) %collective-permute-start.25) | collective-permute-done | bytes 393248 | tf_op jit(solution)/shard_map/ppermute | solution.py:363
  128.4 2.1 %collective-permute-start.26 = (f32[128,384]{1,0:T(8,128)S(1)}, f32[128,384]{1,0:T(8,128)S(1)}, u32[]{:S(2)}, u32[]{:S(2)}) collective-permute-start(f32[128,384]{1,0:T(8,128)S(1)} %select_bitcast_fusion.3), channel_id=1, source_target_pairs={{4,8},{6,10},{8,4},{10,6},{5,9},{7,11},{9,5},{11,7},{20,24},{22,26... | collective-permute-start | bytes 589832 | tf_op jit(solution)/shard_map/ppermute | solution.py:365
  130.5 2.5 %collective-permute-done.23 = f32[128,640]{1,0:T(8,128)S(1)} collective-permute-done((f32[128,640]{1,0:T(8,128)S(1)}, f32[128,640]{1,0:T(8,128)S(1)}, u32[]{:S(2)}, u32[]{:S(2)}) %collective-permute-start.23) | collective-permute-done | bytes 327712 | tf_op jit(solution)/shard_map/ppermute | solution.py:365
  133.0 0.1 bitcast_add_fusion
  133.1 2.9 %collective-permute-done.26 = f32[128,384]{1,0:T(8,128)S(1)} collective-permute-done((f32[128,384]{1,0:T(8,128)S(1)}, f32[128,384]{1,0:T(8,128)S(1)}, u32[]{:S(2)}, u32[]{:S(2)}) %collective-permute-start.26) | collective-permute-done | bytes 196640 | tf_op jit(solution)/shard_map/ppermute | solution.py:365
  136.0 0.9 fusion
  (36 shorter events, 0.7 us)
Async XLA Ops:
  0.6 5.1 %copy-start = (bf16[1,384,2048]{2,1,0:T(8,128)(2,1)S(1)}, bf16[1,384,2048]{2,1,0:T(8,128)(2,1)}, u32[]{:S(2)}) copy-start(bf16[1,384,2048]{2,1,0:T(8,128)(2,1)} %param.9) | copy-start | bytes 4718596
  0.7 1.2 copy-start.3
  2.0 1.1 copy-start.4
  4.2 5.3 %collective-permute-start = (f32[2,128,128]{2,1,0:T(8,128)S(1)}, f32[2,128,128]{2,1,0:T(8,128)S(1)}, u32[]{:S(2)}, u32[]{:S(2)}) collective-permute-start(f32[2,128,128]{2,1,0:T(8,128)S(1)} %get-tuple-element.59), channel_id=1, source_target_pairs={{0,2},{2,0},{4,6},{6,4},{8,10},{10,8},{12,14},{14,12},{1,3},{3,1},... | collective-permute-start | bytes 393224 | tf_op jit(solution)/shard_map/ppermute | solution.py:257
  5.8 7.3 %copy-start.2 = (bf16[1,384,1024]{2,1,0:T(8,128)(2,1)S(1)}, bf16[1,384,1024]{2,1,0:T(8,128)(2,1)}, u32[]{:S(2)}) copy-start(bf16[1,384,1024]{2,1,0:T(8,128)(2,1)} %param.5) | copy-start | bytes 2359300
  6.4 32.6 %collective-permute-start.8 = (f32[384,1024]{1,0:T(8,128)S(1)}, f32[384,1024]{1,0:T(8,128)S(1)}, u32[]{:S(2)}, u32[]{:S(2)}) collective-permute-start(f32[384,1024]{1,0:T(8,128)S(1)} %away.1), channel_id=1, source_target_pairs={{0,1},{1,0},{2,3},{3,2},{4,5},{5,4},{6,7},{7,6},{8,9},{9,8},{10,11... | collective-permute-start | bytes 4718600 | tf_op jit(solution)/shard_map/ppermute | solution.py:263
  6.5 9.0 %collective-permute-start.2 = (f32[2,128,128]{2,1,0:T(8,128)S(1)}, f32[2,128,128]{2,1,0:T(8,128)S(1)}, u32[]{:S(2)}, u32[]{:S(2)}) collective-permute-start(f32[2,128,128]{2,1,0:T(8,128)S(1)} %get-tuple-element.63), channel_id=1, source_target_pairs={{0,2},{2,0},{4,6},{6,4},{8,10},{10,8},{12,14},{14,12},{1,3},{3,1},... | collective-permute-start | bytes 393224 | tf_op jit(solution)/shard_map/ppermute | solution.py:257
  9.5 9.5 %collective-permute-start.1 = (f32[2,128,128]{2,1,0:T(8,128)S(1)}, f32[2,128,128]{2,1,0:T(8,128)S(1)}, u32[]{:S(2)}, u32[]{:S(2)}) collective-permute-start(f32[2,128,128]{2,1,0:T(8,128)S(1)} %add.101), channel_id=1, source_target_pairs={{0,4},{2,6},{4,8},{6,10},{8,12},{10,14},{1,5},{3,7},{5,9},{7,11},{... | collective-permute-start | bytes 393224 | tf_op jit(solution)/shard_map/ppermute | solution.py:219
  13.0 7.9 %copy-start.1 = (bf16[1024,2048]{1,0:T(8,128)(2,1)S(1)}, bf16[1024,2048]{1,0:T(8,128)(2,1)}, u32[]{:S(2)}) copy-start(bf16[1024,2048]{1,0:T(8,128)(2,1)} %w_ref.3) | copy-start | bytes 12582916
  15.5 11.1 %collective-permute-start.4 = (f32[2,128,128]{2,1,0:T(8,128)S(1)}, f32[2,128,128]{2,1,0:T(8,128)S(1)}, u32[]{:S(2)}, u32[]{:S(2)}) collective-permute-start(f32[2,128,128]{2,1,0:T(8,128)S(1)} %add.103), channel_id=1, source_target_pairs={{0,4},{2,6},{4,8},{6,10},{8,12},{10,14},{1,5},{3,7},{5,9},{7,11},{... | collective-permute-start | bytes 393224 | tf_op jit(solution)/shard_map/ppermute | solution.py:219
  19.1 10.0 %collective-permute-start.3 = (f32[2,128,128]{2,1,0:T(8,128)S(1)}, f32[2,128,128]{2,1,0:T(8,128)S(1)}, u32[]{:S(2)}, u32[]{:S(2)}) collective-permute-start(f32[2,128,128]{2,1,0:T(8,128)S(1)} %add.102), channel_id=1, source_target_pairs={{0,8},{2,10},{4,12},{6,14},{1,9},{3,11},{5,13},{7,15},{16,24},{18,... | collective-permute-start | bytes 393224 | tf_op jit(solution)/shard_map/ppermute | solution.py:219
  26.7 4.1 %collective-permute-start.5 = (f32[2,128,128]{2,1,0:T(8,128)S(1)}, f32[2,128,128]{2,1,0:T(8,128)S(1)}, u32[]{:S(2)}, u32[]{:S(2)}) collective-permute-start(f32[2,128,128]{2,1,0:T(8,128)S(1)} %add.106), channel_id=1, source_target_pairs={{0,8},{2,10},{4,12},{6,14},{1,9},{3,11},{5,13},{7,15},{16,24},{18,... | collective-permute-start | bytes 393224 | tf_op jit(solution)/shard_map/ppermute | solution.py:219
  29.1 5.0 %collective-permute-start.6 = (f32[2,128,128]{2,1,0:T(8,128)S(1)}, f32[2,128,128]{2,1,0:T(8,128)S(1)}, u32[]{:S(2)}, u32[]{:S(2)}) collective-permute-start(f32[2,128,128]{2,1,0:T(8,128)S(1)} %get-tuple-element.68), channel_id=1, source_target_pairs={{0,2},{2,0},{4,6},{6,4},{8,10},{10,8},{12,14},{14,12},{1,3},{3,1},... | collective-permute-start | bytes 393224 | tf_op jit(solution)/shard_map/ppermute | solution.py:229
  36.7 2.4 %collective-permute-start.7 = (f32[384,512]{1,0:T(8,128)S(1)}, f32[384,512]{1,0:T(8,128)S(1)}, u32[]{:S(2)}, u32[]{:S(2)}) collective-permute-start(f32[384,512]{1,0:T(8,128)S(1)} %get-tuple-element.70), channel_id=1, source_target_pairs={{0,1},{1,0},{2,3},{3,2},{4,5},{5,4},{6,7},{7,6},{8,9},{9,8},{10,11... | collective-permute-start | bytes 2359304 | tf_op jit(solution)/shard_map/ppermute | solution.py:289
  36.8 5.9 %collective-permute-start.9 = (f32[2,128,128]{2,1,0:T(8,128)S(1)}, f32[2,128,128]{2,1,0:T(8,128)S(1)}, u32[]{:S(2)}, u32[]{:S(2)}) collective-permute-start(f32[2,128,128]{2,1,0:T(8,128)S(1)} %get-tuple-element.109), channel_id=1, source_target_pairs={{0,2},{2,0},{4,6},{6,4},{8,10},{10,8},{12,14},{14,12},{1,3},{3,1},... | collective-permute-start | bytes 393224 | tf_op jit(solution)/shard_map/ppermute | solution.py:229
  42.7 14.8 %collective-permute-start.10 = (f32[2,128,512]{2,1,0:T(8,128)S(1)}, f32[2,128,512]{2,1,0:T(8,128)S(1)}, u32[]{:S(2)}, u32[]{:S(2)}) collective-permute-start(f32[2,128,512]{2,1,0:T(8,128)S(1)} %get-tuple-element.78), channel_id=1, source_target_pairs={{0,2},{2,0},{4,6},{6,4},{8,10},{10,8},{12,14},{14,12},{1,3},{3,1},... | collective-permute-start | bytes 1572872 | tf_op jit(solution)/shard_map/ppermute | solution.py:257
  46.8 15.0 %collective-permute-start.12 = (f32[4,128,128]{2,1,0:T(8,128)S(1)}, f32[4,128,128]{2,1,0:T(8,128)S(1)}, u32[]{:S(2)}, u32[]{:S(2)}) collective-permute-start(f32[4,128,128]{2,1,0:T(8,128)S(1)} %get-tuple-element.82), channel_id=1, source_target_pairs={{0,2},{2,0},{4,6},{6,4},{8,10},{10,8},{12,14},{14,12},{1,3},{3,1},... | collective-permute-start | bytes 786440 | tf_op jit(solution)/shard_map/ppermute | solution.py:257
  61.8 10.8 %collective-permute-start.13 = (f32[384,512]{1,0:T(8,128)S(1)}, f32[384,512]{1,0:T(8,128)S(1)}, u32[]{:S(2)}, u32[]{:S(2)}) collective-permute-start(f32[384,512]{1,0:T(8,128)S(1)} %get-tuple-element.83), channel_id=1, source_target_pairs={{0,1},{1,0},{2,3},{3,2},{4,5},{5,4},{6,7},{7,6},{8,9},{9,8},{10,11... | collective-permute-start | bytes 2359304 | tf_op jit(solution)/shard_map/ppermute | solution.py:305
  61.8 14.5 %collective-permute-start.18 = (f32[2,128,512]{2,1,0:T(8,128)S(1)}, f32[2,128,512]{2,1,0:T(8,128)S(1)}, u32[]{:S(2)}, u32[]{:S(2)}) collective-permute-start(f32[2,128,512]{2,1,0:T(8,128)S(1)} %get-tuple-element.100), channel_id=1, source_target_pairs={{0,2},{2,0},{4,6},{6,4},{8,10},{10,8},{12,14},{14,12},{1,3},{3,1},... | collective-permute-start | bytes 1572872 | tf_op jit(solution)/shard_map/ppermute | solution.py:257
  63.4 9.1 %collective-permute-start.11 = (f32[128,512]{1,0:T(8,128)S(1)}, f32[128,512]{1,0:T(8,128)S(1)}, u32[]{:S(2)}, u32[]{:S(2)}) collective-permute-start(f32[128,512]{1,0:T(8,128)S(1)} %select_bitcast_fusion.2), channel_id=1, source_target_pairs={{0,4},{2,6},{4,0},{6,2},{8,12},{10,14},{12,8},{14,10},{1,5},{3,7},... | collective-permute-start | bytes 786440 | tf_op jit(solution)/shard_map/ppermute | solution.py:352
  74.6 16.4 %collective-permute-start.21 = (f32[2,128,640]{2,1,0:T(8,128)S(1)}, f32[2,128,640]{2,1,0:T(8,128)S(1)}, u32[]{:S(2)}, u32[]{:S(2)}) collective-permute-start(f32[2,128,640]{2,1,0:T(8,128)S(1)} %get-tuple-element.84), channel_id=1, source_target_pairs={{0,2},{2,0},{4,6},{6,4},{8,10},{10,8},{12,14},{14,12},{1,3},{3,1},... | collective-permute-start | bytes 1966088 | tf_op jit(solution)/shard_map/ppermute | solution.py:257
  76.4 10.6 %collective-permute-start.19 = (f32[128,512]{1,0:T(8,128)S(1)}, f32[128,512]{1,0:T(8,128)S(1)}, u32[]{:S(2)}, u32[]{:S(2)}) collective-permute-start(f32[128,512]{1,0:T(8,128)S(1)} %select_bitcast_fusion.1), channel_id=1, source_target_pairs={{0,4},{2,6},{4,0},{6,2},{8,12},{10,14},{12,8},{14,10},{1,5},{3,7},... | collective-permute-start | bytes 786440 | tf_op jit(solution)/shard_map/ppermute | solution.py:352
  80.2 12.2 %collective-permute-start.14 = (f32[4,128,128]{2,1,0:T(8,128)S(1)}, f32[4,128,128]{2,1,0:T(8,128)S(1)}, u32[]{:S(2)}, u32[]{:S(2)}) collective-permute-start(f32[4,128,128]{2,1,0:T(8,128)S(1)} %add.113), channel_id=1, source_target_pairs={{4,0},{6,2},{8,4},{10,6},{12,8},{14,10},{5,1},{7,3},{9,5},{11,7},{... | collective-permute-start | bytes 786440 | tf_op jit(solution)/shard_map/ppermute | solution.py:219
  91.1 25.9 %collective-permute-start.22 = (f32[2,128,640]{2,1,0:T(8,128)S(1)}, f32[2,128,640]{2,1,0:T(8,128)S(1)}, u32[]{:S(2)}, u32[]{:S(2)}) collective-permute-start(f32[2,128,640]{2,1,0:T(8,128)S(1)} %add.124), channel_id=1, source_target_pairs={{0,4},{2,6},{12,8},{14,10},{1,5},{3,7},{13,9},{15,11},{16,20},{18,... | collective-permute-start | bytes 1966088 | tf_op jit(solution)/shard_map/ppermute | solution.py:363
  96.0 20.0 %collective-permute-start.15 = (f32[4,128,128]{2,1,0:T(8,128)S(1)}, f32[4,128,128]{2,1,0:T(8,128)S(1)}, u32[]{:S(2)}, u32[]{:S(2)}) collective-permute-start(f32[4,128,128]{2,1,0:T(8,128)S(1)} %add.114), channel_id=1, source_target_pairs={{8,0},{10,2},{12,4},{14,6},{9,1},{11,3},{13,5},{15,7},{24,16},{26,... | collective-permute-start | bytes 786440 | tf_op jit(solution)/shard_map/ppermute | solution.py:219
  97.3 19.7 %collective-permute-start.24 = (f32[2,128,384]{2,1,0:T(8,128)S(1)}, f32[2,128,384]{2,1,0:T(8,128)S(1)}, u32[]{:S(2)}, u32[]{:S(2)}) collective-permute-start(f32[2,128,384]{2,1,0:T(8,128)S(1)} %get-tuple-element.105), channel_id=1, source_target_pairs={{0,2},{2,0},{4,6},{6,4},{8,10},{10,8},{12,14},{14,12},{1,3},{3,1},... | collective-permute-start | bytes 1179656 | tf_op jit(solution)/shard_map/ppermute | solution.py:257
  98.9 19.5 %collective-permute-start.17 = (f32[128,512]{1,0:T(8,128)S(1)}, f32[128,512]{1,0:T(8,128)S(1)}, u32[]{:S(2)}, u32[]{:S(2)}) collective-permute-start(f32[128,512]{1,0:T(8,128)S(1)} %bitcast_add_fusion.4), channel_id=1, source_target_pairs={{4,12},{6,14},{8,0},{10,2},{5,13},{7,15},{9,1},{11,3},{20,28},{22,... | collective-permute-start | bytes 786440 | tf_op jit(solution)/shard_map/ppermute | solution.py:360
  113.1 8.9 %collective-permute-start.20 = (f32[128,512]{1,0:T(8,128)S(1)}, f32[128,512]{1,0:T(8,128)S(1)}, u32[]{:S(2)}, u32[]{:S(2)}) collective-permute-start(f32[128,512]{1,0:T(8,128)S(1)} %bitcast_add_fusion.1), channel_id=1, source_target_pairs={{4,12},{6,14},{8,0},{10,2},{5,13},{7,15},{9,1},{11,3},{20,28},{22,... | collective-permute-start | bytes 786440 | tf_op jit(solution)/shard_map/ppermute | solution.py:360
  116.0 6.5 %collective-permute-start.16 = (f32[4,128,128]{2,1,0:T(8,128)S(1)}, f32[4,128,128]{2,1,0:T(8,128)S(1)}, u32[]{:S(2)}, u32[]{:S(2)}) collective-permute-start(f32[4,128,128]{2,1,0:T(8,128)S(1)} %get-tuple-element.94), channel_id=1, source_target_pairs={{0,2},{2,0},{4,6},{6,4},{8,10},{10,8},{12,14},{14,12},{1,3},{3,1},... | collective-permute-start | bytes 786440 | tf_op jit(solution)/shard_map/ppermute | solution.py:229
  117.1 11.3 %collective-permute-start.25 = (f32[2,128,384]{2,1,0:T(8,128)S(1)}, f32[2,128,384]{2,1,0:T(8,128)S(1)}, u32[]{:S(2)}, u32[]{:S(2)}) collective-permute-start(f32[2,128,384]{2,1,0:T(8,128)S(1)} %add.128), channel_id=1, source_target_pairs={{0,4},{2,6},{12,8},{14,10},{1,5},{3,7},{13,9},{15,11},{16,20},{18,... | collective-permute-start | bytes 1179656 | tf_op jit(solution)/shard_map/ppermute | solution.py:363
  118.5 14.5 %collective-permute-start.23 = (f32[128,640]{1,0:T(8,128)S(1)}, f32[128,640]{1,0:T(8,128)S(1)}, u32[]{:S(2)}, u32[]{:S(2)}) collective-permute-start(f32[128,640]{1,0:T(8,128)S(1)} %select_bitcast_fusion), channel_id=1, source_target_pairs={{4,8},{6,10},{8,4},{10,6},{5,9},{7,11},{9,5},{11,7},{20,24},{22,26... | collective-permute-start | bytes 983048 | tf_op jit(solution)/shard_map/ppermute | solution.py:365
  128.4 7.6 %collective-permute-start.26 = (f32[128,384]{1,0:T(8,128)S(1)}, f32[128,384]{1,0:T(8,128)S(1)}, u32[]{:S(2)}, u32[]{:S(2)}) collective-permute-start(f32[128,384]{1,0:T(8,128)S(1)} %select_bitcast_fusion.3), channel_id=1, source_target_pairs={{4,8},{6,10},{8,4},{10,6},{5,9},{7,11},{9,5},{11,7},{20,24},{22,26... | collective-permute-start | bytes 589832 | tf_op jit(solution)/shard_map/ppermute | solution.py:365

commit v5 on v4

--- a/solution.py
+++ b/solution.py
@@ -288,7 +288,7 @@
     if fast:
         chunks = product(far, lax.ppermute(far32, "dp", swap), WIDTHS[0])
         near_own = after(near_own, chunks[0][1])
-        landed = chunks[0][0] + trade(after(chunks[0][1], near_other))
+        first_got = trade(after(chunks[0][1], near_other))
     near, near32, near_att, keep, send = call(
         functools.partial(norm_body, NEAR),
         pieces + (state, state),
@@ -297,42 +297,43 @@
         "norm_near",
     )
 
-    scale = 1.0 / math.sqrt(length * count * cores)
+    query_grad, key_local, value_local = call(
+        grads_body,
+        (rows16, rows32, rows32),
+        (place, q, k, v, far_att, *far_prior, near_att, *near_prior),
+        9 * unit * length,
+        "grads",
+    )
     received = trade(send)
     if fast:
+        landed = chunks[0][0] + after(first_got, key_local)
         others = [(kept, trade(after(sent, landed))) for kept, sent in chunks[1:]]
         lines = [toward(landed, lower, odd)]
-        nbo = lax.ppermute(after(near32, landed, received), "dp", swap)
-        chunks = product(after(near, lines[0][0]), nbo, WIDTHS[1])
+        nbo = lax.ppermute(after(near32, landed), "dp", swap)
+    (output,) = call(
+        output_body,
+        (shape((length, width), BF16),),
+        (after(far, key_local), near, out_weight),
+        unit * width,
+        "output",
+    )
+    scale = 1.0 / math.sqrt(length * count * cores)
+    if fast:
+        chunks = product(after(near, output), nbo, WIDTHS[1])
         ready = chunks[0][1]
         near_bases = [kept + trade(sent) for kept, sent in chunks]
-        lines += [toward(kept + after(got, ready), lower, odd) for kept, got in others]
-        weight_grad = scatter(lines, near_bases, lower, outer) * scale
+        kept, got = others[0]
+        base = after(kept + after(got, ready), lines[0][0])
+        lines.append(toward(base, lower, odd))
+        weight_grad = scatter(lines, near_bases, base, lower, outer) * scale
+        pins = [(lines[0][0],), (ready,)]
     else:
         nb = jnp.concatenate([far[:, :PAIR], near, far[:, PAIR:]], axis=1)
         weight = lax.dot_general(nb, g, TN, preferred_element_type=F32)
         weight = lax.psum_scatter(weight, "dp", scatter_dimension=1, tiled=True)
         weight_grad = lax.psum_scatter(weight, "seq", scatter_dimension=0, tiled=True) * scale
-        ready = near
-
-    query_grad, key_local, value_local = call(
-        grads_body,
-        (rows16, rows32, rows32),
-        (place, q, k, v, after(far_att, ready), *far_prior, near_att, *near_prior),
-        9 * unit * length,
-        "grads",
-    )
-    (output,) = call(
-        output_body,
-        (shape((length, width), BF16),),
-        (after(far, ready), near, out_weight),
-        unit * width,
-        "output",
-    )
-    ((own_later, other_later),) = exclusive(
-        [(keep, received)], count, even, True, [(), (output,), (key_local,)]
-    )
-
+        pins = []
+    ((own_later, other_later),) = exclusive([(keep, received)], count, even, True, pins)
     key_grad, value_grad = call(
         final_body,
         (rows16, rows16),
@@ -353,16 +354,17 @@
     return jnp.where(lower, base[1], base[0]) + got, jnp.where(lower, base[0], base[1]) + got
 
 
-def scatter(lines, near_bases, lower, outer):
-    far, near = [], []
-    for half, rest in lines:
-        pin = half
-        far.append(rest + lax.ppermute(half, "seq", along([(1, 3), (2, 0)])))
-    for base in near_bases:
-        base = after(base, pin)
+def scatter(lines, near_bases, landed, lower, outer):
+    far = [rest + lax.ppermute(half, "seq", along([(1, 3), (2, 0)])) for half, rest in lines]
+    near = []
+    pins = [(landed,), (lines[1][0],)]
+    for i, base in enumerate(near_bases):
+        base = after(base, *pins[i])
         got = lax.ppermute(base, "seq", along([(0, 1), (3, 2)]))
-        pin = jnp.where(lower, base[1] + got[1], base[0] + got[0])
-        final = lax.ppermute(pin, "seq", along([(1, 2), (2, 1)]))
+        across = jnp.where(lower, base[1] + got[1], base[0] + got[0])
+        pins[-1] = (*pins[-1], across)
+        across = after(across, *near_bases[i + 1 :])
+        final = lax.ppermute(across, "seq", along([(1, 2), (2, 1)]))
         near.append(jnp.where(lower, base[0] + got[0], base[1] + got[1]) + final)
     return jnp.where(outer, jnp.concatenate(far, axis=1), jnp.concatenate(near, axis=1))
 

time: 137 us -> 138 us (level)
    ppermute x6, waiting for transfers between devices: 5.91 us -> 18.9 us  [exclusive(): got = lax.ppermute(total, 'seq', links(step))]
    ppermute x2, waiting for transfers between devices: 11.5 us -> 0.31 us  [toward(): got = lax.ppermute(out, 'seq', along([(0, 1), (1, 0), (2, 3), (3, 2)]))]
    ppermute x7, waiting for transfers between devices: 20.8 us -> 17.4 us  [trade(): return lax.ppermute(send, 'seq', [(s, s ^ 1) for s in range(count)])]
    ppermute x3, waiting for transfers between devices: 5.59 us -> 7.96 us  [exclusive(): results.append((mine, lax.ppermute(theirs, 'seq', swap)))]
    ppermute x7, starting transfers between devices: 9.07 us -> 6.86 us  [trade(): return lax.ppermute(send, 'seq', [(s, s ^ 1) for s in range(count)])]
    ppermute x6, starting transfers between devices: 13.3 us -> 15.2 us  [exclusive(): got = lax.ppermute(total, 'seq', links(step))]
  transfers between devices with their start and end apart: 27 -> 27, of which waited for: 16 -> 14; matrix products, arithmetic and copies ran while one was open for 1% -> 1% of each run, Pallas kernels for 21% -> 21%
where the time goes in v5:
time: 138 us; the launch traced here: 137 us
  waiting for transfers between devices  53 us (38%)
  starting transfers between devices  48.2 us (35%)
  Pallas kernels  30.4 us (22%)
  local copies, waits for them, and re-layouts  2.38 us (2%)
  other arithmetic  2.25 us (2%)
    pallas_call x11, Pallas kernels, call(): pl.pallas_call(body, out_shape=tuple(out_shapes), in_specs=specs, out_spe...  30.4 us
    ppermute x6, waiting for transfers between devices, exclusive(): got = lax.ppermute(total, 'seq', links(step))  18.9 us
    ppermute x7, waiting for transfers between devices, trade(): return lax.ppermute(send, 'seq', [(s, s ^ 1) for s in range(count)])  17.4 us
    ppermute x6, starting transfers between devices, exclusive(): got = lax.ppermute(total, 'seq', links(step))  15.2 us
    ppermute x2, starting transfers between devices, scatter(): lax.ppermute(half, 'seq', along([(1, 3), (2, 0)]))  8.19 us
    ppermute x3, waiting for transfers between devices, exclusive(): results.append((mine, lax.ppermute(theirs, 'seq', swap)))  7.96 us
    ppermute x2, starting transfers between devices, toward(): got = lax.ppermute(out, 'seq', along([(0, 1), (1, 0), (2, 3), (3, 2)]))  7.47 us
    ppermute x7, starting transfers between devices, trade(): return lax.ppermute(send, 'seq', [(s, s ^ 1) for s in range(count)])  6.86 us
  transfers between devices with their start and end apart: 27, of which 14 were waited for; matrix products, arithmetic and copies ran while one was open for 1% of the time, Pallas kernels for 21%

profile of v5, /device:TPU:12, one launch (start us, length us, event | category | flops | bytes accessed | tf_op | source)
XLA Modules:
  0.0 137.2 jit_solution(11015104815992252336)
XLA Ops:
  0.7 0.1 pad_add_fusion.place
  0.7 1.2 copy-done.3
  2.0 1.1 copy-done.4
  3.1 1.1 state.1
  4.2 1.6 %collective-permute-start = (f32[2,128,128]{2,1,0:T(8,128)S(1)}, f32[2,128,128]{2,1,0:T(8,128)S(1)}, u32[]{:S(2)}, u32[]{:S(2)}) collective-permute-start(f32[2,128,128]{2,1,0:T(8,128)S(1)} %get-tuple-element.61), channel_id=1, source_target_pairs={{0,2},{2,0},{4,6},{6,4},{8,10},{10,8},{12,14},{14,12},{1,3},{3,1},... | collective-permute-start | bytes 393224 | tf_op jit(solution)/shard_map/ppermute | solution.py:257
  5.8 0.6 away.1
  6.4 0.1 collective-permute-start.8
  6.5 0.6 collective-permute-start.2
  7.1 2.4 %collective-permute-done = f32[2,128,128]{2,1,0:T(8,128)S(1)} collective-permute-done((f32[2,128,128]{2,1,0:T(8,128)S(1)}, f32[2,128,128]{2,1,0:T(8,128)S(1)}, u32[]{:S(2)}, u32[]{:S(2)}) %collective-permute-start) | collective-permute-done | bytes 131104 | tf_op jit(solution)/shard_map/ppermute | solution.py:257
  9.5 3.5 %collective-permute-start.1 = (f32[2,128,128]{2,1,0:T(8,128)S(1)}, f32[2,128,128]{2,1,0:T(8,128)S(1)}, u32[]{:S(2)}, u32[]{:S(2)}) collective-permute-start(f32[2,128,128]{2,1,0:T(8,128)S(1)} %add.101), channel_id=1, source_target_pairs={{0,4},{2,6},{4,8},{6,10},{8,12},{10,14},{1,5},{3,7},{5,9},{7,11},{... | collective-permute-start | bytes 393224 | tf_op jit(solution)/shard_map/ppermute | solution.py:219
  13.1 2.4 %local.1.att_ref = f32[384,1024]{1,0:T(8,128)S(1)} custom-call(bf16[384,1024]{1,0:T(8,128)(2,1)S(1)} %bitcast.38, bf16[384,1024]{1,0:T(8,128)(2,1)S(1)} %bitcast.43, bf16[384,1024]{1,0:T(8,128)(2,1)S(1)} %bitcast.47), custom_call_target="tpu_custom_call" | custom-call | flops 56623104 | tf_op jit(solution)/shard_map/local/pallas_call | solution.py:70
  15.5 3.5 %collective-permute-start.4 = (f32[2,128,128]{2,1,0:T(8,128)S(1)}, f32[2,128,128]{2,1,0:T(8,128)S(1)}, u32[]{:S(2)}, u32[]{:S(2)}) collective-permute-start(f32[2,128,128]{2,1,0:T(8,128)S(1)} %add.103), channel_id=1, source_target_pairs={{0,4},{2,6},{4,8},{6,10},{8,12},{10,14},{1,5},{3,7},{5,9},{7,11},{... | collective-permute-start | bytes 393224 | tf_op jit(solution)/shard_map/ppermute | solution.py:219
  19.1 1.9 %collective-permute-start.3 = (f32[2,128,128]{2,1,0:T(8,128)S(1)}, f32[2,128,128]{2,1,0:T(8,128)S(1)}, u32[]{:S(2)}, u32[]{:S(2)}) collective-permute-start(f32[2,128,128]{2,1,0:T(8,128)S(1)} %add.102), channel_id=1, source_target_pairs={{0,8},{2,10},{4,12},{6,14},{1,9},{3,11},{5,13},{7,15},{16,24},{18,... | collective-permute-start | bytes 393224 | tf_op jit(solution)/shard_map/ppermute | solution.py:219
  20.9 2.4 %d_normed.1.dn_ref = f32[384,1024]{1,0:T(8,128)S(1)} custom-call(bf16[384,2048]{1,0:T(8,128)(2,1)S(1)} %bitcast.35, bf16[1024,2048]{1,0:T(8,128)(2,1)S(1)} %copy-done.1), custom_call_target="tpu_custom_call" | custom-call | flops 100663296 | tf_op jit(solution)/shard_map/d_normed/pallas_call | solution.py:70
  23.4 3.3 %collective-permute-done.4 = f32[2,128,128]{2,1,0:T(8,128)S(1)} collective-permute-done((f32[2,128,128]{2,1,0:T(8,128)S(1)}, f32[2,128,128]{2,1,0:T(8,128)S(1)}, u32[]{:S(2)}, u32[]{:S(2)}) %collective-permute-start.4) | collective-permute-done | bytes 131104 | tf_op jit(solution)/shard_map/ppermute | solution.py:219
  26.7 1.5 %collective-permute-start.5 = (f32[2,128,128]{2,1,0:T(8,128)S(1)}, f32[2,128,128]{2,1,0:T(8,128)S(1)}, u32[]{:S(2)}, u32[]{:S(2)}) collective-permute-start(f32[2,128,128]{2,1,0:T(8,128)S(1)} %add.106), channel_id=1, source_target_pairs={{0,8},{2,10},{4,12},{6,14},{1,9},{3,11},{5,13},{7,15},{16,24},{18,... | collective-permute-start | bytes 393224 | tf_op jit(solution)/shard_map/ppermute | solution.py:219
  28.2 0.9 collective-permute-done.3
  29.1 1.6 %collective-permute-start.6 = (f32[2,128,128]{2,1,0:T(8,128)S(1)}, f32[2,128,128]{2,1,0:T(8,128)S(1)}, u32[]{:S(2)}, u32[]{:S(2)}) collective-permute-start(f32[2,128,128]{2,1,0:T(8,128)S(1)} %get-tuple-element.70), channel_id=1, source_target_pairs={{0,2},{2,0},{4,6},{6,4},{8,10},{10,8},{12,14},{14,12},{1,3},{3,1},... | collective-permute-start | bytes 393224 | tf_op jit(solution)/shard_map/ppermute | solution.py:229
  30.8 3.4 %collective-permute-done.6.other_ref.refs_2_ = f32[2,128,128]{2,1,0:T(8,128)S(1)} collective-permute-done((f32[2,128,128]{2,1,0:T(8,128)S(1)}, f32[2,128,128]{2,1,0:T(8,128)S(1)}, u32[]{:S(2)}, u32[]{:S(2)}) %collective-permute-start.6) | collective-permute-done | bytes 131104 | tf_op jit(solution)/shard_map/ppermute | solution.py:229
  34.1 2.5 %norm_far.1 = (bf16[384,512]{1,0:T(8,128)(2,1)S(1)}, f32[384,512]{1,0:T(8,128)S(1)}, bf16[384,512]{1,0:T(8,128)(2,1)S(1)}, f32[2,128,128]{2,1,0:T(8,128)S(1)}, f32[2,128,128]{2,1,0:T(8,128)S(1)}) custom-call(s32[2]{0:T(128)S(1)} %pad_add_fusion.place, bf16[384,1024]{1,0:T(8,128)(2,1)S(1)} %bitcast.39, f32[384,1024]{1,0:T(8,128)S(1)} %local.1.att_ref, ...), custom_call_target="tpu_custom_call" | custom-call | flops 6291456 | tf_op jit(solution)/shard_map/norm_far/pallas_call | solution.py:70
  36.7 0.1 collective-permute-start.7
  36.8 1.6 %collective-permute-start.9 = (f32[2,128,128]{2,1,0:T(8,128)S(1)}, f32[2,128,128]{2,1,0:T(8,128)S(1)}, u32[]{:S(2)}, u32[]{:S(2)}) collective-permute-start(f32[2,128,128]{2,1,0:T(8,128)S(1)} %get-tuple-element.113), channel_id=1, source_target_pairs={{0,2},{2,0},{4,6},{6,4},{8,10},{10,8},{12,14},{14,12},{1,3},{3,1},... | collective-permute-start | bytes 393224 | tf_op jit(solution)/shard_map/ppermute | solution.py:229
  38.4 0.6 collective-permute-done.7.nbo_ref
  39.0 1.8 %weight.2 = (f32[2,128,512]{2,1,0:T(8,128)S(1)}, f32[2,128,512]{2,1,0:T(8,128)S(1)}, f32[2,128,512]{2,1,0:T(8,128)S(1)}, f32[2,128,512]{2,1,0:T(8,128)S(1)}) custom-call(s32[2]{0:T(128)S(1)} %pad_add_fusion.place, bf16[384,512]{1,0:T(8,128)(2,1)S(1)} %get-tuple-element.80.nb_ref.far_ref, bf16[384,2048]{1,0:T(8,128)(2,1)S(1)} %bitcast.36, ...), custom_call_target="tpu_custom_call" | custom-call | flops 50331648 | tf_op jit(solution)/shard_map/weight/pallas_call | solution.py:70
  40.9 1.8 %collective-permute-done.9.other_ref.refs_5_ = f32[2,128,128]{2,1,0:T(8,128)S(1)} collective-permute-done((f32[2,128,128]{2,1,0:T(8,128)S(1)}, f32[2,128,128]{2,1,0:T(8,128)S(1)}, u32[]{:S(2)}, u32[]{:S(2)}) %collective-permute-start.9) | collective-permute-done | bytes 131104 | tf_op jit(solution)/shard_map/ppermute | solution.py:229
  42.7 1.6 %collective-permute-start.11 = (f32[2,128,512]{2,1,0:T(8,128)S(1)}, f32[2,128,512]{2,1,0:T(8,128)S(1)}, u32[]{:S(2)}, u32[]{:S(2)}) collective-permute-start(f32[2,128,512]{2,1,0:T(8,128)S(1)} %get-tuple-element.88), channel_id=1, source_target_pairs={{0,2},{2,0},{4,6},{6,4},{8,10},{10,8},{12,14},{14,12},{1,3},{3,1},... | collective-permute-start | bytes 1572872 | tf_op jit(solution)/shard_map/ppermute | solution.py:257
  44.2 2.6 %norm_near.1 = (bf16[384,512]{1,0:T(8,128)(2,1)S(1)}, f32[384,512]{1,0:T(8,128)S(1)}, bf16[384,512]{1,0:T(8,128)(2,1)S(1)}, f32[4,128,128]{2,1,0:T(8,128)S(1)}, f32[4,128,128]{2,1,0:T(8,128)S(1)}) custom-call(s32[2]{0:T(128)S(1)} %pad_add_fusion.place, bf16[384,1024]{1,0:T(8,128)(2,1)S(1)} %bitcast.40, f32[384,1024]{1,0:T(8,128)S(1)} %local.1.att_ref, ...), custom_call_target="tpu_custom_call" | custom-call | flops 402653184 | tf_op jit(solution)/shard_map/norm_near/pallas_call | solution.py:70
  46.8 8.6 %grads.1 = (bf16[384,1024]{1,0:T(8,128)(2,1)}, f32[384,1024]{1,0:T(8,128)S(1)}, f32[384,1024]{1,0:T(8,128)S(1)}) custom-call(s32[2]{0:T(128)S(1)} %pad_add_fusion.place, bf16[384,1024]{1,0:T(8,128)(2,1)S(1)} %bitcast.41, bf16[384,1024]{1,0:T(8,128)(2,1)S(1)} %bitcast.44, bf16[384,1024]{1,0:T(8,128)(2,1)S(1)} %bitcast.48, ...), custom_call_target="tpu_custom_call" | custom-call | flops 169869312 | tf_op jit(solution)/shard_map/grads/pallas_call | solution.py:70
  55.4 0.8 collective-permute-done.11
  56.2 0.1 add.112
  56.2 0.1 collective-permute-start.14
  56.3 1.6 %collective-permute-start.10 = (f32[4,128,128]{2,1,0:T(8,128)S(1)}, f32[4,128,128]{2,1,0:T(8,128)S(1)}, u32[]{:S(2)}, u32[]{:S(2)}) collective-permute-start(f32[4,128,128]{2,1,0:T(8,128)S(1)} %get-tuple-element.85), channel_id=1, source_target_pairs={{0,2},{2,0},{4,6},{6,4},{8,10},{10,8},{12,14},{14,12},{1,3},{3,1},... | collective-permute-start | bytes 786440 | tf_op jit(solution)/shard_map/ppermute | solution.py:257
  58.0 0.5 collective-permute-start.18
  58.4 3.7 %collective-permute-start.12 = (f32[128,512]{1,0:T(8,128)S(1)}, f32[128,512]{1,0:T(8,128)S(1)}, u32[]{:S(2)}, u32[]{:S(2)}) collective-permute-start(f32[128,512]{1,0:T(8,128)S(1)} %select_bitcast_fusion.2), channel_id=1, source_target_pairs={{0,4},{2,6},{4,0},{6,2},{8,12},{10,14},{12,8},{14,10},{1,5},{3,7},... | collective-permute-start | bytes 786440 | tf_op jit(solution)/shard_map/ppermute | solution.py:353
  62.2 3.5 %output.1 = bf16[384,2048]{1,0:T(8,128)(2,1)} custom-call(bf16[384,512]{1,0:T(8,128)(2,1)S(1)} %get-tuple-element.80.nb_ref.far_ref, bf16[384,512]{1,0:T(8,128)(2,1)S(1)} %get-tuple-element.92.near_ref.nb_ref, bf16[1024,2048]{1,0:T(8,128)(2,1)S(1)} %copy-done.1), custom_call_target="tpu_custom_call" | custom-call | flops 100663296 | tf_op jit(solution)/shard_map/output/pallas_call | solution.py:70
  65.7 2.0 %weight.3 = (f32[2,128,640]{2,1,0:T(8,128)S(1)}, f32[2,128,640]{2,1,0:T(8,128)S(1)}, f32[2,128,384]{2,1,0:T(8,128)S(1)}, f32[2,128,384]{2,1,0:T(8,128)S(1)}) custom-call(s32[2]{0:T(128)S(1)} %pad_add_fusion.place, bf16[384,512]{1,0:T(8,128)(2,1)S(1)} %get-tuple-element.92.near_ref.nb_ref, bf16[384,2048]{1,0:T(8,128)(2,1)S(1)} %bitcast.37, ...), custom_call_target="tpu_custom_call" | custom-call | flops 50331648 | tf_op jit(solution)/shard_map/weight/pallas_call | solution.py:70
  67.7 0.5 collective-permute-start.21
  68.2 0.3 collective-permute-done.12
  68.6 3.6 %collective-permute-start.13 = (f32[4,128,128]{2,1,0:T(8,128)S(1)}, f32[4,128,128]{2,1,0:T(8,128)S(1)}, u32[]{:S(2)}, u32[]{:S(2)}) collective-permute-start(f32[4,128,128]{2,1,0:T(8,128)S(1)} %add.111), channel_id=1, source_target_pairs={{4,0},{6,2},{8,4},{10,6},{12,8},{14,10},{5,1},{7,3},{9,5},{11,7},{... | collective-permute-start | bytes 786440 | tf_op jit(solution)/shard_map/ppermute | solution.py:219
  72.3 4.5 %collective-permute-done.18 = f32[2,128,512]{2,1,0:T(8,128)S(1)} collective-permute-done((f32[2,128,512]{2,1,0:T(8,128)S(1)}, f32[2,128,512]{2,1,0:T(8,128)S(1)}, u32[]{:S(2)}, u32[]{:S(2)}) %collective-permute-start.18) | collective-permute-done | bytes 524320 | tf_op jit(solution)/shard_map/ppermute | solution.py:257
  76.7 0.1 add.120
  76.9 3.7 %collective-permute-start.19 = (f32[128,512]{1,0:T(8,128)S(1)}, f32[128,512]{1,0:T(8,128)S(1)}, u32[]{:S(2)}, u32[]{:S(2)}) collective-permute-start(f32[128,512]{1,0:T(8,128)S(1)} %select_bitcast_fusion.1), channel_id=1, source_target_pairs={{0,4},{2,6},{4,0},{6,2},{8,12},{10,14},{12,8},{14,10},{1,5},{3,7},... | collective-permute-start | bytes 786440 | tf_op jit(solution)/shard_map/ppermute | solution.py:353
  80.6 9.7 %collective-permute-done.21 = f32[2,128,640]{2,1,0:T(8,128)S(1)} collective-permute-done((f32[2,128,640]{2,1,0:T(8,128)S(1)}, f32[2,128,640]{2,1,0:T(8,128)S(1)}, u32[]{:S(2)}, u32[]{:S(2)}) %collective-permute-start.21) | collective-permute-done | bytes 655392 | tf_op jit(solution)/shard_map/ppermute | solution.py:257
  90.3 0.1 add.124
  90.4 1.3 collective-permute-start.22
  91.8 1.3 collective-permute-start.15
  93.0 6.9 %collective-permute-start.17 = (f32[128,512]{1,0:T(8,128)S(1)}, f32[128,512]{1,0:T(8,128)S(1)}, u32[]{:S(2)}, u32[]{:S(2)}) collective-permute-start(f32[128,512]{1,0:T(8,128)S(1)} %bitcast_add_fusion.4), channel_id=1, source_target_pairs={{4,12},{6,14},{8,0},{10,2},{5,13},{7,15},{9,1},{11,3},{20,28},{22,... | collective-permute-start | bytes 786440 | tf_op jit(solution)/shard_map/ppermute | solution.py:358
  99.9 0.5 collective-permute-start.23
  100.5 1.3 collective-permute-start.20
  101.8 14.7 %collective-permute-done.15 = f32[4,128,128]{2,1,0:T(8,128)S(1)} collective-permute-done((f32[4,128,128]{2,1,0:T(8,128)S(1)}, f32[4,128,128]{2,1,0:T(8,128)S(1)}, u32[]{:S(2)}, u32[]{:S(2)}) %collective-permute-start.15) | collective-permute-done | bytes 262176 | tf_op jit(solution)/shard_map/ppermute | solution.py:219
  116.6 0.1 add_select_fusion
  116.7 0.5 collective-permute-start.16
  117.3 0.1 select_bitcast_fusion
  117.3 1.3 collective-permute-start.25
  118.7 0.1 fusion.2
  118.8 1.9 %collective-permute-start.24 = (f32[128,640]{1,0:T(8,128)S(1)}, f32[128,640]{1,0:T(8,128)S(1)}, u32[]{:S(2)}, u32[]{:S(2)}) collective-permute-start(f32[128,640]{1,0:T(8,128)S(1)} %select_bitcast_fusion), channel_id=1, source_target_pairs={{4,8},{6,10},{8,4},{10,6},{5,9},{7,11},{9,5},{11,7},{20,24},{22,26... | collective-permute-start | bytes 983048 | tf_op jit(solution)/shard_map/ppermute | solution.py:367
  120.7 0.1 fusion.1
  120.8 2.8 %collective-permute-done.16.other_ref = f32[4,128,128]{2,1,0:T(8,128)S(1)} collective-permute-done((f32[4,128,128]{2,1,0:T(8,128)S(1)}, f32[4,128,128]{2,1,0:T(8,128)S(1)}, u32[]{:S(2)}, u32[]{:S(2)}) %collective-permute-start.16) | collective-permute-done | bytes 262176 | tf_op jit(solution)/shard_map/ppermute | solution.py:229
  123.7 2.8 %final.1 = (bf16[384,1024]{1,0:T(8,128)(2,1)}, bf16[384,1024]{1,0:T(8,128)(2,1)}) custom-call(s32[2]{0:T(128)S(1)} %pad_add_fusion.place, bf16[384,1024]{1,0:T(8,128)(2,1)S(1)} %bitcast.45, bf16[384,1024]{1,0:T(8,128)(2,1)S(1)} %bitcast.49, f32[384,1024]{1,0:T(8,128)S(1)} %get-tuple-element.79.kl_ref, f32[384,1024]{1,0:T(8,128)S(1)} %get-tuple-element.83.vl_ref, ...), custom_call_target="tpu_custom_call" | custom-call | flops 25165824 | tf_op jit(solution)/shard_map/final/pallas_call | solution.py:70
  126.4 2.3 %collective-permute-done.25 = f32[2,128,384]{2,1,0:T(8,128)S(1)} collective-permute-done((f32[2,128,384]{2,1,0:T(8,128)S(1)}, f32[2,128,384]{2,1,0:T(8,128)S(1)}, u32[]{:S(2)}, u32[]{:S(2)}) %collective-permute-start.25) | collective-permute-done | bytes 393248 | tf_op jit(solution)/shard_map/ppermute | solution.py:363
  128.7 1.9 %collective-permute-start.26 = (f32[128,384]{1,0:T(8,128)S(1)}, f32[128,384]{1,0:T(8,128)S(1)}, u32[]{:S(2)}, u32[]{:S(2)}) collective-permute-start(f32[128,384]{1,0:T(8,128)S(1)} %select_bitcast_fusion.3), channel_id=1, source_target_pairs={{4,8},{6,10},{8,4},{10,6},{5,9},{7,11},{9,5},{11,7},{20,24},{22,26... | collective-permute-start | bytes 589832 | tf_op jit(solution)/shard_map/ppermute | solution.py:367
  130.7 0.1 bitcast_add_fusion
  130.8 5.5 %collective-permute-done.26 = f32[128,384]{1,0:T(8,128)S(1)} collective-permute-done((f32[128,384]{1,0:T(8,128)S(1)}, f32[128,384]{1,0:T(8,128)S(1)}, u32[]{:S(2)}, u32[]{:S(2)}) %collective-permute-start.26) | collective-permute-done | bytes 196640 | tf_op jit(solution)/shard_map/ppermute | solution.py:367
  136.4 0.9 fusion
  (36 shorter events, 0.6 us)
Async XLA Ops:
  0.6 5.1 %copy-start = (bf16[1,384,2048]{2,1,0:T(8,128)(2,1)S(1)}, bf16[1,384,2048]{2,1,0:T(8,128)(2,1)}, u32[]{:S(2)}) copy-start(bf16[1,384,2048]{2,1,0:T(8,128)(2,1)} %param.9) | copy-start | bytes 4718596
  0.7 1.2 copy-start.3
  2.0 1.1 copy-start.4
  4.2 5.3 %collective-permute-start = (f32[2,128,128]{2,1,0:T(8,128)S(1)}, f32[2,128,128]{2,1,0:T(8,128)S(1)}, u32[]{:S(2)}, u32[]{:S(2)}) collective-permute-start(f32[2,128,128]{2,1,0:T(8,128)S(1)} %get-tuple-element.61), channel_id=1, source_target_pairs={{0,2},{2,0},{4,6},{6,4},{8,10},{10,8},{12,14},{14,12},{1,3},{3,1},... | collective-permute-start | bytes 393224 | tf_op jit(solution)/shard_map/ppermute | solution.py:257
  5.8 7.3 %copy-start.2 = (bf16[1,384,1024]{2,1,0:T(8,128)(2,1)S(1)}, bf16[1,384,1024]{2,1,0:T(8,128)(2,1)}, u32[]{:S(2)}) copy-start(bf16[1,384,1024]{2,1,0:T(8,128)(2,1)} %param.5) | copy-start | bytes 2359300
  6.4 32.6 %collective-permute-start.8 = (f32[384,1024]{1,0:T(8,128)S(1)}, f32[384,1024]{1,0:T(8,128)S(1)}, u32[]{:S(2)}, u32[]{:S(2)}) collective-permute-start(f32[384,1024]{1,0:T(8,128)S(1)} %away.1), channel_id=1, source_target_pairs={{0,1},{1,0},{2,3},{3,2},{4,5},{5,4},{6,7},{7,6},{8,9},{9,8},{10,11... | collective-permute-start | bytes 4718600 | tf_op jit(solution)/shard_map/ppermute | solution.py:263
  6.5 9.0 %collective-permute-start.2 = (f32[2,128,128]{2,1,0:T(8,128)S(1)}, f32[2,128,128]{2,1,0:T(8,128)S(1)}, u32[]{:S(2)}, u32[]{:S(2)}) collective-permute-start(f32[2,128,128]{2,1,0:T(8,128)S(1)} %get-tuple-element.65), channel_id=1, source_target_pairs={{0,2},{2,0},{4,6},{6,4},{8,10},{10,8},{12,14},{14,12},{1,3},{3,1},... | collective-permute-start | bytes 393224 | tf_op jit(solution)/shard_map/ppermute | solution.py:257
  9.5 9.5 %collective-permute-start.1 = (f32[2,128,128]{2,1,0:T(8,128)S(1)}, f32[2,128,128]{2,1,0:T(8,128)S(1)}, u32[]{:S(2)}, u32[]{:S(2)}) collective-permute-start(f32[2,128,128]{2,1,0:T(8,128)S(1)} %add.101), channel_id=1, source_target_pairs={{0,4},{2,6},{4,8},{6,10},{8,12},{10,14},{1,5},{3,7},{5,9},{7,11},{... | collective-permute-start | bytes 393224 | tf_op jit(solution)/shard_map/ppermute | solution.py:219
  13.0 7.9 %copy-start.1 = (bf16[1024,2048]{1,0:T(8,128)(2,1)S(1)}, bf16[1024,2048]{1,0:T(8,128)(2,1)}, u32[]{:S(2)}) copy-start(bf16[1024,2048]{1,0:T(8,128)(2,1)} %w_ref.3) | copy-start | bytes 12582916
  15.5 11.1 %collective-permute-start.4 = (f32[2,128,128]{2,1,0:T(8,128)S(1)}, f32[2,128,128]{2,1,0:T(8,128)S(1)}, u32[]{:S(2)}, u32[]{:S(2)}) collective-permute-start(f32[2,128,128]{2,1,0:T(8,128)S(1)} %add.103), channel_id=1, source_target_pairs={{0,4},{2,6},{4,8},{6,10},{8,12},{10,14},{1,5},{3,7},{5,9},{7,11},{... | collective-permute-start | bytes 393224 | tf_op jit(solution)/shard_map/ppermute | solution.py:219
  19.1 10.0 %collective-permute-start.3 = (f32[2,128,128]{2,1,0:T(8,128)S(1)}, f32[2,128,128]{2,1,0:T(8,128)S(1)}, u32[]{:S(2)}, u32[]{:S(2)}) collective-permute-start(f32[2,128,128]{2,1,0:T(8,128)S(1)} %add.102), channel_id=1, source_target_pairs={{0,8},{2,10},{4,12},{6,14},{1,9},{3,11},{5,13},{7,15},{16,24},{18,... | collective-permute-start | bytes 393224 | tf_op jit(solution)/shard_map/ppermute | solution.py:219
  26.7 4.1 %collective-permute-start.5 = (f32[2,128,128]{2,1,0:T(8,128)S(1)}, f32[2,128,128]{2,1,0:T(8,128)S(1)}, u32[]{:S(2)}, u32[]{:S(2)}) collective-permute-start(f32[2,128,128]{2,1,0:T(8,128)S(1)} %add.106), channel_id=1, source_target_pairs={{0,8},{2,10},{4,12},{6,14},{1,9},{3,11},{5,13},{7,15},{16,24},{18,... | collective-permute-start | bytes 393224 | tf_op jit(solution)/shard_map/ppermute | solution.py:219
  29.1 5.0 %collective-permute-start.6 = (f32[2,128,128]{2,1,0:T(8,128)S(1)}, f32[2,128,128]{2,1,0:T(8,128)S(1)}, u32[]{:S(2)}, u32[]{:S(2)}) collective-permute-start(f32[2,128,128]{2,1,0:T(8,128)S(1)} %get-tuple-element.70), channel_id=1, source_target_pairs={{0,2},{2,0},{4,6},{6,4},{8,10},{10,8},{12,14},{14,12},{1,3},{3,1},... | collective-permute-start | bytes 393224 | tf_op jit(solution)/shard_map/ppermute | solution.py:229
  36.7 2.4 %collective-permute-start.7 = (f32[384,512]{1,0:T(8,128)S(1)}, f32[384,512]{1,0:T(8,128)S(1)}, u32[]{:S(2)}, u32[]{:S(2)}) collective-permute-start(f32[384,512]{1,0:T(8,128)S(1)} %get-tuple-element.73), channel_id=1, source_target_pairs={{0,1},{1,0},{2,3},{3,2},{4,5},{5,4},{6,7},{7,6},{8,9},{9,8},{10,11... | collective-permute-start | bytes 2359304 | tf_op jit(solution)/shard_map/ppermute | solution.py:289
  36.8 5.9 %collective-permute-start.9 = (f32[2,128,128]{2,1,0:T(8,128)S(1)}, f32[2,128,128]{2,1,0:T(8,128)S(1)}, u32[]{:S(2)}, u32[]{:S(2)}) collective-permute-start(f32[2,128,128]{2,1,0:T(8,128)S(1)} %get-tuple-element.113), channel_id=1, source_target_pairs={{0,2},{2,0},{4,6},{6,4},{8,10},{10,8},{12,14},{14,12},{1,3},{3,1},... | collective-permute-start | bytes 393224 | tf_op jit(solution)/shard_map/ppermute | solution.py:229
  42.7 13.5 %collective-permute-start.11 = (f32[2,128,512]{2,1,0:T(8,128)S(1)}, f32[2,128,512]{2,1,0:T(8,128)S(1)}, u32[]{:S(2)}, u32[]{:S(2)}) collective-permute-start(f32[2,128,512]{2,1,0:T(8,128)S(1)} %get-tuple-element.88), channel_id=1, source_target_pairs={{0,2},{2,0},{4,6},{6,4},{8,10},{10,8},{12,14},{14,12},{1,3},{3,1},... | collective-permute-start | bytes 1572872 | tf_op jit(solution)/shard_map/ppermute | solution.py:257
  56.2 9.4 %collective-permute-start.14 = (f32[384,512]{1,0:T(8,128)S(1)}, f32[384,512]{1,0:T(8,128)S(1)}, u32[]{:S(2)}, u32[]{:S(2)}) collective-permute-start(f32[384,512]{1,0:T(8,128)S(1)} %get-tuple-element.94), channel_id=1, source_target_pairs={{0,1},{1,0},{2,3},{3,2},{4,5},{5,4},{6,7},{7,6},{8,9},{9,8},{10,11... | collective-permute-start | bytes 2359304 | tf_op jit(solution)/shard_map/ppermute | solution.py:312
  56.3 11.9 %collective-permute-start.10 = (f32[4,128,128]{2,1,0:T(8,128)S(1)}, f32[4,128,128]{2,1,0:T(8,128)S(1)}, u32[]{:S(2)}, u32[]{:S(2)}) collective-permute-start(f32[4,128,128]{2,1,0:T(8,128)S(1)} %get-tuple-element.85), channel_id=1, source_target_pairs={{0,2},{2,0},{4,6},{6,4},{8,10},{10,8},{12,14},{14,12},{1,3},{3,1},... | collective-permute-start | bytes 786440 | tf_op jit(solution)/shard_map/ppermute | solution.py:257
  58.0 18.8 %collective-permute-start.18 = (f32[2,128,512]{2,1,0:T(8,128)S(1)}, f32[2,128,512]{2,1,0:T(8,128)S(1)}, u32[]{:S(2)}, u32[]{:S(2)}) collective-permute-start(f32[2,128,512]{2,1,0:T(8,128)S(1)} %get-tuple-element.102), channel_id=1, source_target_pairs={{0,2},{2,0},{4,6},{6,4},{8,10},{10,8},{12,14},{14,12},{1,3},{3,1},... | collective-permute-start | bytes 1572872 | tf_op jit(solution)/shard_map/ppermute | solution.py:257
  58.4 10.1 %collective-permute-start.12 = (f32[128,512]{1,0:T(8,128)S(1)}, f32[128,512]{1,0:T(8,128)S(1)}, u32[]{:S(2)}, u32[]{:S(2)}) collective-permute-start(f32[128,512]{1,0:T(8,128)S(1)} %select_bitcast_fusion.2), channel_id=1, source_target_pairs={{0,4},{2,6},{4,0},{6,2},{8,12},{10,14},{12,8},{14,10},{1,5},{3,7},... | collective-permute-start | bytes 786440 | tf_op jit(solution)/shard_map/ppermute | solution.py:353
  67.7 22.6 %collective-permute-start.21 = (f32[2,128,640]{2,1,0:T(8,128)S(1)}, f32[2,128,640]{2,1,0:T(8,128)S(1)}, u32[]{:S(2)}, u32[]{:S(2)}) collective-permute-start(f32[2,128,640]{2,1,0:T(8,128)S(1)} %get-tuple-element.95), channel_id=1, source_target_pairs={{0,2},{2,0},{4,6},{6,4},{8,10},{10,8},{12,14},{14,12},{1,3},{3,1},... | collective-permute-start | bytes 1966088 | tf_op jit(solution)/shard_map/ppermute | solution.py:257
  68.6 23.1 %collective-permute-start.13 = (f32[4,128,128]{2,1,0:T(8,128)S(1)}, f32[4,128,128]{2,1,0:T(8,128)S(1)}, u32[]{:S(2)}, u32[]{:S(2)}) collective-permute-start(f32[4,128,128]{2,1,0:T(8,128)S(1)} %add.111), channel_id=1, source_target_pairs={{4,0},{6,2},{8,4},{10,6},{12,8},{14,10},{5,1},{7,3},{9,5},{11,7},{... | collective-permute-start | bytes 786440 | tf_op jit(solution)/shard_map/ppermute | solution.py:219
  76.9 23.6 %collective-permute-start.19 = (f32[128,512]{1,0:T(8,128)S(1)}, f32[128,512]{1,0:T(8,128)S(1)}, u32[]{:S(2)}, u32[]{:S(2)}) collective-permute-start(f32[128,512]{1,0:T(8,128)S(1)} %select_bitcast_fusion.1), channel_id=1, source_target_pairs={{0,4},{2,6},{4,0},{6,2},{8,12},{10,14},{12,8},{14,10},{1,5},{3,7},... | collective-permute-start | bytes 786440 | tf_op jit(solution)/shard_map/ppermute | solution.py:353
  90.4 26.9 %collective-permute-start.22 = (f32[2,128,640]{2,1,0:T(8,128)S(1)}, f32[2,128,640]{2,1,0:T(8,128)S(1)}, u32[]{:S(2)}, u32[]{:S(2)}) collective-permute-start(f32[2,128,640]{2,1,0:T(8,128)S(1)} %add.124), channel_id=1, source_target_pairs={{0,4},{2,6},{12,8},{14,10},{1,5},{3,7},{13,9},{15,11},{16,20},{18,... | collective-permute-start | bytes 1966088 | tf_op jit(solution)/shard_map/ppermute | solution.py:363
  91.8 24.8 %collective-permute-start.15 = (f32[4,128,128]{2,1,0:T(8,128)S(1)}, f32[4,128,128]{2,1,0:T(8,128)S(1)}, u32[]{:S(2)}, u32[]{:S(2)}) collective-permute-start(f32[4,128,128]{2,1,0:T(8,128)S(1)} %add.114), channel_id=1, source_target_pairs={{8,0},{10,2},{12,4},{14,6},{9,1},{11,3},{13,5},{15,7},{24,16},{26,... | collective-permute-start | bytes 786440 | tf_op jit(solution)/shard_map/ppermute | solution.py:219
  93.0 25.6 %collective-permute-start.17 = (f32[128,512]{1,0:T(8,128)S(1)}, f32[128,512]{1,0:T(8,128)S(1)}, u32[]{:S(2)}, u32[]{:S(2)}) collective-permute-start(f32[128,512]{1,0:T(8,128)S(1)} %bitcast_add_fusion.4), channel_id=1, source_target_pairs={{4,12},{6,14},{8,0},{10,2},{5,13},{7,15},{9,1},{11,3},{20,28},{22,... | collective-permute-start | bytes 786440 | tf_op jit(solution)/shard_map/ppermute | solution.py:358
  99.9 17.3 %collective-permute-start.23 = (f32[2,128,384]{2,1,0:T(8,128)S(1)}, f32[2,128,384]{2,1,0:T(8,128)S(1)}, u32[]{:S(2)}, u32[]{:S(2)}) collective-permute-start(f32[2,128,384]{2,1,0:T(8,128)S(1)} %get-tuple-element.108), channel_id=1, source_target_pairs={{0,2},{2,0},{4,6},{6,4},{8,10},{10,8},{12,14},{14,12},{1,3},{3,1},... | collective-permute-start | bytes 1179656 | tf_op jit(solution)/shard_map/ppermute | solution.py:257
  100.5 20.2 %collective-permute-start.20 = (f32[128,512]{1,0:T(8,128)S(1)}, f32[128,512]{1,0:T(8,128)S(1)}, u32[]{:S(2)}, u32[]{:S(2)}) collective-permute-start(f32[128,512]{1,0:T(8,128)S(1)} %bitcast_add_fusion.1), channel_id=1, source_target_pairs={{4,12},{6,14},{8,0},{10,2},{5,13},{7,15},{9,1},{11,3},{20,28},{22,... | collective-permute-start | bytes 786440 | tf_op jit(solution)/shard_map/ppermute | solution.py:358
  116.7 7.0 %collective-permute-start.16 = (f32[4,128,128]{2,1,0:T(8,128)S(1)}, f32[4,128,128]{2,1,0:T(8,128)S(1)}, u32[]{:S(2)}, u32[]{:S(2)}) collective-permute-start(f32[4,128,128]{2,1,0:T(8,128)S(1)} %get-tuple-element.111), channel_id=1, source_target_pairs={{0,2},{2,0},{4,6},{6,4},{8,10},{10,8},{12,14},{14,12},{1,3},{3,1},... | collective-permute-start | bytes 786440 | tf_op jit(solution)/shard_map/ppermute | solution.py:229
  117.3 11.3 %collective-permute-start.25 = (f32[2,128,384]{2,1,0:T(8,128)S(1)}, f32[2,128,384]{2,1,0:T(8,128)S(1)}, u32[]{:S(2)}, u32[]{:S(2)}) collective-permute-start(f32[2,128,384]{2,1,0:T(8,128)S(1)} %add.127), channel_id=1, source_target_pairs={{0,4},{2,6},{12,8},{14,10},{1,5},{3,7},{13,9},{15,11},{16,20},{18,... | collective-permute-start | bytes 1179656 | tf_op jit(solution)/shard_map/ppermute | solution.py:363
  118.8 11.9 %collective-permute-start.24 = (f32[128,640]{1,0:T(8,128)S(1)}, f32[128,640]{1,0:T(8,128)S(1)}, u32[]{:S(2)}, u32[]{:S(2)}) collective-permute-start(f32[128,640]{1,0:T(8,128)S(1)} %select_bitcast_fusion), channel_id=1, source_target_pairs={{4,8},{6,10},{8,4},{10,6},{5,9},{7,11},{9,5},{11,7},{20,24},{22,26... | collective-permute-start | bytes 983048 | tf_op jit(solution)/shard_map/ppermute | solution.py:367
  128.7 7.6 %collective-permute-start.26 = (f32[128,384]{1,0:T(8,128)S(1)}, f32[128,384]{1,0:T(8,128)S(1)}, u32[]{:S(2)}, u32[]{:S(2)}) collective-permute-start(f32[128,384]{1,0:T(8,128)S(1)} %select_bitcast_fusion.3), channel_id=1, source_target_pairs={{4,8},{6,10},{8,4},{10,6},{5,9},{7,11},{9,5},{11,7},{20,24},{22,26... | collective-permute-start | bytes 589832 | tf_op jit(solution)/shard_map/ppermute | solution.py:367

commit v6 on v5

--- a/solution.py
+++ b/solution.py
@@ -194,7 +194,7 @@
         out_ref[:, at(c, size)] = total.astype(BF16)
 
 
-def exclusive(states, count, even, reverse, pins):
+def exclusive(states, count, even, reverse, pins, marks):
     swap = [(s, s ^ 1) for s in range(count)]
     sign = -2 if reverse else 2
     pairs = count // 2
@@ -216,6 +216,7 @@
             total = after(total, *pinned)
             pinned = (total,)
             trail = (total,) if i else ()
+            marks.append(total)
             got = lax.ppermute(total, "seq", links(step))
             sums[i] = got if step == 1 else sums[i] + got
             totals[i] = total + got
@@ -264,7 +265,7 @@
     (att,) = call(local_body, (rows32,), (q, k, v), 3 * unit * length, "local")
     (d_normed,) = call(d_normed_body, (rows32,), (g, out_weight), unit * width, "d_normed")
     far_prior, near_prior = exclusive(
-        [(states[0], trade(states[1])), (states[2], trade(states[3]))], count, even, False, [(away,), (att,), (d_normed,)]
+        [(states[0], trade(states[1])), (states[2], trade(states[3]))], count, even, False, [(away,), (att,), (d_normed,)], []
     )
 
     pieces = (shape((length, part), BF16), shape((length, part), F32), shape((length, part), BF16))
@@ -310,30 +311,35 @@
         others = [(kept, trade(after(sent, landed))) for kept, sent in chunks[1:]]
         lines = [toward(landed, lower, odd)]
         nbo = lax.ppermute(after(near32, landed), "dp", swap)
-    (output,) = call(
-        output_body,
-        (shape((length, width), BF16),),
-        (after(far, key_local), near, out_weight),
-        unit * width,
-        "output",
-    )
     scale = 1.0 / math.sqrt(length * count * cores)
     if fast:
-        chunks = product(after(near, output), nbo, WIDTHS[1])
+        chunks = product(near, nbo, WIDTHS[1])
         ready = chunks[0][1]
-        near_bases = [kept + trade(sent) for kept, sent in chunks]
         kept, got = others[0]
         base = after(kept + after(got, ready), lines[0][0])
         lines.append(toward(base, lower, odd))
-        weight_grad = scatter(lines, near_bases, base, lower, outer) * scale
-        pins = [(lines[0][0],), (ready,)]
+        near_gots = [trade(sent) for _, sent in chunks]
+        hops = [(lines[0][0],), (ready, base), near_gots[1:]]
     else:
         nb = jnp.concatenate([far[:, :PAIR], near, far[:, PAIR:]], axis=1)
         weight = lax.dot_general(nb, g, TN, preferred_element_type=F32)
         weight = lax.psum_scatter(weight, "dp", scatter_dimension=1, tiled=True)
         weight_grad = lax.psum_scatter(weight, "seq", scatter_dimension=0, tiled=True) * scale
-        pins = []
-    ((own_later, other_later),) = exclusive([(keep, received)], count, even, True, pins)
+        hops, ready = [], far
+    (output,) = call(
+        output_body,
+        (shape((length, width), BF16),),
+        (after(far, ready), near, out_weight),
+        unit * width,
+        "output",
+    )
+    hops[:1] = [(*hops[0], output)] if fast else []
+    marks = []
+    ((own_later, other_later),) = exclusive([(keep, received)], count, even, True, hops, marks)
+    if fast:
+        (first_keep, _), (last_keep, _) = chunks
+        near_bases = [first_keep + after(near_gots[0], *marks[1:]), last_keep + near_gots[1]]
+        weight_grad = scatter(lines, near_bases, base, lower, outer) * scale
     key_grad, value_grad = call(
         final_body,
         (rows16, rows16),
@@ -355,7 +361,9 @@
 
 
 def scatter(lines, near_bases, landed, lower, outer):
-    far = [rest + lax.ppermute(half, "seq", along([(1, 3), (2, 0)])) for half, rest in lines]
+    far = []
+    for (half, rest), pin in zip(lines, ((), near_bases[1:])):
+        far.append(rest + lax.ppermute(after(half, *pin), "seq", along([(1, 3), (2, 0)])))
     near = []
     pins = [(landed,), (lines[1][0],)]
     for i, base in enumerate(near_bases):

time: 138 us -> 138 us (level)
    ppermute x7, waiting for transfers between devices: 17.4 us -> 11.9 us  [trade(): return lax.ppermute(send, 'seq', [(s, s ^ 1) for s in range(count)])]
    ppermute x6, waiting for transfers between devices: 18.9 us -> 23.4 us  [exclusive(): got = lax.ppermute(total, 'seq', links(step))]
    ppermute x2, starting transfers between devices: 7.47 us -> 3.8 us  [toward(): got = lax.ppermute(out, 'seq', along([(0, 1), (1, 0), (2, 3), (3, 2)]))]
    ppermute x2, waiting for transfers between devices: 0.31 us -> 3.01 us  [toward(): got = lax.ppermute(out, 'seq', along([(0, 1), (1, 0), (2, 3), (3, 2)]))]
    ppermute x6, starting transfers between devices: 15.2 us -> 17.2 us  [exclusive(): got = lax.ppermute(total, 'seq', links(step))]
  transfers between devices with their start and end apart: 27 -> 27, of which waited for: 14 -> 15; matrix products, arithmetic and copies ran while one was open for 1% -> 1% of each run, Pallas kernels for 21% -> 21%
where the time goes in v6:
time: 138 us; the launch traced here: 137 us
  waiting for transfers between devices  54.2 us (39%)
  starting transfers between devices  46.9 us (34%)
  Pallas kernels  30.6 us (22%)
  local copies, waits for them, and re-layouts  2.38 us (2%)
  other arithmetic  2.19 us (2%)
    pallas_call x11, Pallas kernels, call(): pl.pallas_call(body, out_shape=tuple(out_shapes), in_specs=specs, out_spe...  30.6 us
    ppermute x6, waiting for transfers between devices, exclusive(): got = lax.ppermute(total, 'seq', links(step))  23.4 us
    ppermute x6, starting transfers between devices, exclusive(): got = lax.ppermute(total, 'seq', links(step))  17.2 us
    ppermute x7, waiting for transfers between devices, trade(): return lax.ppermute(send, 'seq', [(s, s ^ 1) for s in range(count)])  11.9 us
    ppermute x2, starting transfers between devices, scatter(): lax.ppermute(after(half, *pin), 'seq', along([(1, 3), (2, 0)]))  8.62 us
    ppermute x3, waiting for transfers between devices, exclusive(): results.append((mine, lax.ppermute(theirs, 'seq', swap)))  7.56 us
    ppermute x7, starting transfers between devices, trade(): return lax.ppermute(send, 'seq', [(s, s ^ 1) for s in range(count)])  6.87 us
    ppermute x2, waiting for transfers between devices, scatter(): final = lax.ppermute(across, 'seq', along([(1, 2), (2, 1)]))  5.54 us
  transfers between devices with their start and end apart: 27, of which 15 were waited for; matrix products, arithmetic and copies ran while one was open for 1% of the time, Pallas kernels for 21%

profile of v6, /device:TPU:12, one launch (start us, length us, event | category | flops | bytes accessed | tf_op | source)
XLA Modules:
  0.0 137.3 jit_solution(7289524459857030187)
XLA Ops:
  0.7 0.1 pad_add_fusion.place
  0.7 1.2 copy-done.3
  2.0 1.1 copy-done.4
  3.1 1.1 state.1
  4.2 1.6 %collective-permute-start = (f32[2,128,128]{2,1,0:T(8,128)S(1)}, f32[2,128,128]{2,1,0:T(8,128)S(1)}, u32[]{:S(2)}, u32[]{:S(2)}) collective-permute-start(f32[2,128,128]{2,1,0:T(8,128)S(1)} %get-tuple-element.63), channel_id=1, source_target_pairs={{0,2},{2,0},{4,6},{6,4},{8,10},{10,8},{12,14},{14,12},{1,3},{3,1},... | collective-permute-start | bytes 393224 | tf_op jit(solution)/shard_map/ppermute | solution.py:258
  5.8 0.6 away.1
  6.4 0.1 collective-permute-start.8
  6.5 0.6 collective-permute-start.2
  7.1 2.4 %collective-permute-done = f32[2,128,128]{2,1,0:T(8,128)S(1)} collective-permute-done((f32[2,128,128]{2,1,0:T(8,128)S(1)}, f32[2,128,128]{2,1,0:T(8,128)S(1)}, u32[]{:S(2)}, u32[]{:S(2)}) %collective-permute-start) | collective-permute-done | bytes 131104 | tf_op jit(solution)/shard_map/ppermute | solution.py:258
  9.5 3.5 %collective-permute-start.1 = (f32[2,128,128]{2,1,0:T(8,128)S(1)}, f32[2,128,128]{2,1,0:T(8,128)S(1)}, u32[]{:S(2)}, u32[]{:S(2)}) collective-permute-start(f32[2,128,128]{2,1,0:T(8,128)S(1)} %add.101), channel_id=1, source_target_pairs={{0,4},{2,6},{4,8},{6,10},{8,12},{10,14},{1,5},{3,7},{5,9},{7,11},{... | collective-permute-start | bytes 393224 | tf_op jit(solution)/shard_map/ppermute | solution.py:220
  13.1 2.4 %local.1.att_ref = f32[384,1024]{1,0:T(8,128)S(1)} custom-call(bf16[384,1024]{1,0:T(8,128)(2,1)S(1)} %bitcast.38, bf16[384,1024]{1,0:T(8,128)(2,1)S(1)} %bitcast.43, bf16[384,1024]{1,0:T(8,128)(2,1)S(1)} %bitcast.47), custom_call_target="tpu_custom_call" | custom-call | flops 56623104 | tf_op jit(solution)/shard_map/local/pallas_call | solution.py:70
  15.5 3.5 %collective-permute-start.4 = (f32[2,128,128]{2,1,0:T(8,128)S(1)}, f32[2,128,128]{2,1,0:T(8,128)S(1)}, u32[]{:S(2)}, u32[]{:S(2)}) collective-permute-start(f32[2,128,128]{2,1,0:T(8,128)S(1)} %add.103), channel_id=1, source_target_pairs={{0,4},{2,6},{4,8},{6,10},{8,12},{10,14},{1,5},{3,7},{5,9},{7,11},{... | collective-permute-start | bytes 393224 | tf_op jit(solution)/shard_map/ppermute | solution.py:220
  19.1 1.9 %collective-permute-start.3 = (f32[2,128,128]{2,1,0:T(8,128)S(1)}, f32[2,128,128]{2,1,0:T(8,128)S(1)}, u32[]{:S(2)}, u32[]{:S(2)}) collective-permute-start(f32[2,128,128]{2,1,0:T(8,128)S(1)} %add.102), channel_id=1, source_target_pairs={{0,8},{2,10},{4,12},{6,14},{1,9},{3,11},{5,13},{7,15},{16,24},{18,... | collective-permute-start | bytes 393224 | tf_op jit(solution)/shard_map/ppermute | solution.py:220
  20.9 2.4 %d_normed.1.dn_ref = f32[384,1024]{1,0:T(8,128)S(1)} custom-call(bf16[384,2048]{1,0:T(8,128)(2,1)S(1)} %bitcast.35, bf16[1024,2048]{1,0:T(8,128)(2,1)S(1)} %copy-done.1), custom_call_target="tpu_custom_call" | custom-call | flops 100663296 | tf_op jit(solution)/shard_map/d_normed/pallas_call | solution.py:70
  23.4 3.3 %collective-permute-done.4 = f32[2,128,128]{2,1,0:T(8,128)S(1)} collective-permute-done((f32[2,128,128]{2,1,0:T(8,128)S(1)}, f32[2,128,128]{2,1,0:T(8,128)S(1)}, u32[]{:S(2)}, u32[]{:S(2)}) %collective-permute-start.4) | collective-permute-done | bytes 131104 | tf_op jit(solution)/shard_map/ppermute | solution.py:220
  26.7 1.5 %collective-permute-start.5 = (f32[2,128,128]{2,1,0:T(8,128)S(1)}, f32[2,128,128]{2,1,0:T(8,128)S(1)}, u32[]{:S(2)}, u32[]{:S(2)}) collective-permute-start(f32[2,128,128]{2,1,0:T(8,128)S(1)} %add.106), channel_id=1, source_target_pairs={{0,8},{2,10},{4,12},{6,14},{1,9},{3,11},{5,13},{7,15},{16,24},{18,... | collective-permute-start | bytes 393224 | tf_op jit(solution)/shard_map/ppermute | solution.py:220
  28.2 0.9 collective-permute-done.3
  29.1 1.6 %collective-permute-start.6 = (f32[2,128,128]{2,1,0:T(8,128)S(1)}, f32[2,128,128]{2,1,0:T(8,128)S(1)}, u32[]{:S(2)}, u32[]{:S(2)}) collective-permute-start(f32[2,128,128]{2,1,0:T(8,128)S(1)} %get-tuple-element.72), channel_id=1, source_target_pairs={{0,2},{2,0},{4,6},{6,4},{8,10},{10,8},{12,14},{14,12},{1,3},{3,1},... | collective-permute-start | bytes 393224 | tf_op jit(solution)/shard_map/ppermute | solution.py:230
  30.8 3.4 %collective-permute-done.6.other_ref.refs_2_ = f32[2,128,128]{2,1,0:T(8,128)S(1)} collective-permute-done((f32[2,128,128]{2,1,0:T(8,128)S(1)}, f32[2,128,128]{2,1,0:T(8,128)S(1)}, u32[]{:S(2)}, u32[]{:S(2)}) %collective-permute-start.6) | collective-permute-done | bytes 131104 | tf_op jit(solution)/shard_map/ppermute | solution.py:230
  34.1 2.5 %norm_far.1 = (bf16[384,512]{1,0:T(8,128)(2,1)S(1)}, f32[384,512]{1,0:T(8,128)S(1)}, bf16[384,512]{1,0:T(8,128)(2,1)S(1)}, f32[2,128,128]{2,1,0:T(8,128)S(1)}, f32[2,128,128]{2,1,0:T(8,128)S(1)}) custom-call(s32[2]{0:T(128)S(1)} %pad_add_fusion.place, bf16[384,1024]{1,0:T(8,128)(2,1)S(1)} %bitcast.39, f32[384,1024]{1,0:T(8,128)S(1)} %local.1.att_ref, ...), custom_call_target="tpu_custom_call" | custom-call | flops 6291456 | tf_op jit(solution)/shard_map/norm_far/pallas_call | solution.py:70
  36.7 0.1 collective-permute-start.7
  36.8 1.6 %collective-permute-start.9 = (f32[2,128,128]{2,1,0:T(8,128)S(1)}, f32[2,128,128]{2,1,0:T(8,128)S(1)}, u32[]{:S(2)}, u32[]{:S(2)}) collective-permute-start(f32[2,128,128]{2,1,0:T(8,128)S(1)} %get-tuple-element.117), channel_id=1, source_target_pairs={{0,2},{2,0},{4,6},{6,4},{8,10},{10,8},{12,14},{14,12},{1,3},{3,1},... | collective-permute-start | bytes 393224 | tf_op jit(solution)/shard_map/ppermute | solution.py:230
  38.4 0.6 collective-permute-done.7.nbo_ref
  39.0 1.8 %weight.2 = (f32[2,128,512]{2,1,0:T(8,128)S(1)}, f32[2,128,512]{2,1,0:T(8,128)S(1)}, f32[2,128,512]{2,1,0:T(8,128)S(1)}, f32[2,128,512]{2,1,0:T(8,128)S(1)}) custom-call(s32[2]{0:T(128)S(1)} %pad_add_fusion.place, bf16[384,512]{1,0:T(8,128)(2,1)S(1)} %get-tuple-element.89.nb_ref.far_ref, bf16[384,2048]{1,0:T(8,128)(2,1)S(1)} %bitcast.36, ...), custom_call_target="tpu_custom_call" | custom-call | flops 50331648 | tf_op jit(solution)/shard_map/weight/pallas_call | solution.py:70
  40.9 1.8 %collective-permute-done.9.other_ref.refs_5_ = f32[2,128,128]{2,1,0:T(8,128)S(1)} collective-permute-done((f32[2,128,128]{2,1,0:T(8,128)S(1)}, f32[2,128,128]{2,1,0:T(8,128)S(1)}, u32[]{:S(2)}, u32[]{:S(2)}) %collective-permute-start.9) | collective-permute-done | bytes 131104 | tf_op jit(solution)/shard_map/ppermute | solution.py:230
  42.7 1.6 %collective-permute-start.10 = (f32[2,128,512]{2,1,0:T(8,128)S(1)}, f32[2,128,512]{2,1,0:T(8,128)S(1)}, u32[]{:S(2)}, u32[]{:S(2)}) collective-permute-start(f32[2,128,512]{2,1,0:T(8,128)S(1)} %get-tuple-element.82), channel_id=1, source_target_pairs={{0,2},{2,0},{4,6},{6,4},{8,10},{10,8},{12,14},{14,12},{1,3},{3,1},... | collective-permute-start | bytes 1572872 | tf_op jit(solution)/shard_map/ppermute | solution.py:258
  44.2 2.6 %norm_near.1 = (bf16[384,512]{1,0:T(8,128)(2,1)S(1)}, f32[384,512]{1,0:T(8,128)S(1)}, bf16[384,512]{1,0:T(8,128)(2,1)S(1)}, f32[4,128,128]{2,1,0:T(8,128)S(1)}, f32[4,128,128]{2,1,0:T(8,128)S(1)}) custom-call(s32[2]{0:T(128)S(1)} %pad_add_fusion.place, bf16[384,1024]{1,0:T(8,128)(2,1)S(1)} %bitcast.40, f32[384,1024]{1,0:T(8,128)S(1)} %local.1.att_ref, ...), custom_call_target="tpu_custom_call" | custom-call | flops 402653184 | tf_op jit(solution)/shard_map/norm_near/pallas_call | solution.py:70
  46.8 8.6 %grads.1 = (bf16[384,1024]{1,0:T(8,128)(2,1)}, f32[384,1024]{1,0:T(8,128)S(1)}, f32[384,1024]{1,0:T(8,128)S(1)}) custom-call(s32[2]{0:T(128)S(1)} %pad_add_fusion.place, bf16[384,1024]{1,0:T(8,128)(2,1)S(1)} %bitcast.41, bf16[384,1024]{1,0:T(8,128)(2,1)S(1)} %bitcast.44, bf16[384,1024]{1,0:T(8,128)(2,1)S(1)} %bitcast.48, ...), custom_call_target="tpu_custom_call" | custom-call | flops 169869312 | tf_op jit(solution)/shard_map/grads/pallas_call | solution.py:70
  55.4 0.8 collective-permute-done.10
  56.2 0.1 add.111
  56.2 0.1 collective-permute-start.11
  56.3 1.6 %collective-permute-start.12 = (f32[4,128,128]{2,1,0:T(8,128)S(1)}, f32[4,128,128]{2,1,0:T(8,128)S(1)}, u32[]{:S(2)}, u32[]{:S(2)}) collective-permute-start(f32[4,128,128]{2,1,0:T(8,128)S(1)} %get-tuple-element.93), channel_id=1, source_target_pairs={{0,2},{2,0},{4,6},{6,4},{8,10},{10,8},{12,14},{14,12},{1,3},{3,1},... | collective-permute-start | bytes 786440 | tf_op jit(solution)/shard_map/ppermute | solution.py:258
  58.0 0.5 collective-permute-start.15
  58.5 3.7 %collective-permute-start.13 = (f32[128,512]{1,0:T(8,128)S(1)}, f32[128,512]{1,0:T(8,128)S(1)}, u32[]{:S(2)}, u32[]{:S(2)}) collective-permute-start(f32[128,512]{1,0:T(8,128)S(1)} %select_bitcast_fusion.2), channel_id=1, source_target_pairs={{0,4},{2,6},{4,0},{6,2},{8,12},{10,14},{12,8},{14,10},{1,5},{3,7},... | collective-permute-start | bytes 786440 | tf_op jit(solution)/shard_map/ppermute | solution.py:359
  62.2 2.2 %weight.3 = (f32[2,128,640]{2,1,0:T(8,128)S(1)}, f32[2,128,640]{2,1,0:T(8,128)S(1)}, f32[2,128,384]{2,1,0:T(8,128)S(1)}, f32[2,128,384]{2,1,0:T(8,128)S(1)}) custom-call(s32[2]{0:T(128)S(1)} %pad_add_fusion.place, bf16[384,512]{1,0:T(8,128)(2,1)S(1)} %get-tuple-element.79.nb_ref.near_ref, bf16[384,2048]{1,0:T(8,128)(2,1)S(1)} %bitcast.37, ...), custom_call_target="tpu_custom_call" | custom-call | flops 50331648 | tf_op jit(solution)/shard_map/weight/pallas_call | solution.py:70
  64.4 0.5 collective-permute-start.22
  64.9 0.5 collective-permute-done.12
  65.5 3.0 %collective-permute-done.13 = f32[128,512]{1,0:T(8,128)S(1)} collective-permute-done((f32[128,512]{1,0:T(8,128)S(1)}, f32[128,512]{1,0:T(8,128)S(1)}, u32[]{:S(2)}, u32[]{:S(2)}) %collective-permute-start.13) | collective-permute-done | bytes 262176 | tf_op jit(solution)/shard_map/ppermute | solution.py:359
  68.6 8.1 %collective-permute-done.15 = f32[2,128,512]{2,1,0:T(8,128)S(1)} collective-permute-done((f32[2,128,512]{2,1,0:T(8,128)S(1)}, f32[2,128,512]{2,1,0:T(8,128)S(1)}, u32[]{:S(2)}, u32[]{:S(2)}) %collective-permute-start.15) | collective-permute-done | bytes 524320 | tf_op jit(solution)/shard_map/ppermute | solution.py:258
  76.7 0.1 add.115
  76.8 3.5 %output.1 = bf16[384,2048]{1,0:T(8,128)(2,1)} custom-call(bf16[384,512]{1,0:T(8,128)(2,1)S(1)} %get-tuple-element.89.nb_ref.far_ref, bf16[384,512]{1,0:T(8,128)(2,1)S(1)} %get-tuple-element.79.nb_ref.near_ref, bf16[1024,2048]{1,0:T(8,128)(2,1)S(1)} %copy-done.1), custom_call_target="tpu_custom_call" | custom-call | flops 100663296 | tf_op jit(solution)/shard_map/output/pallas_call | solution.py:70
  80.3 5.6 %collective-permute-start.14 = (f32[4,128,128]{2,1,0:T(8,128)S(1)}, f32[4,128,128]{2,1,0:T(8,128)S(1)}, u32[]{:S(2)}, u32[]{:S(2)}) collective-permute-start(f32[4,128,128]{2,1,0:T(8,128)S(1)} %add.112), channel_id=1, source_target_pairs={{4,0},{6,2},{8,4},{10,6},{12,8},{14,10},{5,1},{7,3},{9,5},{11,7},{... | collective-permute-start | bytes 786440 | tf_op jit(solution)/shard_map/ppermute | solution.py:220
  85.9 0.1 collective-permute-start.20
  86.0 0.5 collective-permute-start.17
  86.5 6.1 %collective-permute-done.14 = f32[4,128,128]{2,1,0:T(8,128)S(1)} collective-permute-done((f32[4,128,128]{2,1,0:T(8,128)S(1)}, f32[4,128,128]{2,1,0:T(8,128)S(1)}, u32[]{:S(2)}, u32[]{:S(2)}) %collective-permute-start.14) | collective-permute-done | bytes 262176 | tf_op jit(solution)/shard_map/ppermute | solution.py:220
  92.7 0.1 add.125
  92.7 1.3 collective-permute-start.23
  94.0 1.3 collective-permute-start.16
  95.3 5.7 %collective-permute-start.19 = (f32[128,512]{1,0:T(8,128)S(1)}, f32[128,512]{1,0:T(8,128)S(1)}, u32[]{:S(2)}, u32[]{:S(2)}) collective-permute-start(f32[128,512]{1,0:T(8,128)S(1)} %bitcast_add_fusion.4), channel_id=1, source_target_pairs={{4,12},{6,14},{8,0},{10,2},{5,13},{7,15},{9,1},{11,3},{20,28},{22,... | collective-permute-start | bytes 786440 | tf_op jit(solution)/shard_map/ppermute | solution.py:366
  101.2 2.9 %collective-permute-start.21 = (f32[128,512]{1,0:T(8,128)S(1)}, f32[128,512]{1,0:T(8,128)S(1)}, u32[]{:S(2)}, u32[]{:S(2)}) collective-permute-start(f32[128,512]{1,0:T(8,128)S(1)} %bitcast_add_fusion.1), channel_id=1, source_target_pairs={{4,12},{6,14},{8,0},{10,2},{5,13},{7,15},{9,1},{11,3},{20,28},{22,... | collective-permute-start | bytes 786440 | tf_op jit(solution)/shard_map/ppermute | solution.py:366
  104.1 13.1 %collective-permute-done.16 = f32[4,128,128]{2,1,0:T(8,128)S(1)} collective-permute-done((f32[4,128,128]{2,1,0:T(8,128)S(1)}, f32[4,128,128]{2,1,0:T(8,128)S(1)}, u32[]{:S(2)}, u32[]{:S(2)}) %collective-permute-start.16) | collective-permute-done | bytes 262176 | tf_op jit(solution)/shard_map/ppermute | solution.py:220
  117.3 0.1 add_select_fusion
  117.3 0.5 collective-permute-start.18
  117.9 1.3 collective-permute-start.25
  119.2 0.1 fusion.2
  119.3 1.9 %collective-permute-start.24 = (f32[128,640]{1,0:T(8,128)S(1)}, f32[128,640]{1,0:T(8,128)S(1)}, u32[]{:S(2)}, u32[]{:S(2)}) collective-permute-start(f32[128,640]{1,0:T(8,128)S(1)} %select_bitcast_fusion), channel_id=1, source_target_pairs={{4,8},{6,10},{8,4},{10,6},{5,9},{7,11},{9,5},{11,7},{20,24},{22,26... | collective-permute-start | bytes 983048 | tf_op jit(solution)/shard_map/ppermute | solution.py:375
  121.3 0.1 fusion.1
  121.4 2.4 %collective-permute-done.18.other_ref = f32[4,128,128]{2,1,0:T(8,128)S(1)} collective-permute-done((f32[4,128,128]{2,1,0:T(8,128)S(1)}, f32[4,128,128]{2,1,0:T(8,128)S(1)}, u32[]{:S(2)}, u32[]{:S(2)}) %collective-permute-start.18) | collective-permute-done | bytes 262176 | tf_op jit(solution)/shard_map/ppermute | solution.py:230
  123.8 2.8 %final.1 = (bf16[384,1024]{1,0:T(8,128)(2,1)}, bf16[384,1024]{1,0:T(8,128)(2,1)}) custom-call(s32[2]{0:T(128)S(1)} %pad_add_fusion.place, bf16[384,1024]{1,0:T(8,128)(2,1)S(1)} %bitcast.45, bf16[384,1024]{1,0:T(8,128)(2,1)S(1)} %bitcast.49, f32[384,1024]{1,0:T(8,128)S(1)} %get-tuple-element.85.kl_ref, f32[384,1024]{1,0:T(8,128)S(1)} %get-tuple-element.91.vl_ref, ...), custom_call_target="tpu_custom_call" | custom-call | flops 25165824 | tf_op jit(solution)/shard_map/final/pallas_call | solution.py:70
  126.6 2.2 %collective-permute-done.25 = f32[2,128,384]{2,1,0:T(8,128)S(1)} collective-permute-done((f32[2,128,384]{2,1,0:T(8,128)S(1)}, f32[2,128,384]{2,1,0:T(8,128)S(1)}, u32[]{:S(2)}, u32[]{:S(2)}) %collective-permute-start.25) | collective-permute-done | bytes 393248 | tf_op jit(solution)/shard_map/ppermute | solution.py:371
  128.8 1.9 %collective-permute-start.26 = (f32[128,384]{1,0:T(8,128)S(1)}, f32[128,384]{1,0:T(8,128)S(1)}, u32[]{:S(2)}, u32[]{:S(2)}) collective-permute-start(f32[128,384]{1,0:T(8,128)S(1)} %select_bitcast_fusion.3), channel_id=1, source_target_pairs={{4,8},{6,10},{8,4},{10,6},{5,9},{7,11},{9,5},{11,7},{20,24},{22,26... | collective-permute-start | bytes 589832 | tf_op jit(solution)/shard_map/ppermute | solution.py:375
  130.7 0.1 bitcast_add_fusion
  130.8 5.5 %collective-permute-done.26 = f32[128,384]{1,0:T(8,128)S(1)} collective-permute-done((f32[128,384]{1,0:T(8,128)S(1)}, f32[128,384]{1,0:T(8,128)S(1)}, u32[]{:S(2)}, u32[]{:S(2)}) %collective-permute-start.26) | collective-permute-done | bytes 196640 | tf_op jit(solution)/shard_map/ppermute | solution.py:375
  136.4 0.9 fusion
  (36 shorter events, 0.7 us)
Async XLA Ops:
  0.6 5.1 %copy-start = (bf16[1,384,2048]{2,1,0:T(8,128)(2,1)S(1)}, bf16[1,384,2048]{2,1,0:T(8,128)(2,1)}, u32[]{:S(2)}) copy-start(bf16[1,384,2048]{2,1,0:T(8,128)(2,1)} %param.9) | copy-start | bytes 4718596
  0.7 1.2 copy-start.3
  2.0 1.1 copy-start.4
  4.2 5.3 %collective-permute-start = (f32[2,128,128]{2,1,0:T(8,128)S(1)}, f32[2,128,128]{2,1,0:T(8,128)S(1)}, u32[]{:S(2)}, u32[]{:S(2)}) collective-permute-start(f32[2,128,128]{2,1,0:T(8,128)S(1)} %get-tuple-element.63), channel_id=1, source_target_pairs={{0,2},{2,0},{4,6},{6,4},{8,10},{10,8},{12,14},{14,12},{1,3},{3,1},... | collective-permute-start | bytes 393224 | tf_op jit(solution)/shard_map/ppermute | solution.py:258
  5.8 7.3 %copy-start.2 = (bf16[1,384,1024]{2,1,0:T(8,128)(2,1)S(1)}, bf16[1,384,1024]{2,1,0:T(8,128)(2,1)}, u32[]{:S(2)}) copy-start(bf16[1,384,1024]{2,1,0:T(8,128)(2,1)} %param.5) | copy-start | bytes 2359300
  6.4 32.6 %collective-permute-start.8 = (f32[384,1024]{1,0:T(8,128)S(1)}, f32[384,1024]{1,0:T(8,128)S(1)}, u32[]{:S(2)}, u32[]{:S(2)}) collective-permute-start(f32[384,1024]{1,0:T(8,128)S(1)} %away.1), channel_id=1, source_target_pairs={{0,1},{1,0},{2,3},{3,2},{4,5},{5,4},{6,7},{7,6},{8,9},{9,8},{10,11... | collective-permute-start | bytes 4718600 | tf_op jit(solution)/shard_map/ppermute | solution.py:264
  6.5 9.0 %collective-permute-start.2 = (f32[2,128,128]{2,1,0:T(8,128)S(1)}, f32[2,128,128]{2,1,0:T(8,128)S(1)}, u32[]{:S(2)}, u32[]{:S(2)}) collective-permute-start(f32[2,128,128]{2,1,0:T(8,128)S(1)} %get-tuple-element.67), channel_id=1, source_target_pairs={{0,2},{2,0},{4,6},{6,4},{8,10},{10,8},{12,14},{14,12},{1,3},{3,1},... | collective-permute-start | bytes 393224 | tf_op jit(solution)/shard_map/ppermute | solution.py:258
  9.5 9.5 %collective-permute-start.1 = (f32[2,128,128]{2,1,0:T(8,128)S(1)}, f32[2,128,128]{2,1,0:T(8,128)S(1)}, u32[]{:S(2)}, u32[]{:S(2)}) collective-permute-start(f32[2,128,128]{2,1,0:T(8,128)S(1)} %add.101), channel_id=1, source_target_pairs={{0,4},{2,6},{4,8},{6,10},{8,12},{10,14},{1,5},{3,7},{5,9},{7,11},{... | collective-permute-start | bytes 393224 | tf_op jit(solution)/shard_map/ppermute | solution.py:220
  13.0 7.9 %copy-start.1 = (bf16[1024,2048]{1,0:T(8,128)(2,1)S(1)}, bf16[1024,2048]{1,0:T(8,128)(2,1)}, u32[]{:S(2)}) copy-start(bf16[1024,2048]{1,0:T(8,128)(2,1)} %w_ref.3) | copy-start | bytes 12582916
  15.5 11.1 %collective-permute-start.4 = (f32[2,128,128]{2,1,0:T(8,128)S(1)}, f32[2,128,128]{2,1,0:T(8,128)S(1)}, u32[]{:S(2)}, u32[]{:S(2)}) collective-permute-start(f32[2,128,128]{2,1,0:T(8,128)S(1)} %add.103), channel_id=1, source_target_pairs={{0,4},{2,6},{4,8},{6,10},{8,12},{10,14},{1,5},{3,7},{5,9},{7,11},{... | collective-permute-start | bytes 393224 | tf_op jit(solution)/shard_map/ppermute | solution.py:220
  19.1 10.0 %collective-permute-start.3 = (f32[2,128,128]{2,1,0:T(8,128)S(1)}, f32[2,128,128]{2,1,0:T(8,128)S(1)}, u32[]{:S(2)}, u32[]{:S(2)}) collective-permute-start(f32[2,128,128]{2,1,0:T(8,128)S(1)} %add.102), channel_id=1, source_target_pairs={{0,8},{2,10},{4,12},{6,14},{1,9},{3,11},{5,13},{7,15},{16,24},{18,... | collective-permute-start | bytes 393224 | tf_op jit(solution)/shard_map/ppermute | solution.py:220
  26.7 4.1 %collective-permute-start.5 = (f32[2,128,128]{2,1,0:T(8,128)S(1)}, f32[2,128,128]{2,1,0:T(8,128)S(1)}, u32[]{:S(2)}, u32[]{:S(2)}) collective-permute-start(f32[2,128,128]{2,1,0:T(8,128)S(1)} %add.106), channel_id=1, source_target_pairs={{0,8},{2,10},{4,12},{6,14},{1,9},{3,11},{5,13},{7,15},{16,24},{18,... | collective-permute-start | bytes 393224 | tf_op jit(solution)/shard_map/ppermute | solution.py:220
  29.1 5.0 %collective-permute-start.6 = (f32[2,128,128]{2,1,0:T(8,128)S(1)}, f32[2,128,128]{2,1,0:T(8,128)S(1)}, u32[]{:S(2)}, u32[]{:S(2)}) collective-permute-start(f32[2,128,128]{2,1,0:T(8,128)S(1)} %get-tuple-element.72), channel_id=1, source_target_pairs={{0,2},{2,0},{4,6},{6,4},{8,10},{10,8},{12,14},{14,12},{1,3},{3,1},... | collective-permute-start | bytes 393224 | tf_op jit(solution)/shard_map/ppermute | solution.py:230
  36.7 2.4 %collective-permute-start.7 = (f32[384,512]{1,0:T(8,128)S(1)}, f32[384,512]{1,0:T(8,128)S(1)}, u32[]{:S(2)}, u32[]{:S(2)}) collective-permute-start(f32[384,512]{1,0:T(8,128)S(1)} %get-tuple-element.74), channel_id=1, source_target_pairs={{0,1},{1,0},{2,3},{3,2},{4,5},{5,4},{6,7},{7,6},{8,9},{9,8},{10,11... | collective-permute-start | bytes 2359304 | tf_op jit(solution)/shard_map/ppermute | solution.py:290
  36.8 5.9 %collective-permute-start.9 = (f32[2,128,128]{2,1,0:T(8,128)S(1)}, f32[2,128,128]{2,1,0:T(8,128)S(1)}, u32[]{:S(2)}, u32[]{:S(2)}) collective-permute-start(f32[2,128,128]{2,1,0:T(8,128)S(1)} %get-tuple-element.117), channel_id=1, source_target_pairs={{0,2},{2,0},{4,6},{6,4},{8,10},{10,8},{12,14},{14,12},{1,3},{3,1},... | collective-permute-start | bytes 393224 | tf_op jit(solution)/shard_map/ppermute | solution.py:230
  42.7 13.5 %collective-permute-start.10 = (f32[2,128,512]{2,1,0:T(8,128)S(1)}, f32[2,128,512]{2,1,0:T(8,128)S(1)}, u32[]{:S(2)}, u32[]{:S(2)}) collective-permute-start(f32[2,128,512]{2,1,0:T(8,128)S(1)} %get-tuple-element.82), channel_id=1, source_target_pairs={{0,2},{2,0},{4,6},{6,4},{8,10},{10,8},{12,14},{14,12},{1,3},{3,1},... | collective-permute-start | bytes 1572872 | tf_op jit(solution)/shard_map/ppermute | solution.py:258
  56.2 5.9 %collective-permute-start.11 = (f32[384,512]{1,0:T(8,128)S(1)}, f32[384,512]{1,0:T(8,128)S(1)}, u32[]{:S(2)}, u32[]{:S(2)}) collective-permute-start(f32[384,512]{1,0:T(8,128)S(1)} %get-tuple-element.87), channel_id=1, source_target_pairs={{0,1},{1,0},{2,3},{3,2},{4,5},{5,4},{6,7},{7,6},{8,9},{9,8},{10,11... | collective-permute-start | bytes 2359304 | tf_op jit(solution)/shard_map/ppermute | solution.py:313
  56.3 9.2 %collective-permute-start.12 = (f32[4,128,128]{2,1,0:T(8,128)S(1)}, f32[4,128,128]{2,1,0:T(8,128)S(1)}, u32[]{:S(2)}, u32[]{:S(2)}) collective-permute-start(f32[4,128,128]{2,1,0:T(8,128)S(1)} %get-tuple-element.93), channel_id=1, source_target_pairs={{0,2},{2,0},{4,6},{6,4},{8,10},{10,8},{12,14},{14,12},{1,3},{3,1},... | collective-permute-start | bytes 786440 | tf_op jit(solution)/shard_map/ppermute | solution.py:258
  58.0 18.8 %collective-permute-start.15 = (f32[2,128,512]{2,1,0:T(8,128)S(1)}, f32[2,128,512]{2,1,0:T(8,128)S(1)}, u32[]{:S(2)}, u32[]{:S(2)}) collective-permute-start(f32[2,128,512]{2,1,0:T(8,128)S(1)} %get-tuple-element.99), channel_id=1, source_target_pairs={{0,2},{2,0},{4,6},{6,4},{8,10},{10,8},{12,14},{14,12},{1,3},{3,1},... | collective-permute-start | bytes 1572872 | tf_op jit(solution)/shard_map/ppermute | solution.py:258
  58.5 10.1 %collective-permute-start.13 = (f32[128,512]{1,0:T(8,128)S(1)}, f32[128,512]{1,0:T(8,128)S(1)}, u32[]{:S(2)}, u32[]{:S(2)}) collective-permute-start(f32[128,512]{1,0:T(8,128)S(1)} %select_bitcast_fusion.2), channel_id=1, source_target_pairs={{0,4},{2,6},{4,0},{6,2},{8,12},{10,14},{12,8},{14,10},{1,5},{3,7},... | collective-permute-start | bytes 786440 | tf_op jit(solution)/shard_map/ppermute | solution.py:359
  64.4 28.2 %collective-permute-start.22 = (f32[2,128,640]{2,1,0:T(8,128)S(1)}, f32[2,128,640]{2,1,0:T(8,128)S(1)}, u32[]{:S(2)}, u32[]{:S(2)}) collective-permute-start(f32[2,128,640]{2,1,0:T(8,128)S(1)} %get-tuple-element.88), channel_id=1, source_target_pairs={{0,2},{2,0},{4,6},{6,4},{8,10},{10,8},{12,14},{14,12},{1,3},{3,1},... | collective-permute-start | bytes 1966088 | tf_op jit(solution)/shard_map/ppermute | solution.py:258
  80.3 12.3 %collective-permute-start.14 = (f32[4,128,128]{2,1,0:T(8,128)S(1)}, f32[4,128,128]{2,1,0:T(8,128)S(1)}, u32[]{:S(2)}, u32[]{:S(2)}) collective-permute-start(f32[4,128,128]{2,1,0:T(8,128)S(1)} %add.112), channel_id=1, source_target_pairs={{4,0},{6,2},{8,4},{10,6},{12,8},{14,10},{5,1},{7,3},{9,5},{11,7},{... | collective-permute-start | bytes 786440 | tf_op jit(solution)/shard_map/ppermute | solution.py:220
  85.9 15.1 %collective-permute-start.20 = (f32[128,512]{1,0:T(8,128)S(1)}, f32[128,512]{1,0:T(8,128)S(1)}, u32[]{:S(2)}, u32[]{:S(2)}) collective-permute-start(f32[128,512]{1,0:T(8,128)S(1)} %select_bitcast_fusion.1), channel_id=1, source_target_pairs={{0,4},{2,6},{4,0},{6,2},{8,12},{10,14},{12,8},{14,10},{1,5},{3,7},... | collective-permute-start | bytes 786440 | tf_op jit(solution)/shard_map/ppermute | solution.py:359
  86.0 15.1 %collective-permute-start.17 = (f32[2,128,384]{2,1,0:T(8,128)S(1)}, f32[2,128,384]{2,1,0:T(8,128)S(1)}, u32[]{:S(2)}, u32[]{:S(2)}) collective-permute-start(f32[2,128,384]{2,1,0:T(8,128)S(1)} %get-tuple-element.103), channel_id=1, source_target_pairs={{0,2},{2,0},{4,6},{6,4},{8,10},{10,8},{12,14},{14,12},{1,3},{3,1},... | collective-permute-start | bytes 1179656 | tf_op jit(solution)/shard_map/ppermute | solution.py:258
  92.7 25.1 %collective-permute-start.23 = (f32[2,128,640]{2,1,0:T(8,128)S(1)}, f32[2,128,640]{2,1,0:T(8,128)S(1)}, u32[]{:S(2)}, u32[]{:S(2)}) collective-permute-start(f32[2,128,640]{2,1,0:T(8,128)S(1)} %add.125), channel_id=1, source_target_pairs={{0,4},{2,6},{12,8},{14,10},{1,5},{3,7},{13,9},{15,11},{16,20},{18,... | collective-permute-start | bytes 1966088 | tf_op jit(solution)/shard_map/ppermute | solution.py:371
  94.0 23.2 %collective-permute-start.16 = (f32[4,128,128]{2,1,0:T(8,128)S(1)}, f32[4,128,128]{2,1,0:T(8,128)S(1)}, u32[]{:S(2)}, u32[]{:S(2)}) collective-permute-start(f32[4,128,128]{2,1,0:T(8,128)S(1)} %add.114), channel_id=1, source_target_pairs={{8,0},{10,2},{12,4},{14,6},{9,1},{11,3},{13,5},{15,7},{24,16},{26,... | collective-permute-start | bytes 786440 | tf_op jit(solution)/shard_map/ppermute | solution.py:220
  95.3 23.9 %collective-permute-start.19 = (f32[128,512]{1,0:T(8,128)S(1)}, f32[128,512]{1,0:T(8,128)S(1)}, u32[]{:S(2)}, u32[]{:S(2)}) collective-permute-start(f32[128,512]{1,0:T(8,128)S(1)} %bitcast_add_fusion.4), channel_id=1, source_target_pairs={{4,12},{6,14},{8,0},{10,2},{5,13},{7,15},{9,1},{11,3},{20,28},{22,... | collective-permute-start | bytes 786440 | tf_op jit(solution)/shard_map/ppermute | solution.py:366
  101.2 20.1 %collective-permute-start.21 = (f32[128,512]{1,0:T(8,128)S(1)}, f32[128,512]{1,0:T(8,128)S(1)}, u32[]{:S(2)}, u32[]{:S(2)}) collective-permute-start(f32[128,512]{1,0:T(8,128)S(1)} %bitcast_add_fusion.1), channel_id=1, source_target_pairs={{4,12},{6,14},{8,0},{10,2},{5,13},{7,15},{9,1},{11,3},{20,28},{22,... | collective-permute-start | bytes 786440 | tf_op jit(solution)/shard_map/ppermute | solution.py:366
  117.3 6.5 %collective-permute-start.18 = (f32[4,128,128]{2,1,0:T(8,128)S(1)}, f32[4,128,128]{2,1,0:T(8,128)S(1)}, u32[]{:S(2)}, u32[]{:S(2)}) collective-permute-start(f32[4,128,128]{2,1,0:T(8,128)S(1)} %get-tuple-element.104), channel_id=1, source_target_pairs={{0,2},{2,0},{4,6},{6,4},{8,10},{10,8},{12,14},{14,12},{1,3},{3,1},... | collective-permute-start | bytes 786440 | tf_op jit(solution)/shard_map/ppermute | solution.py:230
  117.9 10.8 %collective-permute-start.25 = (f32[2,128,384]{2,1,0:T(8,128)S(1)}, f32[2,128,384]{2,1,0:T(8,128)S(1)}, u32[]{:S(2)}, u32[]{:S(2)}) collective-permute-start(f32[2,128,384]{2,1,0:T(8,128)S(1)} %add.123), channel_id=1, source_target_pairs={{0,4},{2,6},{12,8},{14,10},{1,5},{3,7},{13,9},{15,11},{16,20},{18,... | collective-permute-start | bytes 1179656 | tf_op jit(solution)/shard_map/ppermute | solution.py:371
  119.3 11.4 %collective-permute-start.24 = (f32[128,640]{1,0:T(8,128)S(1)}, f32[128,640]{1,0:T(8,128)S(1)}, u32[]{:S(2)}, u32[]{:S(2)}) collective-permute-start(f32[128,640]{1,0:T(8,128)S(1)} %select_bitcast_fusion), channel_id=1, source_target_pairs={{4,8},{6,10},{8,4},{10,6},{5,9},{7,11},{9,5},{11,7},{20,24},{22,26... | collective-permute-start | bytes 983048 | tf_op jit(solution)/shard_map/ppermute | solution.py:375
  128.8 7.6 %collective-permute-start.26 = (f32[128,384]{1,0:T(8,128)S(1)}, f32[128,384]{1,0:T(8,128)S(1)}, u32[]{:S(2)}, u32[]{:S(2)}) collective-permute-start(f32[128,384]{1,0:T(8,128)S(1)} %select_bitcast_fusion.3), channel_id=1, source_target_pairs={{4,8},{6,10},{8,4},{10,6},{5,9},{7,11},{9,5},{11,7},{20,24},{22,26... | collective-permute-start | bytes 589832 | tf_op jit(solution)/shard_map/ppermute | solution.py:375

commit v7 on v5

--- a/solution.py
+++ b/solution.py
@@ -288,7 +288,7 @@
     if fast:
         chunks = product(far, lax.ppermute(far32, "dp", swap), WIDTHS[0])
         near_own = after(near_own, chunks[0][1])
-        first_got = trade(after(chunks[0][1], near_other))
+        far0_got = trade(after(chunks[0][1], near_other))
     near, near32, near_att, keep, send = call(
         functools.partial(norm_body, NEAR),
         pieces + (state, state),
@@ -297,76 +297,110 @@
         "norm_near",
     )
 
+    received = trade(send)
+    ready = ()
+    if fast:
+        nbo = lax.ppermute(near32, "dp", swap)
+        (near0_keep, near0_send), (near1_keep, near1_send) = product(near, nbo, WIDTHS[1])
+        ready = (near0_send,)
     query_grad, key_local, value_local = call(
         grads_body,
         (rows16, rows32, rows32),
-        (place, q, k, v, far_att, *far_prior, near_att, *near_prior),
+        (place, q, k, v, after(far_att, *ready), *far_prior, near_att, *near_prior),
         9 * unit * length,
         "grads",
     )
-    received = trade(send)
-    if fast:
-        landed = chunks[0][0] + after(first_got, key_local)
-        others = [(kept, trade(after(sent, landed))) for kept, sent in chunks[1:]]
-        lines = [toward(landed, lower, odd)]
-        nbo = lax.ppermute(after(near32, landed), "dp", swap)
-    (output,) = call(
-        output_body,
-        (shape((length, width), BF16),),
-        (after(far, key_local), near, out_weight),
-        unit * width,
-        "output",
-    )
+
+    def finish(own, other):
+        return call(
+            final_body,
+            (rows16, rows16),
+            (place, k, v, key_local, value_local, own, other),
+            4 * unit * HD,
+            "final",
+        )
+
+    def project(rows):
+        return call(
+            output_body,
+            (shape((length, width), BF16),),
+            (rows, near, out_weight),
+            unit * width,
+            "output",
+        )[0]
+
     scale = 1.0 / math.sqrt(length * count * cores)
-    if fast:
-        chunks = product(after(near, output), nbo, WIDTHS[1])
-        ready = chunks[0][1]
-        near_bases = [kept + trade(sent) for kept, sent in chunks]
-        kept, got = others[0]
-        base = after(kept + after(got, ready), lines[0][0])
-        lines.append(toward(base, lower, odd))
-        weight_grad = scatter(lines, near_bases, base, lower, outer) * scale
-        pins = [(lines[0][0],), (ready,)]
-    else:
+    if not fast:
         nb = jnp.concatenate([far[:, :PAIR], near, far[:, PAIR:]], axis=1)
         weight = lax.dot_general(nb, g, TN, preferred_element_type=F32)
         weight = lax.psum_scatter(weight, "dp", scatter_dimension=1, tiled=True)
         weight_grad = lax.psum_scatter(weight, "seq", scatter_dimension=0, tiled=True) * scale
-        pins = []
-    ((own_later, other_later),) = exclusive([(keep, received)], count, even, True, pins)
-    key_grad, value_grad = call(
-        final_body,
-        (rows16, rows16),
-        (place, k, v, key_local, value_local, own_later, other_later),
-        4 * unit * HD,
-        "final",
-    )
-    return output[None], query_grad[None], key_grad[None], value_grad[None], weight_grad
-
-
-def along(links):
-    return [(2 * a + i, 2 * b + i) for a, b in links for i in range(2)]
-
-
-def toward(base, lower, odd):
-    out = jnp.where(odd, base[0], base[1])
-    got = lax.ppermute(out, "seq", along([(0, 1), (1, 0), (2, 3), (3, 2)]))
-    return jnp.where(lower, base[1], base[0]) + got, jnp.where(lower, base[0], base[1]) + got
-
-
-def scatter(lines, near_bases, landed, lower, outer):
-    far = [rest + lax.ppermute(half, "seq", along([(1, 3), (2, 0)])) for half, rest in lines]
-    near = []
-    pins = [(landed,), (lines[1][0],)]
-    for i, base in enumerate(near_bases):
-        base = after(base, *pins[i])
-        got = lax.ppermute(base, "seq", along([(0, 1), (3, 2)]))
-        across = jnp.where(lower, base[1] + got[1], base[0] + got[0])
-        pins[-1] = (*pins[-1], across)
-        across = after(across, *near_bases[i + 1 :])
-        final = lax.ppermute(across, "seq", along([(1, 2), (2, 1)]))
-        near.append(jnp.where(lower, base[0] + got[0], base[1] + got[1]) + final)
-    return jnp.where(outer, jnp.concatenate(far, axis=1), jnp.concatenate(near, axis=1))
+        output = project(far)
+        ((own, other),) = exclusive([(keep, received)], count, even, True, [])
+        key_grad, value_grad = finish(own, other)
+        return output[None], query_grad[None], key_grad[None], value_grad[None], weight_grad
+
+    (far0_keep, _), (far1_keep, far1_send) = chunks
+    far0 = far0_keep + after(far0_got, key_local)
+    far0_in = hop(jnp.where(odd, far0[0], far0[1]), NEXT)
+    far1_got = trade(after(far1_send, far0))
+    near0_got, near1_got = trade(near0_send), trade(near1_send)
+
+    total = keep + after(received, far0)
+    back1 = hop(total, BACK)
+    output = project(after(far, total))
+    far0_in = after(far0_in, output)
+    far0_half = jnp.where(lower, far0[1], far0[0]) + far0_in
+    far0_end = hop(far0_half, OUTWARD)
+    back1 = after(back1, far0_half)
+    total = total + back1
+    back2 = hop(total, BACK2)
+    near0 = near0_keep + after(near0_got, total)
+    near0_in = hop(near0, INWARD)
+    far1 = far1_keep + after(far1_got, near0)
+    far1_out = jnp.where(odd, far1[0], far1[1])
+    far1_in = hop(far1_out, NEXT)
+    near0_in = after(near0_in, far1_out)
+    near0_half = jnp.where(lower, near0[1] + near0_in[1], near0[0] + near0_in[0])
+    near0_end = hop(near0_half, ACROSS)
+    outside = back1 + after(back2, near0_half)
+    theirs = jnp.where(even, outside, outside + keep)
+    other = trade(theirs)
+    own = jnp.where(even, outside + received, outside)
+    near1 = near1_keep + after(near1_got, theirs)
+    near1_in = hop(near1, INWARD)
+    far1_in = after(far1_in, near1)
+    far1_half = jnp.where(lower, far1[1], far1[0]) + far1_in
+    far1_end = hop(far1_half, OUTWARD)
+    key_grad, value_grad = finish(own, after(other, far1_half))
+    near1_in = after(near1_in, key_grad, near0_end)
+    near1_half = jnp.where(lower, near1[1] + near1_in[1], near1[0] + near1_in[0])
+    near1_end = hop(near1_half, ACROSS)
+
+    far_parts = [
+        (jnp.where(lower, base[0], base[1]) + got) + end
+        for base, got, end in ((far0, far0_in, far0_end), (far1, far1_in, far1_end))
+    ]
+    near_parts = [
+        jnp.where(lower, base[0] + got[0], base[1] + got[1]) + end
+        for base, got, end in ((near0, near0_in, near0_end), (near1, near1_in, near1_end))
+    ]
+    weight_grad = jnp.where(
+        outer, jnp.concatenate(far_parts, axis=1), jnp.concatenate(near_parts, axis=1)
+    )
+    return output[None], query_grad[None], key_grad[None], value_grad[None], weight_grad * scale
+
+
+NEXT = ((0, 1), (1, 0), (2, 3), (3, 2))
+OUTWARD = ((1, 3), (2, 0))
+INWARD = ((0, 1), (3, 2))
+ACROSS = ((1, 2), (2, 1))
+BACK = ((1, 0), (2, 1), (3, 2))
+BACK2 = ((2, 0), (3, 1))
+
+
+def hop(block, links):
+    return lax.ppermute(block, "seq", [(2 * a + i, 2 * b + i) for a, b in links for i in range(2)])
 
 
 def solution(mesh):

time: 138 us -> 135 us (0.978)
  waiting for transfers between devices: 53 us -> 43.4 us
  starting transfers between devices: 48.2 us -> 54.8 us
    ppermute x9 -> x11, waiting for transfers between devices: 8.09 us -> 24.4 us  [the longest x10 24.2 us: hop(): lax.ppermute(block, 'seq', [(2 * a + i, 2 * b + i) for a, b in links for...]
    ppermute x6 -> x4, waiting for transfers between devices: 18.9 us -> 4.19 us  [exclusive(): got = lax.ppermute(total, 'seq', links(step))]
    ppermute x9 -> x11, starting transfers between devices: 22.2 us -> 32.9 us  [the longest x10 32.8 us: hop(): lax.ppermute(block, 'seq', [(2 * a + i, 2 * b + i) for a, b in links for...]
    ppermute x7 -> x8, waiting for transfers between devices: 17.4 us -> 9.04 us  [trade(): return lax.ppermute(send, 'seq', [(s, s ^ 1) for s in range(count)])]
    ppermute x6 -> x4, starting transfers between devices: 15.2 us -> 10.3 us  [exclusive(): got = lax.ppermute(total, 'seq', links(step))]
    ppermute x3 -> x2, waiting for transfers between devices: 7.96 us -> 5.15 us  [exclusive(): results.append((mine, lax.ppermute(theirs, 'seq', swap)))]
    ppermute x7 -> x8, starting transfers between devices: 6.86 us -> 8.21 us  [trade(): return lax.ppermute(send, 'seq', [(s, s ^ 1) for s in range(count)])]
    ppermute x3 -> x2, starting transfers between devices: 3.8 us -> 3.26 us  [exclusive(): results.append((mine, lax.ppermute(theirs, 'seq', swap)))]
  transfers between devices with their start and end apart: 27 -> 27, of which waited for: 14 -> 18; matrix products, arithmetic and copies ran while one was open for 1% -> 1% of each run, Pallas kernels for 21% -> 20%
where the time goes in v7:
time: 135 us; the launch traced here: 134 us
  starting transfers between devices  54.8 us (41%)
  waiting for transfers between devices  43.4 us (32%)
  Pallas kernels  30.6 us (23%)
  local copies, waits for them, and re-layouts  2.38 us (2%)
  other arithmetic  2.19 us (2%)
    ppermute x10, starting transfers between devices, hop(): lax.ppermute(block, 'seq', [(2 * a + i, 2 * b + i) for a, b in links for...  32.8 us
    pallas_call x11, Pallas kernels, call(): pl.pallas_call(body, out_shape=tuple(out_shapes), in_specs=specs, out_spe...  30.6 us
    ppermute x10, waiting for transfers between devices, hop(): lax.ppermute(block, 'seq', [(2 * a + i, 2 * b + i) for a, b in links for...  24.2 us
    ppermute x4, starting transfers between devices, exclusive(): got = lax.ppermute(total, 'seq', links(step))  10.3 us
    ppermute x8, waiting for transfers between devices, trade(): return lax.ppermute(send, 'seq', [(s, s ^ 1) for s in range(count)])  9.04 us
    ppermute x8, starting transfers between devices, trade(): return lax.ppermute(send, 'seq', [(s, s ^ 1) for s in range(count)])  8.21 us
    ppermute x2, waiting for transfers between devices, exclusive(): results.append((mine, lax.ppermute(theirs, 'seq', swap)))  5.15 us
    ppermute x4, waiting for transfers between devices, exclusive(): got = lax.ppermute(total, 'seq', links(step))  4.19 us
  transfers between devices with their start and end apart: 27, of which 18 were waited for; matrix products, arithmetic and copies ran while one was open for 1% of the time, Pallas kernels for 20%

profile of v7, /device:TPU:12, one launch (start us, length us, event | category | flops | bytes accessed | tf_op | source)
XLA Modules:
  0.0 134.4 jit_solution(1475144219004720899)
XLA Ops:
  0.7 1.2 copy-done.3
  2.0 1.1 copy-done.4
  3.1 1.1 state.1
  4.2 1.6 %collective-permute-start = (f32[2,128,128]{2,1,0:T(8,128)S(1)}, f32[2,128,128]{2,1,0:T(8,128)S(1)}, u32[]{:S(2)}, u32[]{:S(2)}) collective-permute-start(f32[2,128,128]{2,1,0:T(8,128)S(1)} %get-tuple-element.64), channel_id=1, source_target_pairs={{0,2},{2,0},{4,6},{6,4},{8,10},{10,8},{12,14},{14,12},{1,3},{3,1},... | collective-permute-start | bytes 393224 | tf_op jit(solution)/shard_map/ppermute | solution.py:257
  5.8 0.6 away.1
  6.5 0.6 collective-permute-start.2
  7.1 2.4 %collective-permute-done = f32[2,128,128]{2,1,0:T(8,128)S(1)} collective-permute-done((f32[2,128,128]{2,1,0:T(8,128)S(1)}, f32[2,128,128]{2,1,0:T(8,128)S(1)}, u32[]{:S(2)}, u32[]{:S(2)}) %collective-permute-start) | collective-permute-done | bytes 131104 | tf_op jit(solution)/shard_map/ppermute | solution.py:257
  9.5 3.5 %collective-permute-start.1 = (f32[2,128,128]{2,1,0:T(8,128)S(1)}, f32[2,128,128]{2,1,0:T(8,128)S(1)}, u32[]{:S(2)}, u32[]{:S(2)}) collective-permute-start(f32[2,128,128]{2,1,0:T(8,128)S(1)} %add.101), channel_id=1, source_target_pairs={{0,4},{2,6},{4,8},{6,10},{8,12},{10,14},{1,5},{3,7},{5,9},{7,11},{... | collective-permute-start | bytes 393224 | tf_op jit(solution)/shard_map/ppermute | solution.py:219
  13.1 2.4 %local.1.att_ref = f32[384,1024]{1,0:T(8,128)S(1)} custom-call(bf16[384,1024]{1,0:T(8,128)(2,1)S(1)} %bitcast.38, bf16[384,1024]{1,0:T(8,128)(2,1)S(1)} %bitcast.43, bf16[384,1024]{1,0:T(8,128)(2,1)S(1)} %bitcast.47), custom_call_target="tpu_custom_call" | custom-call | flops 56623104 | tf_op jit(solution)/shard_map/local/pallas_call | solution.py:70
  15.5 3.5 %collective-permute-start.4 = (f32[2,128,128]{2,1,0:T(8,128)S(1)}, f32[2,128,128]{2,1,0:T(8,128)S(1)}, u32[]{:S(2)}, u32[]{:S(2)}) collective-permute-start(f32[2,128,128]{2,1,0:T(8,128)S(1)} %add.103), channel_id=1, source_target_pairs={{0,4},{2,6},{4,8},{6,10},{8,12},{10,14},{1,5},{3,7},{5,9},{7,11},{... | collective-permute-start | bytes 393224 | tf_op jit(solution)/shard_map/ppermute | solution.py:219
  19.1 1.9 %collective-permute-start.3 = (f32[2,128,128]{2,1,0:T(8,128)S(1)}, f32[2,128,128]{2,1,0:T(8,128)S(1)}, u32[]{:S(2)}, u32[]{:S(2)}) collective-permute-start(f32[2,128,128]{2,1,0:T(8,128)S(1)} %add.102), channel_id=1, source_target_pairs={{0,8},{2,10},{4,12},{6,14},{1,9},{3,11},{5,13},{7,15},{16,24},{18,... | collective-permute-start | bytes 393224 | tf_op jit(solution)/shard_map/ppermute | solution.py:219
  20.9 2.4 %d_normed.1.dn_ref = f32[384,1024]{1,0:T(8,128)S(1)} custom-call(bf16[384,2048]{1,0:T(8,128)(2,1)S(1)} %bitcast.35, bf16[1024,2048]{1,0:T(8,128)(2,1)S(1)} %copy-done.1), custom_call_target="tpu_custom_call" | custom-call | flops 100663296 | tf_op jit(solution)/shard_map/d_normed/pallas_call | solution.py:70
  23.4 3.3 %collective-permute-done.4 = f32[2,128,128]{2,1,0:T(8,128)S(1)} collective-permute-done((f32[2,128,128]{2,1,0:T(8,128)S(1)}, f32[2,128,128]{2,1,0:T(8,128)S(1)}, u32[]{:S(2)}, u32[]{:S(2)}) %collective-permute-start.4) | collective-permute-done | bytes 131104 | tf_op jit(solution)/shard_map/ppermute | solution.py:219
  26.7 1.5 %collective-permute-start.5 = (f32[2,128,128]{2,1,0:T(8,128)S(1)}, f32[2,128,128]{2,1,0:T(8,128)S(1)}, u32[]{:S(2)}, u32[]{:S(2)}) collective-permute-start(f32[2,128,128]{2,1,0:T(8,128)S(1)} %add.106), channel_id=1, source_target_pairs={{0,8},{2,10},{4,12},{6,14},{1,9},{3,11},{5,13},{7,15},{16,24},{18,... | collective-permute-start | bytes 393224 | tf_op jit(solution)/shard_map/ppermute | solution.py:219
  28.2 0.9 collective-permute-done.3
  29.1 1.6 %collective-permute-start.6 = (f32[2,128,128]{2,1,0:T(8,128)S(1)}, f32[2,128,128]{2,1,0:T(8,128)S(1)}, u32[]{:S(2)}, u32[]{:S(2)}) collective-permute-start(f32[2,128,128]{2,1,0:T(8,128)S(1)} %get-tuple-element.73), channel_id=1, source_target_pairs={{0,2},{2,0},{4,6},{6,4},{8,10},{10,8},{12,14},{14,12},{1,3},{3,1},... | collective-permute-start | bytes 393224 | tf_op jit(solution)/shard_map/ppermute | solution.py:229
  30.8 3.4 %collective-permute-done.6.other_ref.refs_2_ = f32[2,128,128]{2,1,0:T(8,128)S(1)} collective-permute-done((f32[2,128,128]{2,1,0:T(8,128)S(1)}, f32[2,128,128]{2,1,0:T(8,128)S(1)}, u32[]{:S(2)}, u32[]{:S(2)}) %collective-permute-start.6) | collective-permute-done | bytes 131104 | tf_op jit(solution)/shard_map/ppermute | solution.py:229
  34.1 2.5 %norm_far.1 = (bf16[384,512]{1,0:T(8,128)(2,1)S(1)}, f32[384,512]{1,0:T(8,128)S(1)}, bf16[384,512]{1,0:T(8,128)(2,1)S(1)}, f32[2,128,128]{2,1,0:T(8,128)S(1)}, f32[2,128,128]{2,1,0:T(8,128)S(1)}) custom-call(s32[2]{0:T(128)S(1)} %pad_add_fusion.place, bf16[384,1024]{1,0:T(8,128)(2,1)S(1)} %bitcast.39, f32[384,1024]{1,0:T(8,128)S(1)} %local.1.att_ref, ...), custom_call_target="tpu_custom_call" | custom-call | flops 6291456 | tf_op jit(solution)/shard_map/norm_far/pallas_call | solution.py:70
  36.8 1.6 %collective-permute-start.9 = (f32[2,128,128]{2,1,0:T(8,128)S(1)}, f32[2,128,128]{2,1,0:T(8,128)S(1)}, u32[]{:S(2)}, u32[]{:S(2)}) collective-permute-start(f32[2,128,128]{2,1,0:T(8,128)S(1)} %get-tuple-element.119), channel_id=1, source_target_pairs={{0,2},{2,0},{4,6},{6,4},{8,10},{10,8},{12,14},{14,12},{1,3},{3,1},... | collective-permute-start | bytes 393224 | tf_op jit(solution)/shard_map/ppermute | solution.py:229
  38.4 0.6 collective-permute-done.7.nbo_ref
  39.0 1.8 %weight.2 = (f32[2,128,512]{2,1,0:T(8,128)S(1)}, f32[2,128,512]{2,1,0:T(8,128)S(1)}, f32[2,128,512]{2,1,0:T(8,128)S(1)}, f32[2,128,512]{2,1,0:T(8,128)S(1)}) custom-call(s32[2]{0:T(128)S(1)} %pad_add_fusion.place, bf16[384,512]{1,0:T(8,128)(2,1)S(1)} %get-tuple-element.93.nb_ref.far_ref, bf16[384,2048]{1,0:T(8,128)(2,1)S(1)} %bitcast.36, ...), custom_call_target="tpu_custom_call" | custom-call | flops 50331648 | tf_op jit(solution)/shard_map/weight/pallas_call | solution.py:70
  40.9 1.8 %collective-permute-done.9.other_ref.refs_5_ = f32[2,128,128]{2,1,0:T(8,128)S(1)} collective-permute-done((f32[2,128,128]{2,1,0:T(8,128)S(1)}, f32[2,128,128]{2,1,0:T(8,128)S(1)}, u32[]{:S(2)}, u32[]{:S(2)}) %collective-permute-start.9) | collective-permute-done | bytes 131104 | tf_op jit(solution)/shard_map/ppermute | solution.py:229
  42.7 2.6 %norm_near.1 = (bf16[384,512]{1,0:T(8,128)(2,1)S(1)}, f32[384,512]{1,0:T(8,128)S(1)}, bf16[384,512]{1,0:T(8,128)(2,1)S(1)}, f32[4,128,128]{2,1,0:T(8,128)S(1)}, f32[4,128,128]{2,1,0:T(8,128)S(1)}) custom-call(s32[2]{0:T(128)S(1)} %pad_add_fusion.place, bf16[384,1024]{1,0:T(8,128)(2,1)S(1)} %bitcast.40, f32[384,1024]{1,0:T(8,128)S(1)} %local.1.att_ref, ...), custom_call_target="tpu_custom_call" | custom-call | flops 402653184 | tf_op jit(solution)/shard_map/norm_near/pallas_call | solution.py:70
  45.3 1.6 %collective-permute-start.11 = (f32[2,128,512]{2,1,0:T(8,128)S(1)}, f32[2,128,512]{2,1,0:T(8,128)S(1)}, u32[]{:S(2)}, u32[]{:S(2)}) collective-permute-start(f32[2,128,512]{2,1,0:T(8,128)S(1)} %get-tuple-element.83), channel_id=1, source_target_pairs={{0,2},{2,0},{4,6},{6,4},{8,10},{10,8},{12,14},{14,12},{1,3},{3,1},... | collective-permute-start | bytes 1572872 | tf_op jit(solution)/shard_map/ppermute | solution.py:257
  46.9 0.5 collective-permute-start.10
  47.4 0.2 collective-permute-done.12.nbo_ref
  47.6 2.0 %weight.3 = (f32[2,128,640]{2,1,0:T(8,128)S(1)}, f32[2,128,640]{2,1,0:T(8,128)S(1)}, f32[2,128,384]{2,1,0:T(8,128)S(1)}, f32[2,128,384]{2,1,0:T(8,128)S(1)}) custom-call(s32[2]{0:T(128)S(1)} %pad_add_fusion.place, bf16[384,512]{1,0:T(8,128)(2,1)S(1)} %get-tuple-element.85.nb_ref.near_ref, bf16[384,2048]{1,0:T(8,128)(2,1)S(1)} %bitcast.37, ...), custom_call_target="tpu_custom_call" | custom-call | flops 50331648 | tf_op jit(solution)/shard_map/weight/pallas_call | solution.py:70
  49.6 1.6 %collective-permute-start.16 = (f32[2,128,640]{2,1,0:T(8,128)S(1)}, f32[2,128,640]{2,1,0:T(8,128)S(1)}, u32[]{:S(2)}, u32[]{:S(2)}) collective-permute-start(f32[2,128,640]{2,1,0:T(8,128)S(1)} %get-tuple-element.87), channel_id=1, source_target_pairs={{0,2},{2,0},{4,6},{6,4},{8,10},{10,8},{12,14},{14,12},{1,3},{3,1},... | collective-permute-start | bytes 1966088 | tf_op jit(solution)/shard_map/ppermute | solution.py:257
  51.2 8.8 %grads.1 = (bf16[384,1024]{1,0:T(8,128)(2,1)}, f32[384,1024]{1,0:T(8,128)S(1)}, f32[384,1024]{1,0:T(8,128)S(1)}) custom-call(s32[2]{0:T(128)S(1)} %pad_add_fusion.place, bf16[384,1024]{1,0:T(8,128)(2,1)S(1)} %bitcast.41, bf16[384,1024]{1,0:T(8,128)(2,1)S(1)} %bitcast.44, bf16[384,1024]{1,0:T(8,128)(2,1)S(1)} %bitcast.48, ...), custom_call_target="tpu_custom_call" | custom-call | flops 169869312 | tf_op jit(solution)/shard_map/grads/pallas_call | solution.py:70
  60.0 0.1 collective-permute-done.11
  60.1 0.1 add.111
  60.2 3.7 %collective-permute-start.14 = (f32[128,512]{1,0:T(8,128)S(1)}, f32[128,512]{1,0:T(8,128)S(1)}, u32[]{:S(2)}, u32[]{:S(2)}) collective-permute-start(f32[128,512]{1,0:T(8,128)S(1)} %select_bitcast_fusion.2), channel_id=1, source_target_pairs={{0,4},{2,6},{4,0},{6,2},{8,12},{10,14},{12,8},{14,10},{1,5},{3,7},... | collective-permute-start | bytes 786440 | tf_op jit(solution)/shard_map/ppermute | solution.py:403
  64.0 1.7 %collective-permute-done.10 = f32[4,128,128]{2,1,0:T(8,128)S(1)} collective-permute-done((f32[4,128,128]{2,1,0:T(8,128)S(1)}, f32[4,128,128]{2,1,0:T(8,128)S(1)}, u32[]{:S(2)}, u32[]{:S(2)}) %collective-permute-start.10) | collective-permute-done | bytes 262176 | tf_op jit(solution)/shard_map/ppermute | solution.py:257
  65.8 5.6 %collective-permute-start.13 = (f32[4,128,128]{2,1,0:T(8,128)S(1)}, f32[4,128,128]{2,1,0:T(8,128)S(1)}, u32[]{:S(2)}, u32[]{:S(2)}) collective-permute-start(f32[4,128,128]{2,1,0:T(8,128)S(1)} %add.112), channel_id=1, source_target_pairs={{4,0},{6,2},{8,4},{10,6},{12,8},{14,10},{5,1},{7,3},{9,5},{11,7},{... | collective-permute-start | bytes 786440 | tf_op jit(solution)/shard_map/ppermute | solution.py:403
  71.3 0.3 collective-permute-start.18
  71.7 3.5 %output.1 = bf16[384,2048]{1,0:T(8,128)(2,1)} custom-call(bf16[384,512]{1,0:T(8,128)(2,1)S(1)} %get-tuple-element.93.nb_ref.far_ref, bf16[384,512]{1,0:T(8,128)(2,1)S(1)} %get-tuple-element.85.nb_ref.near_ref, bf16[1024,2048]{1,0:T(8,128)(2,1)S(1)} %copy-done.1), custom_call_target="tpu_custom_call" | custom-call | flops 100663296 | tf_op jit(solution)/shard_map/output/pallas_call | solution.py:70
  75.2 1.0 collective-permute-done.13
  76.3 3.5 %collective-permute-done.16 = f32[2,128,640]{2,1,0:T(8,128)S(1)} collective-permute-done((f32[2,128,640]{2,1,0:T(8,128)S(1)}, f32[2,128,640]{2,1,0:T(8,128)S(1)}, u32[]{:S(2)}, u32[]{:S(2)}) %collective-permute-start.16) | collective-permute-done | bytes 655392 | tf_op jit(solution)/shard_map/ppermute | solution.py:257
  79.8 0.1 add.115
  79.8 1.3 collective-permute-start.17
  81.1 1.6 %collective-permute-start.21 = (f32[2,128,384]{2,1,0:T(8,128)S(1)}, f32[2,128,384]{2,1,0:T(8,128)S(1)}, u32[]{:S(2)}, u32[]{:S(2)}) collective-permute-start(f32[2,128,384]{2,1,0:T(8,128)S(1)} %get-tuple-element.109), channel_id=1, source_target_pairs={{0,2},{2,0},{4,6},{6,4},{8,10},{10,8},{12,14},{14,12},{1,3},{3,1},... | collective-permute-start | bytes 1179656 | tf_op jit(solution)/shard_map/ppermute | solution.py:257
  82.8 1.3 collective-permute-start.15
  84.1 5.6 %collective-permute-start.22 = (f32[128,512]{1,0:T(8,128)S(1)}, f32[128,512]{1,0:T(8,128)S(1)}, u32[]{:S(2)}, u32[]{:S(2)}) collective-permute-start(f32[128,512]{1,0:T(8,128)S(1)} %bitcast_add_fusion.4), channel_id=1, source_target_pairs={{4,12},{6,14},{8,0},{10,2},{5,13},{7,15},{9,1},{11,3},{20,28},{22,... | collective-permute-start | bytes 786440 | tf_op jit(solution)/shard_map/ppermute | solution.py:403
  89.7 1.3 %collective-permute-done.18 = f32[2,128,512]{2,1,0:T(8,128)S(1)} collective-permute-done((f32[2,128,512]{2,1,0:T(8,128)S(1)}, f32[2,128,512]{2,1,0:T(8,128)S(1)}, u32[]{:S(2)}, u32[]{:S(2)}) %collective-permute-start.18) | collective-permute-done | bytes 524320 | tf_op jit(solution)/shard_map/ppermute | solution.py:257
  91.0 0.1 add.116
  91.1 3.7 %collective-permute-start.20 = (f32[128,512]{1,0:T(8,128)S(1)}, f32[128,512]{1,0:T(8,128)S(1)}, u32[]{:S(2)}, u32[]{:S(2)}) collective-permute-start(f32[128,512]{1,0:T(8,128)S(1)} %select_bitcast_fusion.1), channel_id=1, source_target_pairs={{0,4},{2,6},{4,0},{6,2},{8,12},{10,14},{12,8},{14,10},{1,5},{3,7},... | collective-permute-start | bytes 786440 | tf_op jit(solution)/shard_map/ppermute | solution.py:403
  94.9 5.6 %collective-permute-done.17 = f32[2,128,640]{2,1,0:T(8,128)S(1)} collective-permute-done((f32[2,128,640]{2,1,0:T(8,128)S(1)}, f32[2,128,640]{2,1,0:T(8,128)S(1)}, u32[]{:S(2)}, u32[]{:S(2)}) %collective-permute-start.17) | collective-permute-done | bytes 655392 | tf_op jit(solution)/shard_map/ppermute | solution.py:403
  100.4 0.1 select_bitcast_fusion
  100.5 6.8 %collective-permute-done.15 = f32[4,128,128]{2,1,0:T(8,128)S(1)} collective-permute-done((f32[4,128,128]{2,1,0:T(8,128)S(1)}, f32[4,128,128]{2,1,0:T(8,128)S(1)}, u32[]{:S(2)}, u32[]{:S(2)}) %collective-permute-start.15) | collective-permute-done | bytes 262176 | tf_op jit(solution)/shard_map/ppermute | solution.py:403
  107.3 0.1 add_select_fusion
  107.4 0.4 collective-permute-start.19
  107.9 4.7 %collective-permute-start.23 = (f32[128,512]{1,0:T(8,128)S(1)}, f32[128,512]{1,0:T(8,128)S(1)}, u32[]{:S(2)}, u32[]{:S(2)}) collective-permute-start(f32[128,512]{1,0:T(8,128)S(1)} %bitcast_add_fusion.3), channel_id=1, source_target_pairs={{4,12},{6,14},{8,0},{10,2},{5,13},{7,15},{9,1},{11,3},{20,28},{22,... | collective-permute-start | bytes 786440 | tf_op jit(solution)/shard_map/ppermute | solution.py:403
  112.6 2.3 %collective-permute-start.24 = (f32[128,640]{1,0:T(8,128)S(1)}, f32[128,640]{1,0:T(8,128)S(1)}, u32[]{:S(2)}, u32[]{:S(2)}) collective-permute-start(f32[128,640]{1,0:T(8,128)S(1)} %select_bitcast_fusion), channel_id=1, source_target_pairs={{4,8},{6,10},{8,4},{10,6},{5,9},{7,11},{9,5},{11,7},{20,24},{22,26... | collective-permute-start | bytes 983048 | tf_op jit(solution)/shard_map/ppermute | solution.py:403
  114.9 1.3 collective-permute-start.25
  116.3 0.1 fusion.2
  116.4 2.8 %final.1 = (bf16[384,1024]{1,0:T(8,128)(2,1)}, bf16[384,1024]{1,0:T(8,128)(2,1)}) custom-call(s32[2]{0:T(128)S(1)} %pad_add_fusion.place, bf16[384,1024]{1,0:T(8,128)(2,1)S(1)} %bitcast.45, bf16[384,1024]{1,0:T(8,128)(2,1)S(1)} %bitcast.49, f32[384,1024]{1,0:T(8,128)S(1)} %get-tuple-element.90.kl_ref, f32[384,1024]{1,0:T(8,128)S(1)} %get-tuple-element.95.vl_ref, ...), custom_call_target="tpu_custom_call" | custom-call | flops 25165824 | tf_op jit(solution)/shard_map/final/pallas_call | solution.py:70
  119.2 0.2 collective-permute-done.23
  119.3 0.1 fusion.1
  119.4 5.3 %collective-permute-done.24 = f32[128,640]{1,0:T(8,128)S(1)} collective-permute-done((f32[128,640]{1,0:T(8,128)S(1)}, f32[128,640]{1,0:T(8,128)S(1)}, u32[]{:S(2)}, u32[]{:S(2)}) %collective-permute-start.24) | collective-permute-done | bytes 327712 | tf_op jit(solution)/shard_map/ppermute | solution.py:403
  124.8 1.1 collective-permute-done.25
  125.9 3.2 %collective-permute-start.26 = (f32[128,384]{1,0:T(8,128)S(1)}, f32[128,384]{1,0:T(8,128)S(1)}, u32[]{:S(2)}, u32[]{:S(2)}) collective-permute-start(f32[128,384]{1,0:T(8,128)S(1)} %select_bitcast_fusion.3), channel_id=1, source_target_pairs={{4,8},{6,10},{8,4},{10,6},{5,9},{7,11},{9,5},{11,7},{20,24},{22,26... | collective-permute-start | bytes 589832 | tf_op jit(solution)/shard_map/ppermute | solution.py:403
  129.2 0.1 bitcast_add_fusion
  129.3 4.2 %collective-permute-done.26 = f32[128,384]{1,0:T(8,128)S(1)} collective-permute-done((f32[128,384]{1,0:T(8,128)S(1)}, f32[128,384]{1,0:T(8,128)S(1)}, u32[]{:S(2)}, u32[]{:S(2)}) %collective-permute-start.26) | collective-permute-done | bytes 196640 | tf_op jit(solution)/shard_map/ppermute | solution.py:403
  133.5 0.9 fusion
  (36 shorter events, 0.9 us)
Async XLA Ops:
  0.6 5.1 %copy-start = (bf16[1,384,2048]{2,1,0:T(8,128)(2,1)S(1)}, bf16[1,384,2048]{2,1,0:T(8,128)(2,1)}, u32[]{:S(2)}) copy-start(bf16[1,384,2048]{2,1,0:T(8,128)(2,1)} %param.9) | copy-start | bytes 4718596
  0.7 1.2 copy-start.3
  2.0 1.1 copy-start.4
  4.2 5.3 %collective-permute-start = (f32[2,128,128]{2,1,0:T(8,128)S(1)}, f32[2,128,128]{2,1,0:T(8,128)S(1)}, u32[]{:S(2)}, u32[]{:S(2)}) collective-permute-start(f32[2,128,128]{2,1,0:T(8,128)S(1)} %get-tuple-element.64), channel_id=1, source_target_pairs={{0,2},{2,0},{4,6},{6,4},{8,10},{10,8},{12,14},{14,12},{1,3},{3,1},... | collective-permute-start | bytes 393224 | tf_op jit(solution)/shard_map/ppermute | solution.py:257
  5.8 7.3 %copy-start.2 = (bf16[1,384,1024]{2,1,0:T(8,128)(2,1)S(1)}, bf16[1,384,1024]{2,1,0:T(8,128)(2,1)}, u32[]{:S(2)}) copy-start(bf16[1,384,1024]{2,1,0:T(8,128)(2,1)} %param.5) | copy-start | bytes 2359300
  6.4 32.6 %collective-permute-start.8 = (f32[384,1024]{1,0:T(8,128)S(1)}, f32[384,1024]{1,0:T(8,128)S(1)}, u32[]{:S(2)}, u32[]{:S(2)}) collective-permute-start(f32[384,1024]{1,0:T(8,128)S(1)} %away.1), channel_id=1, source_target_pairs={{0,1},{1,0},{2,3},{3,2},{4,5},{5,4},{6,7},{7,6},{8,9},{9,8},{10,11... | collective-permute-start | bytes 4718600 | tf_op jit(solution)/shard_map/ppermute | solution.py:263
  6.5 9.0 %collective-permute-start.2 = (f32[2,128,128]{2,1,0:T(8,128)S(1)}, f32[2,128,128]{2,1,0:T(8,128)S(1)}, u32[]{:S(2)}, u32[]{:S(2)}) collective-permute-start(f32[2,128,128]{2,1,0:T(8,128)S(1)} %get-tuple-element.68), channel_id=1, source_target_pairs={{0,2},{2,0},{4,6},{6,4},{8,10},{10,8},{12,14},{14,12},{1,3},{3,1},... | collective-permute-start | bytes 393224 | tf_op jit(solution)/shard_map/ppermute | solution.py:257
  9.5 9.5 %collective-permute-start.1 = (f32[2,128,128]{2,1,0:T(8,128)S(1)}, f32[2,128,128]{2,1,0:T(8,128)S(1)}, u32[]{:S(2)}, u32[]{:S(2)}) collective-permute-start(f32[2,128,128]{2,1,0:T(8,128)S(1)} %add.101), channel_id=1, source_target_pairs={{0,4},{2,6},{4,8},{6,10},{8,12},{10,14},{1,5},{3,7},{5,9},{7,11},{... | collective-permute-start | bytes 393224 | tf_op jit(solution)/shard_map/ppermute | solution.py:219
  13.0 7.9 %copy-start.1 = (bf16[1024,2048]{1,0:T(8,128)(2,1)S(1)}, bf16[1024,2048]{1,0:T(8,128)(2,1)}, u32[]{:S(2)}) copy-start(bf16[1024,2048]{1,0:T(8,128)(2,1)} %w_ref.3) | copy-start | bytes 12582916
  15.5 11.1 %collective-permute-start.4 = (f32[2,128,128]{2,1,0:T(8,128)S(1)}, f32[2,128,128]{2,1,0:T(8,128)S(1)}, u32[]{:S(2)}, u32[]{:S(2)}) collective-permute-start(f32[2,128,128]{2,1,0:T(8,128)S(1)} %add.103), channel_id=1, source_target_pairs={{0,4},{2,6},{4,8},{6,10},{8,12},{10,14},{1,5},{3,7},{5,9},{7,11},{... | collective-permute-start | bytes 393224 | tf_op jit(solution)/shard_map/ppermute | solution.py:219
  19.1 10.0 %collective-permute-start.3 = (f32[2,128,128]{2,1,0:T(8,128)S(1)}, f32[2,128,128]{2,1,0:T(8,128)S(1)}, u32[]{:S(2)}, u32[]{:S(2)}) collective-permute-start(f32[2,128,128]{2,1,0:T(8,128)S(1)} %add.102), channel_id=1, source_target_pairs={{0,8},{2,10},{4,12},{6,14},{1,9},{3,11},{5,13},{7,15},{16,24},{18,... | collective-permute-start | bytes 393224 | tf_op jit(solution)/shard_map/ppermute | solution.py:219
  26.7 4.1 %collective-permute-start.5 = (f32[2,128,128]{2,1,0:T(8,128)S(1)}, f32[2,128,128]{2,1,0:T(8,128)S(1)}, u32[]{:S(2)}, u32[]{:S(2)}) collective-permute-start(f32[2,128,128]{2,1,0:T(8,128)S(1)} %add.106), channel_id=1, source_target_pairs={{0,8},{2,10},{4,12},{6,14},{1,9},{3,11},{5,13},{7,15},{16,24},{18,... | collective-permute-start | bytes 393224 | tf_op jit(solution)/shard_map/ppermute | solution.py:219
  29.1 5.0 %collective-permute-start.6 = (f32[2,128,128]{2,1,0:T(8,128)S(1)}, f32[2,128,128]{2,1,0:T(8,128)S(1)}, u32[]{:S(2)}, u32[]{:S(2)}) collective-permute-start(f32[2,128,128]{2,1,0:T(8,128)S(1)} %get-tuple-element.73), channel_id=1, source_target_pairs={{0,2},{2,0},{4,6},{6,4},{8,10},{10,8},{12,14},{14,12},{1,3},{3,1},... | collective-permute-start | bytes 393224 | tf_op jit(solution)/shard_map/ppermute | solution.py:229
  36.7 2.4 %collective-permute-start.7 = (f32[384,512]{1,0:T(8,128)S(1)}, f32[384,512]{1,0:T(8,128)S(1)}, u32[]{:S(2)}, u32[]{:S(2)}) collective-permute-start(f32[384,512]{1,0:T(8,128)S(1)} %get-tuple-element.75), channel_id=1, source_target_pairs={{0,1},{1,0},{2,3},{3,2},{4,5},{5,4},{6,7},{7,6},{8,9},{9,8},{10,11... | collective-permute-start | bytes 2359304 | tf_op jit(solution)/shard_map/ppermute | solution.py:289
  36.8 5.9 %collective-permute-start.9 = (f32[2,128,128]{2,1,0:T(8,128)S(1)}, f32[2,128,128]{2,1,0:T(8,128)S(1)}, u32[]{:S(2)}, u32[]{:S(2)}) collective-permute-start(f32[2,128,128]{2,1,0:T(8,128)S(1)} %get-tuple-element.119), channel_id=1, source_target_pairs={{0,2},{2,0},{4,6},{6,4},{8,10},{10,8},{12,14},{14,12},{1,3},{3,1},... | collective-permute-start | bytes 393224 | tf_op jit(solution)/shard_map/ppermute | solution.py:229
  45.2 2.4 %collective-permute-start.12 = (f32[384,512]{1,0:T(8,128)S(1)}, f32[384,512]{1,0:T(8,128)S(1)}, u32[]{:S(2)}, u32[]{:S(2)}) collective-permute-start(f32[384,512]{1,0:T(8,128)S(1)} %get-tuple-element.86), channel_id=1, source_target_pairs={{0,1},{1,0},{2,3},{3,2},{4,5},{5,4},{6,7},{7,6},{8,9},{9,8},{10,11... | collective-permute-start | bytes 2359304 | tf_op jit(solution)/shard_map/ppermute | solution.py:303
  45.3 14.8 %collective-permute-start.11 = (f32[2,128,512]{2,1,0:T(8,128)S(1)}, f32[2,128,512]{2,1,0:T(8,128)S(1)}, u32[]{:S(2)}, u32[]{:S(2)}) collective-permute-start(f32[2,128,512]{2,1,0:T(8,128)S(1)} %get-tuple-element.83), channel_id=1, source_target_pairs={{0,2},{2,0},{4,6},{6,4},{8,10},{10,8},{12,14},{14,12},{1,3},{3,1},... | collective-permute-start | bytes 1572872 | tf_op jit(solution)/shard_map/ppermute | solution.py:257
  46.9 18.8 %collective-permute-start.10 = (f32[4,128,128]{2,1,0:T(8,128)S(1)}, f32[4,128,128]{2,1,0:T(8,128)S(1)}, u32[]{:S(2)}, u32[]{:S(2)}) collective-permute-start(f32[4,128,128]{2,1,0:T(8,128)S(1)} %get-tuple-element.81), channel_id=1, source_target_pairs={{0,2},{2,0},{4,6},{6,4},{8,10},{10,8},{12,14},{14,12},{1,3},{3,1},... | collective-permute-start | bytes 786440 | tf_op jit(solution)/shard_map/ppermute | solution.py:257
  49.6 30.2 %collective-permute-start.16 = (f32[2,128,640]{2,1,0:T(8,128)S(1)}, f32[2,128,640]{2,1,0:T(8,128)S(1)}, u32[]{:S(2)}, u32[]{:S(2)}) collective-permute-start(f32[2,128,640]{2,1,0:T(8,128)S(1)} %get-tuple-element.87), channel_id=1, source_target_pairs={{0,2},{2,0},{4,6},{6,4},{8,10},{10,8},{12,14},{14,12},{1,3},{3,1},... | collective-permute-start | bytes 1966088 | tf_op jit(solution)/shard_map/ppermute | solution.py:257
  60.2 14.9 %collective-permute-start.14 = (f32[128,512]{1,0:T(8,128)S(1)}, f32[128,512]{1,0:T(8,128)S(1)}, u32[]{:S(2)}, u32[]{:S(2)}) collective-permute-start(f32[128,512]{1,0:T(8,128)S(1)} %select_bitcast_fusion.2), channel_id=1, source_target_pairs={{0,4},{2,6},{4,0},{6,2},{8,12},{10,14},{12,8},{14,10},{1,5},{3,7},... | collective-permute-start | bytes 786440 | tf_op jit(solution)/shard_map/ppermute | solution.py:403
  65.8 10.5 %collective-permute-start.13 = (f32[4,128,128]{2,1,0:T(8,128)S(1)}, f32[4,128,128]{2,1,0:T(8,128)S(1)}, u32[]{:S(2)}, u32[]{:S(2)}) collective-permute-start(f32[4,128,128]{2,1,0:T(8,128)S(1)} %add.112), channel_id=1, source_target_pairs={{4,0},{6,2},{8,4},{10,6},{12,8},{14,10},{5,1},{7,3},{9,5},{11,7},{... | collective-permute-start | bytes 786440 | tf_op jit(solution)/shard_map/ppermute | solution.py:403
  71.3 19.7 %collective-permute-start.18 = (f32[2,128,512]{2,1,0:T(8,128)S(1)}, f32[2,128,512]{2,1,0:T(8,128)S(1)}, u32[]{:S(2)}, u32[]{:S(2)}) collective-permute-start(f32[2,128,512]{2,1,0:T(8,128)S(1)} %get-tuple-element.104), channel_id=1, source_target_pairs={{0,2},{2,0},{4,6},{6,4},{8,10},{10,8},{12,14},{14,12},{1,3},{3,1},... | collective-permute-start | bytes 1572872 | tf_op jit(solution)/shard_map/ppermute | solution.py:257
  79.8 20.6 %collective-permute-start.17 = (f32[2,128,640]{2,1,0:T(8,128)S(1)}, f32[2,128,640]{2,1,0:T(8,128)S(1)}, u32[]{:S(2)}, u32[]{:S(2)}) collective-permute-start(f32[2,128,640]{2,1,0:T(8,128)S(1)} %add.115), channel_id=1, source_target_pairs={{0,4},{2,6},{12,8},{14,10},{1,5},{3,7},{13,9},{15,11},{16,20},{18,... | collective-permute-start | bytes 1966088 | tf_op jit(solution)/shard_map/ppermute | solution.py:403
  81.1 26.6 %collective-permute-start.21 = (f32[2,128,384]{2,1,0:T(8,128)S(1)}, f32[2,128,384]{2,1,0:T(8,128)S(1)}, u32[]{:S(2)}, u32[]{:S(2)}) collective-permute-start(f32[2,128,384]{2,1,0:T(8,128)S(1)} %get-tuple-element.109), channel_id=1, source_target_pairs={{0,2},{2,0},{4,6},{6,4},{8,10},{10,8},{12,14},{14,12},{1,3},{3,1},... | collective-permute-start | bytes 1179656 | tf_op jit(solution)/shard_map/ppermute | solution.py:257
  82.8 24.5 %collective-permute-start.15 = (f32[4,128,128]{2,1,0:T(8,128)S(1)}, f32[4,128,128]{2,1,0:T(8,128)S(1)}, u32[]{:S(2)}, u32[]{:S(2)}) collective-permute-start(f32[4,128,128]{2,1,0:T(8,128)S(1)} %add.114), channel_id=1, source_target_pairs={{8,0},{10,2},{12,4},{14,6},{9,1},{11,3},{13,5},{15,7},{24,16},{26,... | collective-permute-start | bytes 786440 | tf_op jit(solution)/shard_map/ppermute | solution.py:403
  84.1 32.2 %collective-permute-start.22 = (f32[128,512]{1,0:T(8,128)S(1)}, f32[128,512]{1,0:T(8,128)S(1)}, u32[]{:S(2)}, u32[]{:S(2)}) collective-permute-start(f32[128,512]{1,0:T(8,128)S(1)} %bitcast_add_fusion.4), channel_id=1, source_target_pairs={{4,12},{6,14},{8,0},{10,2},{5,13},{7,15},{9,1},{11,3},{20,28},{22,... | collective-permute-start | bytes 786440 | tf_op jit(solution)/shard_map/ppermute | solution.py:403
  91.1 16.7 %collective-permute-start.20 = (f32[128,512]{1,0:T(8,128)S(1)}, f32[128,512]{1,0:T(8,128)S(1)}, u32[]{:S(2)}, u32[]{:S(2)}) collective-permute-start(f32[128,512]{1,0:T(8,128)S(1)} %select_bitcast_fusion.1), channel_id=1, source_target_pairs={{0,4},{2,6},{4,0},{6,2},{8,12},{10,14},{12,8},{14,10},{1,5},{3,7},... | collective-permute-start | bytes 786440 | tf_op jit(solution)/shard_map/ppermute | solution.py:403
  107.4 9.0 %collective-permute-start.19 = (f32[4,128,128]{2,1,0:T(8,128)S(1)}, f32[4,128,128]{2,1,0:T(8,128)S(1)}, u32[]{:S(2)}, u32[]{:S(2)}) collective-permute-start(f32[4,128,128]{2,1,0:T(8,128)S(1)} %get-tuple-element.117), channel_id=1, source_target_pairs={{0,2},{2,0},{4,6},{6,4},{8,10},{10,8},{12,14},{14,12},{1,3},{3,1},... | collective-permute-start | bytes 786440 | tf_op jit(solution)/shard_map/ppermute | solution.py:257
  107.9 11.5 %collective-permute-start.23 = (f32[128,512]{1,0:T(8,128)S(1)}, f32[128,512]{1,0:T(8,128)S(1)}, u32[]{:S(2)}, u32[]{:S(2)}) collective-permute-start(f32[128,512]{1,0:T(8,128)S(1)} %bitcast_add_fusion.3), channel_id=1, source_target_pairs={{4,12},{6,14},{8,0},{10,2},{5,13},{7,15},{9,1},{11,3},{20,28},{22,... | collective-permute-start | bytes 786440 | tf_op jit(solution)/shard_map/ppermute | solution.py:403
  112.6 12.1 %collective-permute-start.24 = (f32[128,640]{1,0:T(8,128)S(1)}, f32[128,640]{1,0:T(8,128)S(1)}, u32[]{:S(2)}, u32[]{:S(2)}) collective-permute-start(f32[128,640]{1,0:T(8,128)S(1)} %select_bitcast_fusion), channel_id=1, source_target_pairs={{4,8},{6,10},{8,4},{10,6},{5,9},{7,11},{9,5},{11,7},{20,24},{22,26... | collective-permute-start | bytes 983048 | tf_op jit(solution)/shard_map/ppermute | solution.py:403
  114.9 10.9 %collective-permute-start.25 = (f32[2,128,384]{2,1,0:T(8,128)S(1)}, f32[2,128,384]{2,1,0:T(8,128)S(1)}, u32[]{:S(2)}, u32[]{:S(2)}) collective-permute-start(f32[2,128,384]{2,1,0:T(8,128)S(1)} %add.122), channel_id=1, source_target_pairs={{0,4},{2,6},{12,8},{14,10},{1,5},{3,7},{13,9},{15,11},{16,20},{18,... | collective-permute-start | bytes 1179656 | tf_op jit(solution)/shard_map/ppermute | solution.py:403
  125.9 7.6 %collective-permute-start.26 = (f32[128,384]{1,0:T(8,128)S(1)}, f32[128,384]{1,0:T(8,128)S(1)}, u32[]{:S(2)}, u32[]{:S(2)}) collective-permute-start(f32[128,384]{1,0:T(8,128)S(1)} %select_bitcast_fusion.3), channel_id=1, source_target_pairs={{4,8},{6,10},{8,4},{10,6},{5,9},{7,11},{9,5},{11,7},{20,24},{22,26... | collective-permute-start | bytes 589832 | tf_op jit(solution)/shard_map/ppermute | solution.py:403

commit v8 on v7

--- a/solution.py
+++ b/solution.py
@@ -288,7 +288,6 @@
     if fast:
         chunks = product(far, lax.ppermute(far32, "dp", swap), WIDTHS[0])
         near_own = after(near_own, chunks[0][1])
-        far0_got = trade(after(chunks[0][1], near_other))
     near, near32, near_att, keep, send = call(
         functools.partial(norm_body, NEAR),
         pieces + (state, state),
@@ -298,18 +297,21 @@
     )
 
     received = trade(send)
-    ready = ()
+    total = keep + received
     if fast:
         nbo = lax.ppermute(near32, "dp", swap)
-        (near0_keep, near0_send), (near1_keep, near1_send) = product(near, nbo, WIDTHS[1])
-        ready = (near0_send,)
-    query_grad, key_local, value_local = call(
-        grads_body,
-        (rows16, rows32, rows32),
-        (place, q, k, v, after(far_att, *ready), *far_prior, near_att, *near_prior),
-        9 * unit * length,
-        "grads",
-    )
+        (near0_keep, near0_send), (near1_keep, near1_send) = product(after(near, received), nbo, WIDTHS[1])
+        near0_got = trade(near0_send)
+        far0_got = trade(after(chunks[0][1], received))
+        back1 = hop(total, BACK)
+    def gradients(far_att):
+        return call(
+            grads_body,
+            (rows16, rows32, rows32),
+            (place, q, k, v, far_att, *far_prior, near_att, *near_prior),
+            9 * unit * length,
+            "grads",
+        )
 
     def finish(own, other):
         return call(
@@ -336,38 +338,38 @@
         weight = lax.psum_scatter(weight, "dp", scatter_dimension=1, tiled=True)
         weight_grad = lax.psum_scatter(weight, "seq", scatter_dimension=0, tiled=True) * scale
         output = project(far)
+        query_grad, key_local, value_local = gradients(far_att)
         ((own, other),) = exclusive([(keep, received)], count, even, True, [])
         key_grad, value_grad = finish(own, other)
         return output[None], query_grad[None], key_grad[None], value_grad[None], weight_grad
 
     (far0_keep, _), (far1_keep, far1_send) = chunks
-    far0 = far0_keep + after(far0_got, key_local)
-    far0_in = hop(jnp.where(odd, far0[0], far0[1]), NEXT)
+    near1_got = trade(near1_send)
+    output = project(after(far, near0_send))
+    back1 = after(back1, output)
+    total = total + back1
+    back2 = hop(total, BACK2)
+    far0 = far0_keep + after(far0_got, total)
+    far0_out = jnp.where(odd, far0[0], far0[1])
+    far0_in = hop(far0_out, NEXT)
     far1_got = trade(after(far1_send, far0))
-    near0_got, near1_got = trade(near0_send), trade(near1_send)
-
-    total = keep + after(received, far0)
-    back1 = hop(total, BACK)
-    output = project(after(far, total))
-    far0_in = after(far0_in, output)
+    query_grad, key_local, value_local = gradients(after(far_att, far0_out))
+    far0_in = after(far0_in, key_local)
     far0_half = jnp.where(lower, far0[1], far0[0]) + far0_in
     far0_end = hop(far0_half, OUTWARD)
-    back1 = after(back1, far0_half)
-    total = total + back1
-    back2 = hop(total, BACK2)
-    near0 = near0_keep + after(near0_got, total)
+    near0 = near0_keep + after(near0_got, far0_half)
     near0_in = hop(near0, INWARD)
-    far1 = far1_keep + after(far1_got, near0)
-    far1_out = jnp.where(odd, far1[0], far1[1])
-    far1_in = hop(far1_out, NEXT)
-    near0_in = after(near0_in, far1_out)
-    near0_half = jnp.where(lower, near0[1] + near0_in[1], near0[0] + near0_in[0])
-    near0_end = hop(near0_half, ACROSS)
-    outside = back1 + after(back2, near0_half)
+    outside = back1 + after(back2, near0)
     theirs = jnp.where(even, outside, outside + keep)
     other = trade(theirs)
     own = jnp.where(even, outside + received, outside)
-    near1 = near1_keep + after(near1_got, theirs)
+    far1 = far1_keep + after(far1_got, theirs)
+    far1_out = jnp.where(odd, far1[0], far1[1])
+    far1_in = hop(far1_out, NEXT)
+    near0_in = after(near0_in, far1_out, far0_end)
+    near0_half = jnp.where(lower, near0[1] + near0_in[1], near0[0] + near0_in[0])
+    near0_end = hop(near0_half, ACROSS)
+    near1 = near1_keep + after(near1_got, near0_half)
     near1_in = hop(near1, INWARD)
     far1_in = after(far1_in, near1)
     far1_half = jnp.where(lower, far1[1], far1[0]) + far1_in

time: 135 us -> 130 us (0.963)
  waiting for transfers between devices: 43.4 us -> 40.8 us
  starting transfers between devices: 54.8 us -> 52.9 us
    ppermute x10, waiting for transfers between devices: 24.2 us -> 17.7 us  [hop(): lax.ppermute(block, 'seq', [(2 * a + i, 2 * b + i) for a, b in links for...]
    ppermute x8, waiting for transfers between devices: 9.04 us -> 13 us  [trade(): return lax.ppermute(send, 'seq', [(s, s ^ 1) for s in range(count)])]
    ppermute x10, starting transfers between devices: 32.8 us -> 29.7 us  [hop(): lax.ppermute(block, 'seq', [(2 * a + i, 2 * b + i) for a, b in links for...]
    ppermute x8, starting transfers between devices: 8.21 us -> 9.58 us  [trade(): return lax.ppermute(send, 'seq', [(s, s ^ 1) for s in range(count)])]
  transfers between devices with their start and end apart: 27 -> 27, of which waited for: 18 -> 14; matrix products, arithmetic and copies ran while one was open for 1% -> 1% of each run, Pallas kernels for 20% -> 21%
where the time goes in v8:
time: 130 us
  starting transfers between devices  52.9 us (41%)
  waiting for transfers between devices  40.8 us (31%)
  Pallas kernels  30.4 us (23%)
  local copies, waits for them, and re-layouts  2.38 us (2%)
  other arithmetic  2.25 us (2%)
    pallas_call x11, Pallas kernels, call(): pl.pallas_call(body, out_shape=tuple(out_shapes), in_specs=specs, out_spe...  30.4 us
    ppermute x10, starting transfers between devices, hop(): lax.ppermute(block, 'seq', [(2 * a + i, 2 * b + i) for a, b in links for...  29.7 us
    ppermute x10, waiting for transfers between devices, hop(): lax.ppermute(block, 'seq', [(2 * a + i, 2 * b + i) for a, b in links for...  17.7 us
    ppermute x8, waiting for transfers between devices, trade(): return lax.ppermute(send, 'seq', [(s, s ^ 1) for s in range(count)])  13 us
    ppermute x4, starting transfers between devices, exclusive(): got = lax.ppermute(total, 'seq', links(step))  10.1 us
    ppermute x8, starting transfers between devices, trade(): return lax.ppermute(send, 'seq', [(s, s ^ 1) for s in range(count)])  9.58 us
    ppermute x2, waiting for transfers between devices, exclusive(): results.append((mine, lax.ppermute(theirs, 'seq', swap)))  5.14 us
    ppermute x4, waiting for transfers between devices, exclusive(): got = lax.ppermute(total, 'seq', links(step))  4.37 us
  transfers between devices with their start and end apart: 27, of which 14 were waited for; matrix products, arithmetic and copies ran while one was open for 1% of the time, Pallas kernels for 21%

profile of v8, /device:TPU:12, one launch (start us, length us, event | category | flops | bytes accessed | tf_op | source)
XLA Modules:
  0.0 129.8 jit_solution(10046490263819673517)
XLA Ops:
  0.7 0.1 pad_add_fusion.place
  0.7 1.2 copy-done.3
  2.0 1.1 copy-done.4
  3.1 1.1 state.1
  4.2 1.6 %collective-permute-start = (f32[2,128,128]{2,1,0:T(8,128)S(1)}, f32[2,128,128]{2,1,0:T(8,128)S(1)}, u32[]{:S(2)}, u32[]{:S(2)}) collective-permute-start(f32[2,128,128]{2,1,0:T(8,128)S(1)} %get-tuple-element.64), channel_id=1, source_target_pairs={{0,2},{2,0},{4,6},{6,4},{8,10},{10,8},{12,14},{14,12},{1,3},{3,1},... | collective-permute-start | bytes 393224 | tf_op jit(solution)/shard_map/ppermute | solution.py:257
  5.8 0.6 away.1
  6.4 0.1 collective-permute-start.8
  6.5 0.6 collective-permute-start.2
  7.1 2.4 %collective-permute-done = f32[2,128,128]{2,1,0:T(8,128)S(1)} collective-permute-done((f32[2,128,128]{2,1,0:T(8,128)S(1)}, f32[2,128,128]{2,1,0:T(8,128)S(1)}, u32[]{:S(2)}, u32[]{:S(2)}) %collective-permute-start) | collective-permute-done | bytes 131104 | tf_op jit(solution)/shard_map/ppermute | solution.py:257
  9.5 3.5 %collective-permute-start.1 = (f32[2,128,128]{2,1,0:T(8,128)S(1)}, f32[2,128,128]{2,1,0:T(8,128)S(1)}, u32[]{:S(2)}, u32[]{:S(2)}) collective-permute-start(f32[2,128,128]{2,1,0:T(8,128)S(1)} %add.101), channel_id=1, source_target_pairs={{0,4},{2,6},{4,8},{6,10},{8,12},{10,14},{1,5},{3,7},{5,9},{7,11},{... | collective-permute-start | bytes 393224 | tf_op jit(solution)/shard_map/ppermute | solution.py:219
  13.1 2.4 %local.1.att_ref = f32[384,1024]{1,0:T(8,128)S(1)} custom-call(bf16[384,1024]{1,0:T(8,128)(2,1)S(1)} %bitcast.38, bf16[384,1024]{1,0:T(8,128)(2,1)S(1)} %bitcast.43, bf16[384,1024]{1,0:T(8,128)(2,1)S(1)} %bitcast.47), custom_call_target="tpu_custom_call" | custom-call | flops 56623104 | tf_op jit(solution)/shard_map/local/pallas_call | solution.py:70
  15.5 3.5 %collective-permute-start.4 = (f32[2,128,128]{2,1,0:T(8,128)S(1)}, f32[2,128,128]{2,1,0:T(8,128)S(1)}, u32[]{:S(2)}, u32[]{:S(2)}) collective-permute-start(f32[2,128,128]{2,1,0:T(8,128)S(1)} %add.103), channel_id=1, source_target_pairs={{0,4},{2,6},{4,8},{6,10},{8,12},{10,14},{1,5},{3,7},{5,9},{7,11},{... | collective-permute-start | bytes 393224 | tf_op jit(solution)/shard_map/ppermute | solution.py:219
  19.1 1.9 %collective-permute-start.3 = (f32[2,128,128]{2,1,0:T(8,128)S(1)}, f32[2,128,128]{2,1,0:T(8,128)S(1)}, u32[]{:S(2)}, u32[]{:S(2)}) collective-permute-start(f32[2,128,128]{2,1,0:T(8,128)S(1)} %add.102), channel_id=1, source_target_pairs={{0,8},{2,10},{4,12},{6,14},{1,9},{3,11},{5,13},{7,15},{16,24},{18,... | collective-permute-start | bytes 393224 | tf_op jit(solution)/shard_map/ppermute | solution.py:219
  20.9 2.4 %d_normed.1.dn_ref = f32[384,1024]{1,0:T(8,128)S(1)} custom-call(bf16[384,2048]{1,0:T(8,128)(2,1)S(1)} %bitcast.35, bf16[1024,2048]{1,0:T(8,128)(2,1)S(1)} %copy-done.1), custom_call_target="tpu_custom_call" | custom-call | flops 100663296 | tf_op jit(solution)/shard_map/d_normed/pallas_call | solution.py:70
  23.4 3.3 %collective-permute-done.4 = f32[2,128,128]{2,1,0:T(8,128)S(1)} collective-permute-done((f32[2,128,128]{2,1,0:T(8,128)S(1)}, f32[2,128,128]{2,1,0:T(8,128)S(1)}, u32[]{:S(2)}, u32[]{:S(2)}) %collective-permute-start.4) | collective-permute-done | bytes 131104 | tf_op jit(solution)/shard_map/ppermute | solution.py:219
  26.7 1.3 collective-permute-start.5
  28.0 1.1 collective-permute-done.3
  29.1 1.6 %collective-permute-start.6 = (f32[2,128,128]{2,1,0:T(8,128)S(1)}, f32[2,128,128]{2,1,0:T(8,128)S(1)}, u32[]{:S(2)}, u32[]{:S(2)}) collective-permute-start(f32[2,128,128]{2,1,0:T(8,128)S(1)} %get-tuple-element.73), channel_id=1, source_target_pairs={{0,2},{2,0},{4,6},{6,4},{8,10},{10,8},{12,14},{14,12},{1,3},{3,1},... | collective-permute-start | bytes 393224 | tf_op jit(solution)/shard_map/ppermute | solution.py:229
  30.8 3.4 %collective-permute-done.6.other_ref.refs_2_ = f32[2,128,128]{2,1,0:T(8,128)S(1)} collective-permute-done((f32[2,128,128]{2,1,0:T(8,128)S(1)}, f32[2,128,128]{2,1,0:T(8,128)S(1)}, u32[]{:S(2)}, u32[]{:S(2)}) %collective-permute-start.6) | collective-permute-done | bytes 131104 | tf_op jit(solution)/shard_map/ppermute | solution.py:229
  34.1 2.5 %norm_far.1 = (bf16[384,512]{1,0:T(8,128)(2,1)S(1)}, f32[384,512]{1,0:T(8,128)S(1)}, bf16[384,512]{1,0:T(8,128)(2,1)S(1)}, f32[2,128,128]{2,1,0:T(8,128)S(1)}, f32[2,128,128]{2,1,0:T(8,128)S(1)}) custom-call(s32[2]{0:T(128)S(1)} %pad_add_fusion.place, bf16[384,1024]{1,0:T(8,128)(2,1)S(1)} %bitcast.39, f32[384,1024]{1,0:T(8,128)S(1)} %local.1.att_ref, ...), custom_call_target="tpu_custom_call" | custom-call | flops 6291456 | tf_op jit(solution)/shard_map/norm_far/pallas_call | solution.py:70
  36.7 0.1 collective-permute-start.7
  36.8 1.6 %collective-permute-start.9 = (f32[2,128,128]{2,1,0:T(8,128)S(1)}, f32[2,128,128]{2,1,0:T(8,128)S(1)}, u32[]{:S(2)}, u32[]{:S(2)}) collective-permute-start(f32[2,128,128]{2,1,0:T(8,128)S(1)} %get-tuple-element.119), channel_id=1, source_target_pairs={{0,2},{2,0},{4,6},{6,4},{8,10},{10,8},{12,14},{14,12},{1,3},{3,1},... | collective-permute-start | bytes 393224 | tf_op jit(solution)/shard_map/ppermute | solution.py:229
  38.4 0.6 collective-permute-done.7.nbo_ref
  39.0 1.9 %weight.2 = (f32[2,128,512]{2,1,0:T(8,128)S(1)}, f32[2,128,512]{2,1,0:T(8,128)S(1)}, f32[2,128,512]{2,1,0:T(8,128)S(1)}, f32[2,128,512]{2,1,0:T(8,128)S(1)}) custom-call(s32[2]{0:T(128)S(1)} %pad_add_fusion.place, bf16[384,512]{1,0:T(8,128)(2,1)S(1)} %get-tuple-element.85.nb_ref.far_ref, bf16[384,2048]{1,0:T(8,128)(2,1)S(1)} %bitcast.36, ...), custom_call_target="tpu_custom_call" | custom-call | flops 50331648 | tf_op jit(solution)/shard_map/weight/pallas_call | solution.py:70
  40.9 1.8 %collective-permute-done.9.other_ref.refs_5_ = f32[2,128,128]{2,1,0:T(8,128)S(1)} collective-permute-done((f32[2,128,128]{2,1,0:T(8,128)S(1)}, f32[2,128,128]{2,1,0:T(8,128)S(1)}, u32[]{:S(2)}, u32[]{:S(2)}) %collective-permute-start.9) | collective-permute-done | bytes 131104 | tf_op jit(solution)/shard_map/ppermute | solution.py:229
  42.7 2.6 %norm_near.1 = (bf16[384,512]{1,0:T(8,128)(2,1)S(1)}, f32[384,512]{1,0:T(8,128)S(1)}, bf16[384,512]{1,0:T(8,128)(2,1)S(1)}, f32[4,128,128]{2,1,0:T(8,128)S(1)}, f32[4,128,128]{2,1,0:T(8,128)S(1)}) custom-call(s32[2]{0:T(128)S(1)} %pad_add_fusion.place, bf16[384,1024]{1,0:T(8,128)(2,1)S(1)} %bitcast.40, f32[384,1024]{1,0:T(8,128)S(1)} %local.1.att_ref, ...), custom_call_target="tpu_custom_call" | custom-call | flops 402653184 | tf_op jit(solution)/shard_map/norm_near/pallas_call | solution.py:70
  45.2 0.1 collective-permute-start.11
  45.3 1.6 %collective-permute-start.10 = (f32[4,128,128]{2,1,0:T(8,128)S(1)}, f32[4,128,128]{2,1,0:T(8,128)S(1)}, u32[]{:S(2)}, u32[]{:S(2)}) collective-permute-start(f32[4,128,128]{2,1,0:T(8,128)S(1)} %get-tuple-element.81), channel_id=1, source_target_pairs={{0,2},{2,0},{4,6},{6,4},{8,10},{10,8},{12,14},{14,12},{1,3},{3,1},... | collective-permute-start | bytes 786440 | tf_op jit(solution)/shard_map/ppermute | solution.py:257
  46.9 7.1 %collective-permute-done.10 = f32[4,128,128]{2,1,0:T(8,128)S(1)} collective-permute-done((f32[4,128,128]{2,1,0:T(8,128)S(1)}, f32[4,128,128]{2,1,0:T(8,128)S(1)}, u32[]{:S(2)}, u32[]{:S(2)}) %collective-permute-start.10) | collective-permute-done | bytes 262176 | tf_op jit(solution)/shard_map/ppermute | solution.py:257
  54.0 1.6 %collective-permute-start.12 = (f32[2,128,512]{2,1,0:T(8,128)S(1)}, f32[2,128,512]{2,1,0:T(8,128)S(1)}, u32[]{:S(2)}, u32[]{:S(2)}) collective-permute-start(f32[2,128,512]{2,1,0:T(8,128)S(1)} %get-tuple-element.89), channel_id=1, source_target_pairs={{0,2},{2,0},{4,6},{6,4},{8,10},{10,8},{12,14},{14,12},{1,3},{3,1},... | collective-permute-start | bytes 1572872 | tf_op jit(solution)/shard_map/ppermute | solution.py:257
  55.6 4.1 %collective-permute-start.13 = (f32[4,128,128]{2,1,0:T(8,128)S(1)}, f32[4,128,128]{2,1,0:T(8,128)S(1)}, u32[]{:S(2)}, u32[]{:S(2)}) collective-permute-start(f32[4,128,128]{2,1,0:T(8,128)S(1)} %add.111), channel_id=1, source_target_pairs={{4,0},{6,2},{8,4},{10,6},{12,8},{14,10},{5,1},{7,3},{9,5},{11,7},{... | collective-permute-start | bytes 786440 | tf_op jit(solution)/shard_map/ppermute | solution.py:405
  59.8 2.0 %weight.3 = (f32[2,128,640]{2,1,0:T(8,128)S(1)}, f32[2,128,640]{2,1,0:T(8,128)S(1)}, f32[2,128,384]{2,1,0:T(8,128)S(1)}, f32[2,128,384]{2,1,0:T(8,128)S(1)}) custom-call(s32[2]{0:T(128)S(1)} %pad_add_fusion.place, bf16[384,512]{1,0:T(8,128)(2,1)S(1)} %get-tuple-element.82.nb_ref.near_ref, bf16[384,2048]{1,0:T(8,128)(2,1)S(1)} %bitcast.37, ...), custom_call_target="tpu_custom_call" | custom-call | flops 50331648 | tf_op jit(solution)/shard_map/weight/pallas_call | solution.py:70
  61.8 1.8 %collective-permute-start.15 = (f32[2,128,640]{2,1,0:T(8,128)S(1)}, f32[2,128,640]{2,1,0:T(8,128)S(1)}, u32[]{:S(2)}, u32[]{:S(2)}) collective-permute-start(f32[2,128,640]{2,1,0:T(8,128)S(1)} %get-tuple-element.84), channel_id=1, source_target_pairs={{0,2},{2,0},{4,6},{6,4},{8,10},{10,8},{12,14},{14,12},{1,3},{3,1},... | collective-permute-start | bytes 1966088 | tf_op jit(solution)/shard_map/ppermute | solution.py:257
  63.6 3.5 %output.1 = bf16[384,2048]{1,0:T(8,128)(2,1)} custom-call(bf16[384,512]{1,0:T(8,128)(2,1)S(1)} %get-tuple-element.85.nb_ref.far_ref, bf16[384,512]{1,0:T(8,128)(2,1)S(1)} %get-tuple-element.82.nb_ref.near_ref, bf16[1024,2048]{1,0:T(8,128)(2,1)S(1)} %copy-done.1), custom_call_target="tpu_custom_call" | custom-call | flops 100663296 | tf_op jit(solution)/shard_map/output/pallas_call | solution.py:70
  67.1 1.7 %collective-permute-done.12 = f32[2,128,512]{2,1,0:T(8,128)S(1)} collective-permute-done((f32[2,128,512]{2,1,0:T(8,128)S(1)}, f32[2,128,512]{2,1,0:T(8,128)S(1)}, u32[]{:S(2)}, u32[]{:S(2)}) %collective-permute-start.12) | collective-permute-done | bytes 524320 | tf_op jit(solution)/shard_map/ppermute | solution.py:257
  68.9 0.1 add.113
  69.0 3.6 %collective-permute-start.16 = (f32[128,512]{1,0:T(8,128)S(1)}, f32[128,512]{1,0:T(8,128)S(1)}, u32[]{:S(2)}, u32[]{:S(2)}) collective-permute-start(f32[128,512]{1,0:T(8,128)S(1)} %select_bitcast_fusion.2), channel_id=1, source_target_pairs={{0,4},{2,6},{4,0},{6,2},{8,12},{10,14},{12,8},{14,10},{1,5},{3,7},... | collective-permute-start | bytes 786440 | tf_op jit(solution)/shard_map/ppermute | solution.py:405
  72.6 1.5 %collective-permute-start.14 = (f32[4,128,128]{2,1,0:T(8,128)S(1)}, f32[4,128,128]{2,1,0:T(8,128)S(1)}, u32[]{:S(2)}, u32[]{:S(2)}) collective-permute-start(f32[4,128,128]{2,1,0:T(8,128)S(1)} %add.112), channel_id=1, source_target_pairs={{8,0},{10,2},{12,4},{14,6},{9,1},{11,3},{13,5},{15,7},{24,16},{26,... | collective-permute-start | bytes 786440 | tf_op jit(solution)/shard_map/ppermute | solution.py:405
  74.0 0.3 collective-permute-start.18
  74.4 8.6 %grads.1 = (bf16[384,1024]{1,0:T(8,128)(2,1)}, f32[384,1024]{1,0:T(8,128)S(1)}, f32[384,1024]{1,0:T(8,128)S(1)}) custom-call(s32[2]{0:T(128)S(1)} %pad_add_fusion.place, bf16[384,1024]{1,0:T(8,128)(2,1)S(1)} %bitcast.41, bf16[384,1024]{1,0:T(8,128)(2,1)S(1)} %bitcast.44, bf16[384,1024]{1,0:T(8,128)(2,1)S(1)} %bitcast.48, ...), custom_call_target="tpu_custom_call" | custom-call | flops 169869312 | tf_op jit(solution)/shard_map/grads/pallas_call | solution.py:70
  83.0 0.1 add.115
  83.1 1.3 collective-permute-start.21
  84.4 1.8 %collective-permute-start.20 = (f32[2,128,384]{2,1,0:T(8,128)S(1)}, f32[2,128,384]{2,1,0:T(8,128)S(1)}, u32[]{:S(2)}, u32[]{:S(2)}) collective-permute-start(f32[2,128,384]{2,1,0:T(8,128)S(1)} %get-tuple-element.108), channel_id=1, source_target_pairs={{0,2},{2,0},{4,6},{6,4},{8,10},{10,8},{12,14},{14,12},{1,3},{3,1},... | collective-permute-start | bytes 1179656 | tf_op jit(solution)/shard_map/ppermute | solution.py:257
  86.2 6.1 %collective-permute-start.22 = (f32[128,512]{1,0:T(8,128)S(1)}, f32[128,512]{1,0:T(8,128)S(1)}, u32[]{:S(2)}, u32[]{:S(2)}) collective-permute-start(f32[128,512]{1,0:T(8,128)S(1)} %bitcast_add_fusion.4), channel_id=1, source_target_pairs={{4,12},{6,14},{8,0},{10,2},{5,13},{7,15},{9,1},{11,3},{20,28},{22,... | collective-permute-start | bytes 786440 | tf_op jit(solution)/shard_map/ppermute | solution.py:405
  92.4 0.1 add_select_fusion
  92.4 1.7 %collective-permute-done.18 = f32[2,128,512]{2,1,0:T(8,128)S(1)} collective-permute-done((f32[2,128,512]{2,1,0:T(8,128)S(1)}, f32[2,128,512]{2,1,0:T(8,128)S(1)}, u32[]{:S(2)}, u32[]{:S(2)}) %collective-permute-start.18) | collective-permute-done | bytes 524320 | tf_op jit(solution)/shard_map/ppermute | solution.py:257
  94.1 0.1 add.119
  94.3 3.6 %collective-permute-start.19 = (f32[128,512]{1,0:T(8,128)S(1)}, f32[128,512]{1,0:T(8,128)S(1)}, u32[]{:S(2)}, u32[]{:S(2)}) collective-permute-start(f32[128,512]{1,0:T(8,128)S(1)} %select_bitcast_fusion.1), channel_id=1, source_target_pairs={{0,4},{2,6},{4,0},{6,2},{8,12},{10,14},{12,8},{14,10},{1,5},{3,7},... | collective-permute-start | bytes 786440 | tf_op jit(solution)/shard_map/ppermute | solution.py:405
  97.8 0.3 collective-permute-start.17
  98.1 4.8 %collective-permute-done.21 = f32[2,128,640]{2,1,0:T(8,128)S(1)} collective-permute-done((f32[2,128,640]{2,1,0:T(8,128)S(1)}, f32[2,128,640]{2,1,0:T(8,128)S(1)}, u32[]{:S(2)}, u32[]{:S(2)}) %collective-permute-start.21) | collective-permute-done | bytes 655392 | tf_op jit(solution)/shard_map/ppermute | solution.py:405
  102.9 0.1 select_bitcast_fusion
  103.0 2.7 %collective-permute-done.19 = f32[128,512]{1,0:T(8,128)S(1)} collective-permute-done((f32[128,512]{1,0:T(8,128)S(1)}, f32[128,512]{1,0:T(8,128)S(1)}, u32[]{:S(2)}, u32[]{:S(2)}) %collective-permute-start.19) | collective-permute-done | bytes 262176 | tf_op jit(solution)/shard_map/ppermute | solution.py:405
  105.8 2.6 %collective-permute-start.23 = (f32[128,512]{1,0:T(8,128)S(1)}, f32[128,512]{1,0:T(8,128)S(1)}, u32[]{:S(2)}, u32[]{:S(2)}) collective-permute-start(f32[128,512]{1,0:T(8,128)S(1)} %bitcast_add_fusion.3), channel_id=1, source_target_pairs={{4,12},{6,14},{8,0},{10,2},{5,13},{7,15},{9,1},{11,3},{20,28},{22,... | collective-permute-start | bytes 786440 | tf_op jit(solution)/shard_map/ppermute | solution.py:405
  108.4 3.1 %collective-permute-start.24 = (f32[128,640]{1,0:T(8,128)S(1)}, f32[128,640]{1,0:T(8,128)S(1)}, u32[]{:S(2)}, u32[]{:S(2)}) collective-permute-start(f32[128,640]{1,0:T(8,128)S(1)} %select_bitcast_fusion), channel_id=1, source_target_pairs={{4,8},{6,10},{8,4},{10,6},{5,9},{7,11},{9,5},{11,7},{20,24},{22,26... | collective-permute-start | bytes 983048 | tf_op jit(solution)/shard_map/ppermute | solution.py:405
  111.5 1.3 collective-permute-start.25
  112.8 0.1 fusion.2
  112.9 2.8 %final.1 = (bf16[384,1024]{1,0:T(8,128)(2,1)}, bf16[384,1024]{1,0:T(8,128)(2,1)}) custom-call(s32[2]{0:T(128)S(1)} %pad_add_fusion.place, bf16[384,1024]{1,0:T(8,128)(2,1)S(1)} %bitcast.45, bf16[384,1024]{1,0:T(8,128)(2,1)S(1)} %bitcast.49, f32[384,1024]{1,0:T(8,128)S(1)} %get-tuple-element.96.kl_ref, f32[384,1024]{1,0:T(8,128)S(1)} %get-tuple-element.97.vl_ref, ...), custom_call_target="tpu_custom_call" | custom-call | flops 25165824 | tf_op jit(solution)/shard_map/final/pallas_call | solution.py:70
  115.7 0.1 fusion.1
  115.8 4.4 %collective-permute-done.24 = f32[128,640]{1,0:T(8,128)S(1)} collective-permute-done((f32[128,640]{1,0:T(8,128)S(1)}, f32[128,640]{1,0:T(8,128)S(1)}, u32[]{:S(2)}, u32[]{:S(2)}) %collective-permute-start.24) | collective-permute-done | bytes 327712 | tf_op jit(solution)/shard_map/ppermute | solution.py:405
  120.2 1.1 collective-permute-done.25
  121.3 2.6 %collective-permute-start.26 = (f32[128,384]{1,0:T(8,128)S(1)}, f32[128,384]{1,0:T(8,128)S(1)}, u32[]{:S(2)}, u32[]{:S(2)}) collective-permute-start(f32[128,384]{1,0:T(8,128)S(1)} %select_bitcast_fusion.3), channel_id=1, source_target_pairs={{4,8},{6,10},{8,4},{10,6},{5,9},{7,11},{9,5},{11,7},{20,24},{22,26... | collective-permute-start | bytes 589832 | tf_op jit(solution)/shard_map/ppermute | solution.py:405
  123.9 0.1 bitcast_add_fusion
  124.1 4.8 %collective-permute-done.26 = f32[128,384]{1,0:T(8,128)S(1)} collective-permute-done((f32[128,384]{1,0:T(8,128)S(1)}, f32[128,384]{1,0:T(8,128)S(1)}, u32[]{:S(2)}, u32[]{:S(2)}) %collective-permute-start.26) | collective-permute-done | bytes 196640 | tf_op jit(solution)/shard_map/ppermute | solution.py:405
  128.9 0.9 fusion
  (36 shorter events, 0.6 us)
Async XLA Ops:
  0.6 5.1 %copy-start = (bf16[1,384,2048]{2,1,0:T(8,128)(2,1)S(1)}, bf16[1,384,2048]{2,1,0:T(8,128)(2,1)}, u32[]{:S(2)}) copy-start(bf16[1,384,2048]{2,1,0:T(8,128)(2,1)} %param.9) | copy-start | bytes 4718596
  0.7 1.2 copy-start.3
  2.0 1.1 copy-start.4
  4.2 5.3 %collective-permute-start = (f32[2,128,128]{2,1,0:T(8,128)S(1)}, f32[2,128,128]{2,1,0:T(8,128)S(1)}, u32[]{:S(2)}, u32[]{:S(2)}) collective-permute-start(f32[2,128,128]{2,1,0:T(8,128)S(1)} %get-tuple-element.64), channel_id=1, source_target_pairs={{0,2},{2,0},{4,6},{6,4},{8,10},{10,8},{12,14},{14,12},{1,3},{3,1},... | collective-permute-start | bytes 393224 | tf_op jit(solution)/shard_map/ppermute | solution.py:257
  5.8 7.3 %copy-start.2 = (bf16[1,384,1024]{2,1,0:T(8,128)(2,1)S(1)}, bf16[1,384,1024]{2,1,0:T(8,128)(2,1)}, u32[]{:S(2)}) copy-start(bf16[1,384,1024]{2,1,0:T(8,128)(2,1)} %param.5) | copy-start | bytes 2359300
  6.4 32.6 %collective-permute-start.8 = (f32[384,1024]{1,0:T(8,128)S(1)}, f32[384,1024]{1,0:T(8,128)S(1)}, u32[]{:S(2)}, u32[]{:S(2)}) collective-permute-start(f32[384,1024]{1,0:T(8,128)S(1)} %away.1), channel_id=1, source_target_pairs={{0,1},{1,0},{2,3},{3,2},{4,5},{5,4},{6,7},{7,6},{8,9},{9,8},{10,11... | collective-permute-start | bytes 4718600 | tf_op jit(solution)/shard_map/ppermute | solution.py:263
  6.5 9.0 %collective-permute-start.2 = (f32[2,128,128]{2,1,0:T(8,128)S(1)}, f32[2,128,128]{2,1,0:T(8,128)S(1)}, u32[]{:S(2)}, u32[]{:S(2)}) collective-permute-start(f32[2,128,128]{2,1,0:T(8,128)S(1)} %get-tuple-element.68), channel_id=1, source_target_pairs={{0,2},{2,0},{4,6},{6,4},{8,10},{10,8},{12,14},{14,12},{1,3},{3,1},... | collective-permute-start | bytes 393224 | tf_op jit(solution)/shard_map/ppermute | solution.py:257
  9.5 9.5 %collective-permute-start.1 = (f32[2,128,128]{2,1,0:T(8,128)S(1)}, f32[2,128,128]{2,1,0:T(8,128)S(1)}, u32[]{:S(2)}, u32[]{:S(2)}) collective-permute-start(f32[2,128,128]{2,1,0:T(8,128)S(1)} %add.101), channel_id=1, source_target_pairs={{0,4},{2,6},{4,8},{6,10},{8,12},{10,14},{1,5},{3,7},{5,9},{7,11},{... | collective-permute-start | bytes 393224 | tf_op jit(solution)/shard_map/ppermute | solution.py:219
  13.0 7.9 %copy-start.1 = (bf16[1024,2048]{1,0:T(8,128)(2,1)S(1)}, bf16[1024,2048]{1,0:T(8,128)(2,1)}, u32[]{:S(2)}) copy-start(bf16[1024,2048]{1,0:T(8,128)(2,1)} %w_ref.3) | copy-start | bytes 12582916
  15.5 11.1 %collective-permute-start.4 = (f32[2,128,128]{2,1,0:T(8,128)S(1)}, f32[2,128,128]{2,1,0:T(8,128)S(1)}, u32[]{:S(2)}, u32[]{:S(2)}) collective-permute-start(f32[2,128,128]{2,1,0:T(8,128)S(1)} %add.103), channel_id=1, source_target_pairs={{0,4},{2,6},{4,8},{6,10},{8,12},{10,14},{1,5},{3,7},{5,9},{7,11},{... | collective-permute-start | bytes 393224 | tf_op jit(solution)/shard_map/ppermute | solution.py:219
  19.1 10.0 %collective-permute-start.3 = (f32[2,128,128]{2,1,0:T(8,128)S(1)}, f32[2,128,128]{2,1,0:T(8,128)S(1)}, u32[]{:S(2)}, u32[]{:S(2)}) collective-permute-start(f32[2,128,128]{2,1,0:T(8,128)S(1)} %add.102), channel_id=1, source_target_pairs={{0,8},{2,10},{4,12},{6,14},{1,9},{3,11},{5,13},{7,15},{16,24},{18,... | collective-permute-start | bytes 393224 | tf_op jit(solution)/shard_map/ppermute | solution.py:219
  26.7 4.1 %collective-permute-start.5 = (f32[2,128,128]{2,1,0:T(8,128)S(1)}, f32[2,128,128]{2,1,0:T(8,128)S(1)}, u32[]{:S(2)}, u32[]{:S(2)}) collective-permute-start(f32[2,128,128]{2,1,0:T(8,128)S(1)} %add.106), channel_id=1, source_target_pairs={{0,8},{2,10},{4,12},{6,14},{1,9},{3,11},{5,13},{7,15},{16,24},{18,... | collective-permute-start | bytes 393224 | tf_op jit(solution)/shard_map/ppermute | solution.py:219
  29.1 5.0 %collective-permute-start.6 = (f32[2,128,128]{2,1,0:T(8,128)S(1)}, f32[2,128,128]{2,1,0:T(8,128)S(1)}, u32[]{:S(2)}, u32[]{:S(2)}) collective-permute-start(f32[2,128,128]{2,1,0:T(8,128)S(1)} %get-tuple-element.73), channel_id=1, source_target_pairs={{0,2},{2,0},{4,6},{6,4},{8,10},{10,8},{12,14},{14,12},{1,3},{3,1},... | collective-permute-start | bytes 393224 | tf_op jit(solution)/shard_map/ppermute | solution.py:229
  36.7 2.4 %collective-permute-start.7 = (f32[384,512]{1,0:T(8,128)S(1)}, f32[384,512]{1,0:T(8,128)S(1)}, u32[]{:S(2)}, u32[]{:S(2)}) collective-permute-start(f32[384,512]{1,0:T(8,128)S(1)} %get-tuple-element.75), channel_id=1, source_target_pairs={{0,1},{1,0},{2,3},{3,2},{4,5},{5,4},{6,7},{7,6},{8,9},{9,8},{10,11... | collective-permute-start | bytes 2359304 | tf_op jit(solution)/shard_map/ppermute | solution.py:289
  36.8 5.9 %collective-permute-start.9 = (f32[2,128,128]{2,1,0:T(8,128)S(1)}, f32[2,128,128]{2,1,0:T(8,128)S(1)}, u32[]{:S(2)}, u32[]{:S(2)}) collective-permute-start(f32[2,128,128]{2,1,0:T(8,128)S(1)} %get-tuple-element.119), channel_id=1, source_target_pairs={{0,2},{2,0},{4,6},{6,4},{8,10},{10,8},{12,14},{14,12},{1,3},{3,1},... | collective-permute-start | bytes 393224 | tf_op jit(solution)/shard_map/ppermute | solution.py:229
  45.2 14.5 %collective-permute-start.11 = (f32[384,512]{1,0:T(8,128)S(1)}, f32[384,512]{1,0:T(8,128)S(1)}, u32[]{:S(2)}, u32[]{:S(2)}) collective-permute-start(f32[384,512]{1,0:T(8,128)S(1)} %get-tuple-element.83), channel_id=1, source_target_pairs={{0,1},{1,0},{2,3},{3,2},{4,5},{5,4},{6,7},{7,6},{8,9},{9,8},{10,11... | collective-permute-start | bytes 2359304 | tf_op jit(solution)/shard_map/ppermute | solution.py:302
  45.3 8.7 %collective-permute-start.10 = (f32[4,128,128]{2,1,0:T(8,128)S(1)}, f32[4,128,128]{2,1,0:T(8,128)S(1)}, u32[]{:S(2)}, u32[]{:S(2)}) collective-permute-start(f32[4,128,128]{2,1,0:T(8,128)S(1)} %get-tuple-element.81), channel_id=1, source_target_pairs={{0,2},{2,0},{4,6},{6,4},{8,10},{10,8},{12,14},{14,12},{1,3},{3,1},... | collective-permute-start | bytes 786440 | tf_op jit(solution)/shard_map/ppermute | solution.py:257
  54.0 14.8 %collective-permute-start.12 = (f32[2,128,512]{2,1,0:T(8,128)S(1)}, f32[2,128,512]{2,1,0:T(8,128)S(1)}, u32[]{:S(2)}, u32[]{:S(2)}) collective-permute-start(f32[2,128,512]{2,1,0:T(8,128)S(1)} %get-tuple-element.89), channel_id=1, source_target_pairs={{0,2},{2,0},{4,6},{6,4},{8,10},{10,8},{12,14},{14,12},{1,3},{3,1},... | collective-permute-start | bytes 1572872 | tf_op jit(solution)/shard_map/ppermute | solution.py:257
  55.6 11.4 %collective-permute-start.13 = (f32[4,128,128]{2,1,0:T(8,128)S(1)}, f32[4,128,128]{2,1,0:T(8,128)S(1)}, u32[]{:S(2)}, u32[]{:S(2)}) collective-permute-start(f32[4,128,128]{2,1,0:T(8,128)S(1)} %add.111), channel_id=1, source_target_pairs={{4,0},{6,2},{8,4},{10,6},{12,8},{14,10},{5,1},{7,3},{9,5},{11,7},{... | collective-permute-start | bytes 786440 | tf_op jit(solution)/shard_map/ppermute | solution.py:405
  61.8 21.2 %collective-permute-start.15 = (f32[2,128,640]{2,1,0:T(8,128)S(1)}, f32[2,128,640]{2,1,0:T(8,128)S(1)}, u32[]{:S(2)}, u32[]{:S(2)}) collective-permute-start(f32[2,128,640]{2,1,0:T(8,128)S(1)} %get-tuple-element.84), channel_id=1, source_target_pairs={{0,2},{2,0},{4,6},{6,4},{8,10},{10,8},{12,14},{14,12},{1,3},{3,1},... | collective-permute-start | bytes 1966088 | tf_op jit(solution)/shard_map/ppermute | solution.py:257
  69.0 13.9 %collective-permute-start.16 = (f32[128,512]{1,0:T(8,128)S(1)}, f32[128,512]{1,0:T(8,128)S(1)}, u32[]{:S(2)}, u32[]{:S(2)}) collective-permute-start(f32[128,512]{1,0:T(8,128)S(1)} %select_bitcast_fusion.2), channel_id=1, source_target_pairs={{0,4},{2,6},{4,0},{6,2},{8,12},{10,14},{12,8},{14,10},{1,5},{3,7},... | collective-permute-start | bytes 786440 | tf_op jit(solution)/shard_map/ppermute | solution.py:405
  72.6 19.8 %collective-permute-start.14 = (f32[4,128,128]{2,1,0:T(8,128)S(1)}, f32[4,128,128]{2,1,0:T(8,128)S(1)}, u32[]{:S(2)}, u32[]{:S(2)}) collective-permute-start(f32[4,128,128]{2,1,0:T(8,128)S(1)} %add.112), channel_id=1, source_target_pairs={{8,0},{10,2},{12,4},{14,6},{9,1},{11,3},{13,5},{15,7},{24,16},{26,... | collective-permute-start | bytes 786440 | tf_op jit(solution)/shard_map/ppermute | solution.py:405
  74.0 20.1 %collective-permute-start.18 = (f32[2,128,512]{2,1,0:T(8,128)S(1)}, f32[2,128,512]{2,1,0:T(8,128)S(1)}, u32[]{:S(2)}, u32[]{:S(2)}) collective-permute-start(f32[2,128,512]{2,1,0:T(8,128)S(1)} %get-tuple-element.105), channel_id=1, source_target_pairs={{0,2},{2,0},{4,6},{6,4},{8,10},{10,8},{12,14},{14,12},{1,3},{3,1},... | collective-permute-start | bytes 1572872 | tf_op jit(solution)/shard_map/ppermute | solution.py:257
  83.1 19.8 %collective-permute-start.21 = (f32[2,128,640]{2,1,0:T(8,128)S(1)}, f32[2,128,640]{2,1,0:T(8,128)S(1)}, u32[]{:S(2)}, u32[]{:S(2)}) collective-permute-start(f32[2,128,640]{2,1,0:T(8,128)S(1)} %add.115), channel_id=1, source_target_pairs={{0,4},{2,6},{12,8},{14,10},{1,5},{3,7},{13,9},{15,11},{16,20},{18,... | collective-permute-start | bytes 1966088 | tf_op jit(solution)/shard_map/ppermute | solution.py:405
  84.4 18.6 %collective-permute-start.20 = (f32[2,128,384]{2,1,0:T(8,128)S(1)}, f32[2,128,384]{2,1,0:T(8,128)S(1)}, u32[]{:S(2)}, u32[]{:S(2)}) collective-permute-start(f32[2,128,384]{2,1,0:T(8,128)S(1)} %get-tuple-element.108), channel_id=1, source_target_pairs={{0,2},{2,0},{4,6},{6,4},{8,10},{10,8},{12,14},{14,12},{1,3},{3,1},... | collective-permute-start | bytes 1179656 | tf_op jit(solution)/shard_map/ppermute | solution.py:257
  86.2 11.9 %collective-permute-start.22 = (f32[128,512]{1,0:T(8,128)S(1)}, f32[128,512]{1,0:T(8,128)S(1)}, u32[]{:S(2)}, u32[]{:S(2)}) collective-permute-start(f32[128,512]{1,0:T(8,128)S(1)} %bitcast_add_fusion.4), channel_id=1, source_target_pairs={{4,12},{6,14},{8,0},{10,2},{5,13},{7,15},{9,1},{11,3},{20,28},{22,... | collective-permute-start | bytes 786440 | tf_op jit(solution)/shard_map/ppermute | solution.py:405
  94.3 11.4 %collective-permute-start.19 = (f32[128,512]{1,0:T(8,128)S(1)}, f32[128,512]{1,0:T(8,128)S(1)}, u32[]{:S(2)}, u32[]{:S(2)}) collective-permute-start(f32[128,512]{1,0:T(8,128)S(1)} %select_bitcast_fusion.1), channel_id=1, source_target_pairs={{0,4},{2,6},{4,0},{6,2},{8,12},{10,14},{12,8},{14,10},{1,5},{3,7},... | collective-permute-start | bytes 786440 | tf_op jit(solution)/shard_map/ppermute | solution.py:405
  97.8 15.1 %collective-permute-start.17 = (f32[4,128,128]{2,1,0:T(8,128)S(1)}, f32[4,128,128]{2,1,0:T(8,128)S(1)}, u32[]{:S(2)}, u32[]{:S(2)}) collective-permute-start(f32[4,128,128]{2,1,0:T(8,128)S(1)} %get-tuple-element.117), channel_id=1, source_target_pairs={{0,2},{2,0},{4,6},{6,4},{8,10},{10,8},{12,14},{14,12},{1,3},{3,1},... | collective-permute-start | bytes 786440 | tf_op jit(solution)/shard_map/ppermute | solution.py:257
  105.8 10.0 %collective-permute-start.23 = (f32[128,512]{1,0:T(8,128)S(1)}, f32[128,512]{1,0:T(8,128)S(1)}, u32[]{:S(2)}, u32[]{:S(2)}) collective-permute-start(f32[128,512]{1,0:T(8,128)S(1)} %bitcast_add_fusion.3), channel_id=1, source_target_pairs={{4,12},{6,14},{8,0},{10,2},{5,13},{7,15},{9,1},{11,3},{20,28},{22,... | collective-permute-start | bytes 786440 | tf_op jit(solution)/shard_map/ppermute | solution.py:405
  108.4 11.8 %collective-permute-start.24 = (f32[128,640]{1,0:T(8,128)S(1)}, f32[128,640]{1,0:T(8,128)S(1)}, u32[]{:S(2)}, u32[]{:S(2)}) collective-permute-start(f32[128,640]{1,0:T(8,128)S(1)} %select_bitcast_fusion), channel_id=1, source_target_pairs={{4,8},{6,10},{8,4},{10,6},{5,9},{7,11},{9,5},{11,7},{20,24},{22,26... | collective-permute-start | bytes 983048 | tf_op jit(solution)/shard_map/ppermute | solution.py:405
  111.5 9.8 %collective-permute-start.25 = (f32[2,128,384]{2,1,0:T(8,128)S(1)}, f32[2,128,384]{2,1,0:T(8,128)S(1)}, u32[]{:S(2)}, u32[]{:S(2)}) collective-permute-start(f32[2,128,384]{2,1,0:T(8,128)S(1)} %add.122), channel_id=1, source_target_pairs={{0,4},{2,6},{12,8},{14,10},{1,5},{3,7},{13,9},{15,11},{16,20},{18,... | collective-permute-start | bytes 1179656 | tf_op jit(solution)/shard_map/ppermute | solution.py:405
  121.3 7.6 %collective-permute-start.26 = (f32[128,384]{1,0:T(8,128)S(1)}, f32[128,384]{1,0:T(8,128)S(1)}, u32[]{:S(2)}, u32[]{:S(2)}) collective-permute-start(f32[128,384]{1,0:T(8,128)S(1)} %select_bitcast_fusion.3), channel_id=1, source_target_pairs={{4,8},{6,10},{8,4},{10,6},{5,9},{7,11},{9,5},{11,7},{20,24},{22,26... | collective-permute-start | bytes 589832 | tf_op jit(solution)/shard_map/ppermute | solution.py:405

commit v9 on v8

--- a/solution.py
+++ b/solution.py
@@ -302,7 +302,7 @@
         nbo = lax.ppermute(near32, "dp", swap)
         (near0_keep, near0_send), (near1_keep, near1_send) = product(after(near, received), nbo, WIDTHS[1])
         near0_got = trade(near0_send)
-        far0_got = trade(after(chunks[0][1], received))
+        far0_got = trade(after(chunks[0][1], near_other))
         back1 = hop(total, BACK)
     def gradients(far_att):
         return call(
@@ -374,10 +374,11 @@
     far1_in = after(far1_in, near1)
     far1_half = jnp.where(lower, far1[1], far1[0]) + far1_in
     far1_end = hop(far1_half, OUTWARD)
-    key_grad, value_grad = finish(own, after(other, far1_half))
-    near1_in = after(near1_in, key_grad, near0_end)
+    near1_in = after(near1_in, far1_half)
     near1_half = jnp.where(lower, near1[1] + near1_in[1], near1[0] + near1_in[0])
     near1_end = hop(near1_half, ACROSS)
+    key_grad, value_grad = finish(own, after(other, near1_half))
+    near0_end, far1_end = after(near0_end, near1_half), after(far1_end, near1_half)
 
     far_parts = [
         (jnp.where(lower, base[0], base[1]) + got) + end

time: 130 us -> 125 us (0.962); the launches traced: 130 us -> 123 us
  waiting for transfers between devices: 40.8 us -> 32 us
  starting transfers between devices: 52.9 us -> 54.4 us
    ppermute x10, waiting for transfers between devices: 17.7 us -> 10.7 us  [hop(): lax.ppermute(block, 'seq', [(2 * a + i, 2 * b + i) for a, b in links for...]
    ppermute x10, starting transfers between devices: 29.7 us -> 32.9 us  [hop(): lax.ppermute(block, 'seq', [(2 * a + i, 2 * b + i) for a, b in links for...]
    ppermute x8, waiting for transfers between devices: 13 us -> 11.2 us  [trade(): return lax.ppermute(send, 'seq', [(s, s ^ 1) for s in range(count)])]
    ppermute x8, starting transfers between devices: 9.58 us -> 7.9 us  [trade(): return lax.ppermute(send, 'seq', [(s, s ^ 1) for s in range(count)])]
  transfers between devices with their start and end apart: 27 -> 27, of which waited for: 14 -> 11; matrix products, arithmetic and copies ran while one was open for 1% -> 1% of each run, Pallas kernels for 21% -> 22%
where the time goes in v9:
time: 125 us; the launch traced here: 123 us
  starting transfers between devices  54.4 us (44%)
  waiting for transfers between devices  32 us (26%)
  Pallas kernels  30.4 us (24%)
  local copies, waits for them, and re-layouts  2.38 us (2%)
  other arithmetic  2.25 us (2%)
    ppermute x10, starting transfers between devices, hop(): lax.ppermute(block, 'seq', [(2 * a + i, 2 * b + i) for a, b in links for...  32.9 us
    pallas_call x11, Pallas kernels, call(): pl.pallas_call(body, out_shape=tuple(out_shapes), in_specs=specs, out_spe...  30.4 us
    ppermute x8, waiting for transfers between devices, trade(): return lax.ppermute(send, 'seq', [(s, s ^ 1) for s in range(count)])  11.2 us
    ppermute x10, waiting for transfers between devices, hop(): lax.ppermute(block, 'seq', [(2 * a + i, 2 * b + i) for a, b in links for...  10.7 us
    ppermute x4, starting transfers between devices, exclusive(): got = lax.ppermute(total, 'seq', links(step))  10.1 us
    ppermute x8, starting transfers between devices, trade(): return lax.ppermute(send, 'seq', [(s, s ^ 1) for s in range(count)])  7.9 us
    ppermute x2, waiting for transfers between devices, exclusive(): results.append((mine, lax.ppermute(theirs, 'seq', swap)))  5.14 us
    ppermute x4, waiting for transfers between devices, exclusive(): got = lax.ppermute(total, 'seq', links(step))  4.37 us
  transfers between devices with their start and end apart: 27, of which 11 were waited for; matrix products, arithmetic and copies ran while one was open for 1% of the time, Pallas kernels for 22%

profile of v9, /device:TPU:12, one launch (start us, length us, event | category | flops | bytes accessed | tf_op | source)
XLA Modules:
  0.0 122.5 jit_solution(6239883800400032967)
XLA Ops:
  0.7 0.1 pad_add_fusion.place
  0.7 1.2 %copy-done.3 = bf16[1,384,1024]{2,1,0:T(8,128)(2,1)S(1)} copy-done((bf16[1,384,1024]{2,1,0:T(8,128)(2,1)S(1)}, bf16[1,384,1024]{2,1,0:T(8,128)(2,1)}, u32[]{:S(2)}) %copy-start.3) | copy-done | bytes 786456
  2.0 1.1 copy-done.4
  3.1 1.1 state.1
  4.2 1.6 %collective-permute-start = (f32[2,128,128]{2,1,0:T(8,128)S(1)}, f32[2,128,128]{2,1,0:T(8,128)S(1)}, u32[]{:S(2)}, u32[]{:S(2)}) collective-permute-start(f32[2,128,128]{2,1,0:T(8,128)S(1)} %get-tuple-element.66), channel_id=1, source_target_pairs={{0,2},{2,0},{4,6},{6,4},{8,10},{10,8},{12,14},{14,12},{1,3},{3,1},... | collective-permute-start | bytes 393224 | tf_op jit(solution)/shard_map/ppermute | solution.py:257
  5.8 0.6 away.1
  6.4 0.1 collective-permute-start.8
  6.5 0.6 collective-permute-start.2
  7.1 2.4 %collective-permute-done = f32[2,128,128]{2,1,0:T(8,128)S(1)} collective-permute-done((f32[2,128,128]{2,1,0:T(8,128)S(1)}, f32[2,128,128]{2,1,0:T(8,128)S(1)}, u32[]{:S(2)}, u32[]{:S(2)}) %collective-permute-start) | collective-permute-done | bytes 131104 | tf_op jit(solution)/shard_map/ppermute | solution.py:257
  9.5 3.5 %collective-permute-start.1 = (f32[2,128,128]{2,1,0:T(8,128)S(1)}, f32[2,128,128]{2,1,0:T(8,128)S(1)}, u32[]{:S(2)}, u32[]{:S(2)}) collective-permute-start(f32[2,128,128]{2,1,0:T(8,128)S(1)} %add.101), channel_id=1, source_target_pairs={{0,4},{2,6},{4,8},{6,10},{8,12},{10,14},{1,5},{3,7},{5,9},{7,11},{... | collective-permute-start | bytes 393224 | tf_op jit(solution)/shard_map/ppermute | solution.py:219
  13.1 2.4 %local.1.att_ref = f32[384,1024]{1,0:T(8,128)S(1)} custom-call(bf16[384,1024]{1,0:T(8,128)(2,1)S(1)} %bitcast.38, bf16[384,1024]{1,0:T(8,128)(2,1)S(1)} %bitcast.43, bf16[384,1024]{1,0:T(8,128)(2,1)S(1)} %bitcast.47), custom_call_target="tpu_custom_call" | custom-call | flops 56623104 | tf_op jit(solution)/shard_map/local/pallas_call | solution.py:70
  15.5 3.5 %collective-permute-start.4 = (f32[2,128,128]{2,1,0:T(8,128)S(1)}, f32[2,128,128]{2,1,0:T(8,128)S(1)}, u32[]{:S(2)}, u32[]{:S(2)}) collective-permute-start(f32[2,128,128]{2,1,0:T(8,128)S(1)} %add.103), channel_id=1, source_target_pairs={{0,4},{2,6},{4,8},{6,10},{8,12},{10,14},{1,5},{3,7},{5,9},{7,11},{... | collective-permute-start | bytes 393224 | tf_op jit(solution)/shard_map/ppermute | solution.py:219
  19.1 1.9 %collective-permute-start.3 = (f32[2,128,128]{2,1,0:T(8,128)S(1)}, f32[2,128,128]{2,1,0:T(8,128)S(1)}, u32[]{:S(2)}, u32[]{:S(2)}) collective-permute-start(f32[2,128,128]{2,1,0:T(8,128)S(1)} %add.102), channel_id=1, source_target_pairs={{0,8},{2,10},{4,12},{6,14},{1,9},{3,11},{5,13},{7,15},{16,24},{18,... | collective-permute-start | bytes 393224 | tf_op jit(solution)/shard_map/ppermute | solution.py:219
  20.9 2.4 %d_normed.1.dn_ref = f32[384,1024]{1,0:T(8,128)S(1)} custom-call(bf16[384,2048]{1,0:T(8,128)(2,1)S(1)} %bitcast.35, bf16[1024,2048]{1,0:T(8,128)(2,1)S(1)} %copy-done.1), custom_call_target="tpu_custom_call" | custom-call | flops 100663296 | tf_op jit(solution)/shard_map/d_normed/pallas_call | solution.py:70
  23.4 3.3 %collective-permute-done.4 = f32[2,128,128]{2,1,0:T(8,128)S(1)} collective-permute-done((f32[2,128,128]{2,1,0:T(8,128)S(1)}, f32[2,128,128]{2,1,0:T(8,128)S(1)}, u32[]{:S(2)}, u32[]{:S(2)}) %collective-permute-start.4) | collective-permute-done | bytes 131104 | tf_op jit(solution)/shard_map/ppermute | solution.py:219
  26.7 1.3 %collective-permute-start.5 = (f32[2,128,128]{2,1,0:T(8,128)S(1)}, f32[2,128,128]{2,1,0:T(8,128)S(1)}, u32[]{:S(2)}, u32[]{:S(2)}) collective-permute-start(f32[2,128,128]{2,1,0:T(8,128)S(1)} %add.106), channel_id=1, source_target_pairs={{0,8},{2,10},{4,12},{6,14},{1,9},{3,11},{5,13},{7,15},{16,24},{18,... | collective-permute-start | bytes 393224 | tf_op jit(solution)/shard_map/ppermute | solution.py:219
  28.0 1.1 collective-permute-done.3
  29.1 1.6 %collective-permute-start.6 = (f32[2,128,128]{2,1,0:T(8,128)S(1)}, f32[2,128,128]{2,1,0:T(8,128)S(1)}, u32[]{:S(2)}, u32[]{:S(2)}) collective-permute-start(f32[2,128,128]{2,1,0:T(8,128)S(1)} %get-tuple-element.75), channel_id=1, source_target_pairs={{0,2},{2,0},{4,6},{6,4},{8,10},{10,8},{12,14},{14,12},{1,3},{3,1},... | collective-permute-start | bytes 393224 | tf_op jit(solution)/shard_map/ppermute | solution.py:229
  30.8 3.4 %collective-permute-done.6.other_ref.refs_2_ = f32[2,128,128]{2,1,0:T(8,128)S(1)} collective-permute-done((f32[2,128,128]{2,1,0:T(8,128)S(1)}, f32[2,128,128]{2,1,0:T(8,128)S(1)}, u32[]{:S(2)}, u32[]{:S(2)}) %collective-permute-start.6) | collective-permute-done | bytes 131104 | tf_op jit(solution)/shard_map/ppermute | solution.py:229
  34.1 2.5 %norm_far.1 = (bf16[384,512]{1,0:T(8,128)(2,1)S(1)}, f32[384,512]{1,0:T(8,128)S(1)}, bf16[384,512]{1,0:T(8,128)(2,1)S(1)}, f32[2,128,128]{2,1,0:T(8,128)S(1)}, f32[2,128,128]{2,1,0:T(8,128)S(1)}) custom-call(s32[2]{0:T(128)S(1)} %pad_add_fusion.place, bf16[384,1024]{1,0:T(8,128)(2,1)S(1)} %bitcast.39, f32[384,1024]{1,0:T(8,128)S(1)} %local.1.att_ref, ...), custom_call_target="tpu_custom_call" | custom-call | flops 6291456 | tf_op jit(solution)/shard_map/norm_far/pallas_call | solution.py:70
  36.7 0.1 collective-permute-start.7
  36.8 1.6 %collective-permute-start.9 = (f32[2,128,128]{2,1,0:T(8,128)S(1)}, f32[2,128,128]{2,1,0:T(8,128)S(1)}, u32[]{:S(2)}, u32[]{:S(2)}) collective-permute-start(f32[2,128,128]{2,1,0:T(8,128)S(1)} %get-tuple-element.123), channel_id=1, source_target_pairs={{0,2},{2,0},{4,6},{6,4},{8,10},{10,8},{12,14},{14,12},{1,3},{3,1},... | collective-permute-start | bytes 393224 | tf_op jit(solution)/shard_map/ppermute | solution.py:229
  38.4 0.6 collective-permute-done.7.nbo_ref
  39.0 1.9 %weight.2 = (f32[2,128,512]{2,1,0:T(8,128)S(1)}, f32[2,128,512]{2,1,0:T(8,128)S(1)}, f32[2,128,512]{2,1,0:T(8,128)S(1)}, f32[2,128,512]{2,1,0:T(8,128)S(1)}) custom-call(s32[2]{0:T(128)S(1)} %pad_add_fusion.place, bf16[384,512]{1,0:T(8,128)(2,1)S(1)} %get-tuple-element.87.nb_ref.far_ref, bf16[384,2048]{1,0:T(8,128)(2,1)S(1)} %bitcast.36, ...), custom_call_target="tpu_custom_call" | custom-call | flops 50331648 | tf_op jit(solution)/shard_map/weight/pallas_call | solution.py:70
  40.9 1.8 %collective-permute-done.9.other_ref.refs_5_ = f32[2,128,128]{2,1,0:T(8,128)S(1)} collective-permute-done((f32[2,128,128]{2,1,0:T(8,128)S(1)}, f32[2,128,128]{2,1,0:T(8,128)S(1)}, u32[]{:S(2)}, u32[]{:S(2)}) %collective-permute-start.9) | collective-permute-done | bytes 131104 | tf_op jit(solution)/shard_map/ppermute | solution.py:229
  42.7 2.6 %norm_near.1 = (bf16[384,512]{1,0:T(8,128)(2,1)S(1)}, f32[384,512]{1,0:T(8,128)S(1)}, bf16[384,512]{1,0:T(8,128)(2,1)S(1)}, f32[4,128,128]{2,1,0:T(8,128)S(1)}, f32[4,128,128]{2,1,0:T(8,128)S(1)}) custom-call(s32[2]{0:T(128)S(1)} %pad_add_fusion.place, bf16[384,1024]{1,0:T(8,128)(2,1)S(1)} %bitcast.40, f32[384,1024]{1,0:T(8,128)S(1)} %local.1.att_ref, ...), custom_call_target="tpu_custom_call" | custom-call | flops 402653184 | tf_op jit(solution)/shard_map/norm_near/pallas_call | solution.py:70
  45.2 0.1 collective-permute-start.11
  45.3 1.6 %collective-permute-start.10 = (f32[4,128,128]{2,1,0:T(8,128)S(1)}, f32[4,128,128]{2,1,0:T(8,128)S(1)}, u32[]{:S(2)}, u32[]{:S(2)}) collective-permute-start(f32[4,128,128]{2,1,0:T(8,128)S(1)} %get-tuple-element.83), channel_id=1, source_target_pairs={{0,2},{2,0},{4,6},{6,4},{8,10},{10,8},{12,14},{14,12},{1,3},{3,1},... | collective-permute-start | bytes 786440 | tf_op jit(solution)/shard_map/ppermute | solution.py:257
  46.9 0.5 collective-permute-start.12
  47.4 7.1 %collective-permute-done.10 = f32[4,128,128]{2,1,0:T(8,128)S(1)} collective-permute-done((f32[4,128,128]{2,1,0:T(8,128)S(1)}, f32[4,128,128]{2,1,0:T(8,128)S(1)}, u32[]{:S(2)}, u32[]{:S(2)}) %collective-permute-start.10) | collective-permute-done | bytes 262176 | tf_op jit(solution)/shard_map/ppermute | solution.py:257
  54.5 5.4 %collective-permute-start.13 = (f32[4,128,128]{2,1,0:T(8,128)S(1)}, f32[4,128,128]{2,1,0:T(8,128)S(1)}, u32[]{:S(2)}, u32[]{:S(2)}) collective-permute-start(f32[4,128,128]{2,1,0:T(8,128)S(1)} %add.111), channel_id=1, source_target_pairs={{4,0},{6,2},{8,4},{10,6},{12,8},{14,10},{5,1},{7,3},{9,5},{11,7},{... | collective-permute-start | bytes 786440 | tf_op jit(solution)/shard_map/ppermute | solution.py:406
  59.9 2.0 %weight.3 = (f32[2,128,640]{2,1,0:T(8,128)S(1)}, f32[2,128,640]{2,1,0:T(8,128)S(1)}, f32[2,128,384]{2,1,0:T(8,128)S(1)}, f32[2,128,384]{2,1,0:T(8,128)S(1)}) custom-call(s32[2]{0:T(128)S(1)} %pad_add_fusion.place, bf16[384,512]{1,0:T(8,128)(2,1)S(1)} %get-tuple-element.84.nb_ref.near_ref, bf16[384,2048]{1,0:T(8,128)(2,1)S(1)} %bitcast.37, ...), custom_call_target="tpu_custom_call" | custom-call | flops 50331648 | tf_op jit(solution)/shard_map/weight/pallas_call | solution.py:70
  62.0 0.3 collective-permute-start.15
  62.3 3.5 %output.1 = bf16[384,2048]{1,0:T(8,128)(2,1)} custom-call(bf16[384,512]{1,0:T(8,128)(2,1)S(1)} %get-tuple-element.87.nb_ref.far_ref, bf16[384,512]{1,0:T(8,128)(2,1)S(1)} %get-tuple-element.84.nb_ref.near_ref, bf16[1024,2048]{1,0:T(8,128)(2,1)S(1)} %copy-done.1), custom_call_target="tpu_custom_call" | custom-call | flops 100663296 | tf_op jit(solution)/shard_map/output/pallas_call | solution.py:70
  65.8 0.1 add.113
  66.0 3.4 %collective-permute-start.16 = (f32[128,512]{1,0:T(8,128)S(1)}, f32[128,512]{1,0:T(8,128)S(1)}, u32[]{:S(2)}, u32[]{:S(2)}) collective-permute-start(f32[128,512]{1,0:T(8,128)S(1)} %select_bitcast_fusion.2), channel_id=1, source_target_pairs={{0,4},{2,6},{4,0},{6,2},{8,12},{10,14},{12,8},{14,10},{1,5},{3,7},... | collective-permute-start | bytes 786440 | tf_op jit(solution)/shard_map/ppermute | solution.py:406
  69.4 1.5 %collective-permute-start.14 = (f32[4,128,128]{2,1,0:T(8,128)S(1)}, f32[4,128,128]{2,1,0:T(8,128)S(1)}, u32[]{:S(2)}, u32[]{:S(2)}) collective-permute-start(f32[4,128,128]{2,1,0:T(8,128)S(1)} %add.112), channel_id=1, source_target_pairs={{8,0},{10,2},{12,4},{14,6},{9,1},{11,3},{13,5},{15,7},{24,16},{26,... | collective-permute-start | bytes 786440 | tf_op jit(solution)/shard_map/ppermute | solution.py:406
  70.9 0.3 collective-permute-start.20
  71.2 8.6 %grads.1 = (bf16[384,1024]{1,0:T(8,128)(2,1)}, f32[384,1024]{1,0:T(8,128)S(1)}, f32[384,1024]{1,0:T(8,128)S(1)}) custom-call(s32[2]{0:T(128)S(1)} %pad_add_fusion.place, bf16[384,1024]{1,0:T(8,128)(2,1)S(1)} %bitcast.41, bf16[384,1024]{1,0:T(8,128)(2,1)S(1)} %bitcast.44, bf16[384,1024]{1,0:T(8,128)(2,1)S(1)} %bitcast.48, ...), custom_call_target="tpu_custom_call" | custom-call | flops 169869312 | tf_op jit(solution)/shard_map/grads/pallas_call | solution.py:70
  79.8 0.1 bitcast_add_fusion.4
  79.8 0.1 add.115
  79.9 1.3 %collective-permute-start.19 = (f32[2,128,640]{2,1,0:T(8,128)S(1)}, f32[2,128,640]{2,1,0:T(8,128)S(1)}, u32[]{:S(2)}, u32[]{:S(2)}) collective-permute-start(f32[2,128,640]{2,1,0:T(8,128)S(1)} %add.115), channel_id=1, source_target_pairs={{0,4},{2,6},{12,8},{14,10},{1,5},{3,7},{13,9},{15,11},{16,20},{18,... | collective-permute-start | bytes 1966088 | tf_op jit(solution)/shard_map/ppermute | solution.py:406
  81.2 1.8 %collective-permute-start.18 = (f32[2,128,384]{2,1,0:T(8,128)S(1)}, f32[2,128,384]{2,1,0:T(8,128)S(1)}, u32[]{:S(2)}, u32[]{:S(2)}) collective-permute-start(f32[2,128,384]{2,1,0:T(8,128)S(1)} %get-tuple-element.106), channel_id=1, source_target_pairs={{0,2},{2,0},{4,6},{6,4},{8,10},{10,8},{12,14},{14,12},{1,3},{3,1},... | collective-permute-start | bytes 1179656 | tf_op jit(solution)/shard_map/ppermute | solution.py:257
  83.1 6.1 %collective-permute-start.21 = (f32[128,512]{1,0:T(8,128)S(1)}, f32[128,512]{1,0:T(8,128)S(1)}, u32[]{:S(2)}, u32[]{:S(2)}) collective-permute-start(f32[128,512]{1,0:T(8,128)S(1)} %bitcast_add_fusion.4), channel_id=1, source_target_pairs={{4,12},{6,14},{8,0},{10,2},{5,13},{7,15},{9,1},{11,3},{20,28},{22,... | collective-permute-start | bytes 786440 | tf_op jit(solution)/shard_map/ppermute | solution.py:406
  89.2 0.1 add_select_fusion
  89.3 1.7 %collective-permute-done.20 = f32[2,128,512]{2,1,0:T(8,128)S(1)} collective-permute-done((f32[2,128,512]{2,1,0:T(8,128)S(1)}, f32[2,128,512]{2,1,0:T(8,128)S(1)}, u32[]{:S(2)}, u32[]{:S(2)}) %collective-permute-start.20) | collective-permute-done | bytes 524320 | tf_op jit(solution)/shard_map/ppermute | solution.py:257
  91.0 0.1 add.119
  91.1 3.6 %collective-permute-start.23 = (f32[128,512]{1,0:T(8,128)S(1)}, f32[128,512]{1,0:T(8,128)S(1)}, u32[]{:S(2)}, u32[]{:S(2)}) collective-permute-start(f32[128,512]{1,0:T(8,128)S(1)} %select_bitcast_fusion.1), channel_id=1, source_target_pairs={{0,4},{2,6},{4,0},{6,2},{8,12},{10,14},{12,8},{14,10},{1,5},{3,7},... | collective-permute-start | bytes 786440 | tf_op jit(solution)/shard_map/ppermute | solution.py:406
  94.7 5.6 %collective-permute-done.19 = f32[2,128,640]{2,1,0:T(8,128)S(1)} collective-permute-done((f32[2,128,640]{2,1,0:T(8,128)S(1)}, f32[2,128,640]{2,1,0:T(8,128)S(1)}, u32[]{:S(2)}, u32[]{:S(2)}) %collective-permute-start.19) | collective-permute-done | bytes 655392 | tf_op jit(solution)/shard_map/ppermute | solution.py:406
  100.3 0.1 select_bitcast_fusion
  100.3 3.9 %collective-permute-start.25 = (f32[128,640]{1,0:T(8,128)S(1)}, f32[128,640]{1,0:T(8,128)S(1)}, u32[]{:S(2)}, u32[]{:S(2)}) collective-permute-start(f32[128,640]{1,0:T(8,128)S(1)} %select_bitcast_fusion), channel_id=1, source_target_pairs={{4,8},{6,10},{8,4},{10,6},{5,9},{7,11},{9,5},{11,7},{20,24},{22,26... | collective-permute-start | bytes 983048 | tf_op jit(solution)/shard_map/ppermute | solution.py:406
  104.3 1.3 %collective-permute-start.22 = (f32[2,128,384]{2,1,0:T(8,128)S(1)}, f32[2,128,384]{2,1,0:T(8,128)S(1)}, u32[]{:S(2)}, u32[]{:S(2)}) collective-permute-start(f32[2,128,384]{2,1,0:T(8,128)S(1)} %add.122), channel_id=1, source_target_pairs={{0,4},{2,6},{12,8},{14,10},{1,5},{3,7},{13,9},{15,11},{16,20},{18,... | collective-permute-start | bytes 1179656 | tf_op jit(solution)/shard_map/ppermute | solution.py:406
  105.6 0.1 bitcast_add_fusion.3
  105.7 4.1 %collective-permute-start.24 = (f32[128,512]{1,0:T(8,128)S(1)}, f32[128,512]{1,0:T(8,128)S(1)}, u32[]{:S(2)}, u32[]{:S(2)}) collective-permute-start(f32[128,512]{1,0:T(8,128)S(1)} %bitcast_add_fusion.3), channel_id=1, source_target_pairs={{4,12},{6,14},{8,0},{10,2},{5,13},{7,15},{9,1},{11,3},{20,28},{22,... | collective-permute-start | bytes 786440 | tf_op jit(solution)/shard_map/ppermute | solution.py:406
  109.7 0.1 fusion.2
  109.9 1.2 collective-permute-start.17
  111.0 2.9 %collective-permute-done.22 = f32[2,128,384]{2,1,0:T(8,128)S(1)} collective-permute-done((f32[2,128,384]{2,1,0:T(8,128)S(1)}, f32[2,128,384]{2,1,0:T(8,128)S(1)}, u32[]{:S(2)}, u32[]{:S(2)}) %collective-permute-start.22) | collective-permute-done | bytes 393248 | tf_op jit(solution)/shard_map/ppermute | solution.py:406
  114.0 2.4 %collective-permute-start.26 = (f32[128,384]{1,0:T(8,128)S(1)}, f32[128,384]{1,0:T(8,128)S(1)}, u32[]{:S(2)}, u32[]{:S(2)}) collective-permute-start(f32[128,384]{1,0:T(8,128)S(1)} %select_bitcast_fusion.3), channel_id=1, source_target_pairs={{4,8},{6,10},{8,4},{10,6},{5,9},{7,11},{9,5},{11,7},{20,24},{22,26... | collective-permute-start | bytes 589832 | tf_op jit(solution)/shard_map/ppermute | solution.py:406
  116.5 0.1 bitcast_add_fusion
  116.6 2.8 %final.1 = (bf16[384,1024]{1,0:T(8,128)(2,1)}, bf16[384,1024]{1,0:T(8,128)(2,1)}) custom-call(s32[2]{0:T(128)S(1)} %pad_add_fusion.place, bf16[384,1024]{1,0:T(8,128)(2,1)S(1)} %bitcast.45, bf16[384,1024]{1,0:T(8,128)(2,1)S(1)} %bitcast.49, f32[384,1024]{1,0:T(8,128)S(1)} %get-tuple-element.98.kl_ref, f32[384,1024]{1,0:T(8,128)S(1)} %get-tuple-element.99.vl_ref, ...), custom_call_target="tpu_custom_call" | custom-call | flops 25165824 | tf_op jit(solution)/shard_map/final/pallas_call | solution.py:70
  119.4 0.1 fusion.1
  119.5 2.1 %collective-permute-done.26 = f32[128,384]{1,0:T(8,128)S(1)} collective-permute-done((f32[128,384]{1,0:T(8,128)S(1)}, f32[128,384]{1,0:T(8,128)S(1)}, u32[]{:S(2)}, u32[]{:S(2)}) %collective-permute-start.26) | collective-permute-done | bytes 196640 | tf_op jit(solution)/shard_map/ppermute | solution.py:406
  121.6 0.1 bitcast_add_fusion.5
  121.7 0.9 fusion
  (36 shorter events, 0.5 us)
Async XLA Ops:
  0.6 5.1 %copy-start = (bf16[1,384,2048]{2,1,0:T(8,128)(2,1)S(1)}, bf16[1,384,2048]{2,1,0:T(8,128)(2,1)}, u32[]{:S(2)}) copy-start(bf16[1,384,2048]{2,1,0:T(8,128)(2,1)} %param.9) | copy-start | bytes 4718596
  0.7 1.2 %copy-start.3 = (bf16[1,384,1024]{2,1,0:T(8,128)(2,1)S(1)}, bf16[1,384,1024]{2,1,0:T(8,128)(2,1)}, u32[]{:S(2)}) copy-start(bf16[1,384,1024]{2,1,0:T(8,128)(2,1)} %param.6) | copy-start | bytes 2359300
  2.0 1.1 copy-start.4
  4.2 5.3 %collective-permute-start = (f32[2,128,128]{2,1,0:T(8,128)S(1)}, f32[2,128,128]{2,1,0:T(8,128)S(1)}, u32[]{:S(2)}, u32[]{:S(2)}) collective-permute-start(f32[2,128,128]{2,1,0:T(8,128)S(1)} %get-tuple-element.66), channel_id=1, source_target_pairs={{0,2},{2,0},{4,6},{6,4},{8,10},{10,8},{12,14},{14,12},{1,3},{3,1},... | collective-permute-start | bytes 393224 | tf_op jit(solution)/shard_map/ppermute | solution.py:257
  5.8 7.3 %copy-start.2 = (bf16[1,384,1024]{2,1,0:T(8,128)(2,1)S(1)}, bf16[1,384,1024]{2,1,0:T(8,128)(2,1)}, u32[]{:S(2)}) copy-start(bf16[1,384,1024]{2,1,0:T(8,128)(2,1)} %param.5) | copy-start | bytes 2359300
  6.4 32.6 %collective-permute-start.8 = (f32[384,1024]{1,0:T(8,128)S(1)}, f32[384,1024]{1,0:T(8,128)S(1)}, u32[]{:S(2)}, u32[]{:S(2)}) collective-permute-start(f32[384,1024]{1,0:T(8,128)S(1)} %away.1), channel_id=1, source_target_pairs={{0,1},{1,0},{2,3},{3,2},{4,5},{5,4},{6,7},{7,6},{8,9},{9,8},{10,11... | collective-permute-start | bytes 4718600 | tf_op jit(solution)/shard_map/ppermute | solution.py:263
  6.5 9.0 %collective-permute-start.2 = (f32[2,128,128]{2,1,0:T(8,128)S(1)}, f32[2,128,128]{2,1,0:T(8,128)S(1)}, u32[]{:S(2)}, u32[]{:S(2)}) collective-permute-start(f32[2,128,128]{2,1,0:T(8,128)S(1)} %get-tuple-element.70), channel_id=1, source_target_pairs={{0,2},{2,0},{4,6},{6,4},{8,10},{10,8},{12,14},{14,12},{1,3},{3,1},... | collective-permute-start | bytes 393224 | tf_op jit(solution)/shard_map/ppermute | solution.py:257
  9.5 9.5 %collective-permute-start.1 = (f32[2,128,128]{2,1,0:T(8,128)S(1)}, f32[2,128,128]{2,1,0:T(8,128)S(1)}, u32[]{:S(2)}, u32[]{:S(2)}) collective-permute-start(f32[2,128,128]{2,1,0:T(8,128)S(1)} %add.101), channel_id=1, source_target_pairs={{0,4},{2,6},{4,8},{6,10},{8,12},{10,14},{1,5},{3,7},{5,9},{7,11},{... | collective-permute-start | bytes 393224 | tf_op jit(solution)/shard_map/ppermute | solution.py:219
  13.0 7.9 %copy-start.1 = (bf16[1024,2048]{1,0:T(8,128)(2,1)S(1)}, bf16[1024,2048]{1,0:T(8,128)(2,1)}, u32[]{:S(2)}) copy-start(bf16[1024,2048]{1,0:T(8,128)(2,1)} %w_ref.3) | copy-start | bytes 12582916
  15.5 11.1 %collective-permute-start.4 = (f32[2,128,128]{2,1,0:T(8,128)S(1)}, f32[2,128,128]{2,1,0:T(8,128)S(1)}, u32[]{:S(2)}, u32[]{:S(2)}) collective-permute-start(f32[2,128,128]{2,1,0:T(8,128)S(1)} %add.103), channel_id=1, source_target_pairs={{0,4},{2,6},{4,8},{6,10},{8,12},{10,14},{1,5},{3,7},{5,9},{7,11},{... | collective-permute-start | bytes 393224 | tf_op jit(solution)/shard_map/ppermute | solution.py:219
  19.1 10.0 %collective-permute-start.3 = (f32[2,128,128]{2,1,0:T(8,128)S(1)}, f32[2,128,128]{2,1,0:T(8,128)S(1)}, u32[]{:S(2)}, u32[]{:S(2)}) collective-permute-start(f32[2,128,128]{2,1,0:T(8,128)S(1)} %add.102), channel_id=1, source_target_pairs={{0,8},{2,10},{4,12},{6,14},{1,9},{3,11},{5,13},{7,15},{16,24},{18,... | collective-permute-start | bytes 393224 | tf_op jit(solution)/shard_map/ppermute | solution.py:219
  26.7 4.1 %collective-permute-start.5 = (f32[2,128,128]{2,1,0:T(8,128)S(1)}, f32[2,128,128]{2,1,0:T(8,128)S(1)}, u32[]{:S(2)}, u32[]{:S(2)}) collective-permute-start(f32[2,128,128]{2,1,0:T(8,128)S(1)} %add.106), channel_id=1, source_target_pairs={{0,8},{2,10},{4,12},{6,14},{1,9},{3,11},{5,13},{7,15},{16,24},{18,... | collective-permute-start | bytes 393224 | tf_op jit(solution)/shard_map/ppermute | solution.py:219
  29.1 5.0 %collective-permute-start.6 = (f32[2,128,128]{2,1,0:T(8,128)S(1)}, f32[2,128,128]{2,1,0:T(8,128)S(1)}, u32[]{:S(2)}, u32[]{:S(2)}) collective-permute-start(f32[2,128,128]{2,1,0:T(8,128)S(1)} %get-tuple-element.75), channel_id=1, source_target_pairs={{0,2},{2,0},{4,6},{6,4},{8,10},{10,8},{12,14},{14,12},{1,3},{3,1},... | collective-permute-start | bytes 393224 | tf_op jit(solution)/shard_map/ppermute | solution.py:229
  36.7 2.4 %collective-permute-start.7 = (f32[384,512]{1,0:T(8,128)S(1)}, f32[384,512]{1,0:T(8,128)S(1)}, u32[]{:S(2)}, u32[]{:S(2)}) collective-permute-start(f32[384,512]{1,0:T(8,128)S(1)} %get-tuple-element.77), channel_id=1, source_target_pairs={{0,1},{1,0},{2,3},{3,2},{4,5},{5,4},{6,7},{7,6},{8,9},{9,8},{10,11... | collective-permute-start | bytes 2359304 | tf_op jit(solution)/shard_map/ppermute | solution.py:289
  36.8 5.9 %collective-permute-start.9 = (f32[2,128,128]{2,1,0:T(8,128)S(1)}, f32[2,128,128]{2,1,0:T(8,128)S(1)}, u32[]{:S(2)}, u32[]{:S(2)}) collective-permute-start(f32[2,128,128]{2,1,0:T(8,128)S(1)} %get-tuple-element.123), channel_id=1, source_target_pairs={{0,2},{2,0},{4,6},{6,4},{8,10},{10,8},{12,14},{14,12},{1,3},{3,1},... | collective-permute-start | bytes 393224 | tf_op jit(solution)/shard_map/ppermute | solution.py:229
  45.2 14.7 %collective-permute-start.11 = (f32[384,512]{1,0:T(8,128)S(1)}, f32[384,512]{1,0:T(8,128)S(1)}, u32[]{:S(2)}, u32[]{:S(2)}) collective-permute-start(f32[384,512]{1,0:T(8,128)S(1)} %get-tuple-element.85), channel_id=1, source_target_pairs={{0,1},{1,0},{2,3},{3,2},{4,5},{5,4},{6,7},{7,6},{8,9},{9,8},{10,11... | collective-permute-start | bytes 2359304 | tf_op jit(solution)/shard_map/ppermute | solution.py:302
  45.3 9.2 %collective-permute-start.10 = (f32[4,128,128]{2,1,0:T(8,128)S(1)}, f32[4,128,128]{2,1,0:T(8,128)S(1)}, u32[]{:S(2)}, u32[]{:S(2)}) collective-permute-start(f32[4,128,128]{2,1,0:T(8,128)S(1)} %get-tuple-element.83), channel_id=1, source_target_pairs={{0,2},{2,0},{4,6},{6,4},{8,10},{10,8},{12,14},{14,12},{1,3},{3,1},... | collective-permute-start | bytes 786440 | tf_op jit(solution)/shard_map/ppermute | solution.py:257
  46.9 18.9 %collective-permute-start.12 = (f32[2,128,512]{2,1,0:T(8,128)S(1)}, f32[2,128,512]{2,1,0:T(8,128)S(1)}, u32[]{:S(2)}, u32[]{:S(2)}) collective-permute-start(f32[2,128,512]{2,1,0:T(8,128)S(1)} %get-tuple-element.91), channel_id=1, source_target_pairs={{0,2},{2,0},{4,6},{6,4},{8,10},{10,8},{12,14},{14,12},{1,3},{3,1},... | collective-permute-start | bytes 1572872 | tf_op jit(solution)/shard_map/ppermute | solution.py:257
  54.5 11.3 %collective-permute-start.13 = (f32[4,128,128]{2,1,0:T(8,128)S(1)}, f32[4,128,128]{2,1,0:T(8,128)S(1)}, u32[]{:S(2)}, u32[]{:S(2)}) collective-permute-start(f32[4,128,128]{2,1,0:T(8,128)S(1)} %add.111), channel_id=1, source_target_pairs={{4,0},{6,2},{8,4},{10,6},{12,8},{14,10},{5,1},{7,3},{9,5},{11,7},{... | collective-permute-start | bytes 786440 | tf_op jit(solution)/shard_map/ppermute | solution.py:406
  62.0 17.9 %collective-permute-start.15 = (f32[2,128,640]{2,1,0:T(8,128)S(1)}, f32[2,128,640]{2,1,0:T(8,128)S(1)}, u32[]{:S(2)}, u32[]{:S(2)}) collective-permute-start(f32[2,128,640]{2,1,0:T(8,128)S(1)} %get-tuple-element.86), channel_id=1, source_target_pairs={{0,2},{2,0},{4,6},{6,4},{8,10},{10,8},{12,14},{14,12},{1,3},{3,1},... | collective-permute-start | bytes 1966088 | tf_op jit(solution)/shard_map/ppermute | solution.py:257
  66.0 13.8 %collective-permute-start.16 = (f32[128,512]{1,0:T(8,128)S(1)}, f32[128,512]{1,0:T(8,128)S(1)}, u32[]{:S(2)}, u32[]{:S(2)}) collective-permute-start(f32[128,512]{1,0:T(8,128)S(1)} %select_bitcast_fusion.2), channel_id=1, source_target_pairs={{0,4},{2,6},{4,0},{6,2},{8,12},{10,14},{12,8},{14,10},{1,5},{3,7},... | collective-permute-start | bytes 786440 | tf_op jit(solution)/shard_map/ppermute | solution.py:406
  69.4 19.8 %collective-permute-start.14 = (f32[4,128,128]{2,1,0:T(8,128)S(1)}, f32[4,128,128]{2,1,0:T(8,128)S(1)}, u32[]{:S(2)}, u32[]{:S(2)}) collective-permute-start(f32[4,128,128]{2,1,0:T(8,128)S(1)} %add.112), channel_id=1, source_target_pairs={{8,0},{10,2},{12,4},{14,6},{9,1},{11,3},{13,5},{15,7},{24,16},{26,... | collective-permute-start | bytes 786440 | tf_op jit(solution)/shard_map/ppermute | solution.py:406
  70.9 20.1 %collective-permute-start.20 = (f32[2,128,512]{2,1,0:T(8,128)S(1)}, f32[2,128,512]{2,1,0:T(8,128)S(1)}, u32[]{:S(2)}, u32[]{:S(2)}) collective-permute-start(f32[2,128,512]{2,1,0:T(8,128)S(1)} %get-tuple-element.109), channel_id=1, source_target_pairs={{0,2},{2,0},{4,6},{6,4},{8,10},{10,8},{12,14},{14,12},{1,3},{3,1},... | collective-permute-start | bytes 1572872 | tf_op jit(solution)/shard_map/ppermute | solution.py:257
  79.9 20.3 %collective-permute-start.19 = (f32[2,128,640]{2,1,0:T(8,128)S(1)}, f32[2,128,640]{2,1,0:T(8,128)S(1)}, u32[]{:S(2)}, u32[]{:S(2)}) collective-permute-start(f32[2,128,640]{2,1,0:T(8,128)S(1)} %add.115), channel_id=1, source_target_pairs={{0,4},{2,6},{12,8},{14,10},{1,5},{3,7},{13,9},{15,11},{16,20},{18,... | collective-permute-start | bytes 1966088 | tf_op jit(solution)/shard_map/ppermute | solution.py:406
  81.2 23.0 %collective-permute-start.18 = (f32[2,128,384]{2,1,0:T(8,128)S(1)}, f32[2,128,384]{2,1,0:T(8,128)S(1)}, u32[]{:S(2)}, u32[]{:S(2)}) collective-permute-start(f32[2,128,384]{2,1,0:T(8,128)S(1)} %get-tuple-element.106), channel_id=1, source_target_pairs={{0,2},{2,0},{4,6},{6,4},{8,10},{10,8},{12,14},{14,12},{1,3},{3,1},... | collective-permute-start | bytes 1179656 | tf_op jit(solution)/shard_map/ppermute | solution.py:257
  83.1 11.6 %collective-permute-start.21 = (f32[128,512]{1,0:T(8,128)S(1)}, f32[128,512]{1,0:T(8,128)S(1)}, u32[]{:S(2)}, u32[]{:S(2)}) collective-permute-start(f32[128,512]{1,0:T(8,128)S(1)} %bitcast_add_fusion.4), channel_id=1, source_target_pairs={{4,12},{6,14},{8,0},{10,2},{5,13},{7,15},{9,1},{11,3},{20,28},{22,... | collective-permute-start | bytes 786440 | tf_op jit(solution)/shard_map/ppermute | solution.py:406
  91.1 14.5 %collective-permute-start.23 = (f32[128,512]{1,0:T(8,128)S(1)}, f32[128,512]{1,0:T(8,128)S(1)}, u32[]{:S(2)}, u32[]{:S(2)}) collective-permute-start(f32[128,512]{1,0:T(8,128)S(1)} %select_bitcast_fusion.1), channel_id=1, source_target_pairs={{0,4},{2,6},{4,0},{6,2},{8,12},{10,14},{12,8},{14,10},{1,5},{3,7},... | collective-permute-start | bytes 786440 | tf_op jit(solution)/shard_map/ppermute | solution.py:406
  100.3 16.1 %collective-permute-start.25 = (f32[128,640]{1,0:T(8,128)S(1)}, f32[128,640]{1,0:T(8,128)S(1)}, u32[]{:S(2)}, u32[]{:S(2)}) collective-permute-start(f32[128,640]{1,0:T(8,128)S(1)} %select_bitcast_fusion), channel_id=1, source_target_pairs={{4,8},{6,10},{8,4},{10,6},{5,9},{7,11},{9,5},{11,7},{20,24},{22,26... | collective-permute-start | bytes 983048 | tf_op jit(solution)/shard_map/ppermute | solution.py:406
  104.3 9.7 %collective-permute-start.22 = (f32[2,128,384]{2,1,0:T(8,128)S(1)}, f32[2,128,384]{2,1,0:T(8,128)S(1)}, u32[]{:S(2)}, u32[]{:S(2)}) collective-permute-start(f32[2,128,384]{2,1,0:T(8,128)S(1)} %add.122), channel_id=1, source_target_pairs={{0,4},{2,6},{12,8},{14,10},{1,5},{3,7},{13,9},{15,11},{16,20},{18,... | collective-permute-start | bytes 1179656 | tf_op jit(solution)/shard_map/ppermute | solution.py:406
  105.7 10.8 %collective-permute-start.24 = (f32[128,512]{1,0:T(8,128)S(1)}, f32[128,512]{1,0:T(8,128)S(1)}, u32[]{:S(2)}, u32[]{:S(2)}) collective-permute-start(f32[128,512]{1,0:T(8,128)S(1)} %bitcast_add_fusion.3), channel_id=1, source_target_pairs={{4,12},{6,14},{8,0},{10,2},{5,13},{7,15},{9,1},{11,3},{20,28},{22,... | collective-permute-start | bytes 786440 | tf_op jit(solution)/shard_map/ppermute | solution.py:406
  109.9 6.7 %collective-permute-start.17 = (f32[4,128,128]{2,1,0:T(8,128)S(1)}, f32[4,128,128]{2,1,0:T(8,128)S(1)}, u32[]{:S(2)}, u32[]{:S(2)}) collective-permute-start(f32[4,128,128]{2,1,0:T(8,128)S(1)} %get-tuple-element.121), channel_id=1, source_target_pairs={{0,2},{2,0},{4,6},{6,4},{8,10},{10,8},{12,14},{14,12},{1,3},{3,1},... | collective-permute-start | bytes 786440 | tf_op jit(solution)/shard_map/ppermute | solution.py:257
  114.0 7.6 %collective-permute-start.26 = (f32[128,384]{1,0:T(8,128)S(1)}, f32[128,384]{1,0:T(8,128)S(1)}, u32[]{:S(2)}, u32[]{:S(2)}) collective-permute-start(f32[128,384]{1,0:T(8,128)S(1)} %select_bitcast_fusion.3), channel_id=1, source_target_pairs={{4,8},{6,10},{8,4},{10,6},{5,9},{7,11},{9,5},{11,7},{20,24},{22,26... | collective-permute-start | bytes 589832 | tf_op jit(solution)/shard_map/ppermute | solution.py:406

commit v10 on v9

--- a/solution.py
+++ b/solution.py
@@ -134,34 +134,37 @@
             out[j if whole else i] = dot(q, d_att, TN)
 
 
-def grads_body(place, q_ref, k_ref, v_ref, *refs):
+def grads_body(rows, place, q_ref, k_ref, v_ref, da_ref, own_ref, other_ref, qg_ref, kl_ref, vl_ref):
     low = place[0]
-    qg_ref, kl_ref, vl_ref = refs[-3:]
     lower = causal(q_ref.shape[0], True)
     upper = causal(q_ref.shape[0], False)
-    for rows, (da_ref, own_ref, other_ref) in ((FAR, refs[:3]), (NEAR, refs[3:6])):
+    for i, j in enumerate(rows):
+        for prior, part in ((own_ref, low), (other_ref, 1 - low)):
+            here, there = at(2 * j + part), at(2 * i + part)
+            q, k, v, d_att = q_ref[:, here], k_ref[:, here], v_ref[:, here], da_ref[:, there]
+            cross = jnp.where(lower, dot(d_att, v, NT), 0.0)
+            part_sum = two_pass(cross, k, NN) + two_pass_right(d_att, prior[i], NT)
+            qg_ref[:, there] = part_sum.astype(BF16)
+            cross = jnp.where(upper, dot(v, d_att, NT), 0.0)
+            kl_ref[:, there] = two_pass(cross, q, NN)
+            scores = jnp.where(upper, dot(k, q, NT), 0.0)
+            vl_ref[:, there] = two_pass(scores, d_att, NN)
+
+
+def final_body(place, k_ref, v_ref, *refs):
+    low = place[0]
+    own_ref, other_ref, qg_ref, kg_ref, vg_ref = refs[-5:]
+    for rows, (part_ref, kl_ref, vl_ref) in ((FAR, refs[:3]), (NEAR, refs[3:6])):
         for i, j in enumerate(rows):
-            for prior, part in ((own_ref, low), (other_ref, 1 - low)):
+            qg_ref[:, at(j, PAIR)] = part_ref[:, at(i, PAIR)]
+            for later, part in ((own_ref, low), (other_ref, 1 - low)):
                 here, there = at(2 * j + part), at(2 * i + part)
-                q, k, v, d_att = q_ref[:, here], k_ref[:, here], v_ref[:, here], da_ref[:, there]
-                cross = jnp.where(lower, dot(d_att, v, NT), 0.0)
-                part_sum = two_pass(cross, k, NN) + two_pass_right(d_att, prior[i], NT)
-                qg_ref[:, here] = part_sum.astype(BF16)
-                cross = jnp.where(upper, dot(v, d_att, NT), 0.0)
-                kl_ref[:, here] = two_pass(cross, q, NN)
-                scores = jnp.where(upper, dot(k, q, NT), 0.0)
-                vl_ref[:, here] = two_pass(scores, d_att, NN)
-
-
-def final_body(place, k_ref, v_ref, kl_ref, vl_ref, own_ref, other_ref, kg_ref, vg_ref):
-    low = place[0]
-    for j in range(PAIRS):
-        for later, part in ((own_ref, low), (other_ref, 1 - low)):
-            here = at(2 * j + part)
-            high, rest = halves(later[j])
-            v, k = v_ref[:, here], k_ref[:, here]
-            kg_ref[:, here] = (kl_ref[:, here] + (dot(v, high, NT) + dot(v, rest, NT))).astype(BF16)
-            vg_ref[:, here] = (vl_ref[:, here] + (dot(k, high, NN) + dot(k, rest, NN))).astype(BF16)
+                high, rest = halves(later[j])
+                v, k = v_ref[:, here], k_ref[:, here]
+                k_sum = kl_ref[:, there] + (dot(v, high, NT) + dot(v, rest, NT))
+                kg_ref[:, here] = k_sum.astype(BF16)
+                v_sum = vl_ref[:, there] + (dot(k, high, NN) + dot(k, rest, NN))
+                vg_ref[:, here] = v_sum.astype(BF16)
 
 
 def weight_body(place, nb_ref, g_ref, nbo_ref, go_ref, *outs):
@@ -297,27 +300,20 @@
     )
 
     received = trade(send)
-    total = keep + received
-    if fast:
-        nbo = lax.ppermute(near32, "dp", swap)
-        (near0_keep, near0_send), (near1_keep, near1_send) = product(after(near, received), nbo, WIDTHS[1])
-        near0_got = trade(near0_send)
-        far0_got = trade(after(chunks[0][1], near_other))
-        back1 = hop(total, BACK)
-    def gradients(far_att):
+    def gradients(rows, d_att, prior):
         return call(
-            grads_body,
-            (rows16, rows32, rows32),
-            (place, q, k, v, far_att, *far_prior, near_att, *near_prior),
-            9 * unit * length,
+            functools.partial(grads_body, rows),
+            (pieces[0], pieces[1], pieces[1]),
+            (place, q, k, v, d_att, *prior),
+            5 * unit * length,
             "grads",
         )
 
     def finish(own, other):
         return call(
             final_body,
-            (rows16, rows16),
-            (place, k, v, key_local, value_local, own, other),
+            (rows16, rows16, rows16),
+            (place, k, v, *far_grads, *near_grads, own, other),
             4 * unit * HD,
             "final",
         )
@@ -338,23 +334,31 @@
         weight = lax.psum_scatter(weight, "dp", scatter_dimension=1, tiled=True)
         weight_grad = lax.psum_scatter(weight, "seq", scatter_dimension=0, tiled=True) * scale
         output = project(far)
-        query_grad, key_local, value_local = gradients(far_att)
+        far_grads = gradients(FAR, far_att, far_prior)
+        near_grads = gradients(NEAR, near_att, near_prior)
         ((own, other),) = exclusive([(keep, received)], count, even, True, [])
-        key_grad, value_grad = finish(own, other)
+        query_grad, key_grad, value_grad = finish(own, other)
         return output[None], query_grad[None], key_grad[None], value_grad[None], weight_grad
 
-    (far0_keep, _), (far1_keep, far1_send) = chunks
+    (far0_keep, far0_send), (far1_keep, far1_send) = chunks
+    nbo = lax.ppermute(near32, "dp", swap)
+    far0_got = trade(after(far0_send, near_other))
+    far_grads = gradients(FAR, after(far_att, send), far_prior)
+    received = after(received, far_grads[1])
+    (near0_keep, near0_send), (near1_keep, near1_send) = product(after(near, received), nbo, WIDTHS[1])
+    near0_got = trade(near0_send)
+    total = keep + received
+    back1 = hop(total, BACK)
     near1_got = trade(near1_send)
-    output = project(after(far, near0_send))
-    back1 = after(back1, output)
+    back1 = after(back1, near0_send)
     total = total + back1
     back2 = hop(total, BACK2)
     far0 = far0_keep + after(far0_got, total)
     far0_out = jnp.where(odd, far0[0], far0[1])
     far0_in = hop(far0_out, NEXT)
     far1_got = trade(after(far1_send, far0))
-    query_grad, key_local, value_local = gradients(after(far_att, far0_out))
-    far0_in = after(far0_in, key_local)
+    near_grads = gradients(NEAR, after(near_att, far0_out), near_prior)
+    far0_in = after(far0_in, near_grads[1])
     far0_half = jnp.where(lower, far0[1], far0[0]) + far0_in
     far0_end = hop(far0_half, OUTWARD)
     near0 = near0_keep + after(near0_got, far0_half)
@@ -363,7 +367,8 @@
     theirs = jnp.where(even, outside, outside + keep)
     other = trade(theirs)
     own = jnp.where(even, outside + received, outside)
-    far1 = far1_keep + after(far1_got, theirs)
+    output = project(after(far, theirs))
+    far1 = far1_keep + after(far1_got, output)
     far1_out = jnp.where(odd, far1[0], far1[1])
     far1_in = hop(far1_out, NEXT)
     near0_in = after(near0_in, far1_out, far0_end)
@@ -377,7 +382,7 @@
     near1_in = after(near1_in, far1_half)
     near1_half = jnp.where(lower, near1[1] + near1_in[1], near1[0] + near1_in[0])
     near1_end = hop(near1_half, ACROSS)
-    key_grad, value_grad = finish(own, after(other, near1_half))
+    query_grad, key_grad, value_grad = finish(own, after(other, near1_half))
     near0_end, far1_end = after(near0_end, near1_half), after(far1_end, near1_half)
 
     far_parts = [

time: 125 us -> 125 us (level)
  the two profiles are of different devices: /device:TPU:12 before, /device:TPU:0 now
where the time goes in v10:
time: 125 us
  waiting for transfers between devices  49.7 us (40%)
  starting transfers between devices  38.6 us (31%)
  Pallas kernels  30.8 us (25%)
  local copies, waits for them, and re-layouts  2.39 us (2%)
  other arithmetic  2.15 us (2%)
    pallas_call x12, Pallas kernels, call(): pl.pallas_call(body, out_shape=tuple(out_shapes), in_specs=specs, out_spe...  30.8 us
    ppermute x10, waiting for transfers between devices, hop(): lax.ppermute(block, 'seq', [(2 * a + i, 2 * b + i) for a, b in links for...  24.1 us
    ppermute x4, starting transfers between devices, exclusive(): got = lax.ppermute(total, 'seq', links(step))  17.4 us
    ppermute x8, waiting for transfers between devices, trade(): return lax.ppermute(send, 'seq', [(s, s ^ 1) for s in range(count)])  16.8 us
    ppermute x10, starting transfers between devices, hop(): lax.ppermute(block, 'seq', [(2 * a + i, 2 * b + i) for a, b in links for...  13.9 us
    ppermute x8, starting transfers between devices, trade(): return lax.ppermute(send, 'seq', [(s, s ^ 1) for s in range(count)])  6.99 us
    ppermute x2, waiting for transfers between devices, exclusive(): results.append((mine, lax.ppermute(theirs, 'seq', swap)))  4.35 us
  transfers between devices with their start and end apart: 27, of which 16 were waited for; matrix products, arithmetic and copies ran while one was open for 1% of the time, Pallas kernels for 22%

profile of v10, /device:TPU:0, one launch (start us, length us, event | category | flops | bytes accessed | tf_op | source)
XLA Modules:
  0.0 124.8 jit_solution(6990666421650546645)
XLA Ops:
  0.7 0.1 pad_add_fusion.place
  0.7 1.2 copy-done.2
  2.0 1.1 copy-done.4
  3.1 1.1 state.1
  4.2 3.0 %collective-permute-start = (f32[2,128,128]{2,1,0:T(8,128)S(1)}, f32[2,128,128]{2,1,0:T(8,128)S(1)}, u32[]{:S(2)}, u32[]{:S(2)}) collective-permute-start(f32[2,128,128]{2,1,0:T(8,128)S(1)} %get-tuple-element.72), channel_id=1, source_target_pairs={{0,2},{2,0},{4,6},{6,4},{8,10},{10,8},{12,14},{14,12},{1,3},{3,1},... | collective-permute-start | bytes 393224 | tf_op jit(solution)/shard_map/ppermute | solution.py:260
  7.2 0.6 away.1
  7.9 0.1 collective-permute-start.8
  8.0 0.1 collective-permute-start.2
  8.1 3.0 %collective-permute-done = f32[2,128,128]{2,1,0:T(8,128)S(1)} collective-permute-done((f32[2,128,128]{2,1,0:T(8,128)S(1)}, f32[2,128,128]{2,1,0:T(8,128)S(1)}, u32[]{:S(2)}, u32[]{:S(2)}) %collective-permute-start) | collective-permute-done | bytes 131104 | tf_op jit(solution)/shard_map/ppermute | solution.py:260
  11.1 3.4 %collective-permute-start.1 = (f32[2,128,128]{2,1,0:T(8,128)S(1)}, f32[2,128,128]{2,1,0:T(8,128)S(1)}, u32[]{:S(2)}, u32[]{:S(2)}) collective-permute-start(f32[2,128,128]{2,1,0:T(8,128)S(1)} %add.101), channel_id=1, source_target_pairs={{0,4},{2,6},{4,8},{6,10},{8,12},{10,14},{1,5},{3,7},{5,9},{7,11},{... | collective-permute-start | bytes 393224 | tf_op jit(solution)/shard_map/ppermute | solution.py:222
  14.5 2.4 %local.1.att_ref = f32[384,1024]{1,0:T(8,128)S(1)} custom-call(bf16[384,1024]{1,0:T(8,128)(2,1)S(1)} %bitcast.38, bf16[384,1024]{1,0:T(8,128)(2,1)S(1)} %bitcast.44, bf16[384,1024]{1,0:T(8,128)(2,1)S(1)} %bitcast.49), custom_call_target="tpu_custom_call" | custom-call | flops 56623104 | tf_op jit(solution)/shard_map/local/pallas_call | solution.py:70
  17.0 3.5 %collective-permute-start.4 = (f32[2,128,128]{2,1,0:T(8,128)S(1)}, f32[2,128,128]{2,1,0:T(8,128)S(1)}, u32[]{:S(2)}, u32[]{:S(2)}) collective-permute-start(f32[2,128,128]{2,1,0:T(8,128)S(1)} %add.103), channel_id=1, source_target_pairs={{0,4},{2,6},{4,8},{6,10},{8,12},{10,14},{1,5},{3,7},{5,9},{7,11},{... | collective-permute-start | bytes 393224 | tf_op jit(solution)/shard_map/ppermute | solution.py:222
  20.5 2.9 %collective-permute-start.3 = (f32[2,128,128]{2,1,0:T(8,128)S(1)}, f32[2,128,128]{2,1,0:T(8,128)S(1)}, u32[]{:S(2)}, u32[]{:S(2)}) collective-permute-start(f32[2,128,128]{2,1,0:T(8,128)S(1)} %add.102), channel_id=1, source_target_pairs={{0,8},{2,10},{4,12},{6,14},{1,9},{3,11},{5,13},{7,15},{16,24},{18,... | collective-permute-start | bytes 393224 | tf_op jit(solution)/shard_map/ppermute | solution.py:222
  23.5 2.4 %d_normed.1.dn_ref = f32[384,1024]{1,0:T(8,128)S(1)} custom-call(bf16[384,2048]{1,0:T(8,128)(2,1)S(1)} %bitcast.35, bf16[1024,2048]{1,0:T(8,128)(2,1)S(1)} %copy-done.6), custom_call_target="tpu_custom_call" | custom-call | flops 100663296 | tf_op jit(solution)/shard_map/d_normed/pallas_call | solution.py:70
  25.9 7.6 %collective-permute-start.5 = (f32[2,128,128]{2,1,0:T(8,128)S(1)}, f32[2,128,128]{2,1,0:T(8,128)S(1)}, u32[]{:S(2)}, u32[]{:S(2)}) collective-permute-start(f32[2,128,128]{2,1,0:T(8,128)S(1)} %add.106), channel_id=1, source_target_pairs={{0,8},{2,10},{4,12},{6,14},{1,9},{3,11},{5,13},{7,15},{16,24},{18,... | collective-permute-start | bytes 393224 | tf_op jit(solution)/shard_map/ppermute | solution.py:222
  33.6 0.1 collective-permute-start.6
  33.6 2.4 %collective-permute-done.5 = f32[2,128,128]{2,1,0:T(8,128)S(1)} collective-permute-done((f32[2,128,128]{2,1,0:T(8,128)S(1)}, f32[2,128,128]{2,1,0:T(8,128)S(1)}, u32[]{:S(2)}, u32[]{:S(2)}) %collective-permute-start.5) | collective-permute-done | bytes 131104 | tf_op jit(solution)/shard_map/ppermute | solution.py:222
  36.1 2.5 %collective-permute-done.6.other_ref = f32[2,128,128]{2,1,0:T(8,128)S(1)} collective-permute-done((f32[2,128,128]{2,1,0:T(8,128)S(1)}, f32[2,128,128]{2,1,0:T(8,128)S(1)}, u32[]{:S(2)}, u32[]{:S(2)}) %collective-permute-start.6) | collective-permute-done | bytes 131104 | tf_op jit(solution)/shard_map/ppermute | solution.py:232
  38.6 2.5 %norm_far.1 = (bf16[384,512]{1,0:T(8,128)(2,1)S(1)}, f32[384,512]{1,0:T(8,128)S(1)}, bf16[384,512]{1,0:T(8,128)(2,1)S(1)}, f32[2,128,128]{2,1,0:T(8,128)S(1)}, f32[2,128,128]{2,1,0:T(8,128)S(1)}) custom-call(s32[2]{0:T(128)S(1)} %pad_add_fusion.place, bf16[384,1024]{1,0:T(8,128)(2,1)S(1)} %bitcast.39, f32[384,1024]{1,0:T(8,128)S(1)} %local.1.att_ref, ...), custom_call_target="tpu_custom_call" | custom-call | flops 6291456 | tf_op jit(solution)/shard_map/norm_far/pallas_call | solution.py:70
  41.1 0.1 collective-permute-start.7
  41.2 0.1 collective-permute-start.9
  41.3 2.2 %collective-permute-done.7.nbo_ref = f32[384,512]{1,0:T(8,128)S(1)} collective-permute-done((f32[384,512]{1,0:T(8,128)S(1)}, f32[384,512]{1,0:T(8,128)S(1)}, u32[]{:S(2)}, u32[]{:S(2)}) %collective-permute-start.7) | collective-permute-done | bytes 786464 | tf_op jit(solution)/shard_map/ppermute | solution.py:292
  43.5 1.8 %weight.2 = (f32[2,128,512]{2,1,0:T(8,128)S(1)}, f32[2,128,512]{2,1,0:T(8,128)S(1)}, f32[2,128,512]{2,1,0:T(8,128)S(1)}, f32[2,128,512]{2,1,0:T(8,128)S(1)}) custom-call(s32[2]{0:T(128)S(1)} %pad_add_fusion.place, bf16[384,512]{1,0:T(8,128)(2,1)S(1)} %get-tuple-element.111.nb_ref.far_ref, bf16[384,2048]{1,0:T(8,128)(2,1)S(1)} %bitcast.36, ...), custom_call_target="tpu_custom_call" | custom-call | flops 50331648 | tf_op jit(solution)/shard_map/weight/pallas_call | solution.py:70
  45.3 1.8 %collective-permute-done.9.other_ref = f32[2,128,128]{2,1,0:T(8,128)S(1)} collective-permute-done((f32[2,128,128]{2,1,0:T(8,128)S(1)}, f32[2,128,128]{2,1,0:T(8,128)S(1)}, u32[]{:S(2)}, u32[]{:S(2)}) %collective-permute-start.9) | collective-permute-done | bytes 131104 | tf_op jit(solution)/shard_map/ppermute | solution.py:232
  47.1 2.6 %norm_near.1 = (bf16[384,512]{1,0:T(8,128)(2,1)S(1)}, f32[384,512]{1,0:T(8,128)S(1)}, bf16[384,512]{1,0:T(8,128)(2,1)S(1)}, f32[4,128,128]{2,1,0:T(8,128)S(1)}, f32[4,128,128]{2,1,0:T(8,128)S(1)}) custom-call(s32[2]{0:T(128)S(1)} %pad_add_fusion.place, bf16[384,1024]{1,0:T(8,128)(2,1)S(1)} %bitcast.40, f32[384,1024]{1,0:T(8,128)S(1)} %local.1.att_ref, ...), custom_call_target="tpu_custom_call" | custom-call | flops 402653184 | tf_op jit(solution)/shard_map/norm_near/pallas_call | solution.py:70
  49.7 0.1 collective-permute-start.12
  49.8 0.3 collective-permute-start.10
  50.1 1.8 %collective-permute-start.15 = (f32[2,128,512]{2,1,0:T(8,128)S(1)}, f32[2,128,512]{2,1,0:T(8,128)S(1)}, u32[]{:S(2)}, u32[]{:S(2)}) collective-permute-start(f32[2,128,512]{2,1,0:T(8,128)S(1)} %get-tuple-element.102), channel_id=1, source_target_pairs={{0,2},{2,0},{4,6},{6,4},{8,10},{10,8},{12,14},{14,12},{1,3},{3,1},... | collective-permute-start | bytes 1572872 | tf_op jit(solution)/shard_map/ppermute | solution.py:260
  51.9 4.3 %grads.2 = (bf16[384,512]{1,0:T(8,128)(2,1)S(1)}, f32[384,512]{1,0:T(8,128)S(1)}, f32[384,512]{1,0:T(8,128)S(1)}) custom-call(s32[2]{0:T(128)S(1)} %pad_add_fusion.place, bf16[384,1024]{1,0:T(8,128)(2,1)S(1)} %bitcast.41, bf16[384,1024]{1,0:T(8,128)(2,1)S(1)} %bitcast.45, bf16[384,1024]{1,0:T(8,128)(2,1)S(1)} %bitcast.50, ...), custom_call_target="tpu_custom_call" | custom-call | flops 94371840 | tf_op jit(solution)/shard_map/grads/pallas_call | solution.py:70
  56.2 2.7 %collective-permute-done.10 = f32[4,128,128]{2,1,0:T(8,128)S(1)} collective-permute-done((f32[4,128,128]{2,1,0:T(8,128)S(1)}, f32[4,128,128]{2,1,0:T(8,128)S(1)}, u32[]{:S(2)}, u32[]{:S(2)}) %collective-permute-start.10) | collective-permute-done | bytes 262176 | tf_op jit(solution)/shard_map/ppermute | solution.py:260
  59.0 1.5 %collective-permute-start.11 = (f32[4,128,128]{2,1,0:T(8,128)S(1)}, f32[4,128,128]{2,1,0:T(8,128)S(1)}, u32[]{:S(2)}, u32[]{:S(2)}) collective-permute-start(f32[4,128,128]{2,1,0:T(8,128)S(1)} %add.111), channel_id=1, source_target_pairs={{4,0},{6,2},{8,4},{10,6},{12,8},{14,10},{5,1},{7,3},{9,5},{11,7},{... | collective-permute-start | bytes 786440 | tf_op jit(solution)/shard_map/ppermute | solution.py:411
  60.5 2.0 %weight.3 = (f32[2,128,640]{2,1,0:T(8,128)S(1)}, f32[2,128,640]{2,1,0:T(8,128)S(1)}, f32[2,128,384]{2,1,0:T(8,128)S(1)}, f32[2,128,384]{2,1,0:T(8,128)S(1)}) custom-call(s32[2]{0:T(128)S(1)} %pad_add_fusion.place, bf16[384,512]{1,0:T(8,128)(2,1)S(1)} %get-tuple-element.95.nb_ref.near_ref, bf16[384,2048]{1,0:T(8,128)(2,1)S(1)} %bitcast.37, ...), custom_call_target="tpu_custom_call" | custom-call | flops 50331648 | tf_op jit(solution)/shard_map/weight/pallas_call | solution.py:70
  62.5 0.3 collective-permute-start.14
  62.8 5.7 %collective-permute-done.11 = f32[4,128,128]{2,1,0:T(8,128)S(1)} collective-permute-done((f32[4,128,128]{2,1,0:T(8,128)S(1)}, f32[4,128,128]{2,1,0:T(8,128)S(1)}, u32[]{:S(2)}, u32[]{:S(2)}) %collective-permute-start.11) | collective-permute-done | bytes 262176 | tf_op jit(solution)/shard_map/ppermute | solution.py:411
  68.5 1.7 %collective-permute-done.15 = f32[2,128,512]{2,1,0:T(8,128)S(1)} collective-permute-done((f32[2,128,512]{2,1,0:T(8,128)S(1)}, f32[2,128,512]{2,1,0:T(8,128)S(1)}, u32[]{:S(2)}, u32[]{:S(2)}) %collective-permute-start.15) | collective-permute-done | bytes 524320 | tf_op jit(solution)/shard_map/ppermute | solution.py:260
  70.2 0.1 add.113
  70.3 0.1 collective-permute-start.16
  70.4 1.3 %collective-permute-start.13 = (f32[4,128,128]{2,1,0:T(8,128)S(1)}, f32[4,128,128]{2,1,0:T(8,128)S(1)}, u32[]{:S(2)}, u32[]{:S(2)}) collective-permute-start(f32[4,128,128]{2,1,0:T(8,128)S(1)} %add.112), channel_id=1, source_target_pairs={{8,0},{10,2},{12,4},{14,6},{9,1},{11,3},{13,5},{15,7},{24,16},{26,... | collective-permute-start | bytes 786440 | tf_op jit(solution)/shard_map/ppermute | solution.py:411
  71.7 0.3 collective-permute-start.20
  72.0 4.4 %grads.3 = (bf16[384,512]{1,0:T(8,128)(2,1)S(1)}, f32[384,512]{1,0:T(8,128)S(1)}, f32[384,512]{1,0:T(8,128)S(1)}) custom-call(s32[2]{0:T(128)S(1)} %pad_add_fusion.place, bf16[384,1024]{1,0:T(8,128)(2,1)S(1)} %bitcast.42, bf16[384,1024]{1,0:T(8,128)(2,1)S(1)} %bitcast.46, bf16[384,1024]{1,0:T(8,128)(2,1)S(1)} %bitcast.51, ...), custom_call_target="tpu_custom_call" | custom-call | flops 94371840 | tf_op jit(solution)/shard_map/grads/pallas_call | solution.py:70
  76.4 4.5 %collective-permute-done.16 = f32[128,512]{1,0:T(8,128)S(1)} collective-permute-done((f32[128,512]{1,0:T(8,128)S(1)}, f32[128,512]{1,0:T(8,128)S(1)}, u32[]{:S(2)}, u32[]{:S(2)}) %collective-permute-start.16) | collective-permute-done | bytes 262176 | tf_op jit(solution)/shard_map/ppermute | solution.py:411
  81.0 3.2 %collective-permute-done.14 = f32[2,128,640]{2,1,0:T(8,128)S(1)} collective-permute-done((f32[2,128,640]{2,1,0:T(8,128)S(1)}, f32[2,128,640]{2,1,0:T(8,128)S(1)}, u32[]{:S(2)}, u32[]{:S(2)}) %collective-permute-start.14) | collective-permute-done | bytes 655392 | tf_op jit(solution)/shard_map/ppermute | solution.py:260
  84.3 1.3 %collective-permute-start.19 = (f32[2,128,640]{2,1,0:T(8,128)S(1)}, f32[2,128,640]{2,1,0:T(8,128)S(1)}, u32[]{:S(2)}, u32[]{:S(2)}) collective-permute-start(f32[2,128,640]{2,1,0:T(8,128)S(1)} %add.115), channel_id=1, source_target_pairs={{0,4},{2,6},{12,8},{14,10},{1,5},{3,7},{13,9},{15,11},{16,20},{18,... | collective-permute-start | bytes 1966088 | tf_op jit(solution)/shard_map/ppermute | solution.py:411
  85.6 0.8 collective-permute-start.18
  86.4 1.3 %collective-permute-start.21 = (f32[128,512]{1,0:T(8,128)S(1)}, f32[128,512]{1,0:T(8,128)S(1)}, u32[]{:S(2)}, u32[]{:S(2)}) collective-permute-start(f32[128,512]{1,0:T(8,128)S(1)} %bitcast_add_fusion.4), channel_id=1, source_target_pairs={{4,12},{6,14},{8,0},{10,2},{5,13},{7,15},{9,1},{11,3},{20,28},{22,... | collective-permute-start | bytes 786440 | tf_op jit(solution)/shard_map/ppermute | solution.py:411
  87.7 0.1 add_select_fusion
  87.8 3.5 %output.1 = bf16[384,2048]{1,0:T(8,128)(2,1)} custom-call(bf16[384,512]{1,0:T(8,128)(2,1)S(1)} %get-tuple-element.111.nb_ref.far_ref, bf16[384,512]{1,0:T(8,128)(2,1)S(1)} %get-tuple-element.95.nb_ref.near_ref, bf16[1024,2048]{1,0:T(8,128)(2,1)S(1)} %copy-done.6), custom_call_target="tpu_custom_call" | custom-call | flops 100663296 | tf_op jit(solution)/shard_map/output/pallas_call | solution.py:70
  91.3 4.2 %collective-permute-done.20 = f32[2,128,512]{2,1,0:T(8,128)S(1)} collective-permute-done((f32[2,128,512]{2,1,0:T(8,128)S(1)}, f32[2,128,512]{2,1,0:T(8,128)S(1)}, u32[]{:S(2)}, u32[]{:S(2)}) %collective-permute-start.20) | collective-permute-done | bytes 524320 | tf_op jit(solution)/shard_map/ppermute | solution.py:260
  95.5 0.1 add.119
  95.7 0.4 collective-permute-done.21
  96.1 4.7 %collective-permute-done.19 = f32[2,128,640]{2,1,0:T(8,128)S(1)} collective-permute-done((f32[2,128,640]{2,1,0:T(8,128)S(1)}, f32[2,128,640]{2,1,0:T(8,128)S(1)}, u32[]{:S(2)}, u32[]{:S(2)}) %collective-permute-start.19) | collective-permute-done | bytes 655392 | tf_op jit(solution)/shard_map/ppermute | solution.py:411
  100.8 0.7 collective-permute-start.25
  101.5 1.9 %collective-permute-done.18 = f32[2,128,384]{2,1,0:T(8,128)S(1)} collective-permute-done((f32[2,128,384]{2,1,0:T(8,128)S(1)}, f32[2,128,384]{2,1,0:T(8,128)S(1)}, u32[]{:S(2)}, u32[]{:S(2)}) %collective-permute-start.18) | collective-permute-done | bytes 393248 | tf_op jit(solution)/shard_map/ppermute | solution.py:260
  103.5 5.7 %collective-permute-start.22 = (f32[2,128,384]{2,1,0:T(8,128)S(1)}, f32[2,128,384]{2,1,0:T(8,128)S(1)}, u32[]{:S(2)}, u32[]{:S(2)}) collective-permute-start(f32[2,128,384]{2,1,0:T(8,128)S(1)} %add.122), channel_id=1, source_target_pairs={{0,4},{2,6},{12,8},{14,10},{1,5},{3,7},{13,9},{15,11},{16,20},{18,... | collective-permute-start | bytes 1179656 | tf_op jit(solution)/shard_map/ppermute | solution.py:411
  109.3 1.3 %collective-permute-start.24 = (f32[128,512]{1,0:T(8,128)S(1)}, f32[128,512]{1,0:T(8,128)S(1)}, u32[]{:S(2)}, u32[]{:S(2)}) collective-permute-start(f32[128,512]{1,0:T(8,128)S(1)} %bitcast_add_fusion.3), channel_id=1, source_target_pairs={{4,12},{6,14},{8,0},{10,2},{5,13},{7,15},{9,1},{11,3},{20,28},{22,... | collective-permute-start | bytes 786440 | tf_op jit(solution)/shard_map/ppermute | solution.py:411
  110.6 0.1 fusion.2
  110.7 0.3 collective-permute-start.17
  111.0 3.4 %collective-permute-done.22 = f32[2,128,384]{2,1,0:T(8,128)S(1)} collective-permute-done((f32[2,128,384]{2,1,0:T(8,128)S(1)}, f32[2,128,384]{2,1,0:T(8,128)S(1)}, u32[]{:S(2)}, u32[]{:S(2)}) %collective-permute-start.22) | collective-permute-done | bytes 393248 | tf_op jit(solution)/shard_map/ppermute | solution.py:411
  114.5 0.7 collective-permute-start.26
  115.2 5.4 %collective-permute-done.24 = f32[128,512]{1,0:T(8,128)S(1)} collective-permute-done((f32[128,512]{1,0:T(8,128)S(1)}, f32[128,512]{1,0:T(8,128)S(1)}, u32[]{:S(2)}, u32[]{:S(2)}) %collective-permute-start.24) | collective-permute-done | bytes 262176 | tf_op jit(solution)/shard_map/ppermute | solution.py:411
  120.6 0.1 bitcast_add_fusion
  120.7 3.1 %final.1 = (bf16[384,1024]{1,0:T(8,128)(2,1)}, bf16[384,1024]{1,0:T(8,128)(2,1)}, bf16[384,1024]{1,0:T(8,128)(2,1)}) custom-call(s32[2]{0:T(128)S(1)} %pad_add_fusion.place, bf16[384,1024]{1,0:T(8,128)(2,1)S(1)} %bitcast.47, bf16[384,1024]{1,0:T(8,128)(2,1)S(1)} %bitcast.52, bf16[384,512]{1,0:T(8,128)(2,1)S(1)} %get-tuple-element.112.refs_0_, ...), custom_call_target="tpu_custom_call" | custom-call | flops 25165824 | tf_op jit(solution)/shard_map/final/pallas_call | solution.py:70
  123.7 0.1 fusion.1
  123.9 0.9 fusion
  (41 shorter events, 0.8 us)
Async XLA Ops:
  0.6 6.6 %copy-start = (bf16[1,384,2048]{2,1,0:T(8,128)(2,1)S(1)}, bf16[1,384,2048]{2,1,0:T(8,128)(2,1)}, u32[]{:S(2)}) copy-start(bf16[1,384,2048]{2,1,0:T(8,128)(2,1)} %param.9) | copy-start | bytes 4718596
  0.7 1.2 copy-start.2
  2.0 1.1 copy-start.4
  4.2 6.9 %collective-permute-start = (f32[2,128,128]{2,1,0:T(8,128)S(1)}, f32[2,128,128]{2,1,0:T(8,128)S(1)}, u32[]{:S(2)}, u32[]{:S(2)}) collective-permute-start(f32[2,128,128]{2,1,0:T(8,128)S(1)} %get-tuple-element.72), channel_id=1, source_target_pairs={{0,2},{2,0},{4,6},{6,4},{8,10},{10,8},{12,14},{14,12},{1,3},{3,1},... | collective-permute-start | bytes 393224 | tf_op jit(solution)/shard_map/ppermute | solution.py:260
  7.2 7.3 %copy-start.1 = (bf16[1,384,1024]{2,1,0:T(8,128)(2,1)S(1)}, bf16[1,384,1024]{2,1,0:T(8,128)(2,1)}, u32[]{:S(2)}) copy-start(bf16[1,384,1024]{2,1,0:T(8,128)(2,1)} %param.5) | copy-start | bytes 2359300
  7.9 35.6 %collective-permute-start.8 = (f32[384,1024]{1,0:T(8,128)S(1)}, f32[384,1024]{1,0:T(8,128)S(1)}, u32[]{:S(2)}, u32[]{:S(2)}) collective-permute-start(f32[384,1024]{1,0:T(8,128)S(1)} %away.1), channel_id=1, source_target_pairs={{0,1},{1,0},{2,3},{3,2},{4,5},{5,4},{6,7},{7,6},{8,9},{9,8},{10,11... | collective-permute-start | bytes 4718600 | tf_op jit(solution)/shard_map/ppermute | solution.py:266
  8.0 9.0 %collective-permute-start.2 = (f32[2,128,128]{2,1,0:T(8,128)S(1)}, f32[2,128,128]{2,1,0:T(8,128)S(1)}, u32[]{:S(2)}, u32[]{:S(2)}) collective-permute-start(f32[2,128,128]{2,1,0:T(8,128)S(1)} %get-tuple-element.76), channel_id=1, source_target_pairs={{0,2},{2,0},{4,6},{6,4},{8,10},{10,8},{12,14},{14,12},{1,3},{3,1},... | collective-permute-start | bytes 393224 | tf_op jit(solution)/shard_map/ppermute | solution.py:260
  11.1 9.4 %collective-permute-start.1 = (f32[2,128,128]{2,1,0:T(8,128)S(1)}, f32[2,128,128]{2,1,0:T(8,128)S(1)}, u32[]{:S(2)}, u32[]{:S(2)}) collective-permute-start(f32[2,128,128]{2,1,0:T(8,128)S(1)} %add.101), channel_id=1, source_target_pairs={{0,4},{2,6},{4,8},{6,10},{8,12},{10,14},{1,5},{3,7},{5,9},{7,11},{... | collective-permute-start | bytes 393224 | tf_op jit(solution)/shard_map/ppermute | solution.py:222
  14.5 9.0 %copy-start.6 = (bf16[1024,2048]{1,0:T(8,128)(2,1)S(1)}, bf16[1024,2048]{1,0:T(8,128)(2,1)}, u32[]{:S(2)}) copy-start(bf16[1024,2048]{1,0:T(8,128)(2,1)} %w_ref.3) | copy-start | bytes 12582916
  17.0 8.9 %collective-permute-start.4 = (f32[2,128,128]{2,1,0:T(8,128)S(1)}, f32[2,128,128]{2,1,0:T(8,128)S(1)}, u32[]{:S(2)}, u32[]{:S(2)}) collective-permute-start(f32[2,128,128]{2,1,0:T(8,128)S(1)} %add.103), channel_id=1, source_target_pairs={{0,4},{2,6},{4,8},{6,10},{8,12},{10,14},{1,5},{3,7},{5,9},{7,11},{... | collective-permute-start | bytes 393224 | tf_op jit(solution)/shard_map/ppermute | solution.py:222
  20.5 13.0 %collective-permute-start.3 = (f32[2,128,128]{2,1,0:T(8,128)S(1)}, f32[2,128,128]{2,1,0:T(8,128)S(1)}, u32[]{:S(2)}, u32[]{:S(2)}) collective-permute-start(f32[2,128,128]{2,1,0:T(8,128)S(1)} %add.102), channel_id=1, source_target_pairs={{0,8},{2,10},{4,12},{6,14},{1,9},{3,11},{5,13},{7,15},{16,24},{18,... | collective-permute-start | bytes 393224 | tf_op jit(solution)/shard_map/ppermute | solution.py:222
  25.9 10.1 %collective-permute-start.5 = (f32[2,128,128]{2,1,0:T(8,128)S(1)}, f32[2,128,128]{2,1,0:T(8,128)S(1)}, u32[]{:S(2)}, u32[]{:S(2)}) collective-permute-start(f32[2,128,128]{2,1,0:T(8,128)S(1)} %add.106), channel_id=1, source_target_pairs={{0,8},{2,10},{4,12},{6,14},{1,9},{3,11},{5,13},{7,15},{16,24},{18,... | collective-permute-start | bytes 393224 | tf_op jit(solution)/shard_map/ppermute | solution.py:222
  33.6 5.0 %collective-permute-start.6 = (f32[2,128,128]{2,1,0:T(8,128)S(1)}, f32[2,128,128]{2,1,0:T(8,128)S(1)}, u32[]{:S(2)}, u32[]{:S(2)}) collective-permute-start(f32[2,128,128]{2,1,0:T(8,128)S(1)} %get-tuple-element.81), channel_id=1, source_target_pairs={{0,2},{2,0},{4,6},{6,4},{8,10},{10,8},{12,14},{14,12},{1,3},{3,1},... | collective-permute-start | bytes 393224 | tf_op jit(solution)/shard_map/ppermute | solution.py:232
  41.1 2.4 %collective-permute-start.7 = (f32[384,512]{1,0:T(8,128)S(1)}, f32[384,512]{1,0:T(8,128)S(1)}, u32[]{:S(2)}, u32[]{:S(2)}) collective-permute-start(f32[384,512]{1,0:T(8,128)S(1)} %get-tuple-element.83), channel_id=1, source_target_pairs={{0,1},{1,0},{2,3},{3,2},{4,5},{5,4},{6,7},{7,6},{8,9},{9,8},{10,11... | collective-permute-start | bytes 2359304 | tf_op jit(solution)/shard_map/ppermute | solution.py:292
  41.2 5.9 %collective-permute-start.9 = (f32[2,128,128]{2,1,0:T(8,128)S(1)}, f32[2,128,128]{2,1,0:T(8,128)S(1)}, u32[]{:S(2)}, u32[]{:S(2)}) collective-permute-start(f32[2,128,128]{2,1,0:T(8,128)S(1)} %get-tuple-element.135), channel_id=1, source_target_pairs={{0,2},{2,0},{4,6},{6,4},{8,10},{10,8},{12,14},{14,12},{1,3},{3,1},... | collective-permute-start | bytes 393224 | tf_op jit(solution)/shard_map/ppermute | solution.py:232
  47.1 4.7 %copy-start.5 = (bf16[1,384,1024]{2,1,0:T(8,128)(2,1)S(1)}, bf16[1,384,1024]{2,1,0:T(8,128)(2,1)}, u32[]{:S(2)}) copy-start(bf16[1,384,1024]{2,1,0:T(8,128)(2,1)} %param.7) | copy-start | bytes 2359300
  49.7 10.8 %collective-permute-start.12 = (f32[384,512]{1,0:T(8,128)S(1)}, f32[384,512]{1,0:T(8,128)S(1)}, u32[]{:S(2)}, u32[]{:S(2)}) collective-permute-start(f32[384,512]{1,0:T(8,128)S(1)} %get-tuple-element.96), channel_id=1, source_target_pairs={{0,1},{1,0},{2,3},{3,2},{4,5},{5,4},{6,7},{7,6},{8,9},{9,8},{10,11... | collective-permute-start | bytes 2359304 | tf_op jit(solution)/shard_map/ppermute | solution.py:344
  49.8 9.2 %collective-permute-start.10 = (f32[4,128,128]{2,1,0:T(8,128)S(1)}, f32[4,128,128]{2,1,0:T(8,128)S(1)}, u32[]{:S(2)}, u32[]{:S(2)}) collective-permute-start(f32[4,128,128]{2,1,0:T(8,128)S(1)} %get-tuple-element.89), channel_id=1, source_target_pairs={{0,2},{2,0},{4,6},{6,4},{8,10},{10,8},{12,14},{14,12},{1,3},{3,1},... | collective-permute-start | bytes 786440 | tf_op jit(solution)/shard_map/ppermute | solution.py:260
  50.1 20.1 %collective-permute-start.15 = (f32[2,128,512]{2,1,0:T(8,128)S(1)}, f32[2,128,512]{2,1,0:T(8,128)S(1)}, u32[]{:S(2)}, u32[]{:S(2)}) collective-permute-start(f32[2,128,512]{2,1,0:T(8,128)S(1)} %get-tuple-element.102), channel_id=1, source_target_pairs={{0,2},{2,0},{4,6},{6,4},{8,10},{10,8},{12,14},{14,12},{1,3},{3,1},... | collective-permute-start | bytes 1572872 | tf_op jit(solution)/shard_map/ppermute | solution.py:260
  59.0 9.5 %collective-permute-start.11 = (f32[4,128,128]{2,1,0:T(8,128)S(1)}, f32[4,128,128]{2,1,0:T(8,128)S(1)}, u32[]{:S(2)}, u32[]{:S(2)}) collective-permute-start(f32[4,128,128]{2,1,0:T(8,128)S(1)} %add.111), channel_id=1, source_target_pairs={{4,0},{6,2},{8,4},{10,6},{12,8},{14,10},{5,1},{7,3},{9,5},{11,7},{... | collective-permute-start | bytes 786440 | tf_op jit(solution)/shard_map/ppermute | solution.py:411
  62.5 21.7 %collective-permute-start.14 = (f32[2,128,640]{2,1,0:T(8,128)S(1)}, f32[2,128,640]{2,1,0:T(8,128)S(1)}, u32[]{:S(2)}, u32[]{:S(2)}) collective-permute-start(f32[2,128,640]{2,1,0:T(8,128)S(1)} %get-tuple-element.97), channel_id=1, source_target_pairs={{0,2},{2,0},{4,6},{6,4},{8,10},{10,8},{12,14},{14,12},{1,3},{3,1},... | collective-permute-start | bytes 1966088 | tf_op jit(solution)/shard_map/ppermute | solution.py:260
  70.3 10.6 %collective-permute-start.16 = (f32[128,512]{1,0:T(8,128)S(1)}, f32[128,512]{1,0:T(8,128)S(1)}, u32[]{:S(2)}, u32[]{:S(2)}) collective-permute-start(f32[128,512]{1,0:T(8,128)S(1)} %select_bitcast_fusion.2), channel_id=1, source_target_pairs={{0,4},{2,6},{4,0},{6,2},{8,12},{10,14},{12,8},{14,10},{1,5},{3,7},... | collective-permute-start | bytes 786440 | tf_op jit(solution)/shard_map/ppermute | solution.py:411
  70.4 17.3 %collective-permute-start.13 = (f32[4,128,128]{2,1,0:T(8,128)S(1)}, f32[4,128,128]{2,1,0:T(8,128)S(1)}, u32[]{:S(2)}, u32[]{:S(2)}) collective-permute-start(f32[4,128,128]{2,1,0:T(8,128)S(1)} %add.112), channel_id=1, source_target_pairs={{8,0},{10,2},{12,4},{14,6},{9,1},{11,3},{13,5},{15,7},{24,16},{26,... | collective-permute-start | bytes 786440 | tf_op jit(solution)/shard_map/ppermute | solution.py:411
  71.7 23.8 %collective-permute-start.20 = (f32[2,128,512]{2,1,0:T(8,128)S(1)}, f32[2,128,512]{2,1,0:T(8,128)S(1)}, u32[]{:S(2)}, u32[]{:S(2)}) collective-permute-start(f32[2,128,512]{2,1,0:T(8,128)S(1)} %get-tuple-element.120), channel_id=1, source_target_pairs={{0,2},{2,0},{4,6},{6,4},{8,10},{10,8},{12,14},{14,12},{1,3},{3,1},... | collective-permute-start | bytes 1572872 | tf_op jit(solution)/shard_map/ppermute | solution.py:260
  84.3 16.5 %collective-permute-start.19 = (f32[2,128,640]{2,1,0:T(8,128)S(1)}, f32[2,128,640]{2,1,0:T(8,128)S(1)}, u32[]{:S(2)}, u32[]{:S(2)}) collective-permute-start(f32[2,128,640]{2,1,0:T(8,128)S(1)} %add.115), channel_id=1, source_target_pairs={{0,4},{2,6},{12,8},{14,10},{1,5},{3,7},{13,9},{15,11},{16,20},{18,... | collective-permute-start | bytes 1966088 | tf_op jit(solution)/shard_map/ppermute | solution.py:411
  85.6 17.8 %collective-permute-start.18 = (f32[2,128,384]{2,1,0:T(8,128)S(1)}, f32[2,128,384]{2,1,0:T(8,128)S(1)}, u32[]{:S(2)}, u32[]{:S(2)}) collective-permute-start(f32[2,128,384]{2,1,0:T(8,128)S(1)} %get-tuple-element.117), channel_id=1, source_target_pairs={{0,2},{2,0},{4,6},{6,4},{8,10},{10,8},{12,14},{14,12},{1,3},{3,1},... | collective-permute-start | bytes 1179656 | tf_op jit(solution)/shard_map/ppermute | solution.py:260
  86.4 9.6 %collective-permute-start.21 = (f32[128,512]{1,0:T(8,128)S(1)}, f32[128,512]{1,0:T(8,128)S(1)}, u32[]{:S(2)}, u32[]{:S(2)}) collective-permute-start(f32[128,512]{1,0:T(8,128)S(1)} %bitcast_add_fusion.4), channel_id=1, source_target_pairs={{4,12},{6,14},{8,0},{10,2},{5,13},{7,15},{9,1},{11,3},{20,28},{22,... | collective-permute-start | bytes 786440 | tf_op jit(solution)/shard_map/ppermute | solution.py:411
  95.6 13.6 %collective-permute-start.23 = (f32[128,512]{1,0:T(8,128)S(1)}, f32[128,512]{1,0:T(8,128)S(1)}, u32[]{:S(2)}, u32[]{:S(2)}) collective-permute-start(f32[128,512]{1,0:T(8,128)S(1)} %select_bitcast_fusion.1), channel_id=1, source_target_pairs={{0,4},{2,6},{4,0},{6,2},{8,12},{10,14},{12,8},{14,10},{1,5},{3,7},... | collective-permute-start | bytes 786440 | tf_op jit(solution)/shard_map/ppermute | solution.py:411
  100.8 14.4 %collective-permute-start.25 = (f32[128,640]{1,0:T(8,128)S(1)}, f32[128,640]{1,0:T(8,128)S(1)}, u32[]{:S(2)}, u32[]{:S(2)}) collective-permute-start(f32[128,640]{1,0:T(8,128)S(1)} %select_bitcast_fusion), channel_id=1, source_target_pairs={{4,8},{6,10},{8,4},{10,6},{5,9},{7,11},{9,5},{11,7},{20,24},{22,26... | collective-permute-start | bytes 983048 | tf_op jit(solution)/shard_map/ppermute | solution.py:411
  103.5 11.0 %collective-permute-start.22 = (f32[2,128,384]{2,1,0:T(8,128)S(1)}, f32[2,128,384]{2,1,0:T(8,128)S(1)}, u32[]{:S(2)}, u32[]{:S(2)}) collective-permute-start(f32[2,128,384]{2,1,0:T(8,128)S(1)} %add.122), channel_id=1, source_target_pairs={{0,4},{2,6},{12,8},{14,10},{1,5},{3,7},{13,9},{15,11},{16,20},{18,... | collective-permute-start | bytes 1179656 | tf_op jit(solution)/shard_map/ppermute | solution.py:411
  109.3 11.3 %collective-permute-start.24 = (f32[128,512]{1,0:T(8,128)S(1)}, f32[128,512]{1,0:T(8,128)S(1)}, u32[]{:S(2)}, u32[]{:S(2)}) collective-permute-start(f32[128,512]{1,0:T(8,128)S(1)} %bitcast_add_fusion.3), channel_id=1, source_target_pairs={{4,12},{6,14},{8,0},{10,2},{5,13},{7,15},{9,1},{11,3},{20,28},{22,... | collective-permute-start | bytes 786440 | tf_op jit(solution)/shard_map/ppermute | solution.py:411
  110.7 10.0 %copy-start.3 = (bf16[1,384,1024]{2,1,0:T(8,128)(2,1)S(1)}, bf16[1,384,1024]{2,1,0:T(8,128)(2,1)}, u32[]{:S(2)}) copy-start(bf16[1,384,1024]{2,1,0:T(8,128)(2,1)} %param.6) | copy-start | bytes 2359300
  110.7 10.0 %collective-permute-start.17 = (f32[4,128,128]{2,1,0:T(8,128)S(1)}, f32[4,128,128]{2,1,0:T(8,128)S(1)}, u32[]{:S(2)}, u32[]{:S(2)}) collective-permute-start(f32[4,128,128]{2,1,0:T(8,128)S(1)} %get-tuple-element.134), channel_id=1, source_target_pairs={{0,2},{2,0},{4,6},{6,4},{8,10},{10,8},{12,14},{14,12},{1,3},{3,1},... | collective-permute-start | bytes 786440 | tf_op jit(solution)/shard_map/ppermute | solution.py:260
  114.5 9.3 %collective-permute-start.26 = (f32[128,384]{1,0:T(8,128)S(1)}, f32[128,384]{1,0:T(8,128)S(1)}, u32[]{:S(2)}, u32[]{:S(2)}) collective-permute-start(f32[128,384]{1,0:T(8,128)S(1)} %select_bitcast_fusion.3), channel_id=1, source_target_pairs={{4,8},{6,10},{8,4},{10,6},{5,9},{7,11},{9,5},{11,7},{20,24},{22,26... | collective-permute-start | bytes 589832 | tf_op jit(solution)/shard_map/ppermute | solution.py:411

commit v11 on v10

--- a/solution.py
+++ b/solution.py
@@ -267,7 +267,7 @@
     (att,) = call(local_body, (rows32,), (q, k, v), 3 * unit * length, "local")
     (d_normed,) = call(d_normed_body, (rows32,), (g, out_weight), unit * width, "d_normed")
     far_prior, near_prior = exclusive(
-        [(states[0], trade(states[1])), (states[2], trade(states[3]))], count, even, False, [(away,), (att,), (d_normed,)]
+        [(states[0], trade(states[1])), (states[2], trade(states[3]))], count, even, False, [(away,), (), (att, d_normed)]
     )
 
     pieces = (shape((length, part), BF16), shape((length, part), F32), shape((length, part), BF16))
@@ -371,19 +371,19 @@
     far1 = far1_keep + after(far1_got, output)
     far1_out = jnp.where(odd, far1[0], far1[1])
     far1_in = hop(far1_out, NEXT)
-    near0_in = after(near0_in, far1_out, far0_end)
+    near1 = near1_keep + after(near1_got, far1_out)
+    near1_in = hop(near1, INWARD)
+    near0_in = after(near0_in, near1, far0_end)
     near0_half = jnp.where(lower, near0[1] + near0_in[1], near0[0] + near0_in[0])
     near0_end = hop(near0_half, ACROSS)
-    near1 = near1_keep + after(near1_got, near0_half)
-    near1_in = hop(near1, INWARD)
-    far1_in = after(far1_in, near1)
+    far1_in = after(far1_in, near0_half)
     far1_half = jnp.where(lower, far1[1], far1[0]) + far1_in
     far1_end = hop(far1_half, OUTWARD)
-    near1_in = after(near1_in, far1_half)
+    near1_in = after(near1_in, far1_half, near0_end)
     near1_half = jnp.where(lower, near1[1] + near1_in[1], near1[0] + near1_in[0])
     near1_end = hop(near1_half, ACROSS)
     query_grad, key_grad, value_grad = finish(own, after(other, near1_half))
-    near0_end, far1_end = after(near0_end, near1_half), after(far1_end, near1_half)
+    far1_end = after(far1_end, near1_half)
 
     far_parts = [
         (jnp.where(lower, base[0], base[1]) + got) + end

time: 125 us -> 127 us (1.016)
  starting transfers between devices: 38.6 us -> 49 us
  waiting for transfers between devices: 49.7 us -> 40.8 us
    ppermute x2, starting transfers between devices: 0.14 us -> 5.67 us  [exclusive(): results.append((mine, lax.ppermute(theirs, 'seq', swap)))]
    ppermute x10, starting transfers between devices: 13.9 us -> 18.8 us  [hop(): lax.ppermute(block, 'seq', [(2 * a + i, 2 * b + i) for a, b in links for...]
    ppermute x4, starting transfers between devices: 17.4 us -> 12.7 us  [exclusive(): got = lax.ppermute(total, 'seq', links(step))]
    ppermute x8, starting transfers between devices: 6.99 us -> 11.5 us  [trade(): return lax.ppermute(send, 'seq', [(s, s ^ 1) for s in range(count)])]
    ppermute x10, waiting for transfers between devices: 24.1 us -> 20.2 us  [hop(): lax.ppermute(block, 'seq', [(2 * a + i, 2 * b + i) for a, b in links for...]
    ppermute x4, waiting for transfers between devices: 2.37 us -> 0.01 us  [exclusive(): got = lax.ppermute(total, 'seq', links(step))]
    ppermute x1, waiting for transfers between devices: 2.19 us -> 0.18 us  [per_device(): chunks = product(far, lax.ppermute(far32, 'dp', swap), WIDTHS[0])]
    ppermute x8, waiting for transfers between devices: 16.8 us -> 15.4 us  [trade(): return lax.ppermute(send, 'seq', [(s, s ^ 1) for s in range(count)])]
  transfers between devices with their start and end apart: 27 -> 27, of which waited for: 16 -> 13; matrix products, arithmetic and copies ran while one was open for 1% -> 1% of each run, Pallas kernels for 22% -> 22%
where the time goes in v11:
time: 127 us; the launch traced here: 126 us
  starting transfers between devices  49 us (39%)
  waiting for transfers between devices  40.8 us (32%)
  Pallas kernels  30.8 us (24%)
  local copies, waits for them, and re-layouts  2.39 us (2%)
  other arithmetic  2.16 us (2%)
    pallas_call x12, Pallas kernels, call(): pl.pallas_call(body, out_shape=tuple(out_shapes), in_specs=specs, out_spe...  30.8 us
    ppermute x10, waiting for transfers between devices, hop(): lax.ppermute(block, 'seq', [(2 * a + i, 2 * b + i) for a, b in links for...  20.2 us
    ppermute x10, starting transfers between devices, hop(): lax.ppermute(block, 'seq', [(2 * a + i, 2 * b + i) for a, b in links for...  18.8 us
    ppermute x8, waiting for transfers between devices, trade(): return lax.ppermute(send, 'seq', [(s, s ^ 1) for s in range(count)])  15.4 us
    ppermute x4, starting transfers between devices, exclusive(): got = lax.ppermute(total, 'seq', links(step))  12.7 us
    ppermute x8, starting transfers between devices, trade(): return lax.ppermute(send, 'seq', [(s, s ^ 1) for s in range(count)])  11.5 us
    ppermute x2, starting transfers between devices, exclusive(): results.append((mine, lax.ppermute(theirs, 'seq', swap)))  5.67 us
    ppermute x2, waiting for transfers between devices, exclusive(): results.append((mine, lax.ppermute(theirs, 'seq', swap)))  4.97 us
  transfers between devices with their start and end apart: 27, of which 13 were waited for; matrix products, arithmetic and copies ran while one was open for 1% of the time, Pallas kernels for 22%

profile of v11, /device:TPU:0, one launch (start us, length us, event | category | flops | bytes accessed | tf_op | source)
XLA Modules:
  0.0 126.2 jit_solution(7108158328330408795)
XLA Ops:
  0.7 0.1 pad_add_fusion.place
  0.7 1.2 copy-done.2
  2.0 1.1 copy-done.4
  3.1 1.1 state.1
  4.2 3.0 %collective-permute-start = (f32[2,128,128]{2,1,0:T(8,128)S(1)}, f32[2,128,128]{2,1,0:T(8,128)S(1)}, u32[]{:S(2)}, u32[]{:S(2)}) collective-permute-start(f32[2,128,128]{2,1,0:T(8,128)S(1)} %get-tuple-element.71), channel_id=1, source_target_pairs={{0,2},{2,0},{4,6},{6,4},{8,10},{10,8},{12,14},{14,12},{1,3},{3,1},... | collective-permute-start | bytes 393224 | tf_op jit(solution)/shard_map/ppermute | solution.py:260
  7.2 0.6 away.1
  7.9 0.1 collective-permute-start.8
  8.0 0.1 collective-permute-start.2
  8.1 3.0 %collective-permute-done = f32[2,128,128]{2,1,0:T(8,128)S(1)} collective-permute-done((f32[2,128,128]{2,1,0:T(8,128)S(1)}, f32[2,128,128]{2,1,0:T(8,128)S(1)}, u32[]{:S(2)}, u32[]{:S(2)}) %collective-permute-start) | collective-permute-done | bytes 131104 | tf_op jit(solution)/shard_map/ppermute | solution.py:260
  11.1 3.4 %collective-permute-start.1 = (f32[2,128,128]{2,1,0:T(8,128)S(1)}, f32[2,128,128]{2,1,0:T(8,128)S(1)}, u32[]{:S(2)}, u32[]{:S(2)}) collective-permute-start(f32[2,128,128]{2,1,0:T(8,128)S(1)} %add.101), channel_id=1, source_target_pairs={{0,4},{2,6},{4,8},{6,10},{8,12},{10,14},{1,5},{3,7},{5,9},{7,11},{... | collective-permute-start | bytes 393224 | tf_op jit(solution)/shard_map/ppermute | solution.py:222
  14.5 3.5 %collective-permute-start.4 = (f32[2,128,128]{2,1,0:T(8,128)S(1)}, f32[2,128,128]{2,1,0:T(8,128)S(1)}, u32[]{:S(2)}, u32[]{:S(2)}) collective-permute-start(f32[2,128,128]{2,1,0:T(8,128)S(1)} %add.103), channel_id=1, source_target_pairs={{0,4},{2,6},{4,8},{6,10},{8,12},{10,14},{1,5},{3,7},{5,9},{7,11},{... | collective-permute-start | bytes 393224 | tf_op jit(solution)/shard_map/ppermute | solution.py:222
  18.1 4.6 %collective-permute-start.3 = (f32[2,128,128]{2,1,0:T(8,128)S(1)}, f32[2,128,128]{2,1,0:T(8,128)S(1)}, u32[]{:S(2)}, u32[]{:S(2)}) collective-permute-start(f32[2,128,128]{2,1,0:T(8,128)S(1)} %add.102), channel_id=1, source_target_pairs={{0,8},{2,10},{4,12},{6,14},{1,9},{3,11},{5,13},{7,15},{16,24},{18,... | collective-permute-start | bytes 393224 | tf_op jit(solution)/shard_map/ppermute | solution.py:222
  22.6 2.4 %local.1.att_ref = f32[384,1024]{1,0:T(8,128)S(1)} custom-call(bf16[384,1024]{1,0:T(8,128)(2,1)S(1)} %bitcast.38, bf16[384,1024]{1,0:T(8,128)(2,1)S(1)} %bitcast.44, bf16[384,1024]{1,0:T(8,128)(2,1)S(1)} %bitcast.49), custom_call_target="tpu_custom_call" | custom-call | flops 56623104 | tf_op jit(solution)/shard_map/local/pallas_call | solution.py:70
  25.1 2.4 %d_normed.1.dn_ref = f32[384,1024]{1,0:T(8,128)S(1)} custom-call(bf16[384,2048]{1,0:T(8,128)(2,1)S(1)} %bitcast.35, bf16[1024,2048]{1,0:T(8,128)(2,1)S(1)} %copy-done.6), custom_call_target="tpu_custom_call" | custom-call | flops 100663296 | tf_op jit(solution)/shard_map/d_normed/pallas_call | solution.py:70
  27.6 1.3 %collective-permute-start.5 = (f32[2,128,128]{2,1,0:T(8,128)S(1)}, f32[2,128,128]{2,1,0:T(8,128)S(1)}, u32[]{:S(2)}, u32[]{:S(2)}) collective-permute-start(f32[2,128,128]{2,1,0:T(8,128)S(1)} %add.106), channel_id=1, source_target_pairs={{0,8},{2,10},{4,12},{6,14},{1,9},{3,11},{5,13},{7,15},{16,24},{18,... | collective-permute-start | bytes 393224 | tf_op jit(solution)/shard_map/ppermute | solution.py:222
  28.9 3.6 %collective-permute-start.6 = (f32[2,128,128]{2,1,0:T(8,128)S(1)}, f32[2,128,128]{2,1,0:T(8,128)S(1)}, u32[]{:S(2)}, u32[]{:S(2)}) collective-permute-start(f32[2,128,128]{2,1,0:T(8,128)S(1)} %get-tuple-element.80), channel_id=1, source_target_pairs={{0,2},{2,0},{4,6},{6,4},{8,10},{10,8},{12,14},{14,12},{1,3},{3,1},... | collective-permute-start | bytes 393224 | tf_op jit(solution)/shard_map/ppermute | solution.py:232
  32.5 2.9 %collective-permute-done.6.other_ref = f32[2,128,128]{2,1,0:T(8,128)S(1)} collective-permute-done((f32[2,128,128]{2,1,0:T(8,128)S(1)}, f32[2,128,128]{2,1,0:T(8,128)S(1)}, u32[]{:S(2)}, u32[]{:S(2)}) %collective-permute-start.6) | collective-permute-done | bytes 131104 | tf_op jit(solution)/shard_map/ppermute | solution.py:232
  35.5 2.5 %norm_far.1 = (bf16[384,512]{1,0:T(8,128)(2,1)S(1)}, f32[384,512]{1,0:T(8,128)S(1)}, bf16[384,512]{1,0:T(8,128)(2,1)S(1)}, f32[2,128,128]{2,1,0:T(8,128)S(1)}, f32[2,128,128]{2,1,0:T(8,128)S(1)}) custom-call(s32[2]{0:T(128)S(1)} %pad_add_fusion.place, bf16[384,1024]{1,0:T(8,128)(2,1)S(1)} %bitcast.39, f32[384,1024]{1,0:T(8,128)S(1)} %local.1.att_ref, ...), custom_call_target="tpu_custom_call" | custom-call | flops 6291456 | tf_op jit(solution)/shard_map/norm_far/pallas_call | solution.py:70
  38.0 0.1 collective-permute-start.7
  38.1 2.1 %collective-permute-start.9 = (f32[2,128,128]{2,1,0:T(8,128)S(1)}, f32[2,128,128]{2,1,0:T(8,128)S(1)}, u32[]{:S(2)}, u32[]{:S(2)}) collective-permute-start(f32[2,128,128]{2,1,0:T(8,128)S(1)} %get-tuple-element.133), channel_id=1, source_target_pairs={{0,2},{2,0},{4,6},{6,4},{8,10},{10,8},{12,14},{14,12},{1,3},{3,1},... | collective-permute-start | bytes 393224 | tf_op jit(solution)/shard_map/ppermute | solution.py:232
  40.2 0.2 collective-permute-done.7.nbo_ref
  40.4 1.8 %weight.2 = (f32[2,128,512]{2,1,0:T(8,128)S(1)}, f32[2,128,512]{2,1,0:T(8,128)S(1)}, f32[2,128,512]{2,1,0:T(8,128)S(1)}, f32[2,128,512]{2,1,0:T(8,128)S(1)}) custom-call(s32[2]{0:T(128)S(1)} %pad_add_fusion.place, bf16[384,512]{1,0:T(8,128)(2,1)S(1)} %get-tuple-element.110.nb_ref.far_ref, bf16[384,2048]{1,0:T(8,128)(2,1)S(1)} %bitcast.36, ...), custom_call_target="tpu_custom_call" | custom-call | flops 50331648 | tf_op jit(solution)/shard_map/weight/pallas_call | solution.py:70
  42.2 2.1 %collective-permute-done.9.other_ref = f32[2,128,128]{2,1,0:T(8,128)S(1)} collective-permute-done((f32[2,128,128]{2,1,0:T(8,128)S(1)}, f32[2,128,128]{2,1,0:T(8,128)S(1)}, u32[]{:S(2)}, u32[]{:S(2)}) %collective-permute-start.9) | collective-permute-done | bytes 131104 | tf_op jit(solution)/shard_map/ppermute | solution.py:232
  44.3 2.6 %norm_near.1 = (bf16[384,512]{1,0:T(8,128)(2,1)S(1)}, f32[384,512]{1,0:T(8,128)S(1)}, bf16[384,512]{1,0:T(8,128)(2,1)S(1)}, f32[4,128,128]{2,1,0:T(8,128)S(1)}, f32[4,128,128]{2,1,0:T(8,128)S(1)}) custom-call(s32[2]{0:T(128)S(1)} %pad_add_fusion.place, bf16[384,1024]{1,0:T(8,128)(2,1)S(1)} %bitcast.40, f32[384,1024]{1,0:T(8,128)S(1)} %local.1.att_ref, ...), custom_call_target="tpu_custom_call" | custom-call | flops 402653184 | tf_op jit(solution)/shard_map/norm_near/pallas_call | solution.py:70
  46.8 0.1 collective-permute-start.12
  46.9 1.8 %collective-permute-start.10 = (f32[4,128,128]{2,1,0:T(8,128)S(1)}, f32[4,128,128]{2,1,0:T(8,128)S(1)}, u32[]{:S(2)}, u32[]{:S(2)}) collective-permute-start(f32[4,128,128]{2,1,0:T(8,128)S(1)} %get-tuple-element.88), channel_id=1, source_target_pairs={{0,2},{2,0},{4,6},{6,4},{8,10},{10,8},{12,14},{14,12},{1,3},{3,1},... | collective-permute-start | bytes 786440 | tf_op jit(solution)/shard_map/ppermute | solution.py:260
  48.7 0.3 collective-permute-start.15
  49.0 4.3 %grads.2 = (bf16[384,512]{1,0:T(8,128)(2,1)S(1)}, f32[384,512]{1,0:T(8,128)S(1)}, f32[384,512]{1,0:T(8,128)S(1)}) custom-call(s32[2]{0:T(128)S(1)} %pad_add_fusion.place, bf16[384,1024]{1,0:T(8,128)(2,1)S(1)} %bitcast.41, bf16[384,1024]{1,0:T(8,128)(2,1)S(1)} %bitcast.45, bf16[384,1024]{1,0:T(8,128)(2,1)S(1)} %bitcast.50, ...), custom_call_target="tpu_custom_call" | custom-call | flops 94371840 | tf_op jit(solution)/shard_map/grads/pallas_call | solution.py:70
  53.3 2.7 %collective-permute-done.10 = f32[4,128,128]{2,1,0:T(8,128)S(1)} collective-permute-done((f32[4,128,128]{2,1,0:T(8,128)S(1)}, f32[4,128,128]{2,1,0:T(8,128)S(1)}, u32[]{:S(2)}, u32[]{:S(2)}) %collective-permute-start.10) | collective-permute-done | bytes 262176 | tf_op jit(solution)/shard_map/ppermute | solution.py:260
  56.1 1.5 %collective-permute-start.11 = (f32[4,128,128]{2,1,0:T(8,128)S(1)}, f32[4,128,128]{2,1,0:T(8,128)S(1)}, u32[]{:S(2)}, u32[]{:S(2)}) collective-permute-start(f32[4,128,128]{2,1,0:T(8,128)S(1)} %add.111), channel_id=1, source_target_pairs={{4,0},{6,2},{8,4},{10,6},{12,8},{14,10},{5,1},{7,3},{9,5},{11,7},{... | collective-permute-start | bytes 786440 | tf_op jit(solution)/shard_map/ppermute | solution.py:411
  57.6 2.0 %weight.3 = (f32[2,128,640]{2,1,0:T(8,128)S(1)}, f32[2,128,640]{2,1,0:T(8,128)S(1)}, f32[2,128,384]{2,1,0:T(8,128)S(1)}, f32[2,128,384]{2,1,0:T(8,128)S(1)}) custom-call(s32[2]{0:T(128)S(1)} %pad_add_fusion.place, bf16[384,512]{1,0:T(8,128)(2,1)S(1)} %get-tuple-element.94.nb_ref.near_ref, bf16[384,2048]{1,0:T(8,128)(2,1)S(1)} %bitcast.37, ...), custom_call_target="tpu_custom_call" | custom-call | flops 50331648 | tf_op jit(solution)/shard_map/weight/pallas_call | solution.py:70
  59.6 1.8 %collective-permute-start.14 = (f32[2,128,640]{2,1,0:T(8,128)S(1)}, f32[2,128,640]{2,1,0:T(8,128)S(1)}, u32[]{:S(2)}, u32[]{:S(2)}) collective-permute-start(f32[2,128,640]{2,1,0:T(8,128)S(1)} %get-tuple-element.96), channel_id=1, source_target_pairs={{0,2},{2,0},{4,6},{6,4},{8,10},{10,8},{12,14},{14,12},{1,3},{3,1},... | collective-permute-start | bytes 1966088 | tf_op jit(solution)/shard_map/ppermute | solution.py:260
  61.4 4.2 %collective-permute-done.11 = f32[4,128,128]{2,1,0:T(8,128)S(1)} collective-permute-done((f32[4,128,128]{2,1,0:T(8,128)S(1)}, f32[4,128,128]{2,1,0:T(8,128)S(1)}, u32[]{:S(2)}, u32[]{:S(2)}) %collective-permute-start.11) | collective-permute-done | bytes 262176 | tf_op jit(solution)/shard_map/ppermute | solution.py:411
  65.7 1.6 %collective-permute-done.15 = f32[2,128,512]{2,1,0:T(8,128)S(1)} collective-permute-done((f32[2,128,512]{2,1,0:T(8,128)S(1)}, f32[2,128,512]{2,1,0:T(8,128)S(1)}, u32[]{:S(2)}, u32[]{:S(2)}) %collective-permute-start.15) | collective-permute-done | bytes 524320 | tf_op jit(solution)/shard_map/ppermute | solution.py:260
  67.3 0.1 add.113
  67.4 1.9 %collective-permute-start.16 = (f32[128,512]{1,0:T(8,128)S(1)}, f32[128,512]{1,0:T(8,128)S(1)}, u32[]{:S(2)}, u32[]{:S(2)}) collective-permute-start(f32[128,512]{1,0:T(8,128)S(1)} %select_bitcast_fusion.2), channel_id=1, source_target_pairs={{0,4},{2,6},{4,0},{6,2},{8,12},{10,14},{12,8},{14,10},{1,5},{3,7},... | collective-permute-start | bytes 786440 | tf_op jit(solution)/shard_map/ppermute | solution.py:411
  69.3 1.3 %collective-permute-start.13 = (f32[4,128,128]{2,1,0:T(8,128)S(1)}, f32[4,128,128]{2,1,0:T(8,128)S(1)}, u32[]{:S(2)}, u32[]{:S(2)}) collective-permute-start(f32[4,128,128]{2,1,0:T(8,128)S(1)} %add.112), channel_id=1, source_target_pairs={{8,0},{10,2},{12,4},{14,6},{9,1},{11,3},{13,5},{15,7},{24,16},{26,... | collective-permute-start | bytes 786440 | tf_op jit(solution)/shard_map/ppermute | solution.py:411
  70.6 1.8 %collective-permute-start.19 = (f32[2,128,512]{2,1,0:T(8,128)S(1)}, f32[2,128,512]{2,1,0:T(8,128)S(1)}, u32[]{:S(2)}, u32[]{:S(2)}) collective-permute-start(f32[2,128,512]{2,1,0:T(8,128)S(1)} %get-tuple-element.119), channel_id=1, source_target_pairs={{0,2},{2,0},{4,6},{6,4},{8,10},{10,8},{12,14},{14,12},{1,3},{3,1},... | collective-permute-start | bytes 1572872 | tf_op jit(solution)/shard_map/ppermute | solution.py:260
  72.4 4.4 %grads.3 = (bf16[384,512]{1,0:T(8,128)(2,1)S(1)}, f32[384,512]{1,0:T(8,128)S(1)}, f32[384,512]{1,0:T(8,128)S(1)}) custom-call(s32[2]{0:T(128)S(1)} %pad_add_fusion.place, bf16[384,1024]{1,0:T(8,128)(2,1)S(1)} %bitcast.42, bf16[384,1024]{1,0:T(8,128)(2,1)S(1)} %bitcast.46, bf16[384,1024]{1,0:T(8,128)(2,1)S(1)} %bitcast.51, ...), custom_call_target="tpu_custom_call" | custom-call | flops 94371840 | tf_op jit(solution)/shard_map/grads/pallas_call | solution.py:70
  76.8 1.9 %collective-permute-done.16 = f32[128,512]{1,0:T(8,128)S(1)} collective-permute-done((f32[128,512]{1,0:T(8,128)S(1)}, f32[128,512]{1,0:T(8,128)S(1)}, u32[]{:S(2)}, u32[]{:S(2)}) %collective-permute-start.16) | collective-permute-done | bytes 262176 | tf_op jit(solution)/shard_map/ppermute | solution.py:411
  78.7 2.6 %collective-permute-done.14 = f32[2,128,640]{2,1,0:T(8,128)S(1)} collective-permute-done((f32[2,128,640]{2,1,0:T(8,128)S(1)}, f32[2,128,640]{2,1,0:T(8,128)S(1)}, u32[]{:S(2)}, u32[]{:S(2)}) %collective-permute-start.14) | collective-permute-done | bytes 655392 | tf_op jit(solution)/shard_map/ppermute | solution.py:260
  81.4 0.1 add.115
  81.4 3.7 %collective-permute-start.22 = (f32[2,128,640]{2,1,0:T(8,128)S(1)}, f32[2,128,640]{2,1,0:T(8,128)S(1)}, u32[]{:S(2)}, u32[]{:S(2)}) collective-permute-start(f32[2,128,640]{2,1,0:T(8,128)S(1)} %add.115), channel_id=1, source_target_pairs={{0,4},{2,6},{12,8},{14,10},{1,5},{3,7},{13,9},{15,11},{16,20},{18,... | collective-permute-start | bytes 1966088 | tf_op jit(solution)/shard_map/ppermute | solution.py:411
  85.2 1.8 %collective-permute-start.18 = (f32[2,128,384]{2,1,0:T(8,128)S(1)}, f32[2,128,384]{2,1,0:T(8,128)S(1)}, u32[]{:S(2)}, u32[]{:S(2)}) collective-permute-start(f32[2,128,384]{2,1,0:T(8,128)S(1)} %get-tuple-element.116), channel_id=1, source_target_pairs={{0,2},{2,0},{4,6},{6,4},{8,10},{10,8},{12,14},{14,12},{1,3},{3,1},... | collective-permute-start | bytes 1179656 | tf_op jit(solution)/shard_map/ppermute | solution.py:260
  87.0 1.3 %collective-permute-start.23 = (f32[128,512]{1,0:T(8,128)S(1)}, f32[128,512]{1,0:T(8,128)S(1)}, u32[]{:S(2)}, u32[]{:S(2)}) collective-permute-start(f32[128,512]{1,0:T(8,128)S(1)} %bitcast_add_fusion.4), channel_id=1, source_target_pairs={{4,12},{6,14},{8,0},{10,2},{5,13},{7,15},{9,1},{11,3},{20,28},{22,... | collective-permute-start | bytes 786440 | tf_op jit(solution)/shard_map/ppermute | solution.py:411
  88.3 0.1 add_select_fusion
  88.4 3.5 %output.1 = bf16[384,2048]{1,0:T(8,128)(2,1)} custom-call(bf16[384,512]{1,0:T(8,128)(2,1)S(1)} %get-tuple-element.110.nb_ref.far_ref, bf16[384,512]{1,0:T(8,128)(2,1)S(1)} %get-tuple-element.94.nb_ref.near_ref, bf16[1024,2048]{1,0:T(8,128)(2,1)S(1)} %copy-done.6), custom_call_target="tpu_custom_call" | custom-call | flops 100663296 | tf_op jit(solution)/shard_map/output/pallas_call | solution.py:70
  91.9 0.7 collective-permute-done.19
  92.6 0.1 add.119
  92.7 2.7 %collective-permute-start.21 = (f32[128,512]{1,0:T(8,128)S(1)}, f32[128,512]{1,0:T(8,128)S(1)}, u32[]{:S(2)}, u32[]{:S(2)}) collective-permute-start(f32[128,512]{1,0:T(8,128)S(1)} %select_bitcast_fusion.1), channel_id=1, source_target_pairs={{0,4},{2,6},{4,0},{6,2},{8,12},{10,14},{12,8},{14,10},{1,5},{3,7},... | collective-permute-start | bytes 786440 | tf_op jit(solution)/shard_map/ppermute | solution.py:411
  95.4 0.9 collective-permute-start.17
  96.3 4.7 %collective-permute-done.18 = f32[2,128,384]{2,1,0:T(8,128)S(1)} collective-permute-done((f32[2,128,384]{2,1,0:T(8,128)S(1)}, f32[2,128,384]{2,1,0:T(8,128)S(1)}, u32[]{:S(2)}, u32[]{:S(2)}) %collective-permute-start.18) | collective-permute-done | bytes 393248 | tf_op jit(solution)/shard_map/ppermute | solution.py:260
  101.1 3.7 %collective-permute-start.20 = (f32[2,128,384]{2,1,0:T(8,128)S(1)}, f32[2,128,384]{2,1,0:T(8,128)S(1)}, u32[]{:S(2)}, u32[]{:S(2)}) collective-permute-start(f32[2,128,384]{2,1,0:T(8,128)S(1)} %add.120), channel_id=1, source_target_pairs={{0,4},{2,6},{12,8},{14,10},{1,5},{3,7},{13,9},{15,11},{16,20},{18,... | collective-permute-start | bytes 1179656 | tf_op jit(solution)/shard_map/ppermute | solution.py:411
  104.8 0.1 select_bitcast_fusion
  104.9 0.8 collective-permute-start.24
  105.8 1.3 %collective-permute-start.25 = (f32[128,512]{1,0:T(8,128)S(1)}, f32[128,512]{1,0:T(8,128)S(1)}, u32[]{:S(2)}, u32[]{:S(2)}) collective-permute-start(f32[128,512]{1,0:T(8,128)S(1)} %bitcast_add_fusion.3), channel_id=1, source_target_pairs={{4,12},{6,14},{8,0},{10,2},{5,13},{7,15},{9,1},{11,3},{20,28},{22,... | collective-permute-start | bytes 786440 | tf_op jit(solution)/shard_map/ppermute | solution.py:411
  107.1 0.1 fusion.2
  107.2 5.3 %collective-permute-done.20 = f32[2,128,384]{2,1,0:T(8,128)S(1)} collective-permute-done((f32[2,128,384]{2,1,0:T(8,128)S(1)}, f32[2,128,384]{2,1,0:T(8,128)S(1)}, u32[]{:S(2)}, u32[]{:S(2)}) %collective-permute-start.20) | collective-permute-done | bytes 393248 | tf_op jit(solution)/shard_map/ppermute | solution.py:411
  112.6 0.7 collective-permute-start.26
  113.2 8.7 %collective-permute-done.25 = f32[128,512]{1,0:T(8,128)S(1)} collective-permute-done((f32[128,512]{1,0:T(8,128)S(1)}, f32[128,512]{1,0:T(8,128)S(1)}, u32[]{:S(2)}, u32[]{:S(2)}) %collective-permute-start.25) | collective-permute-done | bytes 262176 | tf_op jit(solution)/shard_map/ppermute | solution.py:411
  122.0 3.1 %final.1 = (bf16[384,1024]{1,0:T(8,128)(2,1)}, bf16[384,1024]{1,0:T(8,128)(2,1)}, bf16[384,1024]{1,0:T(8,128)(2,1)}) custom-call(s32[2]{0:T(128)S(1)} %pad_add_fusion.place, bf16[384,1024]{1,0:T(8,128)(2,1)S(1)} %bitcast.47, bf16[384,1024]{1,0:T(8,128)(2,1)S(1)} %bitcast.52, bf16[384,512]{1,0:T(8,128)(2,1)S(1)} %get-tuple-element.111.refs_0_, ...), custom_call_target="tpu_custom_call" | custom-call | flops 25165824 | tf_op jit(solution)/shard_map/final/pallas_call | solution.py:70
  125.0 0.1 bitcast_add_fusion
  125.1 0.1 fusion.1
  125.3 0.9 fusion
  (41 shorter events, 0.6 us)
Async XLA Ops:
  0.6 6.6 %copy-start = (bf16[1,384,2048]{2,1,0:T(8,128)(2,1)S(1)}, bf16[1,384,2048]{2,1,0:T(8,128)(2,1)}, u32[]{:S(2)}) copy-start(bf16[1,384,2048]{2,1,0:T(8,128)(2,1)} %param.9) | copy-start | bytes 4718596
  0.7 1.2 copy-start.2
  2.0 1.1 copy-start.4
  4.2 6.9 %collective-permute-start = (f32[2,128,128]{2,1,0:T(8,128)S(1)}, f32[2,128,128]{2,1,0:T(8,128)S(1)}, u32[]{:S(2)}, u32[]{:S(2)}) collective-permute-start(f32[2,128,128]{2,1,0:T(8,128)S(1)} %get-tuple-element.71), channel_id=1, source_target_pairs={{0,2},{2,0},{4,6},{6,4},{8,10},{10,8},{12,14},{14,12},{1,3},{3,1},... | collective-permute-start | bytes 393224 | tf_op jit(solution)/shard_map/ppermute | solution.py:260
  7.2 15.4 %copy-start.1 = (bf16[1,384,1024]{2,1,0:T(8,128)(2,1)S(1)}, bf16[1,384,1024]{2,1,0:T(8,128)(2,1)}, u32[]{:S(2)}) copy-start(bf16[1,384,1024]{2,1,0:T(8,128)(2,1)} %param.5) | copy-start | bytes 2359300
  7.9 32.5 %collective-permute-start.8 = (f32[384,1024]{1,0:T(8,128)S(1)}, f32[384,1024]{1,0:T(8,128)S(1)}, u32[]{:S(2)}, u32[]{:S(2)}) collective-permute-start(f32[384,1024]{1,0:T(8,128)S(1)} %away.1), channel_id=1, source_target_pairs={{0,1},{1,0},{2,3},{3,2},{4,5},{5,4},{6,7},{7,6},{8,9},{9,8},{10,11... | collective-permute-start | bytes 4718600 | tf_op jit(solution)/shard_map/ppermute | solution.py:266
  8.0 6.5 %collective-permute-start.2 = (f32[2,128,128]{2,1,0:T(8,128)S(1)}, f32[2,128,128]{2,1,0:T(8,128)S(1)}, u32[]{:S(2)}, u32[]{:S(2)}) collective-permute-start(f32[2,128,128]{2,1,0:T(8,128)S(1)} %get-tuple-element.75), channel_id=1, source_target_pairs={{0,2},{2,0},{4,6},{6,4},{8,10},{10,8},{12,14},{14,12},{1,3},{3,1},... | collective-permute-start | bytes 393224 | tf_op jit(solution)/shard_map/ppermute | solution.py:260
  11.1 6.9 %collective-permute-start.1 = (f32[2,128,128]{2,1,0:T(8,128)S(1)}, f32[2,128,128]{2,1,0:T(8,128)S(1)}, u32[]{:S(2)}, u32[]{:S(2)}) collective-permute-start(f32[2,128,128]{2,1,0:T(8,128)S(1)} %add.101), channel_id=1, source_target_pairs={{0,4},{2,6},{4,8},{6,10},{8,12},{10,14},{1,5},{3,7},{5,9},{7,11},{... | collective-permute-start | bytes 393224 | tf_op jit(solution)/shard_map/ppermute | solution.py:222
  14.5 13.0 %collective-permute-start.4 = (f32[2,128,128]{2,1,0:T(8,128)S(1)}, f32[2,128,128]{2,1,0:T(8,128)S(1)}, u32[]{:S(2)}, u32[]{:S(2)}) collective-permute-start(f32[2,128,128]{2,1,0:T(8,128)S(1)} %add.103), channel_id=1, source_target_pairs={{0,4},{2,6},{4,8},{6,10},{8,12},{10,14},{1,5},{3,7},{5,9},{7,11},{... | collective-permute-start | bytes 393224 | tf_op jit(solution)/shard_map/ppermute | solution.py:222
  18.0 7.1 %copy-start.6 = (bf16[1024,2048]{1,0:T(8,128)(2,1)S(1)}, bf16[1024,2048]{1,0:T(8,128)(2,1)}, u32[]{:S(2)}) copy-start(bf16[1024,2048]{1,0:T(8,128)(2,1)} %w_ref.3) | copy-start | bytes 12582916
  18.1 10.8 %collective-permute-start.3 = (f32[2,128,128]{2,1,0:T(8,128)S(1)}, f32[2,128,128]{2,1,0:T(8,128)S(1)}, u32[]{:S(2)}, u32[]{:S(2)}) collective-permute-start(f32[2,128,128]{2,1,0:T(8,128)S(1)} %add.102), channel_id=1, source_target_pairs={{0,8},{2,10},{4,12},{6,14},{1,9},{3,11},{5,13},{7,15},{16,24},{18,... | collective-permute-start | bytes 393224 | tf_op jit(solution)/shard_map/ppermute | solution.py:222
  27.6 4.9 %collective-permute-start.5 = (f32[2,128,128]{2,1,0:T(8,128)S(1)}, f32[2,128,128]{2,1,0:T(8,128)S(1)}, u32[]{:S(2)}, u32[]{:S(2)}) collective-permute-start(f32[2,128,128]{2,1,0:T(8,128)S(1)} %add.106), channel_id=1, source_target_pairs={{0,8},{2,10},{4,12},{6,14},{1,9},{3,11},{5,13},{7,15},{16,24},{18,... | collective-permute-start | bytes 393224 | tf_op jit(solution)/shard_map/ppermute | solution.py:222
  28.9 6.5 %collective-permute-start.6 = (f32[2,128,128]{2,1,0:T(8,128)S(1)}, f32[2,128,128]{2,1,0:T(8,128)S(1)}, u32[]{:S(2)}, u32[]{:S(2)}) collective-permute-start(f32[2,128,128]{2,1,0:T(8,128)S(1)} %get-tuple-element.80), channel_id=1, source_target_pairs={{0,2},{2,0},{4,6},{6,4},{8,10},{10,8},{12,14},{14,12},{1,3},{3,1},... | collective-permute-start | bytes 393224 | tf_op jit(solution)/shard_map/ppermute | solution.py:232
  38.0 2.4 %collective-permute-start.7 = (f32[384,512]{1,0:T(8,128)S(1)}, f32[384,512]{1,0:T(8,128)S(1)}, u32[]{:S(2)}, u32[]{:S(2)}) collective-permute-start(f32[384,512]{1,0:T(8,128)S(1)} %get-tuple-element.82), channel_id=1, source_target_pairs={{0,1},{1,0},{2,3},{3,2},{4,5},{5,4},{6,7},{7,6},{8,9},{9,8},{10,11... | collective-permute-start | bytes 2359304 | tf_op jit(solution)/shard_map/ppermute | solution.py:292
  38.1 6.2 %collective-permute-start.9 = (f32[2,128,128]{2,1,0:T(8,128)S(1)}, f32[2,128,128]{2,1,0:T(8,128)S(1)}, u32[]{:S(2)}, u32[]{:S(2)}) collective-permute-start(f32[2,128,128]{2,1,0:T(8,128)S(1)} %get-tuple-element.133), channel_id=1, source_target_pairs={{0,2},{2,0},{4,6},{6,4},{8,10},{10,8},{12,14},{14,12},{1,3},{3,1},... | collective-permute-start | bytes 393224 | tf_op jit(solution)/shard_map/ppermute | solution.py:232
  44.3 4.7 %copy-start.5 = (bf16[1,384,1024]{2,1,0:T(8,128)(2,1)S(1)}, bf16[1,384,1024]{2,1,0:T(8,128)(2,1)}, u32[]{:S(2)}) copy-start(bf16[1,384,1024]{2,1,0:T(8,128)(2,1)} %param.7) | copy-start | bytes 2359300
  46.8 10.8 %collective-permute-start.12 = (f32[384,512]{1,0:T(8,128)S(1)}, f32[384,512]{1,0:T(8,128)S(1)}, u32[]{:S(2)}, u32[]{:S(2)}) collective-permute-start(f32[384,512]{1,0:T(8,128)S(1)} %get-tuple-element.95), channel_id=1, source_target_pairs={{0,1},{1,0},{2,3},{3,2},{4,5},{5,4},{6,7},{7,6},{8,9},{9,8},{10,11... | collective-permute-start | bytes 2359304 | tf_op jit(solution)/shard_map/ppermute | solution.py:344
  46.9 9.2 %collective-permute-start.10 = (f32[4,128,128]{2,1,0:T(8,128)S(1)}, f32[4,128,128]{2,1,0:T(8,128)S(1)}, u32[]{:S(2)}, u32[]{:S(2)}) collective-permute-start(f32[4,128,128]{2,1,0:T(8,128)S(1)} %get-tuple-element.88), channel_id=1, source_target_pairs={{0,2},{2,0},{4,6},{6,4},{8,10},{10,8},{12,14},{14,12},{1,3},{3,1},... | collective-permute-start | bytes 786440 | tf_op jit(solution)/shard_map/ppermute | solution.py:260
  48.7 18.6 %collective-permute-start.15 = (f32[2,128,512]{2,1,0:T(8,128)S(1)}, f32[2,128,512]{2,1,0:T(8,128)S(1)}, u32[]{:S(2)}, u32[]{:S(2)}) collective-permute-start(f32[2,128,512]{2,1,0:T(8,128)S(1)} %get-tuple-element.101), channel_id=1, source_target_pairs={{0,2},{2,0},{4,6},{6,4},{8,10},{10,8},{12,14},{14,12},{1,3},{3,1},... | collective-permute-start | bytes 1572872 | tf_op jit(solution)/shard_map/ppermute | solution.py:260
  56.1 9.5 %collective-permute-start.11 = (f32[4,128,128]{2,1,0:T(8,128)S(1)}, f32[4,128,128]{2,1,0:T(8,128)S(1)}, u32[]{:S(2)}, u32[]{:S(2)}) collective-permute-start(f32[4,128,128]{2,1,0:T(8,128)S(1)} %add.111), channel_id=1, source_target_pairs={{4,0},{6,2},{8,4},{10,6},{12,8},{14,10},{5,1},{7,3},{9,5},{11,7},{... | collective-permute-start | bytes 786440 | tf_op jit(solution)/shard_map/ppermute | solution.py:411
  59.6 21.7 %collective-permute-start.14 = (f32[2,128,640]{2,1,0:T(8,128)S(1)}, f32[2,128,640]{2,1,0:T(8,128)S(1)}, u32[]{:S(2)}, u32[]{:S(2)}) collective-permute-start(f32[2,128,640]{2,1,0:T(8,128)S(1)} %get-tuple-element.96), channel_id=1, source_target_pairs={{0,2},{2,0},{4,6},{6,4},{8,10},{10,8},{12,14},{14,12},{1,3},{3,1},... | collective-permute-start | bytes 1966088 | tf_op jit(solution)/shard_map/ppermute | solution.py:260
  67.4 11.2 %collective-permute-start.16 = (f32[128,512]{1,0:T(8,128)S(1)}, f32[128,512]{1,0:T(8,128)S(1)}, u32[]{:S(2)}, u32[]{:S(2)}) collective-permute-start(f32[128,512]{1,0:T(8,128)S(1)} %select_bitcast_fusion.2), channel_id=1, source_target_pairs={{0,4},{2,6},{4,0},{6,2},{8,12},{10,14},{12,8},{14,10},{1,5},{3,7},... | collective-permute-start | bytes 786440 | tf_op jit(solution)/shard_map/ppermute | solution.py:411
  69.3 19.0 %collective-permute-start.13 = (f32[4,128,128]{2,1,0:T(8,128)S(1)}, f32[4,128,128]{2,1,0:T(8,128)S(1)}, u32[]{:S(2)}, u32[]{:S(2)}) collective-permute-start(f32[4,128,128]{2,1,0:T(8,128)S(1)} %add.112), channel_id=1, source_target_pairs={{8,0},{10,2},{12,4},{14,6},{9,1},{11,3},{13,5},{15,7},{24,16},{26,... | collective-permute-start | bytes 786440 | tf_op jit(solution)/shard_map/ppermute | solution.py:411
  70.6 22.0 %collective-permute-start.19 = (f32[2,128,512]{2,1,0:T(8,128)S(1)}, f32[2,128,512]{2,1,0:T(8,128)S(1)}, u32[]{:S(2)}, u32[]{:S(2)}) collective-permute-start(f32[2,128,512]{2,1,0:T(8,128)S(1)} %get-tuple-element.119), channel_id=1, source_target_pairs={{0,2},{2,0},{4,6},{6,4},{8,10},{10,8},{12,14},{14,12},{1,3},{3,1},... | collective-permute-start | bytes 1572872 | tf_op jit(solution)/shard_map/ppermute | solution.py:260
  81.4 23.4 %collective-permute-start.22 = (f32[2,128,640]{2,1,0:T(8,128)S(1)}, f32[2,128,640]{2,1,0:T(8,128)S(1)}, u32[]{:S(2)}, u32[]{:S(2)}) collective-permute-start(f32[2,128,640]{2,1,0:T(8,128)S(1)} %add.115), channel_id=1, source_target_pairs={{0,4},{2,6},{12,8},{14,10},{1,5},{3,7},{13,9},{15,11},{16,20},{18,... | collective-permute-start | bytes 1966088 | tf_op jit(solution)/shard_map/ppermute | solution.py:411
  85.2 15.8 %collective-permute-start.18 = (f32[2,128,384]{2,1,0:T(8,128)S(1)}, f32[2,128,384]{2,1,0:T(8,128)S(1)}, u32[]{:S(2)}, u32[]{:S(2)}) collective-permute-start(f32[2,128,384]{2,1,0:T(8,128)S(1)} %get-tuple-element.116), channel_id=1, source_target_pairs={{0,2},{2,0},{4,6},{6,4},{8,10},{10,8},{12,14},{14,12},{1,3},{3,1},... | collective-permute-start | bytes 1179656 | tf_op jit(solution)/shard_map/ppermute | solution.py:260
  87.0 17.8 %collective-permute-start.23 = (f32[128,512]{1,0:T(8,128)S(1)}, f32[128,512]{1,0:T(8,128)S(1)}, u32[]{:S(2)}, u32[]{:S(2)}) collective-permute-start(f32[128,512]{1,0:T(8,128)S(1)} %bitcast_add_fusion.4), channel_id=1, source_target_pairs={{4,12},{6,14},{8,0},{10,2},{5,13},{7,15},{9,1},{11,3},{20,28},{22,... | collective-permute-start | bytes 786440 | tf_op jit(solution)/shard_map/ppermute | solution.py:411
  92.7 13.0 %collective-permute-start.21 = (f32[128,512]{1,0:T(8,128)S(1)}, f32[128,512]{1,0:T(8,128)S(1)}, u32[]{:S(2)}, u32[]{:S(2)}) collective-permute-start(f32[128,512]{1,0:T(8,128)S(1)} %select_bitcast_fusion.1), channel_id=1, source_target_pairs={{0,4},{2,6},{4,0},{6,2},{8,12},{10,14},{12,8},{14,10},{1,5},{3,7},... | collective-permute-start | bytes 786440 | tf_op jit(solution)/shard_map/ppermute | solution.py:411
  95.4 26.5 %collective-permute-start.17 = (f32[4,128,128]{2,1,0:T(8,128)S(1)}, f32[4,128,128]{2,1,0:T(8,128)S(1)}, u32[]{:S(2)}, u32[]{:S(2)}) collective-permute-start(f32[4,128,128]{2,1,0:T(8,128)S(1)} %get-tuple-element.132), channel_id=1, source_target_pairs={{0,2},{2,0},{4,6},{6,4},{8,10},{10,8},{12,14},{14,12},{1,3},{3,1},... | collective-permute-start | bytes 786440 | tf_op jit(solution)/shard_map/ppermute | solution.py:260
  101.1 11.5 %collective-permute-start.20 = (f32[2,128,384]{2,1,0:T(8,128)S(1)}, f32[2,128,384]{2,1,0:T(8,128)S(1)}, u32[]{:S(2)}, u32[]{:S(2)}) collective-permute-start(f32[2,128,384]{2,1,0:T(8,128)S(1)} %add.120), channel_id=1, source_target_pairs={{0,4},{2,6},{12,8},{14,10},{1,5},{3,7},{13,9},{15,11},{16,20},{18,... | collective-permute-start | bytes 1179656 | tf_op jit(solution)/shard_map/ppermute | solution.py:411
  104.9 17.1 %copy-start.3 = (bf16[1,384,1024]{2,1,0:T(8,128)(2,1)S(1)}, bf16[1,384,1024]{2,1,0:T(8,128)(2,1)}, u32[]{:S(2)}) copy-start(bf16[1,384,1024]{2,1,0:T(8,128)(2,1)} %param.6) | copy-start | bytes 2359300
  104.9 7.6 %collective-permute-start.24 = (f32[128,640]{1,0:T(8,128)S(1)}, f32[128,640]{1,0:T(8,128)S(1)}, u32[]{:S(2)}, u32[]{:S(2)}) collective-permute-start(f32[128,640]{1,0:T(8,128)S(1)} %select_bitcast_fusion), channel_id=1, source_target_pairs={{4,8},{6,10},{8,4},{10,6},{5,9},{7,11},{9,5},{11,7},{20,24},{22,26... | collective-permute-start | bytes 983048 | tf_op jit(solution)/shard_map/ppermute | solution.py:411
  105.8 16.2 %collective-permute-start.25 = (f32[128,512]{1,0:T(8,128)S(1)}, f32[128,512]{1,0:T(8,128)S(1)}, u32[]{:S(2)}, u32[]{:S(2)}) collective-permute-start(f32[128,512]{1,0:T(8,128)S(1)} %bitcast_add_fusion.3), channel_id=1, source_target_pairs={{4,12},{6,14},{8,0},{10,2},{5,13},{7,15},{9,1},{11,3},{20,28},{22,... | collective-permute-start | bytes 786440 | tf_op jit(solution)/shard_map/ppermute | solution.py:411
  112.6 12.7 %collective-permute-start.26 = (f32[128,384]{1,0:T(8,128)S(1)}, f32[128,384]{1,0:T(8,128)S(1)}, u32[]{:S(2)}, u32[]{:S(2)}) collective-permute-start(f32[128,384]{1,0:T(8,128)S(1)} %select_bitcast_fusion.3), channel_id=1, source_target_pairs={{4,8},{6,10},{8,4},{10,6},{5,9},{7,11},{9,5},{11,7},{20,24},{22,26... | collective-permute-start | bytes 589832 | tf_op jit(solution)/shard_map/ppermute | solution.py:411

commit v12 on v11

--- a/solution.py
+++ b/solution.py
@@ -14,7 +14,7 @@
 PAIRS = H // 2
 FAR = (0, 3)
 NEAR = (1, 2)
-WIDTHS = ((4, 4), (5, 3))
+WIDTHS = ((3, 5), (6, 2))
 EPSILON = 1e-06
 F32 = jnp.float32
 BF16 = jnp.bfloat16
@@ -267,7 +267,7 @@
     (att,) = call(local_body, (rows32,), (q, k, v), 3 * unit * length, "local")
     (d_normed,) = call(d_normed_body, (rows32,), (g, out_weight), unit * width, "d_normed")
     far_prior, near_prior = exclusive(
-        [(states[0], trade(states[1])), (states[2], trade(states[3]))], count, even, False, [(away,), (), (att, d_normed)]
+        [(states[0], trade(states[1])), (states[2], trade(states[3]))], count, even, False, [(away,), (att,), (d_normed,)]
     )
 
     pieces = (shape((length, part), BF16), shape((length, part), F32), shape((length, part), BF16))
@@ -347,7 +347,7 @@
     received = after(received, far_grads[1])
     (near0_keep, near0_send), (near1_keep, near1_send) = product(after(near, received), nbo, WIDTHS[1])
     near0_got = trade(near0_send)
-    total = keep + received
+    total = keep + after(received, near0_send)
     back1 = hop(total, BACK)
     near1_got = trade(near1_send)
     back1 = after(back1, near0_send)
@@ -365,7 +365,6 @@
     near0_in = hop(near0, INWARD)
     outside = back1 + after(back2, near0)
     theirs = jnp.where(even, outside, outside + keep)
-    other = trade(theirs)
     own = jnp.where(even, outside + received, outside)
     output = project(after(far, theirs))
     far1 = far1_keep + after(far1_got, output)
@@ -373,6 +372,7 @@
     far1_in = hop(far1_out, NEXT)
     near1 = near1_keep + after(near1_got, far1_out)
     near1_in = hop(near1, INWARD)
+    other = trade(after(theirs, near1))
     near0_in = after(near0_in, near1, far0_end)
     near0_half = jnp.where(lower, near0[1] + near0_in[1], near0[0] + near0_in[0])
     near0_end = hop(near0_half, ACROSS)

time: 127 us -> 130 us (1.024)
  waiting for transfers between devices: 40.8 us -> 56.5 us
  starting transfers between devices: 49 us -> 37.1 us
    ppermute x10, starting transfers between devices: 18.8 us -> 12.5 us  [hop(): lax.ppermute(block, 'seq', [(2 * a + i, 2 * b + i) for a, b in links for...]
    ppermute x10, waiting for transfers between devices: 20.2 us -> 26.3 us  [hop(): lax.ppermute(block, 'seq', [(2 * a + i, 2 * b + i) for a, b in links for...]
    ppermute x8, waiting for transfers between devices: 15.4 us -> 21.4 us  [trade(): return lax.ppermute(send, 'seq', [(s, s ^ 1) for s in range(count)])]
    ppermute x2, starting transfers between devices: 5.67 us -> 0.14 us  [exclusive(): results.append((mine, lax.ppermute(theirs, 'seq', swap)))]
    ppermute x4, starting transfers between devices: 12.7 us -> 17.5 us  [exclusive(): got = lax.ppermute(total, 'seq', links(step))]
    ppermute x8, starting transfers between devices: 11.5 us -> 6.75 us  [trade(): return lax.ppermute(send, 'seq', [(s, s ^ 1) for s in range(count)])]
    ppermute x4, waiting for transfers between devices: 0.01 us -> 2.19 us  [exclusive(): got = lax.ppermute(total, 'seq', links(step))]
    ppermute x1, waiting for transfers between devices: 0.18 us -> 2.19 us  [per_device(): chunks = product(far, lax.ppermute(far32, 'dp', swap), WIDTHS[0])]
  transfers between devices with their start and end apart: 27 -> 27, of which waited for: 13 -> 14; matrix products, arithmetic and copies ran while one was open for 1% -> 1% of each run, Pallas kernels for 22% -> 21%
where the time goes in v12:
time: 130 us
  waiting for transfers between devices  56.5 us (43%)
  starting transfers between devices  37.1 us (29%)
  Pallas kernels  30.8 us (24%)
  local copies, waits for them, and re-layouts  2.39 us (2%)
  other arithmetic  2.1 us (2%)
    pallas_call x12, Pallas kernels, call(): pl.pallas_call(body, out_shape=tuple(out_shapes), in_specs=specs, out_spe...  30.8 us
    ppermute x10, waiting for transfers between devices, hop(): lax.ppermute(block, 'seq', [(2 * a + i, 2 * b + i) for a, b in links for...  26.3 us
    ppermute x8, waiting for transfers between devices, trade(): return lax.ppermute(send, 'seq', [(s, s ^ 1) for s in range(count)])  21.4 us
    ppermute x4, starting transfers between devices, exclusive(): got = lax.ppermute(total, 'seq', links(step))  17.5 us
    ppermute x10, starting transfers between devices, hop(): lax.ppermute(block, 'seq', [(2 * a + i, 2 * b + i) for a, b in links for...  12.5 us
    ppermute x8, starting transfers between devices, trade(): return lax.ppermute(send, 'seq', [(s, s ^ 1) for s in range(count)])  6.75 us
    ppermute x2, waiting for transfers between devices, exclusive(): results.append((mine, lax.ppermute(theirs, 'seq', swap)))  4.39 us
  transfers between devices with their start and end apart: 27, of which 14 were waited for; matrix products, arithmetic and copies ran while one was open for 1% of the time, Pallas kernels for 21%

profile of v12, /device:TPU:0, one launch (start us, length us, event | category | flops | bytes accessed | tf_op | source)
XLA Modules:
  0.0 130.0 jit_solution(7235998672408588652)
XLA Ops:
  0.7 0.1 pad_add_fusion.place
  0.7 1.2 copy-done.2
  2.0 1.1 copy-done.4
  3.1 1.1 state.1
  4.2 3.0 %collective-permute-start = (f32[2,128,128]{2,1,0:T(8,128)S(1)}, f32[2,128,128]{2,1,0:T(8,128)S(1)}, u32[]{:S(2)}, u32[]{:S(2)}) collective-permute-start(f32[2,128,128]{2,1,0:T(8,128)S(1)} %get-tuple-element.73), channel_id=1, source_target_pairs={{0,2},{2,0},{4,6},{6,4},{8,10},{10,8},{12,14},{14,12},{1,3},{3,1},... | collective-permute-start | bytes 393224 | tf_op jit(solution)/shard_map/ppermute | solution.py:260
  7.2 0.6 away.1
  7.9 0.1 collective-permute-start.8
  8.0 0.1 collective-permute-start.2
  8.1 3.0 %collective-permute-done = f32[2,128,128]{2,1,0:T(8,128)S(1)} collective-permute-done((f32[2,128,128]{2,1,0:T(8,128)S(1)}, f32[2,128,128]{2,1,0:T(8,128)S(1)}, u32[]{:S(2)}, u32[]{:S(2)}) %collective-permute-start) | collective-permute-done | bytes 131104 | tf_op jit(solution)/shard_map/ppermute | solution.py:260
  11.1 3.4 %collective-permute-start.1 = (f32[2,128,128]{2,1,0:T(8,128)S(1)}, f32[2,128,128]{2,1,0:T(8,128)S(1)}, u32[]{:S(2)}, u32[]{:S(2)}) collective-permute-start(f32[2,128,128]{2,1,0:T(8,128)S(1)} %add.101), channel_id=1, source_target_pairs={{0,4},{2,6},{4,8},{6,10},{8,12},{10,14},{1,5},{3,7},{5,9},{7,11},{... | collective-permute-start | bytes 393224 | tf_op jit(solution)/shard_map/ppermute | solution.py:222
  14.5 2.4 %local.1.att_ref = f32[384,1024]{1,0:T(8,128)S(1)} custom-call(bf16[384,1024]{1,0:T(8,128)(2,1)S(1)} %bitcast.38, bf16[384,1024]{1,0:T(8,128)(2,1)S(1)} %bitcast.44, bf16[384,1024]{1,0:T(8,128)(2,1)S(1)} %bitcast.49), custom_call_target="tpu_custom_call" | custom-call | flops 56623104 | tf_op jit(solution)/shard_map/local/pallas_call | solution.py:70
  17.0 3.5 %collective-permute-start.4 = (f32[2,128,128]{2,1,0:T(8,128)S(1)}, f32[2,128,128]{2,1,0:T(8,128)S(1)}, u32[]{:S(2)}, u32[]{:S(2)}) collective-permute-start(f32[2,128,128]{2,1,0:T(8,128)S(1)} %add.103), channel_id=1, source_target_pairs={{0,4},{2,6},{4,8},{6,10},{8,12},{10,14},{1,5},{3,7},{5,9},{7,11},{... | collective-permute-start | bytes 393224 | tf_op jit(solution)/shard_map/ppermute | solution.py:222
  20.5 2.9 %collective-permute-start.3 = (f32[2,128,128]{2,1,0:T(8,128)S(1)}, f32[2,128,128]{2,1,0:T(8,128)S(1)}, u32[]{:S(2)}, u32[]{:S(2)}) collective-permute-start(f32[2,128,128]{2,1,0:T(8,128)S(1)} %add.102), channel_id=1, source_target_pairs={{0,8},{2,10},{4,12},{6,14},{1,9},{3,11},{5,13},{7,15},{16,24},{18,... | collective-permute-start | bytes 393224 | tf_op jit(solution)/shard_map/ppermute | solution.py:222
  23.5 2.4 %d_normed.1.dn_ref = f32[384,1024]{1,0:T(8,128)S(1)} custom-call(bf16[384,2048]{1,0:T(8,128)(2,1)S(1)} %bitcast.35, bf16[1024,2048]{1,0:T(8,128)(2,1)S(1)} %copy-done.6), custom_call_target="tpu_custom_call" | custom-call | flops 100663296 | tf_op jit(solution)/shard_map/d_normed/pallas_call | solution.py:70
  25.9 7.8 %collective-permute-start.5 = (f32[2,128,128]{2,1,0:T(8,128)S(1)}, f32[2,128,128]{2,1,0:T(8,128)S(1)}, u32[]{:S(2)}, u32[]{:S(2)}) collective-permute-start(f32[2,128,128]{2,1,0:T(8,128)S(1)} %add.106), channel_id=1, source_target_pairs={{0,8},{2,10},{4,12},{6,14},{1,9},{3,11},{5,13},{7,15},{16,24},{18,... | collective-permute-start | bytes 393224 | tf_op jit(solution)/shard_map/ppermute | solution.py:222
  33.7 0.1 collective-permute-start.6
  33.8 2.2 %collective-permute-done.5 = f32[2,128,128]{2,1,0:T(8,128)S(1)} collective-permute-done((f32[2,128,128]{2,1,0:T(8,128)S(1)}, f32[2,128,128]{2,1,0:T(8,128)S(1)}, u32[]{:S(2)}, u32[]{:S(2)}) %collective-permute-start.5) | collective-permute-done | bytes 131104 | tf_op jit(solution)/shard_map/ppermute | solution.py:222
  36.0 2.7 %collective-permute-done.6.other_ref = f32[2,128,128]{2,1,0:T(8,128)S(1)} collective-permute-done((f32[2,128,128]{2,1,0:T(8,128)S(1)}, f32[2,128,128]{2,1,0:T(8,128)S(1)}, u32[]{:S(2)}, u32[]{:S(2)}) %collective-permute-start.6) | collective-permute-done | bytes 131104 | tf_op jit(solution)/shard_map/ppermute | solution.py:232
  38.8 2.5 %norm_far.1 = (bf16[384,512]{1,0:T(8,128)(2,1)S(1)}, f32[384,512]{1,0:T(8,128)S(1)}, bf16[384,512]{1,0:T(8,128)(2,1)S(1)}, f32[2,128,128]{2,1,0:T(8,128)S(1)}, f32[2,128,128]{2,1,0:T(8,128)S(1)}) custom-call(s32[2]{0:T(128)S(1)} %pad_add_fusion.place, bf16[384,1024]{1,0:T(8,128)(2,1)S(1)} %bitcast.39, f32[384,1024]{1,0:T(8,128)S(1)} %local.1.att_ref, ...), custom_call_target="tpu_custom_call" | custom-call | flops 6291456 | tf_op jit(solution)/shard_map/norm_far/pallas_call | solution.py:70
  41.3 0.1 collective-permute-start.7
  41.4 0.1 collective-permute-start.9
  41.5 2.2 %collective-permute-done.7.nbo_ref = f32[384,512]{1,0:T(8,128)S(1)} collective-permute-done((f32[384,512]{1,0:T(8,128)S(1)}, f32[384,512]{1,0:T(8,128)S(1)}, u32[]{:S(2)}, u32[]{:S(2)}) %collective-permute-start.7) | collective-permute-done | bytes 786464 | tf_op jit(solution)/shard_map/ppermute | solution.py:292
  43.7 2.0 %weight.2 = (f32[2,128,384]{2,1,0:T(8,128)S(1)}, f32[2,128,384]{2,1,0:T(8,128)S(1)}, f32[2,128,640]{2,1,0:T(8,128)S(1)}, f32[2,128,640]{2,1,0:T(8,128)S(1)}) custom-call(s32[2]{0:T(128)S(1)} %pad_add_fusion.place, bf16[384,512]{1,0:T(8,128)(2,1)S(1)} %get-tuple-element.113.nb_ref.far_ref, bf16[384,2048]{1,0:T(8,128)(2,1)S(1)} %bitcast.36, ...), custom_call_target="tpu_custom_call" | custom-call | flops 50331648 | tf_op jit(solution)/shard_map/weight/pallas_call | solution.py:70
  45.7 1.7 %collective-permute-done.9.other_ref = f32[2,128,128]{2,1,0:T(8,128)S(1)} collective-permute-done((f32[2,128,128]{2,1,0:T(8,128)S(1)}, f32[2,128,128]{2,1,0:T(8,128)S(1)}, u32[]{:S(2)}, u32[]{:S(2)}) %collective-permute-start.9) | collective-permute-done | bytes 131104 | tf_op jit(solution)/shard_map/ppermute | solution.py:232
  47.3 2.6 %norm_near.1 = (bf16[384,512]{1,0:T(8,128)(2,1)S(1)}, f32[384,512]{1,0:T(8,128)S(1)}, bf16[384,512]{1,0:T(8,128)(2,1)S(1)}, f32[4,128,128]{2,1,0:T(8,128)S(1)}, f32[4,128,128]{2,1,0:T(8,128)S(1)}) custom-call(s32[2]{0:T(128)S(1)} %pad_add_fusion.place, bf16[384,1024]{1,0:T(8,128)(2,1)S(1)} %bitcast.40, f32[384,1024]{1,0:T(8,128)S(1)} %local.1.att_ref, ...), custom_call_target="tpu_custom_call" | custom-call | flops 402653184 | tf_op jit(solution)/shard_map/norm_near/pallas_call | solution.py:70
  49.9 0.1 collective-permute-start.11
  50.0 0.3 collective-permute-start.10
  50.3 1.8 %collective-permute-start.15 = (f32[2,128,384]{2,1,0:T(8,128)S(1)}, f32[2,128,384]{2,1,0:T(8,128)S(1)}, u32[]{:S(2)}, u32[]{:S(2)}) collective-permute-start(f32[2,128,384]{2,1,0:T(8,128)S(1)} %get-tuple-element.104), channel_id=1, source_target_pairs={{0,2},{2,0},{4,6},{6,4},{8,10},{10,8},{12,14},{14,12},{1,3},{3,1},... | collective-permute-start | bytes 1179656 | tf_op jit(solution)/shard_map/ppermute | solution.py:260
  52.1 4.3 %grads.2 = (bf16[384,512]{1,0:T(8,128)(2,1)S(1)}, f32[384,512]{1,0:T(8,128)S(1)}, f32[384,512]{1,0:T(8,128)S(1)}) custom-call(s32[2]{0:T(128)S(1)} %pad_add_fusion.place, bf16[384,1024]{1,0:T(8,128)(2,1)S(1)} %bitcast.41, bf16[384,1024]{1,0:T(8,128)(2,1)S(1)} %bitcast.45, bf16[384,1024]{1,0:T(8,128)(2,1)S(1)} %bitcast.50, ...), custom_call_target="tpu_custom_call" | custom-call | flops 94371840 | tf_op jit(solution)/shard_map/grads/pallas_call | solution.py:70
  56.4 2.7 %collective-permute-done.10 = f32[4,128,128]{2,1,0:T(8,128)S(1)} collective-permute-done((f32[4,128,128]{2,1,0:T(8,128)S(1)}, f32[4,128,128]{2,1,0:T(8,128)S(1)}, u32[]{:S(2)}, u32[]{:S(2)}) %collective-permute-start.10) | collective-permute-done | bytes 262176 | tf_op jit(solution)/shard_map/ppermute | solution.py:260
  59.1 1.8 %weight.3 = (f32[2,128,768]{2,1,0:T(8,128)S(1)}, f32[2,128,768]{2,1,0:T(8,128)S(1)}, f32[2,128,256]{2,1,0:T(8,128)S(1)}, f32[2,128,256]{2,1,0:T(8,128)S(1)}) custom-call(s32[2]{0:T(128)S(1)} %pad_add_fusion.place, bf16[384,512]{1,0:T(8,128)(2,1)S(1)} %get-tuple-element.96.nb_ref.near_ref, bf16[384,2048]{1,0:T(8,128)(2,1)S(1)} %bitcast.37, ...), custom_call_target="tpu_custom_call" | custom-call | flops 50331648 | tf_op jit(solution)/shard_map/weight/pallas_call | solution.py:70
  61.0 1.3 collective-permute-start.12
  62.3 0.3 collective-permute-start.14
  62.6 7.7 %collective-permute-done.12 = f32[4,128,128]{2,1,0:T(8,128)S(1)} collective-permute-done((f32[4,128,128]{2,1,0:T(8,128)S(1)}, f32[4,128,128]{2,1,0:T(8,128)S(1)}, u32[]{:S(2)}, u32[]{:S(2)}) %collective-permute-start.12) | collective-permute-done | bytes 262176 | tf_op jit(solution)/shard_map/ppermute | solution.py:411
  70.5 0.1 collective-permute-start.16
  70.6 1.5 %collective-permute-start.13 = (f32[4,128,128]{2,1,0:T(8,128)S(1)}, f32[4,128,128]{2,1,0:T(8,128)S(1)}, u32[]{:S(2)}, u32[]{:S(2)}) collective-permute-start(f32[4,128,128]{2,1,0:T(8,128)S(1)} %add.112), channel_id=1, source_target_pairs={{8,0},{10,2},{12,4},{14,6},{9,1},{11,3},{13,5},{15,7},{24,16},{26,... | collective-permute-start | bytes 786440 | tf_op jit(solution)/shard_map/ppermute | solution.py:411
  72.1 0.3 collective-permute-start.18
  72.4 4.4 %grads.3 = (bf16[384,512]{1,0:T(8,128)(2,1)S(1)}, f32[384,512]{1,0:T(8,128)S(1)}, f32[384,512]{1,0:T(8,128)S(1)}) custom-call(s32[2]{0:T(128)S(1)} %pad_add_fusion.place, bf16[384,1024]{1,0:T(8,128)(2,1)S(1)} %bitcast.42, bf16[384,1024]{1,0:T(8,128)(2,1)S(1)} %bitcast.46, bf16[384,1024]{1,0:T(8,128)(2,1)S(1)} %bitcast.51, ...), custom_call_target="tpu_custom_call" | custom-call | flops 94371840 | tf_op jit(solution)/shard_map/grads/pallas_call | solution.py:70
  76.8 1.5 %collective-permute-done.16 = f32[128,384]{1,0:T(8,128)S(1)} collective-permute-done((f32[128,384]{1,0:T(8,128)S(1)}, f32[128,384]{1,0:T(8,128)S(1)}, u32[]{:S(2)}, u32[]{:S(2)}) %collective-permute-start.16) | collective-permute-done | bytes 196640 | tf_op jit(solution)/shard_map/ppermute | solution.py:411
  78.3 6.1 %collective-permute-done.14 = f32[2,128,768]{2,1,0:T(8,128)S(1)} collective-permute-done((f32[2,128,768]{2,1,0:T(8,128)S(1)}, f32[2,128,768]{2,1,0:T(8,128)S(1)}, u32[]{:S(2)}, u32[]{:S(2)}) %collective-permute-start.14) | collective-permute-done | bytes 786464 | tf_op jit(solution)/shard_map/ppermute | solution.py:260
  84.4 0.1 add.115
  84.5 3.0 %collective-permute-start.22 = (f32[2,128,768]{2,1,0:T(8,128)S(1)}, f32[2,128,768]{2,1,0:T(8,128)S(1)}, u32[]{:S(2)}, u32[]{:S(2)}) collective-permute-start(f32[2,128,768]{2,1,0:T(8,128)S(1)} %add.115), channel_id=1, source_target_pairs={{0,4},{2,6},{12,8},{14,10},{1,5},{3,7},{13,9},{15,11},{16,20},{18,... | collective-permute-start | bytes 2359304 | tf_op jit(solution)/shard_map/ppermute | solution.py:411
  87.6 0.3 collective-permute-start.17
  87.9 1.3 collective-permute-start.23
  89.2 0.1 add_select_fusion
  89.3 3.5 %output.1 = bf16[384,2048]{1,0:T(8,128)(2,1)} custom-call(bf16[384,512]{1,0:T(8,128)(2,1)S(1)} %get-tuple-element.113.nb_ref.far_ref, bf16[384,512]{1,0:T(8,128)(2,1)S(1)} %get-tuple-element.96.nb_ref.near_ref, bf16[1024,2048]{1,0:T(8,128)(2,1)S(1)} %copy-done.6), custom_call_target="tpu_custom_call" | custom-call | flops 100663296 | tf_op jit(solution)/shard_map/output/pallas_call | solution.py:70
  92.8 5.7 %collective-permute-done.18 = f32[2,128,640]{2,1,0:T(8,128)S(1)} collective-permute-done((f32[2,128,640]{2,1,0:T(8,128)S(1)}, f32[2,128,640]{2,1,0:T(8,128)S(1)}, u32[]{:S(2)}, u32[]{:S(2)}) %collective-permute-start.18) | collective-permute-done | bytes 655392 | tf_op jit(solution)/shard_map/ppermute | solution.py:260
  98.5 0.1 add.119
  98.6 1.2 collective-permute-start.21
  99.7 3.9 %collective-permute-done.17 = f32[2,128,256]{2,1,0:T(8,128)S(1)} collective-permute-done((f32[2,128,256]{2,1,0:T(8,128)S(1)}, f32[2,128,256]{2,1,0:T(8,128)S(1)}, u32[]{:S(2)}, u32[]{:S(2)}) %collective-permute-start.17) | collective-permute-done | bytes 262176 | tf_op jit(solution)/shard_map/ppermute | solution.py:260
  103.7 1.4 %collective-permute-start.20 = (f32[2,128,256]{2,1,0:T(8,128)S(1)}, f32[2,128,256]{2,1,0:T(8,128)S(1)}, u32[]{:S(2)}, u32[]{:S(2)}) collective-permute-start(f32[2,128,256]{2,1,0:T(8,128)S(1)} %add.120), channel_id=1, source_target_pairs={{0,4},{2,6},{12,8},{14,10},{1,5},{3,7},{13,9},{15,11},{16,20},{18,... | collective-permute-start | bytes 786440 | tf_op jit(solution)/shard_map/ppermute | solution.py:411
  105.0 0.6 collective-permute-start.19
  105.6 0.1 select_bitcast_fusion
  105.7 0.8 collective-permute-start.24
  106.6 5.5 %collective-permute-done.21 = f32[128,640]{1,0:T(8,128)S(1)} collective-permute-done((f32[128,640]{1,0:T(8,128)S(1)}, f32[128,640]{1,0:T(8,128)S(1)}, u32[]{:S(2)}, u32[]{:S(2)}) %collective-permute-start.21) | collective-permute-done | bytes 327712 | tf_op jit(solution)/shard_map/ppermute | solution.py:411
  112.1 1.3 collective-permute-start.25
  113.4 0.1 fusion.2
  113.5 1.4 %collective-permute-done.20 = f32[2,128,256]{2,1,0:T(8,128)S(1)} collective-permute-done((f32[2,128,256]{2,1,0:T(8,128)S(1)}, f32[2,128,256]{2,1,0:T(8,128)S(1)}, u32[]{:S(2)}, u32[]{:S(2)}) %collective-permute-start.20) | collective-permute-done | bytes 262176 | tf_op jit(solution)/shard_map/ppermute | solution.py:411
  114.9 0.7 collective-permute-start.26
  115.6 10.2 %collective-permute-done.25 = f32[128,640]{1,0:T(8,128)S(1)} collective-permute-done((f32[128,640]{1,0:T(8,128)S(1)}, f32[128,640]{1,0:T(8,128)S(1)}, u32[]{:S(2)}, u32[]{:S(2)}) %collective-permute-start.25) | collective-permute-done | bytes 327712 | tf_op jit(solution)/shard_map/ppermute | solution.py:411
  125.8 3.1 %final.1 = (bf16[384,1024]{1,0:T(8,128)(2,1)}, bf16[384,1024]{1,0:T(8,128)(2,1)}, bf16[384,1024]{1,0:T(8,128)(2,1)}) custom-call(s32[2]{0:T(128)S(1)} %pad_add_fusion.place, bf16[384,1024]{1,0:T(8,128)(2,1)S(1)} %bitcast.47, bf16[384,1024]{1,0:T(8,128)(2,1)S(1)} %bitcast.52, bf16[384,512]{1,0:T(8,128)(2,1)S(1)} %get-tuple-element.114.refs_0_, ...), custom_call_target="tpu_custom_call" | custom-call | flops 25165824 | tf_op jit(solution)/shard_map/final/pallas_call | solution.py:70
  128.8 0.1 bitcast_add_fusion
  128.9 0.1 fusion.1
  129.1 0.9 fusion
  (41 shorter events, 0.6 us)
Async XLA Ops:
  0.6 6.6 %copy-start = (bf16[1,384,2048]{2,1,0:T(8,128)(2,1)S(1)}, bf16[1,384,2048]{2,1,0:T(8,128)(2,1)}, u32[]{:S(2)}) copy-start(bf16[1,384,2048]{2,1,0:T(8,128)(2,1)} %param.9) | copy-start | bytes 4718596
  0.7 1.2 copy-start.2
  2.0 1.1 copy-start.4
  4.2 6.9 %collective-permute-start = (f32[2,128,128]{2,1,0:T(8,128)S(1)}, f32[2,128,128]{2,1,0:T(8,128)S(1)}, u32[]{:S(2)}, u32[]{:S(2)}) collective-permute-start(f32[2,128,128]{2,1,0:T(8,128)S(1)} %get-tuple-element.73), channel_id=1, source_target_pairs={{0,2},{2,0},{4,6},{6,4},{8,10},{10,8},{12,14},{14,12},{1,3},{3,1},... | collective-permute-start | bytes 393224 | tf_op jit(solution)/shard_map/ppermute | solution.py:260
  7.2 7.3 %copy-start.1 = (bf16[1,384,1024]{2,1,0:T(8,128)(2,1)S(1)}, bf16[1,384,1024]{2,1,0:T(8,128)(2,1)}, u32[]{:S(2)}) copy-start(bf16[1,384,1024]{2,1,0:T(8,128)(2,1)} %param.5) | copy-start | bytes 2359300
  7.9 35.8 %collective-permute-start.8 = (f32[384,1024]{1,0:T(8,128)S(1)}, f32[384,1024]{1,0:T(8,128)S(1)}, u32[]{:S(2)}, u32[]{:S(2)}) collective-permute-start(f32[384,1024]{1,0:T(8,128)S(1)} %away.1), channel_id=1, source_target_pairs={{0,1},{1,0},{2,3},{3,2},{4,5},{5,4},{6,7},{7,6},{8,9},{9,8},{10,11... | collective-permute-start | bytes 4718600 | tf_op jit(solution)/shard_map/ppermute | solution.py:266
  8.0 9.0 %collective-permute-start.2 = (f32[2,128,128]{2,1,0:T(8,128)S(1)}, f32[2,128,128]{2,1,0:T(8,128)S(1)}, u32[]{:S(2)}, u32[]{:S(2)}) collective-permute-start(f32[2,128,128]{2,1,0:T(8,128)S(1)} %get-tuple-element.77), channel_id=1, source_target_pairs={{0,2},{2,0},{4,6},{6,4},{8,10},{10,8},{12,14},{14,12},{1,3},{3,1},... | collective-permute-start | bytes 393224 | tf_op jit(solution)/shard_map/ppermute | solution.py:260
  11.1 9.4 %collective-permute-start.1 = (f32[2,128,128]{2,1,0:T(8,128)S(1)}, f32[2,128,128]{2,1,0:T(8,128)S(1)}, u32[]{:S(2)}, u32[]{:S(2)}) collective-permute-start(f32[2,128,128]{2,1,0:T(8,128)S(1)} %add.101), channel_id=1, source_target_pairs={{0,4},{2,6},{4,8},{6,10},{8,12},{10,14},{1,5},{3,7},{5,9},{7,11},{... | collective-permute-start | bytes 393224 | tf_op jit(solution)/shard_map/ppermute | solution.py:222
  14.5 9.0 %copy-start.6 = (bf16[1024,2048]{1,0:T(8,128)(2,1)S(1)}, bf16[1024,2048]{1,0:T(8,128)(2,1)}, u32[]{:S(2)}) copy-start(bf16[1024,2048]{1,0:T(8,128)(2,1)} %w_ref.3) | copy-start | bytes 12582916
  17.0 8.9 %collective-permute-start.4 = (f32[2,128,128]{2,1,0:T(8,128)S(1)}, f32[2,128,128]{2,1,0:T(8,128)S(1)}, u32[]{:S(2)}, u32[]{:S(2)}) collective-permute-start(f32[2,128,128]{2,1,0:T(8,128)S(1)} %add.103), channel_id=1, source_target_pairs={{0,4},{2,6},{4,8},{6,10},{8,12},{10,14},{1,5},{3,7},{5,9},{7,11},{... | collective-permute-start | bytes 393224 | tf_op jit(solution)/shard_map/ppermute | solution.py:222
  20.5 13.2 %collective-permute-start.3 = (f32[2,128,128]{2,1,0:T(8,128)S(1)}, f32[2,128,128]{2,1,0:T(8,128)S(1)}, u32[]{:S(2)}, u32[]{:S(2)}) collective-permute-start(f32[2,128,128]{2,1,0:T(8,128)S(1)} %add.102), channel_id=1, source_target_pairs={{0,8},{2,10},{4,12},{6,14},{1,9},{3,11},{5,13},{7,15},{16,24},{18,... | collective-permute-start | bytes 393224 | tf_op jit(solution)/shard_map/ppermute | solution.py:222
  25.9 10.1 %collective-permute-start.5 = (f32[2,128,128]{2,1,0:T(8,128)S(1)}, f32[2,128,128]{2,1,0:T(8,128)S(1)}, u32[]{:S(2)}, u32[]{:S(2)}) collective-permute-start(f32[2,128,128]{2,1,0:T(8,128)S(1)} %add.106), channel_id=1, source_target_pairs={{0,8},{2,10},{4,12},{6,14},{1,9},{3,11},{5,13},{7,15},{16,24},{18,... | collective-permute-start | bytes 393224 | tf_op jit(solution)/shard_map/ppermute | solution.py:222
  33.7 5.0 %collective-permute-start.6 = (f32[2,128,128]{2,1,0:T(8,128)S(1)}, f32[2,128,128]{2,1,0:T(8,128)S(1)}, u32[]{:S(2)}, u32[]{:S(2)}) collective-permute-start(f32[2,128,128]{2,1,0:T(8,128)S(1)} %get-tuple-element.82), channel_id=1, source_target_pairs={{0,2},{2,0},{4,6},{6,4},{8,10},{10,8},{12,14},{14,12},{1,3},{3,1},... | collective-permute-start | bytes 393224 | tf_op jit(solution)/shard_map/ppermute | solution.py:232
  41.3 2.4 %collective-permute-start.7 = (f32[384,512]{1,0:T(8,128)S(1)}, f32[384,512]{1,0:T(8,128)S(1)}, u32[]{:S(2)}, u32[]{:S(2)}) collective-permute-start(f32[384,512]{1,0:T(8,128)S(1)} %get-tuple-element.84), channel_id=1, source_target_pairs={{0,1},{1,0},{2,3},{3,2},{4,5},{5,4},{6,7},{7,6},{8,9},{9,8},{10,11... | collective-permute-start | bytes 2359304 | tf_op jit(solution)/shard_map/ppermute | solution.py:292
  41.4 5.9 %collective-permute-start.9 = (f32[2,128,128]{2,1,0:T(8,128)S(1)}, f32[2,128,128]{2,1,0:T(8,128)S(1)}, u32[]{:S(2)}, u32[]{:S(2)}) collective-permute-start(f32[2,128,128]{2,1,0:T(8,128)S(1)} %get-tuple-element.137), channel_id=1, source_target_pairs={{0,2},{2,0},{4,6},{6,4},{8,10},{10,8},{12,14},{14,12},{1,3},{3,1},... | collective-permute-start | bytes 393224 | tf_op jit(solution)/shard_map/ppermute | solution.py:232
  47.3 4.7 %copy-start.5 = (bf16[1,384,1024]{2,1,0:T(8,128)(2,1)S(1)}, bf16[1,384,1024]{2,1,0:T(8,128)(2,1)}, u32[]{:S(2)}) copy-start(bf16[1,384,1024]{2,1,0:T(8,128)(2,1)} %param.7) | copy-start | bytes 2359300
  49.9 9.3 %collective-permute-start.11 = (f32[384,512]{1,0:T(8,128)S(1)}, f32[384,512]{1,0:T(8,128)S(1)}, u32[]{:S(2)}, u32[]{:S(2)}) collective-permute-start(f32[384,512]{1,0:T(8,128)S(1)} %get-tuple-element.97), channel_id=1, source_target_pairs={{0,1},{1,0},{2,3},{3,2},{4,5},{5,4},{6,7},{7,6},{8,9},{9,8},{10,11... | collective-permute-start | bytes 2359304 | tf_op jit(solution)/shard_map/ppermute | solution.py:344
  50.0 9.2 %collective-permute-start.10 = (f32[4,128,128]{2,1,0:T(8,128)S(1)}, f32[4,128,128]{2,1,0:T(8,128)S(1)}, u32[]{:S(2)}, u32[]{:S(2)}) collective-permute-start(f32[4,128,128]{2,1,0:T(8,128)S(1)} %get-tuple-element.90), channel_id=1, source_target_pairs={{0,2},{2,0},{4,6},{6,4},{8,10},{10,8},{12,14},{14,12},{1,3},{3,1},... | collective-permute-start | bytes 786440 | tf_op jit(solution)/shard_map/ppermute | solution.py:260
  50.3 20.1 %collective-permute-start.15 = (f32[2,128,384]{2,1,0:T(8,128)S(1)}, f32[2,128,384]{2,1,0:T(8,128)S(1)}, u32[]{:S(2)}, u32[]{:S(2)}) collective-permute-start(f32[2,128,384]{2,1,0:T(8,128)S(1)} %get-tuple-element.104), channel_id=1, source_target_pairs={{0,2},{2,0},{4,6},{6,4},{8,10},{10,8},{12,14},{14,12},{1,3},{3,1},... | collective-permute-start | bytes 1179656 | tf_op jit(solution)/shard_map/ppermute | solution.py:260
  61.0 9.3 %collective-permute-start.12 = (f32[4,128,128]{2,1,0:T(8,128)S(1)}, f32[4,128,128]{2,1,0:T(8,128)S(1)}, u32[]{:S(2)}, u32[]{:S(2)}) collective-permute-start(f32[4,128,128]{2,1,0:T(8,128)S(1)} %add.111), channel_id=1, source_target_pairs={{4,0},{6,2},{8,4},{10,6},{12,8},{14,10},{5,1},{7,3},{9,5},{11,7},{... | collective-permute-start | bytes 786440 | tf_op jit(solution)/shard_map/ppermute | solution.py:411
  62.3 22.1 %collective-permute-start.14 = (f32[2,128,768]{2,1,0:T(8,128)S(1)}, f32[2,128,768]{2,1,0:T(8,128)S(1)}, u32[]{:S(2)}, u32[]{:S(2)}) collective-permute-start(f32[2,128,768]{2,1,0:T(8,128)S(1)} %get-tuple-element.98), channel_id=1, source_target_pairs={{0,2},{2,0},{4,6},{6,4},{8,10},{10,8},{12,14},{14,12},{1,3},{3,1},... | collective-permute-start | bytes 2359304 | tf_op jit(solution)/shard_map/ppermute | solution.py:260
  70.5 7.8 %collective-permute-start.16 = (f32[128,384]{1,0:T(8,128)S(1)}, f32[128,384]{1,0:T(8,128)S(1)}, u32[]{:S(2)}, u32[]{:S(2)}) collective-permute-start(f32[128,384]{1,0:T(8,128)S(1)} %select_bitcast_fusion.2), channel_id=1, source_target_pairs={{0,4},{2,6},{4,0},{6,2},{8,12},{10,14},{12,8},{14,10},{1,5},{3,7},... | collective-permute-start | bytes 589832 | tf_op jit(solution)/shard_map/ppermute | solution.py:411
  70.6 18.6 %collective-permute-start.13 = (f32[4,128,128]{2,1,0:T(8,128)S(1)}, f32[4,128,128]{2,1,0:T(8,128)S(1)}, u32[]{:S(2)}, u32[]{:S(2)}) collective-permute-start(f32[4,128,128]{2,1,0:T(8,128)S(1)} %add.112), channel_id=1, source_target_pairs={{8,0},{10,2},{12,4},{14,6},{9,1},{11,3},{13,5},{15,7},{24,16},{26,... | collective-permute-start | bytes 786440 | tf_op jit(solution)/shard_map/ppermute | solution.py:411
  72.1 26.4 %collective-permute-start.18 = (f32[2,128,640]{2,1,0:T(8,128)S(1)}, f32[2,128,640]{2,1,0:T(8,128)S(1)}, u32[]{:S(2)}, u32[]{:S(2)}) collective-permute-start(f32[2,128,640]{2,1,0:T(8,128)S(1)} %get-tuple-element.122), channel_id=1, source_target_pairs={{0,2},{2,0},{4,6},{6,4},{8,10},{10,8},{12,14},{14,12},{1,3},{3,1},... | collective-permute-start | bytes 1966088 | tf_op jit(solution)/shard_map/ppermute | solution.py:260
  84.5 21.1 %collective-permute-start.22 = (f32[2,128,768]{2,1,0:T(8,128)S(1)}, f32[2,128,768]{2,1,0:T(8,128)S(1)}, u32[]{:S(2)}, u32[]{:S(2)}) collective-permute-start(f32[2,128,768]{2,1,0:T(8,128)S(1)} %add.115), channel_id=1, source_target_pairs={{0,4},{2,6},{12,8},{14,10},{1,5},{3,7},{13,9},{15,11},{16,20},{18,... | collective-permute-start | bytes 2359304 | tf_op jit(solution)/shard_map/ppermute | solution.py:411
  87.6 16.1 %collective-permute-start.17 = (f32[2,128,256]{2,1,0:T(8,128)S(1)}, f32[2,128,256]{2,1,0:T(8,128)S(1)}, u32[]{:S(2)}, u32[]{:S(2)}) collective-permute-start(f32[2,128,256]{2,1,0:T(8,128)S(1)} %get-tuple-element.119), channel_id=1, source_target_pairs={{0,2},{2,0},{4,6},{6,4},{8,10},{10,8},{12,14},{14,12},{1,3},{3,1},... | collective-permute-start | bytes 786440 | tf_op jit(solution)/shard_map/ppermute | solution.py:260
  87.9 17.7 %collective-permute-start.23 = (f32[128,384]{1,0:T(8,128)S(1)}, f32[128,384]{1,0:T(8,128)S(1)}, u32[]{:S(2)}, u32[]{:S(2)}) collective-permute-start(f32[128,384]{1,0:T(8,128)S(1)} %bitcast_add_fusion.4), channel_id=1, source_target_pairs={{4,12},{6,14},{8,0},{10,2},{5,13},{7,15},{9,1},{11,3},{20,28},{22,... | collective-permute-start | bytes 589832 | tf_op jit(solution)/shard_map/ppermute | solution.py:411
  98.6 13.5 %collective-permute-start.21 = (f32[128,640]{1,0:T(8,128)S(1)}, f32[128,640]{1,0:T(8,128)S(1)}, u32[]{:S(2)}, u32[]{:S(2)}) collective-permute-start(f32[128,640]{1,0:T(8,128)S(1)} %select_bitcast_fusion.1), channel_id=1, source_target_pairs={{0,4},{2,6},{4,0},{6,2},{8,12},{10,14},{12,8},{14,10},{1,5},{3,7},... | collective-permute-start | bytes 983048 | tf_op jit(solution)/shard_map/ppermute | solution.py:411
  103.7 11.2 %collective-permute-start.20 = (f32[2,128,256]{2,1,0:T(8,128)S(1)}, f32[2,128,256]{2,1,0:T(8,128)S(1)}, u32[]{:S(2)}, u32[]{:S(2)}) collective-permute-start(f32[2,128,256]{2,1,0:T(8,128)S(1)} %add.120), channel_id=1, source_target_pairs={{0,4},{2,6},{12,8},{14,10},{1,5},{3,7},{13,9},{15,11},{16,20},{18,... | collective-permute-start | bytes 786440 | tf_op jit(solution)/shard_map/ppermute | solution.py:411
  105.0 20.7 %collective-permute-start.19 = (f32[4,128,128]{2,1,0:T(8,128)S(1)}, f32[4,128,128]{2,1,0:T(8,128)S(1)}, u32[]{:S(2)}, u32[]{:S(2)}) collective-permute-start(f32[4,128,128]{2,1,0:T(8,128)S(1)} %get-tuple-element.125), channel_id=1, source_target_pairs={{0,2},{2,0},{4,6},{6,4},{8,10},{10,8},{12,14},{14,12},{1,3},{3,1},... | collective-permute-start | bytes 786440 | tf_op jit(solution)/shard_map/ppermute | solution.py:260
  105.7 20.0 %copy-start.3 = (bf16[1,384,1024]{2,1,0:T(8,128)(2,1)S(1)}, bf16[1,384,1024]{2,1,0:T(8,128)(2,1)}, u32[]{:S(2)}) copy-start(bf16[1,384,1024]{2,1,0:T(8,128)(2,1)} %param.6) | copy-start | bytes 2359300
  105.7 9.2 %collective-permute-start.24 = (f32[128,768]{1,0:T(8,128)S(1)}, f32[128,768]{1,0:T(8,128)S(1)}, u32[]{:S(2)}, u32[]{:S(2)}) collective-permute-start(f32[128,768]{1,0:T(8,128)S(1)} %select_bitcast_fusion), channel_id=1, source_target_pairs={{4,8},{6,10},{8,4},{10,6},{5,9},{7,11},{9,5},{11,7},{20,24},{22,26... | collective-permute-start | bytes 1179656 | tf_op jit(solution)/shard_map/ppermute | solution.py:411
  112.1 13.6 %collective-permute-start.25 = (f32[128,640]{1,0:T(8,128)S(1)}, f32[128,640]{1,0:T(8,128)S(1)}, u32[]{:S(2)}, u32[]{:S(2)}) collective-permute-start(f32[128,640]{1,0:T(8,128)S(1)} %bitcast_add_fusion.2), channel_id=1, source_target_pairs={{4,12},{6,14},{8,0},{10,2},{5,13},{7,15},{9,1},{11,3},{20,28},{22,... | collective-permute-start | bytes 983048 | tf_op jit(solution)/shard_map/ppermute | solution.py:411
  114.9 14.1 %collective-permute-start.26 = (f32[128,256]{1,0:T(8,128)S(1)}, f32[128,256]{1,0:T(8,128)S(1)}, u32[]{:S(2)}, u32[]{:S(2)}) collective-permute-start(f32[128,256]{1,0:T(8,128)S(1)} %select_bitcast_fusion.3), channel_id=1, source_target_pairs={{4,8},{6,10},{8,4},{10,6},{5,9},{7,11},{9,5},{11,7},{20,24},{22,26... | collective-permute-start | bytes 393224 | tf_op jit(solution)/shard_map/ppermute | solution.py:411

commit v13 on v10

--- a/solution.py
+++ b/solution.py
@@ -14,7 +14,7 @@
 PAIRS = H // 2
 FAR = (0, 3)
 NEAR = (1, 2)
-WIDTHS = ((4, 4), (5, 3))
+WIDTHS = ((4, 4), (4, 4))
 EPSILON = 1e-06
 F32 = jnp.float32
 BF16 = jnp.bfloat16

time: 125 us -> 139 us (1.11)
  the two profiles are of different devices: /device:TPU:0 before, /device:TPU:12 now
where the time goes in v13:
time: 139 us; the launch traced here: 136 us
  starting transfers between devices  51 us (37%)
  waiting for transfers between devices  48.8 us (35%)
  Pallas kernels  30.6 us (22%)
  other arithmetic  2.42 us (2%)
  local copies, waits for them, and re-layouts  2.39 us (2%)
    pallas_call x12, Pallas kernels, call(): pl.pallas_call(body, out_shape=tuple(out_shapes), in_specs=specs, out_spe...  30.6 us
    ppermute x10, starting transfers between devices, hop(): lax.ppermute(block, 'seq', [(2 * a + i, 2 * b + i) for a, b in links for...  30.6 us
    ppermute x10, waiting for transfers between devices, hop(): lax.ppermute(block, 'seq', [(2 * a + i, 2 * b + i) for a, b in links for...  27.2 us
    ppermute x8, waiting for transfers between devices, trade(): return lax.ppermute(send, 'seq', [(s, s ^ 1) for s in range(count)])  11.5 us
    ppermute x4, starting transfers between devices, exclusive(): got = lax.ppermute(total, 'seq', links(step))  10.1 us
    ppermute x8, starting transfers between devices, trade(): return lax.ppermute(send, 'seq', [(s, s ^ 1) for s in range(count)])  6.74 us
    ppermute x2, waiting for transfers between devices, exclusive(): results.append((mine, lax.ppermute(theirs, 'seq', swap)))  5.16 us
    ppermute x4, waiting for transfers between devices, exclusive(): got = lax.ppermute(total, 'seq', links(step))  4.37 us
  transfers between devices with their start and end apart: 27, of which 16 were waited for; matrix products, arithmetic and copies ran while one was open for 1% of the time, Pallas kernels for 20%

profile of v13, /device:TPU:12, one launch (start us, length us, event | category | flops | bytes accessed | tf_op | source)
XLA Modules:
  0.0 136.2 jit_solution(18214366029040533704)
XLA Ops:
  0.7 1.2 copy-done.2
  2.0 1.1 copy-done.4
  3.1 1.1 state.1
  4.2 1.6 %collective-permute-start = (f32[2,128,128]{2,1,0:T(8,128)S(1)}, f32[2,128,128]{2,1,0:T(8,128)S(1)}, u32[]{:S(2)}, u32[]{:S(2)}) collective-permute-start(f32[2,128,128]{2,1,0:T(8,128)S(1)} %get-tuple-element.72), channel_id=1, source_target_pairs={{0,2},{2,0},{4,6},{6,4},{8,10},{10,8},{12,14},{14,12},{1,3},{3,1},... | collective-permute-start | bytes 393224 | tf_op jit(solution)/shard_map/ppermute | solution.py:260
  5.8 0.6 away.1
  6.5 0.6 collective-permute-start.2
  7.1 2.4 %collective-permute-done = f32[2,128,128]{2,1,0:T(8,128)S(1)} collective-permute-done((f32[2,128,128]{2,1,0:T(8,128)S(1)}, f32[2,128,128]{2,1,0:T(8,128)S(1)}, u32[]{:S(2)}, u32[]{:S(2)}) %collective-permute-start) | collective-permute-done | bytes 131104 | tf_op jit(solution)/shard_map/ppermute | solution.py:260
  9.5 3.5 %collective-permute-start.1 = (f32[2,128,128]{2,1,0:T(8,128)S(1)}, f32[2,128,128]{2,1,0:T(8,128)S(1)}, u32[]{:S(2)}, u32[]{:S(2)}) collective-permute-start(f32[2,128,128]{2,1,0:T(8,128)S(1)} %add.101), channel_id=1, source_target_pairs={{0,4},{2,6},{4,8},{6,10},{8,12},{10,14},{1,5},{3,7},{5,9},{7,11},{... | collective-permute-start | bytes 393224 | tf_op jit(solution)/shard_map/ppermute | solution.py:222
  13.1 2.4 %local.1.att_ref = f32[384,1024]{1,0:T(8,128)S(1)} custom-call(bf16[384,1024]{1,0:T(8,128)(2,1)S(1)} %bitcast.38, bf16[384,1024]{1,0:T(8,128)(2,1)S(1)} %bitcast.44, bf16[384,1024]{1,0:T(8,128)(2,1)S(1)} %bitcast.49), custom_call_target="tpu_custom_call" | custom-call | flops 56623104 | tf_op jit(solution)/shard_map/local/pallas_call | solution.py:70
  15.5 3.5 %collective-permute-start.4 = (f32[2,128,128]{2,1,0:T(8,128)S(1)}, f32[2,128,128]{2,1,0:T(8,128)S(1)}, u32[]{:S(2)}, u32[]{:S(2)}) collective-permute-start(f32[2,128,128]{2,1,0:T(8,128)S(1)} %add.103), channel_id=1, source_target_pairs={{0,4},{2,6},{4,8},{6,10},{8,12},{10,14},{1,5},{3,7},{5,9},{7,11},{... | collective-permute-start | bytes 393224 | tf_op jit(solution)/shard_map/ppermute | solution.py:222
  19.1 1.9 %collective-permute-start.3 = (f32[2,128,128]{2,1,0:T(8,128)S(1)}, f32[2,128,128]{2,1,0:T(8,128)S(1)}, u32[]{:S(2)}, u32[]{:S(2)}) collective-permute-start(f32[2,128,128]{2,1,0:T(8,128)S(1)} %add.102), channel_id=1, source_target_pairs={{0,8},{2,10},{4,12},{6,14},{1,9},{3,11},{5,13},{7,15},{16,24},{18,... | collective-permute-start | bytes 393224 | tf_op jit(solution)/shard_map/ppermute | solution.py:222
  20.9 2.4 %d_normed.1.dn_ref = f32[384,1024]{1,0:T(8,128)S(1)} custom-call(bf16[384,2048]{1,0:T(8,128)(2,1)S(1)} %bitcast.35, bf16[1024,2048]{1,0:T(8,128)(2,1)S(1)} %copy-done.6), custom_call_target="tpu_custom_call" | custom-call | flops 100663296 | tf_op jit(solution)/shard_map/d_normed/pallas_call | solution.py:70
  23.4 3.3 %collective-permute-done.4 = f32[2,128,128]{2,1,0:T(8,128)S(1)} collective-permute-done((f32[2,128,128]{2,1,0:T(8,128)S(1)}, f32[2,128,128]{2,1,0:T(8,128)S(1)}, u32[]{:S(2)}, u32[]{:S(2)}) %collective-permute-start.4) | collective-permute-done | bytes 131104 | tf_op jit(solution)/shard_map/ppermute | solution.py:222
  26.7 1.3 collective-permute-start.5
  28.0 1.1 collective-permute-done.3
  29.1 1.6 %collective-permute-start.6 = (f32[2,128,128]{2,1,0:T(8,128)S(1)}, f32[2,128,128]{2,1,0:T(8,128)S(1)}, u32[]{:S(2)}, u32[]{:S(2)}) collective-permute-start(f32[2,128,128]{2,1,0:T(8,128)S(1)} %get-tuple-element.81), channel_id=1, source_target_pairs={{0,2},{2,0},{4,6},{6,4},{8,10},{10,8},{12,14},{14,12},{1,3},{3,1},... | collective-permute-start | bytes 393224 | tf_op jit(solution)/shard_map/ppermute | solution.py:232
  30.8 3.4 %collective-permute-done.6.other_ref = f32[2,128,128]{2,1,0:T(8,128)S(1)} collective-permute-done((f32[2,128,128]{2,1,0:T(8,128)S(1)}, f32[2,128,128]{2,1,0:T(8,128)S(1)}, u32[]{:S(2)}, u32[]{:S(2)}) %collective-permute-start.6) | collective-permute-done | bytes 131104 | tf_op jit(solution)/shard_map/ppermute | solution.py:232
  34.1 2.5 %norm_far.1 = (bf16[384,512]{1,0:T(8,128)(2,1)S(1)}, f32[384,512]{1,0:T(8,128)S(1)}, bf16[384,512]{1,0:T(8,128)(2,1)S(1)}, f32[2,128,128]{2,1,0:T(8,128)S(1)}, f32[2,128,128]{2,1,0:T(8,128)S(1)}) custom-call(s32[2]{0:T(128)S(1)} %pad_add_fusion.place, bf16[384,1024]{1,0:T(8,128)(2,1)S(1)} %bitcast.39, f32[384,1024]{1,0:T(8,128)S(1)} %local.1.att_ref, ...), custom_call_target="tpu_custom_call" | custom-call | flops 6291456 | tf_op jit(solution)/shard_map/norm_far/pallas_call | solution.py:70
  36.8 1.6 %collective-permute-start.9 = (f32[2,128,128]{2,1,0:T(8,128)S(1)}, f32[2,128,128]{2,1,0:T(8,128)S(1)}, u32[]{:S(2)}, u32[]{:S(2)}) collective-permute-start(f32[2,128,128]{2,1,0:T(8,128)S(1)} %get-tuple-element.135), channel_id=1, source_target_pairs={{0,2},{2,0},{4,6},{6,4},{8,10},{10,8},{12,14},{14,12},{1,3},{3,1},... | collective-permute-start | bytes 393224 | tf_op jit(solution)/shard_map/ppermute | solution.py:232
  38.4 0.6 collective-permute-done.7.nbo_ref
  39.0 1.8 %weight.2 = (f32[2,128,512]{2,1,0:T(8,128)S(1)}, f32[2,128,512]{2,1,0:T(8,128)S(1)}, f32[2,128,512]{2,1,0:T(8,128)S(1)}, f32[2,128,512]{2,1,0:T(8,128)S(1)}) custom-call(s32[2]{0:T(128)S(1)} %pad_add_fusion.place, bf16[384,512]{1,0:T(8,128)(2,1)S(1)} %get-tuple-element.111.nb_ref.far_ref, bf16[384,2048]{1,0:T(8,128)(2,1)S(1)} %bitcast.36, ...), custom_call_target="tpu_custom_call" | custom-call | flops 50331648 | tf_op jit(solution)/shard_map/weight/pallas_call | solution.py:70
  40.9 1.8 %collective-permute-done.9.other_ref = f32[2,128,128]{2,1,0:T(8,128)S(1)} collective-permute-done((f32[2,128,128]{2,1,0:T(8,128)S(1)}, f32[2,128,128]{2,1,0:T(8,128)S(1)}, u32[]{:S(2)}, u32[]{:S(2)}) %collective-permute-start.9) | collective-permute-done | bytes 131104 | tf_op jit(solution)/shard_map/ppermute | solution.py:232
  42.7 2.6 %norm_near.1 = (bf16[384,512]{1,0:T(8,128)(2,1)S(1)}, f32[384,512]{1,0:T(8,128)S(1)}, bf16[384,512]{1,0:T(8,128)(2,1)S(1)}, f32[4,128,128]{2,1,0:T(8,128)S(1)}, f32[4,128,128]{2,1,0:T(8,128)S(1)}) custom-call(s32[2]{0:T(128)S(1)} %pad_add_fusion.place, bf16[384,1024]{1,0:T(8,128)(2,1)S(1)} %bitcast.40, f32[384,1024]{1,0:T(8,128)S(1)} %local.1.att_ref, ...), custom_call_target="tpu_custom_call" | custom-call | flops 402653184 | tf_op jit(solution)/shard_map/norm_near/pallas_call | solution.py:70
  45.3 1.6 %collective-permute-start.10 = (f32[4,128,128]{2,1,0:T(8,128)S(1)}, f32[4,128,128]{2,1,0:T(8,128)S(1)}, u32[]{:S(2)}, u32[]{:S(2)}) collective-permute-start(f32[4,128,128]{2,1,0:T(8,128)S(1)} %get-tuple-element.89), channel_id=1, source_target_pairs={{0,2},{2,0},{4,6},{6,4},{8,10},{10,8},{12,14},{14,12},{1,3},{3,1},... | collective-permute-start | bytes 786440 | tf_op jit(solution)/shard_map/ppermute | solution.py:260
  46.9 0.5 collective-permute-start.15
  47.4 4.3 %grads.2 = (bf16[384,512]{1,0:T(8,128)(2,1)S(1)}, f32[384,512]{1,0:T(8,128)S(1)}, f32[384,512]{1,0:T(8,128)S(1)}) custom-call(s32[2]{0:T(128)S(1)} %pad_add_fusion.place, bf16[384,1024]{1,0:T(8,128)(2,1)S(1)} %bitcast.41, bf16[384,1024]{1,0:T(8,128)(2,1)S(1)} %bitcast.45, bf16[384,1024]{1,0:T(8,128)(2,1)S(1)} %bitcast.50, ...), custom_call_target="tpu_custom_call" | custom-call | flops 94371840 | tf_op jit(solution)/shard_map/grads/pallas_call | solution.py:70
  51.8 2.7 %collective-permute-done.10 = f32[4,128,128]{2,1,0:T(8,128)S(1)} collective-permute-done((f32[4,128,128]{2,1,0:T(8,128)S(1)}, f32[4,128,128]{2,1,0:T(8,128)S(1)}, u32[]{:S(2)}, u32[]{:S(2)}) %collective-permute-start.10) | collective-permute-done | bytes 262176 | tf_op jit(solution)/shard_map/ppermute | solution.py:260
  54.5 5.6 %collective-permute-start.11 = (f32[4,128,128]{2,1,0:T(8,128)S(1)}, f32[4,128,128]{2,1,0:T(8,128)S(1)}, u32[]{:S(2)}, u32[]{:S(2)}) collective-permute-start(f32[4,128,128]{2,1,0:T(8,128)S(1)} %add.111), channel_id=1, source_target_pairs={{4,0},{6,2},{8,4},{10,6},{12,8},{14,10},{5,1},{7,3},{9,5},{11,7},{... | collective-permute-start | bytes 786440 | tf_op jit(solution)/shard_map/ppermute | solution.py:411
  60.1 1.8 %weight.3 = (f32[2,128,512]{2,1,0:T(8,128)S(1)}, f32[2,128,512]{2,1,0:T(8,128)S(1)}, f32[2,128,512]{2,1,0:T(8,128)S(1)}, f32[2,128,512]{2,1,0:T(8,128)S(1)}) custom-call(s32[2]{0:T(128)S(1)} %pad_add_fusion.place, bf16[384,512]{1,0:T(8,128)(2,1)S(1)} %get-tuple-element.95.nb_ref.near_ref, bf16[384,2048]{1,0:T(8,128)(2,1)S(1)} %bitcast.37, ...), custom_call_target="tpu_custom_call" | custom-call | flops 50331648 | tf_op jit(solution)/shard_map/weight/pallas_call | solution.py:70
  62.0 0.3 collective-permute-start.14
  62.3 2.8 %collective-permute-done.11 = f32[4,128,128]{2,1,0:T(8,128)S(1)} collective-permute-done((f32[4,128,128]{2,1,0:T(8,128)S(1)}, f32[4,128,128]{2,1,0:T(8,128)S(1)}, u32[]{:S(2)}, u32[]{:S(2)}) %collective-permute-start.11) | collective-permute-done | bytes 262176 | tf_op jit(solution)/shard_map/ppermute | solution.py:411
  65.2 0.6 collective-permute-done.15
  65.7 0.1 add.113
  65.8 3.6 %collective-permute-start.16 = (f32[128,512]{1,0:T(8,128)S(1)}, f32[128,512]{1,0:T(8,128)S(1)}, u32[]{:S(2)}, u32[]{:S(2)}) collective-permute-start(f32[128,512]{1,0:T(8,128)S(1)} %select_bitcast_fusion.3), channel_id=1, source_target_pairs={{0,4},{2,6},{4,0},{6,2},{8,12},{10,14},{12,8},{14,10},{1,5},{3,7},... | collective-permute-start | bytes 786440 | tf_op jit(solution)/shard_map/ppermute | solution.py:411
  69.4 1.3 collective-permute-start.13
  70.7 0.3 collective-permute-start.20
  71.0 4.4 %grads.3 = (bf16[384,512]{1,0:T(8,128)(2,1)S(1)}, f32[384,512]{1,0:T(8,128)S(1)}, f32[384,512]{1,0:T(8,128)S(1)}) custom-call(s32[2]{0:T(128)S(1)} %pad_add_fusion.place, bf16[384,1024]{1,0:T(8,128)(2,1)S(1)} %bitcast.42, bf16[384,1024]{1,0:T(8,128)(2,1)S(1)} %bitcast.46, bf16[384,1024]{1,0:T(8,128)(2,1)S(1)} %bitcast.51, ...), custom_call_target="tpu_custom_call" | custom-call | flops 94371840 | tf_op jit(solution)/shard_map/grads/pallas_call | solution.py:70
  75.4 2.1 %collective-permute-done.16 = f32[128,512]{1,0:T(8,128)S(1)} collective-permute-done((f32[128,512]{1,0:T(8,128)S(1)}, f32[128,512]{1,0:T(8,128)S(1)}, u32[]{:S(2)}, u32[]{:S(2)}) %collective-permute-start.16) | collective-permute-done | bytes 262176 | tf_op jit(solution)/shard_map/ppermute | solution.py:411
  77.5 0.1 add.115
  77.6 1.3 collective-permute-start.19
  78.9 1.1 collective-permute-start.18
  80.0 5.5 %collective-permute-start.21 = (f32[128,512]{1,0:T(8,128)S(1)}, f32[128,512]{1,0:T(8,128)S(1)}, u32[]{:S(2)}, u32[]{:S(2)}) collective-permute-start(f32[128,512]{1,0:T(8,128)S(1)} %bitcast_add_fusion.5), channel_id=1, source_target_pairs={{4,12},{6,14},{8,0},{10,2},{5,13},{7,15},{9,1},{11,3},{20,28},{22,... | collective-permute-start | bytes 786440 | tf_op jit(solution)/shard_map/ppermute | solution.py:411
  85.6 3.5 %output.1 = bf16[384,2048]{1,0:T(8,128)(2,1)} custom-call(bf16[384,512]{1,0:T(8,128)(2,1)S(1)} %get-tuple-element.111.nb_ref.far_ref, bf16[384,512]{1,0:T(8,128)(2,1)S(1)} %get-tuple-element.95.nb_ref.near_ref, bf16[1024,2048]{1,0:T(8,128)(2,1)S(1)} %copy-done.6), custom_call_target="tpu_custom_call" | custom-call | flops 100663296 | tf_op jit(solution)/shard_map/output/pallas_call | solution.py:70
  89.2 0.7 collective-permute-done.21
  89.9 3.2 %collective-permute-done.19 = f32[2,128,512]{2,1,0:T(8,128)S(1)} collective-permute-done((f32[2,128,512]{2,1,0:T(8,128)S(1)}, f32[2,128,512]{2,1,0:T(8,128)S(1)}, u32[]{:S(2)}, u32[]{:S(2)}) %collective-permute-start.19) | collective-permute-done | bytes 524320 | tf_op jit(solution)/shard_map/ppermute | solution.py:411
  93.1 0.1 select_bitcast_fusion.1
  93.2 5.8 %collective-permute-done.18 = f32[2,128,512]{2,1,0:T(8,128)S(1)} collective-permute-done((f32[2,128,512]{2,1,0:T(8,128)S(1)}, f32[2,128,512]{2,1,0:T(8,128)S(1)}, u32[]{:S(2)}, u32[]{:S(2)}) %collective-permute-start.18) | collective-permute-done | bytes 524320 | tf_op jit(solution)/shard_map/ppermute | solution.py:260
  99.0 0.1 add.122
  99.1 1.3 collective-permute-start.22
  100.4 3.6 %collective-permute-start.23 = (f32[128,512]{1,0:T(8,128)S(1)}, f32[128,512]{1,0:T(8,128)S(1)}, u32[]{:S(2)}, u32[]{:S(2)}) collective-permute-start(f32[128,512]{1,0:T(8,128)S(1)} %select_bitcast_fusion.2), channel_id=1, source_target_pairs={{0,4},{2,6},{4,0},{6,2},{8,12},{10,14},{12,8},{14,10},{1,5},{3,7},... | collective-permute-start | bytes 786440 | tf_op jit(solution)/shard_map/ppermute | solution.py:411
  103.9 0.1 fusion.2
  104.0 0.8 collective-permute-start.17
  104.8 3.4 %collective-permute-start.25 = (f32[128,512]{1,0:T(8,128)S(1)}, f32[128,512]{1,0:T(8,128)S(1)}, u32[]{:S(2)}, u32[]{:S(2)}) collective-permute-start(f32[128,512]{1,0:T(8,128)S(1)} %select_bitcast_fusion.1), channel_id=1, source_target_pairs={{4,8},{6,10},{8,4},{10,6},{5,9},{7,11},{9,5},{11,7},{20,24},{22,26... | collective-permute-start | bytes 786440 | tf_op jit(solution)/shard_map/ppermute | solution.py:411
  108.3 12.9 %collective-permute-done.23 = f32[128,512]{1,0:T(8,128)S(1)} collective-permute-done((f32[128,512]{1,0:T(8,128)S(1)}, f32[128,512]{1,0:T(8,128)S(1)}, u32[]{:S(2)}, u32[]{:S(2)}) %collective-permute-start.23) | collective-permute-done | bytes 262176 | tf_op jit(solution)/shard_map/ppermute | solution.py:411
  121.3 2.7 %collective-permute-start.24 = (f32[128,512]{1,0:T(8,128)S(1)}, f32[128,512]{1,0:T(8,128)S(1)}, u32[]{:S(2)}, u32[]{:S(2)}) collective-permute-start(f32[128,512]{1,0:T(8,128)S(1)} %bitcast_add_fusion.4), channel_id=1, source_target_pairs={{4,12},{6,14},{8,0},{10,2},{5,13},{7,15},{9,1},{11,3},{20,28},{22,... | collective-permute-start | bytes 786440 | tf_op jit(solution)/shard_map/ppermute | solution.py:411
  124.0 0.1 select_bitcast_fusion
  124.1 2.3 %collective-permute-start.26 = (f32[128,512]{1,0:T(8,128)S(1)}, f32[128,512]{1,0:T(8,128)S(1)}, u32[]{:S(2)}, u32[]{:S(2)}) collective-permute-start(f32[128,512]{1,0:T(8,128)S(1)} %select_bitcast_fusion), channel_id=1, source_target_pairs={{4,8},{6,10},{8,4},{10,6},{5,9},{7,11},{9,5},{11,7},{20,24},{22,26... | collective-permute-start | bytes 786440 | tf_op jit(solution)/shard_map/ppermute | solution.py:411
  126.4 0.1 bitcast_add_fusion.1
  126.6 4.2 %collective-permute-done.24 = f32[128,512]{1,0:T(8,128)S(1)} collective-permute-done((f32[128,512]{1,0:T(8,128)S(1)}, f32[128,512]{1,0:T(8,128)S(1)}, u32[]{:S(2)}, u32[]{:S(2)}) %collective-permute-start.24) | collective-permute-done | bytes 262176 | tf_op jit(solution)/shard_map/ppermute | solution.py:411
  130.7 3.0 %final.1 = (bf16[384,1024]{1,0:T(8,128)(2,1)}, bf16[384,1024]{1,0:T(8,128)(2,1)}, bf16[384,1024]{1,0:T(8,128)(2,1)}) custom-call(s32[2]{0:T(128)S(1)} %pad_add_fusion.place, bf16[384,1024]{1,0:T(8,128)(2,1)S(1)} %bitcast.47, bf16[384,1024]{1,0:T(8,128)(2,1)S(1)} %bitcast.52, bf16[384,512]{1,0:T(8,128)(2,1)S(1)} %get-tuple-element.112.refs_0_, ...), custom_call_target="tpu_custom_call" | custom-call | flops 25165824 | tf_op jit(solution)/shard_map/final/pallas_call | solution.py:70
  133.8 0.1 fusion.1
  133.9 1.3 collective-permute-done.26
  135.2 0.1 bitcast_add_fusion
  135.4 0.9 fusion
  (41 shorter events, 0.9 us)
Async XLA Ops:
  0.6 5.1 %copy-start = (bf16[1,384,2048]{2,1,0:T(8,128)(2,1)S(1)}, bf16[1,384,2048]{2,1,0:T(8,128)(2,1)}, u32[]{:S(2)}) copy-start(bf16[1,384,2048]{2,1,0:T(8,128)(2,1)} %param.9) | copy-start | bytes 4718596
  0.7 1.2 copy-start.2
  2.0 1.1 copy-start.4
  4.2 5.3 %collective-permute-start = (f32[2,128,128]{2,1,0:T(8,128)S(1)}, f32[2,128,128]{2,1,0:T(8,128)S(1)}, u32[]{:S(2)}, u32[]{:S(2)}) collective-permute-start(f32[2,128,128]{2,1,0:T(8,128)S(1)} %get-tuple-element.72), channel_id=1, source_target_pairs={{0,2},{2,0},{4,6},{6,4},{8,10},{10,8},{12,14},{14,12},{1,3},{3,1},... | collective-permute-start | bytes 393224 | tf_op jit(solution)/shard_map/ppermute | solution.py:260
  5.8 7.3 %copy-start.1 = (bf16[1,384,1024]{2,1,0:T(8,128)(2,1)S(1)}, bf16[1,384,1024]{2,1,0:T(8,128)(2,1)}, u32[]{:S(2)}) copy-start(bf16[1,384,1024]{2,1,0:T(8,128)(2,1)} %param.5) | copy-start | bytes 2359300
  6.4 32.6 %collective-permute-start.8 = (f32[384,1024]{1,0:T(8,128)S(1)}, f32[384,1024]{1,0:T(8,128)S(1)}, u32[]{:S(2)}, u32[]{:S(2)}) collective-permute-start(f32[384,1024]{1,0:T(8,128)S(1)} %away.1), channel_id=1, source_target_pairs={{0,1},{1,0},{2,3},{3,2},{4,5},{5,4},{6,7},{7,6},{8,9},{9,8},{10,11... | collective-permute-start | bytes 4718600 | tf_op jit(solution)/shard_map/ppermute | solution.py:266
  6.5 9.0 %collective-permute-start.2 = (f32[2,128,128]{2,1,0:T(8,128)S(1)}, f32[2,128,128]{2,1,0:T(8,128)S(1)}, u32[]{:S(2)}, u32[]{:S(2)}) collective-permute-start(f32[2,128,128]{2,1,0:T(8,128)S(1)} %get-tuple-element.76), channel_id=1, source_target_pairs={{0,2},{2,0},{4,6},{6,4},{8,10},{10,8},{12,14},{14,12},{1,3},{3,1},... | collective-permute-start | bytes 393224 | tf_op jit(solution)/shard_map/ppermute | solution.py:260
  9.5 9.5 %collective-permute-start.1 = (f32[2,128,128]{2,1,0:T(8,128)S(1)}, f32[2,128,128]{2,1,0:T(8,128)S(1)}, u32[]{:S(2)}, u32[]{:S(2)}) collective-permute-start(f32[2,128,128]{2,1,0:T(8,128)S(1)} %add.101), channel_id=1, source_target_pairs={{0,4},{2,6},{4,8},{6,10},{8,12},{10,14},{1,5},{3,7},{5,9},{7,11},{... | collective-permute-start | bytes 393224 | tf_op jit(solution)/shard_map/ppermute | solution.py:222
  13.0 7.9 %copy-start.6 = (bf16[1024,2048]{1,0:T(8,128)(2,1)S(1)}, bf16[1024,2048]{1,0:T(8,128)(2,1)}, u32[]{:S(2)}) copy-start(bf16[1024,2048]{1,0:T(8,128)(2,1)} %w_ref.3) | copy-start | bytes 12582916
  15.5 11.1 %collective-permute-start.4 = (f32[2,128,128]{2,1,0:T(8,128)S(1)}, f32[2,128,128]{2,1,0:T(8,128)S(1)}, u32[]{:S(2)}, u32[]{:S(2)}) collective-permute-start(f32[2,128,128]{2,1,0:T(8,128)S(1)} %add.103), channel_id=1, source_target_pairs={{0,4},{2,6},{4,8},{6,10},{8,12},{10,14},{1,5},{3,7},{5,9},{7,11},{... | collective-permute-start | bytes 393224 | tf_op jit(solution)/shard_map/ppermute | solution.py:222
  19.1 10.0 %collective-permute-start.3 = (f32[2,128,128]{2,1,0:T(8,128)S(1)}, f32[2,128,128]{2,1,0:T(8,128)S(1)}, u32[]{:S(2)}, u32[]{:S(2)}) collective-permute-start(f32[2,128,128]{2,1,0:T(8,128)S(1)} %add.102), channel_id=1, source_target_pairs={{0,8},{2,10},{4,12},{6,14},{1,9},{3,11},{5,13},{7,15},{16,24},{18,... | collective-permute-start | bytes 393224 | tf_op jit(solution)/shard_map/ppermute | solution.py:222
  26.7 4.1 %collective-permute-start.5 = (f32[2,128,128]{2,1,0:T(8,128)S(1)}, f32[2,128,128]{2,1,0:T(8,128)S(1)}, u32[]{:S(2)}, u32[]{:S(2)}) collective-permute-start(f32[2,128,128]{2,1,0:T(8,128)S(1)} %add.106), channel_id=1, source_target_pairs={{0,8},{2,10},{4,12},{6,14},{1,9},{3,11},{5,13},{7,15},{16,24},{18,... | collective-permute-start | bytes 393224 | tf_op jit(solution)/shard_map/ppermute | solution.py:222
  29.1 5.0 %collective-permute-start.6 = (f32[2,128,128]{2,1,0:T(8,128)S(1)}, f32[2,128,128]{2,1,0:T(8,128)S(1)}, u32[]{:S(2)}, u32[]{:S(2)}) collective-permute-start(f32[2,128,128]{2,1,0:T(8,128)S(1)} %get-tuple-element.81), channel_id=1, source_target_pairs={{0,2},{2,0},{4,6},{6,4},{8,10},{10,8},{12,14},{14,12},{1,3},{3,1},... | collective-permute-start | bytes 393224 | tf_op jit(solution)/shard_map/ppermute | solution.py:232
  36.7 2.4 %collective-permute-start.7 = (f32[384,512]{1,0:T(8,128)S(1)}, f32[384,512]{1,0:T(8,128)S(1)}, u32[]{:S(2)}, u32[]{:S(2)}) collective-permute-start(f32[384,512]{1,0:T(8,128)S(1)} %get-tuple-element.83), channel_id=1, source_target_pairs={{0,1},{1,0},{2,3},{3,2},{4,5},{5,4},{6,7},{7,6},{8,9},{9,8},{10,11... | collective-permute-start | bytes 2359304 | tf_op jit(solution)/shard_map/ppermute | solution.py:292
  36.8 5.9 %collective-permute-start.9 = (f32[2,128,128]{2,1,0:T(8,128)S(1)}, f32[2,128,128]{2,1,0:T(8,128)S(1)}, u32[]{:S(2)}, u32[]{:S(2)}) collective-permute-start(f32[2,128,128]{2,1,0:T(8,128)S(1)} %get-tuple-element.135), channel_id=1, source_target_pairs={{0,2},{2,0},{4,6},{6,4},{8,10},{10,8},{12,14},{14,12},{1,3},{3,1},... | collective-permute-start | bytes 393224 | tf_op jit(solution)/shard_map/ppermute | solution.py:232
  42.7 4.7 %copy-start.5 = (bf16[1,384,1024]{2,1,0:T(8,128)(2,1)S(1)}, bf16[1,384,1024]{2,1,0:T(8,128)(2,1)}, u32[]{:S(2)}) copy-start(bf16[1,384,1024]{2,1,0:T(8,128)(2,1)} %param.7) | copy-start | bytes 2359300
  45.2 14.9 %collective-permute-start.12 = (f32[384,512]{1,0:T(8,128)S(1)}, f32[384,512]{1,0:T(8,128)S(1)}, u32[]{:S(2)}, u32[]{:S(2)}) collective-permute-start(f32[384,512]{1,0:T(8,128)S(1)} %get-tuple-element.96), channel_id=1, source_target_pairs={{0,1},{1,0},{2,3},{3,2},{4,5},{5,4},{6,7},{7,6},{8,9},{9,8},{10,11... | collective-permute-start | bytes 2359304 | tf_op jit(solution)/shard_map/ppermute | solution.py:344
  45.3 9.2 %collective-permute-start.10 = (f32[4,128,128]{2,1,0:T(8,128)S(1)}, f32[4,128,128]{2,1,0:T(8,128)S(1)}, u32[]{:S(2)}, u32[]{:S(2)}) collective-permute-start(f32[4,128,128]{2,1,0:T(8,128)S(1)} %get-tuple-element.89), channel_id=1, source_target_pairs={{0,2},{2,0},{4,6},{6,4},{8,10},{10,8},{12,14},{14,12},{1,3},{3,1},... | collective-permute-start | bytes 786440 | tf_op jit(solution)/shard_map/ppermute | solution.py:260
  46.9 18.8 %collective-permute-start.15 = (f32[2,128,512]{2,1,0:T(8,128)S(1)}, f32[2,128,512]{2,1,0:T(8,128)S(1)}, u32[]{:S(2)}, u32[]{:S(2)}) collective-permute-start(f32[2,128,512]{2,1,0:T(8,128)S(1)} %get-tuple-element.102), channel_id=1, source_target_pairs={{0,2},{2,0},{4,6},{6,4},{8,10},{10,8},{12,14},{14,12},{1,3},{3,1},... | collective-permute-start | bytes 1572872 | tf_op jit(solution)/shard_map/ppermute | solution.py:260
  54.5 10.6 %collective-permute-start.11 = (f32[4,128,128]{2,1,0:T(8,128)S(1)}, f32[4,128,128]{2,1,0:T(8,128)S(1)}, u32[]{:S(2)}, u32[]{:S(2)}) collective-permute-start(f32[4,128,128]{2,1,0:T(8,128)S(1)} %add.111), channel_id=1, source_target_pairs={{4,0},{6,2},{8,4},{10,6},{12,8},{14,10},{5,1},{7,3},{9,5},{11,7},{... | collective-permute-start | bytes 786440 | tf_op jit(solution)/shard_map/ppermute | solution.py:411
  62.0 15.6 %collective-permute-start.14 = (f32[2,128,512]{2,1,0:T(8,128)S(1)}, f32[2,128,512]{2,1,0:T(8,128)S(1)}, u32[]{:S(2)}, u32[]{:S(2)}) collective-permute-start(f32[2,128,512]{2,1,0:T(8,128)S(1)} %get-tuple-element.97), channel_id=1, source_target_pairs={{0,2},{2,0},{4,6},{6,4},{8,10},{10,8},{12,14},{14,12},{1,3},{3,1},... | collective-permute-start | bytes 1572872 | tf_op jit(solution)/shard_map/ppermute | solution.py:260
  65.8 11.6 %collective-permute-start.16 = (f32[128,512]{1,0:T(8,128)S(1)}, f32[128,512]{1,0:T(8,128)S(1)}, u32[]{:S(2)}, u32[]{:S(2)}) collective-permute-start(f32[128,512]{1,0:T(8,128)S(1)} %select_bitcast_fusion.3), channel_id=1, source_target_pairs={{0,4},{2,6},{4,0},{6,2},{8,12},{10,14},{12,8},{14,10},{1,5},{3,7},... | collective-permute-start | bytes 786440 | tf_op jit(solution)/shard_map/ppermute | solution.py:411
  69.4 16.1 %collective-permute-start.13 = (f32[4,128,128]{2,1,0:T(8,128)S(1)}, f32[4,128,128]{2,1,0:T(8,128)S(1)}, u32[]{:S(2)}, u32[]{:S(2)}) collective-permute-start(f32[4,128,128]{2,1,0:T(8,128)S(1)} %add.112), channel_id=1, source_target_pairs={{8,0},{10,2},{12,4},{14,6},{9,1},{11,3},{13,5},{15,7},{24,16},{26,... | collective-permute-start | bytes 786440 | tf_op jit(solution)/shard_map/ppermute | solution.py:411
  70.7 18.4 %collective-permute-start.20 = (f32[2,128,512]{2,1,0:T(8,128)S(1)}, f32[2,128,512]{2,1,0:T(8,128)S(1)}, u32[]{:S(2)}, u32[]{:S(2)}) collective-permute-start(f32[2,128,512]{2,1,0:T(8,128)S(1)} %get-tuple-element.120), channel_id=1, source_target_pairs={{0,2},{2,0},{4,6},{6,4},{8,10},{10,8},{12,14},{14,12},{1,3},{3,1},... | collective-permute-start | bytes 1572872 | tf_op jit(solution)/shard_map/ppermute | solution.py:260
  77.6 15.5 %collective-permute-start.19 = (f32[2,128,512]{2,1,0:T(8,128)S(1)}, f32[2,128,512]{2,1,0:T(8,128)S(1)}, u32[]{:S(2)}, u32[]{:S(2)}) collective-permute-start(f32[2,128,512]{2,1,0:T(8,128)S(1)} %add.115), channel_id=1, source_target_pairs={{0,4},{2,6},{12,8},{14,10},{1,5},{3,7},{13,9},{15,11},{16,20},{18,... | collective-permute-start | bytes 1572872 | tf_op jit(solution)/shard_map/ppermute | solution.py:411
  78.9 20.1 %collective-permute-start.18 = (f32[2,128,512]{2,1,0:T(8,128)S(1)}, f32[2,128,512]{2,1,0:T(8,128)S(1)}, u32[]{:S(2)}, u32[]{:S(2)}) collective-permute-start(f32[2,128,512]{2,1,0:T(8,128)S(1)} %get-tuple-element.117), channel_id=1, source_target_pairs={{0,2},{2,0},{4,6},{6,4},{8,10},{10,8},{12,14},{14,12},{1,3},{3,1},... | collective-permute-start | bytes 1572872 | tf_op jit(solution)/shard_map/ppermute | solution.py:260
  80.0 10.0 %collective-permute-start.21 = (f32[128,512]{1,0:T(8,128)S(1)}, f32[128,512]{1,0:T(8,128)S(1)}, u32[]{:S(2)}, u32[]{:S(2)}) collective-permute-start(f32[128,512]{1,0:T(8,128)S(1)} %bitcast_add_fusion.5), channel_id=1, source_target_pairs={{4,12},{6,14},{8,0},{10,2},{5,13},{7,15},{9,1},{11,3},{20,28},{22,... | collective-permute-start | bytes 786440 | tf_op jit(solution)/shard_map/ppermute | solution.py:411
  99.1 25.0 %collective-permute-start.22 = (f32[2,128,512]{2,1,0:T(8,128)S(1)}, f32[2,128,512]{2,1,0:T(8,128)S(1)}, u32[]{:S(2)}, u32[]{:S(2)}) collective-permute-start(f32[2,128,512]{2,1,0:T(8,128)S(1)} %add.122), channel_id=1, source_target_pairs={{0,4},{2,6},{12,8},{14,10},{1,5},{3,7},{13,9},{15,11},{16,20},{18,... | collective-permute-start | bytes 1572872 | tf_op jit(solution)/shard_map/ppermute | solution.py:411
  100.4 20.8 %collective-permute-start.23 = (f32[128,512]{1,0:T(8,128)S(1)}, f32[128,512]{1,0:T(8,128)S(1)}, u32[]{:S(2)}, u32[]{:S(2)}) collective-permute-start(f32[128,512]{1,0:T(8,128)S(1)} %select_bitcast_fusion.2), channel_id=1, source_target_pairs={{0,4},{2,6},{4,0},{6,2},{8,12},{10,14},{12,8},{14,10},{1,5},{3,7},... | collective-permute-start | bytes 786440 | tf_op jit(solution)/shard_map/ppermute | solution.py:411
  104.0 26.7 %collective-permute-start.17 = (f32[4,128,128]{2,1,0:T(8,128)S(1)}, f32[4,128,128]{2,1,0:T(8,128)S(1)}, u32[]{:S(2)}, u32[]{:S(2)}) collective-permute-start(f32[4,128,128]{2,1,0:T(8,128)S(1)} %get-tuple-element.134), channel_id=1, source_target_pairs={{0,2},{2,0},{4,6},{6,4},{8,10},{10,8},{12,14},{14,12},{1,3},{3,1},... | collective-permute-start | bytes 786440 | tf_op jit(solution)/shard_map/ppermute | solution.py:260
  104.8 21.6 %collective-permute-start.25 = (f32[128,512]{1,0:T(8,128)S(1)}, f32[128,512]{1,0:T(8,128)S(1)}, u32[]{:S(2)}, u32[]{:S(2)}) collective-permute-start(f32[128,512]{1,0:T(8,128)S(1)} %select_bitcast_fusion.1), channel_id=1, source_target_pairs={{4,8},{6,10},{8,4},{10,6},{5,9},{7,11},{9,5},{11,7},{20,24},{22,26... | collective-permute-start | bytes 786440 | tf_op jit(solution)/shard_map/ppermute | solution.py:411
  121.3 9.5 %copy-start.3 = (bf16[1,384,1024]{2,1,0:T(8,128)(2,1)S(1)}, bf16[1,384,1024]{2,1,0:T(8,128)(2,1)}, u32[]{:S(2)}) copy-start(bf16[1,384,1024]{2,1,0:T(8,128)(2,1)} %param.6) | copy-start | bytes 2359300
  121.3 9.5 %collective-permute-start.24 = (f32[128,512]{1,0:T(8,128)S(1)}, f32[128,512]{1,0:T(8,128)S(1)}, u32[]{:S(2)}, u32[]{:S(2)}) collective-permute-start(f32[128,512]{1,0:T(8,128)S(1)} %bitcast_add_fusion.4), channel_id=1, source_target_pairs={{4,12},{6,14},{8,0},{10,2},{5,13},{7,15},{9,1},{11,3},{20,28},{22,... | collective-permute-start | bytes 786440 | tf_op jit(solution)/shard_map/ppermute | solution.py:411
  124.1 11.1 %collective-permute-start.26 = (f32[128,512]{1,0:T(8,128)S(1)}, f32[128,512]{1,0:T(8,128)S(1)}, u32[]{:S(2)}, u32[]{:S(2)}) collective-permute-start(f32[128,512]{1,0:T(8,128)S(1)} %select_bitcast_fusion), channel_id=1, source_target_pairs={{4,8},{6,10},{8,4},{10,6},{5,9},{7,11},{9,5},{11,7},{20,24},{22,26... | collective-permute-start | bytes 786440 | tf_op jit(solution)/shard_map/ppermute | solution.py:411
